TPU v7x, 32 devices: a whole 2x2x4 slice. The times are simulated.
32 devices in a mesh: seq: 4 (over z), batch: 8 (over y, x, core).
Axes of the slice: x: 2, y: 2, z: 4, core: 2. Of those that a mesh axis runs over, the one named last changes fastest.
Arguments:
- inputs: bfloat16 [16, 512, 1024], P('batch', 'seq'), may hold values from -6 to 6
- lengths: int32 [16, 3], P('batch'), may hold values from 1 to 256, 512 in all within a row
- ln1_gain: bfloat16 [1024], replicated, may hold values from 0.5 to 1.5
- ln1_bias: bfloat16 [1024], replicated, may hold values from -1 to 1
- ln2_gain: bfloat16 [1024], replicated, may hold values from 0.5 to 1.5
- ln2_bias: bfloat16 [1024], replicated, may hold values from -1 to 1
- qkv_weight: bfloat16 [1024, 3072], replicated, may hold values from -0.1875 to 0.1875
- qkv_bias: bfloat16 [3072], replicated, may hold values from -1 to 1
- dense_weight: bfloat16 [1024, 1024], replicated, may hold values from -1.5 to 1.5
- dense_bias: bfloat16 [1024], replicated, may hold values from -1 to 1
- up_weight: bfloat16 [1024, 4096], replicated, may hold values from -0.1875 to 0.1875
- up_bias: bfloat16 [4096], replicated, may hold values from -1 to 1
- down_weight: bfloat16 [4096, 1024], replicated, may hold values from -0.09375 to 0.09375
- down_bias: bfloat16 [1024], replicated, may hold values from -1 to 1
- qmc_points: float32 [64, 64], replicated, may hold values from -4 to 4
- qmc_weights: float32 [64], replicated, may hold values from 0.25 to 4
- cotangent: bfloat16 [16, 512, 1024], P('batch', 'seq'), may hold values from -6 to 6
Outputs:
- output: bfloat16 [16, 512, 1024], P('batch', 'seq')
- input_grad: float32 [16, 512, 1024], P('batch', 'seq')
- ln1_gain_grad: float32 [1024], P('batch')
- ln1_bias_grad: float32 [1024], P('batch')
- ln2_gain_grad: float32 [1024], P('batch')
- ln2_bias_grad: float32 [1024], P('batch')
- qkv_weight_grad: float32 [1024, 3072], P('batch')
- qkv_bias_grad: float32 [3072], P('batch')
- dense_weight_grad: float32 [1024, 1024], P('batch')
- dense_bias_grad: float32 [1024], P('batch')
- up_weight_grad: float32 [1024, 4096], P('batch')
- up_bias_grad: float32 [4096], P('batch')
- down_weight_grad: float32 [4096, 1024], P('batch')
- down_bias_grad: float32 [1024], P('batch')
Inputs may be any that keep to these rules, and one draw needn't show every extreme that they name: `lengths`: each row sums to 512; its largest entry is exactly 256.
All inputs are finite; a program needn't handle non-finite values.
Results may differ from a plain program's by a relative error of at most 0.015.
Values sent between devices are 32-bit elements; how exact they have to be, the bound alone decides.
No kernel may reach another device: no remote copies, remote signals or barrier semaphores. Data moves between devices by JAX's collectives and lax.ppermute only.
A program may use at most 192 MiB of HBM per device.

v0:
```python
from functools import partial

import jax
import jax.numpy as jnp
from jax import lax
from jax.sharding import PartitionSpec as P

D = 1024
HEADS = 16
HEAD = 64
ROT = 16
FEAT = 64
GROUP = 64


HIGH = lax.Precision.HIGHEST
EPSILON = 1e-05
ROTARY_BASE = 10000.0


def prefix(part, axis, combine, identity, reverse):
    count = lax.axis_size(axis)
    place = lax.axis_index(axis)
    ahead = count - 1 - place if reverse else place
    gathered = jax.tree.map(lambda a: lax.all_gather(a, axis), part)
    state = jax.tree.map(lambda a, e: jnp.zeros_like(a) + jnp.asarray(e, a.dtype), part, identity)

    def one(step, state):
        source = count - 1 - step if reverse else step
        return combine(
            state, jax.tree.map(lambda a: lax.dynamic_index_in_dim(a, source, 0, False), gathered)
        )

    return lax.fori_loop(0, ahead, one, state)


def layer_norm(values, norm_gain, norm_shift):
    center = jnp.mean(values, axis=-1, keepdims=True)
    centered = values - center
    spread = jnp.mean(centered * centered, axis=-1, keepdims=True)
    return centered * lax.rsqrt(spread + EPSILON) * norm_gain + norm_shift


def rotary_tables(positions):
    half_rot = ROT // 2
    freqs_table = ROTARY_BASE ** (-2.0 * jnp.arange(half_rot, dtype=jnp.float32) / ROT)
    angles = positions.astype(jnp.float32)[:, None] * freqs_table[None, :]
    angles = jnp.concatenate([angles, angles], axis=-1)
    return (jnp.cos(angles), jnp.sin(angles))


def rotate(heads_in, cos_table, sin_table):
    half_rot = ROT // 2
    rotary_part = heads_in[..., :ROT]
    turned = jnp.concatenate([-rotary_part[..., half_rot:], rotary_part[..., :half_rot]], axis=-1)
    rotated = rotary_part * cos_table[:, None, :] + turned * sin_table[:, None, :]
    return jnp.concatenate([rotated, heads_in[..., ROT:]], axis=-1)


def dct_matrix():
    freq_rows = jnp.arange(HEAD, dtype=jnp.float32)[:, None]
    sample_cols = jnp.arange(HEAD, dtype=jnp.float32)[None, :]
    cosines = jnp.cos(jnp.pi * (sample_cols + 0.5) * freq_rows / HEAD) * jnp.sqrt(2.0 / HEAD)
    return jnp.where(freq_rows == 0.0, cosines * jnp.sqrt(0.5), cosines)


def feature_map(heads_in, dct_basis, points, feature_weights):
    scaled = heads_in * HEAD ** (-0.25)
    spectrum = jnp.einsum("...n,kn->...k", scaled, dct_basis, precision=HIGH)
    projected = jnp.einsum("...k,km->...m", spectrum, points, precision=HIGH)
    energy = 0.5 * jnp.sum(scaled * scaled, axis=-1, keepdims=True)
    return feature_weights * jnp.exp(projected - energy)


def chain_states(earlier, later):
    passing = 1.0 - later[2]
    return (
        later[0] + passing[:, None, None, None] * earlier[0],
        later[1] + passing[:, None, None] * earlier[1],
        jnp.maximum(earlier[2], later[2]),
    )


def shards(
    inputs,
    lengths,
    ln1_gain,
    ln1_bias,
    ln2_gain,
    ln2_bias,
    qkv_weight,
    qkv_bias,
    dense_weight,
    dense_bias,
    up_weight,
    up_bias,
    down_weight,
    down_bias,
    qmc_points,
    qmc_weights,
    cotangent,
):
    narrow = jnp.bfloat16
    wide_type = jnp.float32
    seqs_here, context = (inputs.shape[0], inputs.shape[1])
    group_count = context // GROUP
    positions = lax.axis_index("seq") * context + jnp.arange(context, dtype=jnp.int32)
    doc_starts = jnp.cumsum(lengths, axis=1) - lengths
    doc_ids = (
        jnp.sum((doc_starts[:, None, :] <= positions[None, :, None]).astype(jnp.int32), axis=2) - 1
    )
    group_first = positions[::GROUP] - 1
    before = (
        jnp.sum((doc_starts[:, None, :] <= group_first[None, :, None]).astype(jnp.int32), axis=2)
        - 1
    )
    group_ids = doc_ids.reshape(seqs_here, group_count, GROUP)
    group_ends = group_ids[:, :, -1]
    entry_doc = before[:, 0]
    last_doc = doc_ids[:, -1]
    order_index = jnp.arange(group_count)
    token_index = jnp.arange(GROUP)
    use_state = (group_ids == before[:, :, None]).astype(wide_type)
    keep_keys = (group_ids == group_ends[:, :, None]).astype(wide_type)
    causal = token_index[:, None] >= token_index[None, :]
    intra_mask = ((group_ids[..., :, None] == group_ids[..., None, :]) & causal).astype(wide_type)
    carry_in = (before == entry_doc[:, None]).astype(wide_type)
    link_mask = (
        (group_ends[:, None, :] == before[:, :, None])
        & (order_index[:, None] > order_index[None, :])
    ).astype(wide_type)
    to_end = (group_ends == last_doc[:, None]).astype(wide_type)
    reset_flag = (last_doc != entry_doc).astype(wide_type)
    inputs_wide = inputs.astype(wide_type)
    normed_attn, attn_norm_back = jax.vjp(
        layer_norm, inputs_wide, ln1_gain.astype(wide_type), ln1_bias.astype(wide_type)
    )
    normed_mlp, mlp_norm_back = jax.vjp(
        layer_norm, inputs_wide, ln2_gain.astype(wide_type), ln2_bias.astype(wide_type)
    )
    attn_in = normed_attn.astype(narrow)
    mlp_in = normed_mlp.astype(narrow)
    qkv_proj = (
        jnp.dot(attn_in, qkv_weight, preferred_element_type=wide_type) + qkv_bias.astype(wide_type)
    ).reshape(seqs_here, context, HEADS, 3 * HEAD)
    cos_table, sin_table = rotary_tables(positions)
    dct_basis = dct_matrix()

    def both_features(query_heads, key_heads):
        return (
            feature_map(
                rotate(query_heads, cos_table, sin_table), dct_basis, qmc_points, qmc_weights
            ),
            feature_map(
                rotate(key_heads, cos_table, sin_table), dct_basis, qmc_points, qmc_weights
            ),
        )

    feats_pair, feature_back = jax.vjp(
        both_features, qkv_proj[..., :HEAD], qkv_proj[..., HEAD : 2 * HEAD]
    )
    shape_groups = (seqs_here, group_count, GROUP, HEADS)
    query_low = feats_pair[0].astype(narrow).reshape(shape_groups + (FEAT,))
    key_low = feats_pair[1].astype(narrow).reshape(shape_groups + (FEAT,))
    value_low = qkv_proj[..., 2 * HEAD :].astype(narrow).reshape(shape_groups + (HEAD,))
    query_wide = query_low.astype(wide_type)
    keep_narrow = keep_keys.astype(narrow)
    key_kept = key_low * keep_narrow[..., None, None]
    local_state = jnp.einsum(
        "bcshm,bcshe->bchme", key_kept, value_low, preferred_element_type=wide_type
    )
    local_norm = jnp.einsum(
        "bcshm,bcs->bchm", key_low, keep_narrow, preferred_element_type=wide_type
    )
    out_state = jnp.einsum("bc,bchme->bhme", to_end, local_state, precision=HIGH)
    out_norm = jnp.einsum("bc,bchm->bhm", to_end, local_norm, precision=HIGH)
    zero_state = jnp.zeros_like(out_state)
    zero_norm = jnp.zeros_like(out_norm)
    zero_flag = jnp.zeros_like(reset_flag)
    in_state, in_norm, flag_seen = prefix(
        (out_state, out_norm, reset_flag),
        "seq",
        chain_states,
        (zero_state, zero_norm, zero_flag),
        False,
    )
    group_state = carry_in[..., None, None, None] * in_state[:, None] + jnp.einsum(
        "bcd,bdhme->bchme", link_mask, local_state, precision=HIGH
    )
    group_norm = carry_in[..., None, None] * in_norm[:, None] + jnp.einsum(
        "bcd,bdhm->bchm", link_mask, local_norm, precision=HIGH
    )
    state_low = group_state.astype(narrow)
    scores = (
        jnp.einsum("bcthm,bcshm->bchts", query_low, key_low, preferred_element_type=wide_type)
        * intra_mask[:, :, None]
    )
    scores_low = scores.astype(narrow)
    numerator = jnp.einsum(
        "bchts,bcshe->bcthe", scores_low, value_low, preferred_element_type=wide_type
    ) + use_state[..., None, None] * jnp.einsum(
        "bcthm,bchme->bcthe", query_low, state_low, preferred_element_type=wide_type
    )
    denominator = jnp.swapaxes(jnp.sum(scores_low.astype(wide_type), axis=-1), 2, 3) + use_state[
        ..., None
    ] * jnp.einsum("bcthm,bchm->bcth", query_wide, group_norm, precision=HIGH)
    heads_out = numerator / denominator[..., None]
    attn_low = heads_out.reshape(seqs_here, context, D).astype(narrow)
    attn_out = jnp.dot(
        attn_low, dense_weight, preferred_element_type=wide_type
    ) + dense_bias.astype(wide_type)
    up_proj = jnp.dot(mlp_in, up_weight, preferred_element_type=wide_type) + up_bias.astype(
        wide_type
    )
    activation, gelu_back = jax.vjp(partial(jax.nn.gelu, approximate=False), up_proj)
    act_low = activation.astype(narrow)
    mlp_out = jnp.dot(act_low, down_weight, preferred_element_type=wide_type) + down_bias.astype(
        wide_type
    )
    output = (inputs_wide + attn_out + mlp_out).astype(narrow)
    cot_wide = cotangent.astype(wide_type)
    bias_grad = jnp.sum(cot_wide, axis=(0, 1))
    dense_grad = jnp.einsum("bti,btj->ij", attn_low, cotangent, preferred_element_type=wide_type)
    down_grad = jnp.einsum("bti,btj->ij", act_low, cotangent, preferred_element_type=wide_type)
    attn_grad = jnp.einsum("btj,ij->bti", cotangent, dense_weight, preferred_element_type=wide_type)
    act_grad = jnp.einsum("btj,ij->bti", cotangent, down_weight, preferred_element_type=wide_type)
    up_grad_low = gelu_back(act_grad)[0].astype(narrow)
    up_weight_grad = jnp.einsum(
        "bti,btj->ij", mlp_in, up_grad_low, preferred_element_type=wide_type
    )
    up_bias_grad = jnp.sum(up_grad_low.astype(wide_type), axis=(0, 1))
    mlp_norm_grad = jnp.einsum(
        "btj,ij->bti", up_grad_low, up_weight, preferred_element_type=wide_type
    )
    heads_grad = attn_grad.reshape(shape_groups + (HEAD,))
    numer_grad = (heads_grad / denominator[..., None]).astype(narrow)
    denom_grad = -jnp.sum(heads_grad * heads_out, axis=-1) / denominator
    scores_grad = (
        jnp.einsum("bcthe,bcshe->bchts", numer_grad, value_low, preferred_element_type=wide_type)
        + jnp.swapaxes(denom_grad, 2, 3)[..., None]
    )
    scores_grad_low = (scores_grad * intra_mask[:, :, None]).astype(narrow)
    numer_used = numer_grad * use_state.astype(narrow)[..., None, None]
    denom_used = denom_grad * use_state[..., None]
    query_grad = (
        jnp.einsum("bchts,bcshm->bcthm", scores_grad_low, key_low, preferred_element_type=wide_type)
        + jnp.einsum("bcthe,bchme->bcthm", numer_used, state_low, preferred_element_type=wide_type)
        + denom_used[..., None] * group_norm[:, :, None]
    )
    key_grad = jnp.einsum(
        "bchts,bcthm->bcshm", scores_grad_low, query_low, preferred_element_type=wide_type
    )
    value_grad = jnp.einsum(
        "bchts,bcthe->bcshe", scores_low, numer_grad, preferred_element_type=wide_type
    )
    state_grad = jnp.einsum(
        "bcthm,bcthe->bchme", query_low, numer_used, preferred_element_type=wide_type
    )
    norm_grad = jnp.einsum("bcthm,bcth->bchm", query_wide, denom_used, precision=HIGH)
    in_state_grad = jnp.einsum("bc,bchme->bhme", carry_in, state_grad, precision=HIGH)
    in_norm_grad = jnp.einsum("bc,bchm->bhm", carry_in, norm_grad, precision=HIGH)
    out_state_grad, out_norm_grad, flag_after = prefix(
        (in_state_grad, in_norm_grad, reset_flag),
        "seq",
        chain_states,
        (zero_state, zero_norm, zero_flag),
        True,
    )
    local_grad = (
        jnp.einsum("bcd,bchme->bdhme", link_mask, state_grad, precision=HIGH)
        + to_end[..., None, None, None] * out_state_grad[:, None]
    ).astype(narrow)
    local_norm_grad = (
        jnp.einsum("bcd,bchm->bdhm", link_mask, norm_grad, precision=HIGH)
        + to_end[..., None, None] * out_norm_grad[:, None]
    )
    keep_wide = keep_keys[..., None, None]
    key_grad = key_grad + keep_wide * (
        jnp.einsum("bcshe,bchme->bcshm", value_low, local_grad, preferred_element_type=wide_type)
        + local_norm_grad[:, :, None]
    )
    value_grad = value_grad + keep_wide * jnp.einsum(
        "bcshm,bchme->bcshe", key_low, local_grad, preferred_element_type=wide_type
    )
    heads_shape = (seqs_here, context, HEADS)
    query_heads_grad, key_heads_grad = feature_back(
        (query_grad.reshape(heads_shape + (FEAT,)), key_grad.reshape(heads_shape + (FEAT,)))
    )
    qkv_grad = (
        jnp.concatenate(
            [query_heads_grad, key_heads_grad, value_grad.reshape(heads_shape + (HEAD,))], axis=-1
        )
        .reshape(seqs_here, context, 3 * D)
        .astype(narrow)
    )
    qkv_weight_grad = jnp.einsum("bti,btj->ij", attn_in, qkv_grad, preferred_element_type=wide_type)
    qkv_bias_grad = jnp.sum(qkv_grad.astype(wide_type), axis=(0, 1))
    attn_norm_grad = jnp.einsum(
        "btj,ij->bti", qkv_grad, qkv_weight, preferred_element_type=wide_type
    )
    input_from_attn, attn_gain_grad, attn_shift_grad = attn_norm_back(attn_norm_grad)
    input_from_mlp, mlp_gain_grad, mlp_shift_grad = mlp_norm_back(mlp_norm_grad)
    input_grad = cot_wide + input_from_attn + input_from_mlp
    shared = (
        lax.psum_scatter(attn_gain_grad, "batch", scatter_dimension=0, tiled=True),
        lax.psum_scatter(attn_shift_grad, "batch", scatter_dimension=0, tiled=True),
        lax.psum_scatter(mlp_gain_grad, "batch", scatter_dimension=0, tiled=True),
        lax.psum_scatter(mlp_shift_grad, "batch", scatter_dimension=0, tiled=True),
        lax.psum_scatter(qkv_weight_grad, "batch", scatter_dimension=0, tiled=True),
        lax.psum_scatter(qkv_bias_grad, "batch", scatter_dimension=0, tiled=True),
        lax.psum_scatter(dense_grad, "batch", scatter_dimension=0, tiled=True),
        lax.psum_scatter(bias_grad, "batch", scatter_dimension=0, tiled=True),
        lax.psum_scatter(up_weight_grad, "batch", scatter_dimension=0, tiled=True),
        lax.psum_scatter(up_bias_grad, "batch", scatter_dimension=0, tiled=True),
        lax.psum_scatter(down_grad, "batch", scatter_dimension=0, tiled=True),
    )
    totals = lax.psum(
        (
            shared[0],
            shared[1],
            shared[2],
            shared[3],
            shared[4],
            shared[5],
            shared[6],
            shared[7],
            shared[8],
            shared[9],
            shared[10],
        ),
        "seq",
    )
    return (
        output,
        input_grad,
        totals[0],
        totals[1],
        totals[2],
        totals[3],
        totals[4],
        totals[5],
        totals[6],
        totals[7],
        totals[8],
        totals[9],
        totals[10],
        totals[7],
    )


def solution(mesh):
    placed = (
        P("batch", "seq", None),
        P("batch", None),
        P(),
        P(),
        P(),
        P(),
        P(),
        P(),
        P(),
        P(),
        P(),
        P(),
        P(),
        P(),
        P(),
        P(),
        P("batch", "seq", None),
    )
    return jax.shard_map(
        shards,
        mesh=mesh,
        in_specs=placed,
        out_specs=(
            P("batch", "seq", None),
            P("batch", "seq", None),
            P("batch"),
            P("batch"),
            P("batch"),
            P("batch"),
            P("batch", None),
            P("batch"),
            P("batch", None),
            P("batch"),
            P("batch", None),
            P("batch"),
            P("batch", None),
            P("batch"),
        ),
        check_vma=False,
    )
```

profile of v0, /device:TPU:0, one launch (start us, length us, event | category | flops | bytes accessed | tf_op | source)
XLA Modules:
  0.0 885.1 jit_solution(3447240641703507481)
XLA Ops:
  14.2 6.6 fusion.27
  20.7 3.9 copy.247
  43.6 3.8 multiply_convert_fusion.4
  47.4 3.2 reshape.429
  54.9 5.5 fusion.37
  62.2 23.9 %all-reduce.8 = f32[8]{0:T(128)S(1)} all-reduce(f32[8]{0:T(128)S(1)} %dynamic-update-slice), channel_id=3, replica_groups=mesh['seq'=4,'batch'=8] {'seq'}, use_global_device_ids=true, to_apply=%add.8 | all-reduce | flops 8 | bytes 64
  86.1 3.7 copy.253
  90.4 2.8 fusion.30
  93.2 2.8 reshape.430
  96.0 3.0 copy.266
  99.0 3.2 reshape.428
  105.0 14.2 %all-gather.2 = f32[8,16,64]{2,1,0:T(8,128)S(1)} all-gather(f32[2,16,64]{2,1,0:T(8,128)S(1)} %bitcast.239), channel_id=4, replica_groups=mesh['seq'=4,'batch'=8] {'seq'}, dimensions={0}, use_global_device_ids=true | all-gather | bytes 40960 | tf_op jit(solution)/shard_map/all_gather | solution.py:25
  122.6 2.7 convert_reduce_fusion.2
  128.1 17.1 %all-gather.8.cloned.1.call-done = f32[8,16,64,64]{3,2,1,0:T(8,128)} async-done(((f32[2,16,64,64]{3,2,1,0:T(8,128)}), f32[8,16,64,64]{3,2,1,0:T(8,128)}) %all-gather.8.cloned.1.call-update) | async-done | bytes 2097168 | tf_op jit(solution)/shard_map/all_gather | solution.py:25
  145.4 9.0 %add_convert_fusion.2 = bf16[2,2,16,64,64]{4,1,3,2,0:T(2,128)(2,1)S(1)} fusion(f32[2,2,16,64,64]{4,3,2,1,0:T(8,128)} %copy-done.31, f32[2,16,64,64]{3,2,1,0:T(8,128)S(1)} %get-tuple-element.186, f32[2,2]{1,0:T(2,128)} %get-tuple-element.258, pred[2,2,2]{1,2,0:T(4,128)(4,1)} %compare_and_fusion), kind=kOutput, calls=%fused_computation.65 | convolution fusion | flops 7077888 | bytes 2097176 | tf_op jit(solution)/shard_map/bcd,bdhme->bchme/dot_general | solution.py:187
  161.1 5.5 fusion.34
  166.7 2.9 copy.265
  178.1 3.0 copy.276
  181.0 3.4 reshape.431
  186.4 18.6 %all-gather.4 = f32[8,16,64]{2,1,0:T(8,128)S(1)} all-gather(f32[2,16,64]{2,1,0:T(8,128)S(1)} %bitcast.240), channel_id=6, replica_groups=mesh['seq'=4,'batch'=8] {'seq'}, dimensions={0}, use_global_device_ids=true | all-gather | bytes 40960 | tf_op jit(solution)/shard_map/all_gather | solution.py:25
  205.0 3.9 convolution_bitcast_fusion.3
  208.9 3.9 fusion.118
  212.9 3.6 fusion.108
  218.5 35.4 %all-gather.10.cloned.1.call-done = f32[8,16,64,64]{3,2,1,0:T(8,128)} async-done(((f32[2,16,64,64]{3,2,1,0:T(8,128)}), f32[8,16,64,64]{3,2,1,0:T(8,128)}) %all-gather.10.cloned.1.call-update) | async-done | bytes 2097168 | tf_op jit(solution)/shard_map/all_gather | solution.py:25
  254.0 7.4 while.31
  261.4 8.4 add_convert_fusion.1
  269.8 3.8 copy.287
  273.6 3.0 add_bitcast_fusion
  278.7 3.1 reshape.433
  282.8 2.8 add_bitcast_fusion.1
  285.6 3.0 copy.285
  288.5 3.5 reshape.432
  301.8 6.5 convolution_bitcast_fusion.2
  309.1 7.1 fusion.81
  316.2 10.7 %multiply_convert_fusion = (bf16[2,128,4096]{2,1,0:T(8,128)(2,1)}, f32[2,128,4096]{2,1,0:T(8,128)S(1)}) fusion(f32[2,128,4096]{2,1,0:T(8,128)S(1)} %get-tuple-element.293, u8[128,4096]{1,0:T(8,128)(4,1)S(1)} %get-tuple-element.191, u8[128,4096]{1,0:T(8,128)(4,1)S(1)} %get-tuple-element.190), kind=kLoop, calls=%fused_computation.35 | loop fusion | flops 73400320 | bytes 11534336 | tf_op jit(solution)/shard_map/convert_element_type | solution.py:216
  326.9 8.3 convert_reduce_fusion
  336.5 8.9 %convolution_bitcast_fusion.1 = f32[1024,4096]{1,0:T(8,128)} fusion(bf16[2,128,4096]{2,1,0:T(8,128)(2,1)S(1)} %get-tuple-element.300, bf16[2,128,1024]{2,1,0:T(8,128)(2,1)S(1)} %copy-done.4, f32[1024]{0:T(1024)S(1)} %convert_element_type.209, f32[1024]{0:T(1024)S(1)} %convert_element_type.208, f32[2,128]{1,0:T(2,128)S(1)} %fusion.168, ...), kind=kOutput, calls=%fused_computation.11 | convolution fusion | flops 2149056512 | bytes 19408896 | tf_op jit(solution)/shard_map/bti,btj->ij/dot_general | solution.py:228
  345.4 9.9 %convolution_bitcast_fusion = f32[4096,1024]{1,0:T(8,128)} fusion(bf16[2,128,4096]{2,1,0:T(8,128)(2,1)} %get-tuple-element.262, bf16[2,128,1024]{2,1,0:T(8,128)(2,1)S(1)} %copy-done.20), kind=kOutput, calls=%fused_computation.10 | convolution fusion | flops 2147483648 | bytes 19398656 | tf_op jit(solution)/shard_map/bti,btj->ij/dot_general | solution.py:224
  355.7 47.6 %reduce-scatter.5.cloned.1.call-done = f32[128,3072]{1,0:T(8,128)} async-done(((f32[1024,3072]{1,0:T(8,128)}), f32[128,3072]{1,0:T(8,128)}) %reduce-scatter.5.cloned.1.call-update) | async-done | bytes 1572880 | tf_op jit(solution)/shard_map/reduce_scatter | solution.py:309
  403.3 119.8 %reduce-scatter.9.cloned.1.call-done = f32[128,4096]{1,0:T(8,128)} async-done(((f32[1024,4096]{1,0:T(8,128)}), f32[128,4096]{1,0:T(8,128)}) %reduce-scatter.9.cloned.1.call-update) | async-done | bytes 2097168 | tf_op jit(solution)/shard_map/reduce_scatter | solution.py:313
  523.1 119.8 %reduce-scatter.11.cloned.1.call-done = f32[512,1024]{1,0:T(8,128)} async-done(((f32[4096,1024]{1,0:T(8,128)}), f32[512,1024]{1,0:T(8,128)}) %reduce-scatter.11.cloned.1.call-update) | async-done | bytes 2097168 | tf_op jit(solution)/shard_map/reduce_scatter | solution.py:315
  645.6 7.5 fusion.8
  653.1 5.8 fusion.62
  660.5 5.7 fusion.187
  668.9 25.6 %all-reduce.16 = (f32[1024]{0:T(1024)S(1)}, f32[1024]{0:T(1024)S(1)}, f32[1024]{0:T(1024)S(1)}, f32[1024]{0:T(1024)S(1)}, f32[3072]{0:T(1024)S(1)}, /*index=5*/f32[1024]{0:T(1024)S(1)}, f32[4096]{0:T(1024)S(1)}) all-reduce(f32[1024]{0:T(1024)S(1)} %get-tuple-element.201, ...), channel_id=7, replica_groups=mesh['seq'=4,'batch'=8] {'batch'}, use_global_device_ids=true, to_apply=%region_20.21.clone | all-reduce | flops 12288 | bytes 98304
  695.0 15.0 %all-reduce.17 = (f32[128]{0:T(128)}, f32[128]{0:T(128)}, f32[128]{0:T(128)}, f32[128]{0:T(128)}, f32[384]{0:T(512)}, /*index=5*/f32[128]{0:T(128)S(1)}, f32[512]{0:T(512)}) all-reduce(f32[128]{0:T(128)S(1)} %dynamic-slice.2, f32[128]{0:T(128)S(1)} %dynamic-slice.4, ...), channel_id=1, replica_groups=mesh['seq'=4,'batch'=8] {'seq'}, use_global_device_ids=true, to_apply=%region_21.22 | all-reduce | flops 1536 | bytes 12288 | tf_op jit(solution)/shard_map/psum | solution.py:317
  710.0 160.2 %all-reduce.21.cloned.1.call-done = (f32[128,3072]{1,0:T(8,128)}, f32[128,1024]{1,0:T(8,128)}, f32[128,4096]{1,0:T(8,128)}, f32[512,1024]{1,0:T(8,128)}) async-done(((f32[128,3072]{1,0:T(8,128)}, f32[128,1024]{1,0:T(8,128)}, f32[128,4096]{1,0:T(8,128)}, f32[512,1024]{1,0:T(8,128)}), (f32[128,3072]{1,0:T(8,128)}, f32[128,1024]{1,0:T(8,128)}, f32[128,4096]{1,0:T(8,128)}, ...) | async-done | bytes 6291472 | tf_op jit(solution)/shard_map/psum | solution.py:317
  870.7 2.9 copy.424
  (307 shorter events, 92.3 us)
Async XLA Ops:
  7.2 83.2 %copy-start = (bf16[1024,1024]{1,0:T(8,128)(2,1)S(1)}, bf16[1024,1024]{1,0:T(8,128)(2,1)}, u32[]{:S(2)}) copy-start(bf16[1024,1024]{1,0:T(8,128)(2,1)} %param.29) | copy-start | bytes 6291460
  7.2 138.0 %all-gather.8.cloned.1.call-start = ((), (), s32[]{:S(2)}) async-start(), calls=%async_computation.8 | async-start | bytes 5242880 | tf_op jit(solution)/shard_map/all_gather | solution.py:25
  7.3 25.5 %copy-start.62 = (pred[64]{0:T(512)(128)(4,1)}, pred[64]{0:T(512)(128)(4,1)S(1)}, u32[]{:S(2)}) copy-start(pred[64]{0:T(512)(128)(4,1)S(1)} %iota_compare_fusion.2) | copy-start | bytes 196
  7.3 25.5 %copy-start.64 = (f32[64]{0:T(128)}, f32[64]{0:T(128)S(1)}, u32[]{:S(2)}) copy-start(f32[64]{0:T(128)S(1)} %add_multiply_fusion) | copy-start | bytes 772
  9.5 41.7 %copy-start.44 = (s32[2,2,64]{2,1,0:T(2,128)}, s32[2,2,64]{2,1,0:T(2,128)S(1)}, u32[]{:S(2)}) copy-start(s32[2,2,64]{2,1,0:T(2,128)S(1)} %sub.97) | copy-start | bytes 3076
  30.5 9.3 %copy-start.39 = (f32[64,64]{1,0:T(8,128)S(1)}, f32[64,64]{1,0:T(8,128)}, u32[]{:S(2)}) copy-start(f32[64,64]{1,0:T(8,128)} %param.35) | copy-start | bytes 49156
  32.8 10.8 %copy-start.60 = (f32[64]{0:T(128)S(1)}, f32[64]{0:T(128)}, u32[]{:S(2)}) copy-start(f32[64]{0:T(128)} %param.36) | copy-start | bytes 772
  35.7 26.0 %copy-start.53 = (s32[2,2]{1,0:T(2,128)}, s32[2,2]{1,0:T(2,128)S(1)}, u32[]{:S(2)}) copy-start(s32[2,2]{1,0:T(2,128)S(1)} %broadcast_add_fusion) | copy-start | bytes 52
  35.9 15.4 %copy-start.51 = (s32[2,2,1]{1,0,2:T(2,128)}, s32[2,2,1]{1,0,2:T(2,128)S(1)}, u32[]{:S(2)}) copy-start(s32[2,2,1]{1,0,2:T(2,128)S(1)} %copy.342) | copy-start | bytes 52
  39.8 85.5 %copy-start.1 = (bf16[2,2,64,16,64]{4,2,3,1,0:T(8,128)(2,1)}, bf16[2,2,64,16,64]{4,2,3,1,0:T(8,128)(2,1)S(1)}, u32[]{:S(2)}) copy-start(bf16[2,2,64,16,64]{4,2,3,1,0:T(8,128)(2,1)S(1)} %copy.259) | copy-start | bytes 1572868
  51.9 8.6 copy-start.78
  60.4 193.5 %all-gather.10.cloned.1.call-start = ((), (), s32[]{:S(2)}) async-start(), calls=%async_computation.9 | async-start | bytes 5242880 | tf_op jit(solution)/shard_map/all_gather | solution.py:25
  96.0 23.2 %copy-start.54 = (s32[2,2]{1,0:T(2,128)S(1)}, s32[2,2]{1,0:T(2,128)}, u32[]{:S(2)}) copy-start(s32[2,2]{1,0:T(2,128)} %copy-done.53) | copy-start | bytes 52
  96.0 24.5 %copy-start.52 = (s32[2,2,1]{1,0,2:T(2,128)S(1)}, s32[2,2,1]{1,0,2:T(2,128)}, u32[]{:S(2)}) copy-start(s32[2,2,1]{1,0,2:T(2,128)} %copy-done.51) | copy-start | bytes 52
  96.0 25.9 %copy-start.45 = (s32[2,2,64]{2,1,0:T(2,128)S(1)}, s32[2,2,64]{2,1,0:T(2,128)}, u32[]{:S(2)}) copy-start(s32[2,2,64]{2,1,0:T(2,128)} %copy-done.44) | copy-start | bytes 3076
  145.4 9.2 %copy-start.71 = (pred[2,2,2]{1,2,0:T(4,128)(4,1)S(1)}, pred[2,2,2]{1,2,0:T(4,128)(4,1)}, u32[]{:S(2)}) copy-start(pred[2,2,2]{1,2,0:T(4,128)(4,1)} %compare_and_fusion) | copy-start | bytes 28
  145.4 9.2 %copy-start.73 = (f32[2,2]{1,0:T(2,128)S(1)}, f32[2,2]{1,0:T(2,128)}, u32[]{:S(2)}) copy-start(f32[2,2]{1,0:T(2,128)} %get-tuple-element.258) | copy-start | bytes 52
  145.4 9.2 %copy-start.81 = (f32[2,2,1,16,64]{4,2,3,1,0:T(1,128)S(1)}, f32[2,2,1,16,64]{4,2,3,1,0:T(1,128)}, u32[]{:S(2)}) copy-start(f32[2,2,1,16,64]{4,2,3,1,0:T(1,128)} %copy-done.80) | copy-start | bytes 49156
  145.4 9.4 %copy-start.16 = (bf16[2,2,64,16,64]{2,1,4,3,0:T(2,128)(2,1)S(1)}, bf16[2,2,64,16,64]{2,1,4,3,0:T(2,128)(2,1)}, u32[]{:S(2)}) copy-start(bf16[2,2,64,16,64]{2,1,4,3,0:T(2,128)(2,1)} %reshape.428) | copy-start | bytes 1572868
  145.4 11.0 %copy-start.42 = (f32[2,2,16,64]{3,2,1,0:T(8,128)S(1)}, f32[2,2,16,64]{3,2,1,0:T(8,128)}, u32[]{:S(2)}) copy-start(f32[2,2,16,64]{3,2,1,0:T(8,128)} %get-tuple-element.295) | copy-start | bytes 49156
  145.4 11.0 %copy-start.46 = (f32[2,2,64]{2,1,0:T(2,128)S(1)}, f32[2,2,64]{2,1,0:T(2,128)}, u32[]{:S(2)}) copy-start(f32[2,2,64]{2,1,0:T(2,128)} %get-tuple-element.257) | copy-start | bytes 3076
  145.4 11.0 %copy-start.34 = (f32[2,2,64,16,64]{2,4,3,1,0:T(8,128)S(1)}, f32[2,2,64,16,64]{2,4,3,1,0:T(8,128)}, u32[]{:S(2)}) copy-start(f32[2,2,64,16,64]{2,4,3,1,0:T(8,128)} %copy.266) | copy-start | bytes 3145732
  145.4 11.0 %copy-start.35 = (f32[2,2,16,64,64]{4,3,2,1,0:T(8,128)S(1)}, f32[2,2,16,64,64]{4,3,2,1,0:T(8,128)}, u32[]{:S(2)}) copy-start(f32[2,2,16,64,64]{4,3,2,1,0:T(8,128)} %fusion.196) | copy-start | bytes 3145732
  159.0 7.6 copy-start.49
  161.1 11.1 %copy-start.47 = (f32[2,2,64]{2,1,0:T(2,128)S(1)}, f32[2,2,64]{2,1,0:T(2,128)}, u32[]{:S(2)}) copy-start(f32[2,2,64]{2,1,0:T(2,128)} %get-tuple-element.257) | copy-start | bytes 3076
  161.1 12.9 %copy-start.2 = (bf16[2,2,64,16,64]{4,2,3,1,0:T(8,128)(2,1)S(1)}, bf16[2,2,64,16,64]{4,2,3,1,0:T(8,128)(2,1)}, u32[]{:S(2)}) copy-start(bf16[2,2,64,16,64]{4,2,3,1,0:T(8,128)(2,1)} %copy-done.1) | copy-start | bytes 1572868
  166.6 189.1 %reduce-scatter.7.cloned.1.call-start = ((), (), s32[]{:S(2)}) async-start(), calls=%async_computation.5 | async-start | bytes 4718592 | tf_op jit(solution)/shard_map/reduce_scatter | solution.py:311
  178.0 6.4 copy-start.17
  178.1 8.2 copy-start.75
  186.2 18.8 %copy-start.79 = (f32[2,2,16,1,64]{4,3,2,1,0:T(1,128)}, f32[2,2,16,1,64]{4,3,2,1,0:T(1,128)S(1)}, u32[]{:S(2)}) copy-start(f32[2,2,16,1,64]{4,3,2,1,0:T(1,128)S(1)} %fusion.104) | copy-start | bytes 49156
  208.9 7.5 copy-start.10
  208.9 7.5 copy-start.27
  218.4 184.9 %reduce-scatter.5.cloned.1.call-start = ((), (), s32[]{:S(2)}) async-start(), calls=%async_computation.4 | async-start | bytes 14155776 | tf_op jit(solution)/shard_map/reduce_scatter | solution.py:309
  261.4 12.2 %copy-start.50 = (f32[2,2,64]{2,1,0:T(2,128)S(1)}, f32[2,2,64]{2,1,0:T(2,128)}, u32[]{:S(2)}) copy-start(f32[2,2,64]{2,1,0:T(2,128)} %get-tuple-element.290) | copy-start | bytes 3076
  273.6 8.2 copy-start.70
  273.6 8.2 copy-start.72
  273.6 9.1 %copy-start.3 = (bf16[2,2,64,16,64]{4,2,3,1,0:T(8,128)(2,1)S(1)}, bf16[2,2,64,16,64]{4,2,3,1,0:T(8,128)(2,1)}, u32[]{:S(2)}) copy-start(bf16[2,2,64,16,64]{4,2,3,1,0:T(8,128)(2,1)} %copy-done.1) | copy-start | bytes 1572868
  285.6 6.5 copy-start.6
  285.6 6.5 copy-start.61
  308.4 214.8 %reduce-scatter.9.cloned.1.call-start = ((), (), s32[]{:S(2)}) async-start(), calls=%async_computation.6 | async-start | bytes 18874368 | tf_op jit(solution)/shard_map/reduce_scatter | solution.py:313
  316.2 10.7 %copy-start.20 = (bf16[2,128,1024]{2,1,0:T(8,128)(2,1)S(1)}, bf16[2,128,1024]{2,1,0:T(8,128)(2,1)}, u32[]{:S(2)}) copy-start(bf16[2,128,1024]{2,1,0:T(8,128)(2,1)} %param.37) | copy-start | bytes 1572868
  345.4 297.6 %reduce-scatter.11.cloned.1.call-start = ((), (), s32[]{:S(2)}) async-start(), calls=%async_computation.7 | async-start | bytes 18874368 | tf_op jit(solution)/shard_map/reduce_scatter | solution.py:315
  355.4 287.6 %copy-start.77 = (u32[32]{0:T(128)S(1)}, u32[32]{0:T(128)}, u32[]{:S(2)}) copy-start(u32[32]{0:T(128)} %constant.214) | copy-start | bytes 388
  355.4 290.1 %copy-start.68 = (bf16[1024]{0:T(1024)(128)(2,1)S(1)}, bf16[1024]{0:T(1024)(128)(2,1)}, u32[]{:S(2)}) copy-start(bf16[1024]{0:T(1024)(128)(2,1)} %param.30) | copy-start | bytes 6148
  355.4 290.1 %copy-start.69 = (bf16[1024]{0:T(1024)(128)(2,1)S(1)}, bf16[1024]{0:T(1024)(128)(2,1)}, u32[]{:S(2)}) copy-start(bf16[1024]{0:T(1024)(128)(2,1)} %param.34) | copy-start | bytes 6148
  355.4 514.7 %all-reduce.21.cloned.1.call-start = ((), (), s32[]{:S(2)}) async-start(), calls=%async_computation.10 | async-start | bytes 12582912 | tf_op jit(solution)/shard_map/psum | solution.py:317
  645.6 7.5 copy-start.19
  710.0 166.8 %copy-start.76 = (f32[128]{0:T(128)}, f32[128]{0:T(128)S(1)}, u32[]{:S(2)}) copy-start(f32[128]{0:T(128)S(1)} %get-tuple-element.491) | copy-start | bytes 1540
  (41 other events, 109.1 us)
Sparse Core Ops, SparseCore 0:
  60.5 84.6 all-gather.7
  166.7 87.1 all-gather.9
  257.2 49.8 reduce-scatter.6
  310.9 92.4 reduce-scatter.4
  407.1 115.9 reduce-scatter.8
  527.0 115.9 reduce-scatter.10
  645.8 224.3 all-reduce.20
where the time goes:
time: 889 us; the launch traced here: 885 us
  waiting for transfers between devices  500 us (56%)
  matrix products  152 us (17%)
  blocking collectives  97.2 us (11%)
  local copies, waits for them, and re-layouts  77.1 us (9%)
  other arithmetic  39.5 us (4%)
  between operations  18.1 us (2%)
    psum x1, waiting for transfers between devices, shards(): lax.psum((shared[0], shared[1], shared[2], shared[3], shared[4], shared[5...  160 us
    reduce_scatter x1, waiting for transfers between devices, shards(): lax.psum_scatter(down_grad, 'batch', scatter_dimension=0, tiled=True)  120 us
    reduce_scatter x1, waiting for transfers between devices, shards(): lax.psum_scatter(up_weight_grad, 'batch', scatter_dimension=0, tiled=True)  120 us
    all_gather x2, waiting for transfers between devices, prefix(): gathered = jax.tree.map(lambda a: lax.all_gather(a, axis), part)  52.5 us
    unnamed x2, blocking collectives  49.5 us
    reduce_scatter x1, waiting for transfers between devices, shards(): lax.psum_scatter(qkv_weight_grad, 'batch', scatter_dimension=0, tiled=True)  47.6 us
    all_gather x2, blocking collectives, prefix(): gathered = jax.tree.map(lambda a: lax.all_gather(a, axis), part)  32.8 us
    unnamed x181, local copies, waits for them, and re-layouts  21.7 us
  transfers between devices with their start and end apart: 7, of which 6 were waited for; matrix products, arithmetic and copies ran while one was open for 20% of the time, Pallas kernels for 0%

commit v1 on v0

--- a/solution.py
+++ b/solution.py
@@ -18,27 +18,109 @@
 ROTARY_BASE = 10000.0
 
 
-def prefix(part, axis, combine, identity, reverse):
+def shift_rows(value, axis, by):
     count = lax.axis_size(axis)
-    place = lax.axis_index(axis)
-    ahead = count - 1 - place if reverse else place
-    gathered = jax.tree.map(lambda a: lax.all_gather(a, axis), part)
-    state = jax.tree.map(lambda a, e: jnp.zeros_like(a) + jnp.asarray(e, a.dtype), part, identity)
-
-    def one(step, state):
-        source = count - 1 - step if reverse else step
-        return combine(
-            state, jax.tree.map(lambda a: lax.dynamic_index_in_dim(a, source, 0, False), gathered)
+    return lax.ppermute(
+        value, axis, [(i, i + by) for i in range(count) if 0 <= i + by < count]
+    )
+
+
+def carried(own, passing, axis, by):
+    hops = max(1, lax.axis_size(axis) // 2)
+    arrived = jax.tree.map(lambda a: shift_rows(a, axis, by), own)
+    for _ in range(hops - 1):
+        arrived = jax.tree.map(
+            lambda a, e: shift_rows(
+                a + passing.reshape(passing.shape + (1,) * (a.ndim - 1)) * e, axis, by
+            ),
+            own,
+            arrived,
         )
-
-    return lax.fori_loop(0, ahead, one, state)
-
-
-def layer_norm(values, norm_gain, norm_shift):
-    center = jnp.mean(values, axis=-1, keepdims=True)
-    centered = values - center
-    spread = jnp.mean(centered * centered, axis=-1, keepdims=True)
-    return centered * lax.rsqrt(spread + EPSILON) * norm_gain + norm_shift
+    return arrived
+
+
+def swap(value, bit):
+    count = lax.axis_size("batch")
+    return lax.ppermute(value, "batch", [(i, i ^ (1 << bit)) for i in range(count)])
+
+
+def line_sum(part):
+    count = lax.axis_size("seq")
+    if count == 1:
+        return part
+    if count % 2:
+        return lax.psum(part, "seq")
+    place = lax.axis_index("seq")
+    half = count // 2
+    for k in range(half - 1):
+        part = part + lax.ppermute(part, "seq", [(k, k + 1), (count - 1 - k, count - 2 - k)])
+    part = part + lax.ppermute(part, "seq", [(half - 1, half), (half, half - 1)])
+    for k in range(half - 2, -1, -1):
+        back = lax.ppermute(part, "seq", [(k + 1, k), (count - 2 - k, count - 1 - k)])
+        part = jnp.where((place == k) | (place == count - 1 - k), back, part)
+    return part
+
+
+def owner_order(bits):
+    return sorted(
+        range(1 << len(bits)), key=lambda r: tuple(-((r >> bit) & 1) for bit in bits)
+    )
+
+
+def halving(send, keep, bits, shift):
+    for step, bit in enumerate(bits):
+        held = keep + swap(send, bit + shift)
+        if step + 1 < len(bits):
+            half = held.shape[0] // 2
+            send, keep = held[:half], held[half:]
+    return held
+
+
+def scatter_vectors(vectors):
+    count = lax.axis_size("batch")
+    me = lax.axis_index("batch")
+    pieces = jnp.concatenate([v.reshape(count, -1) for v in vectors], axis=1)
+    bits = list(range(count.bit_length() - 1))
+    order = owner_order(bits)
+    rows = [lax.dynamic_slice_in_dim(pieces, r ^ me, 1, 0) for r in order]
+    half = count // 2
+    held = halving(jnp.concatenate(rows[:half]), jnp.concatenate(rows[half:]), bits, 0)
+    total = line_sum(held)[0]
+    out, at = [], 0
+    for v in vectors:
+        out.append(total[at : at + v.shape[0] // count])
+        at += v.shape[0] // count
+    return out
+
+
+def owner_blocks(features, width, order, at=0, size=None):
+    count = lax.axis_size("batch")
+    me = lax.axis_index("batch")
+    size = width if size is None else size
+
+    def pick(rel):
+        return lax.dynamic_slice_in_dim(features, (rel ^ me) * width + at, size, 1)
+
+    mine = jnp.concatenate([pick(2 * r) for r in order], axis=1)
+    other = jnp.concatenate([pick(2 * r + 1) for r in order], axis=1)
+    return mine, other
+
+
+def pair_gather(mine, other):
+    arrived = swap(other.astype(jnp.float32), 0)
+    arrived = arrived * jnp.where(lax.axis_index("seq") < lax.axis_size("seq"), 1.0, 0.5)
+    return jnp.concatenate([mine, arrived.astype(jnp.bfloat16)], axis=0)
+
+
+def grad_scatter(left, right, bits):
+    half = left.shape[1] // 2
+    send = lax.dot_general(
+        left[:, :half], right, (((0,), (0,)), ((), ())), preferred_element_type=jnp.float32
+    )
+    keep = lax.dot_general(
+        left[:, half:], right, (((0,), (0,)), ((), ())), preferred_element_type=jnp.float32
+    )
+    return line_sum(halving(send, keep, bits, 1))
 
 
 def rotary_tables(positions):
@@ -70,15 +152,6 @@
     projected = jnp.einsum("...k,km->...m", spectrum, points, precision=HIGH)
     energy = 0.5 * jnp.sum(scaled * scaled, axis=-1, keepdims=True)
     return feature_weights * jnp.exp(projected - energy)
-
-
-def chain_states(earlier, later):
-    passing = 1.0 - later[2]
-    return (
-        later[0] + passing[:, None, None, None] * earlier[0],
-        later[1] + passing[:, None, None] * earlier[1],
-        jnp.maximum(earlier[2], later[2]),
-    )
 
 
 def shards(
@@ -132,14 +205,33 @@
     to_end = (group_ends == last_doc[:, None]).astype(wide_type)
     reset_flag = (last_doc != entry_doc).astype(wide_type)
     inputs_wide = inputs.astype(wide_type)
-    normed_attn, attn_norm_back = jax.vjp(
-        layer_norm, inputs_wide, ln1_gain.astype(wide_type), ln1_bias.astype(wide_type)
-    )
-    normed_mlp, mlp_norm_back = jax.vjp(
-        layer_norm, inputs_wide, ln2_gain.astype(wide_type), ln2_bias.astype(wide_type)
-    )
-    attn_in = normed_attn.astype(narrow)
-    mlp_in = normed_mlp.astype(narrow)
+    owners = lax.axis_size("batch")
+    owner_bits = list(range(owners.bit_length() - 2))
+    orders = (owner_bits, owner_bits[::-1])
+    flat = (seqs_here * context, D)
+    center = jnp.mean(inputs_wide, axis=-1, keepdims=True)
+    centered = inputs_wide - center
+    spread = jnp.mean(centered * centered, axis=-1, keepdims=True)
+    inv_spread = lax.rsqrt(spread + EPSILON)
+    normed = centered * inv_spread
+    attn_in = (normed * ln1_gain.astype(wide_type) + ln1_bias.astype(wide_type)).astype(narrow)
+    mlp_in = (normed * ln2_gain.astype(wide_type) + ln2_bias.astype(wide_type)).astype(narrow)
+    cot_flat = cotangent.reshape(flat)
+    cot_pair = pair_gather(cot_flat, cot_flat)
+    norm_pairs = []
+    for bits in orders:
+        mine_a, other_a = owner_blocks(attn_in.reshape(flat), D // owners, owner_order(bits))
+        mine_m, other_m = owner_blocks(mlp_in.reshape(flat), D // owners, owner_order(bits))
+        norm_pairs.append(
+            jnp.split(
+                pair_gather(
+                    jnp.concatenate([mine_a, mine_m], axis=1),
+                    jnp.concatenate([other_a, other_m], axis=1),
+                ),
+                2,
+                axis=1,
+            )
+        )
     qkv_proj = (
         jnp.dot(attn_in, qkv_weight, preferred_element_type=wide_type) + qkv_bias.astype(wide_type)
     ).reshape(seqs_here, context, HEADS, 3 * HEAD)
@@ -174,16 +266,8 @@
     )
     out_state = jnp.einsum("bc,bchme->bhme", to_end, local_state, precision=HIGH)
     out_norm = jnp.einsum("bc,bchm->bhm", to_end, local_norm, precision=HIGH)
-    zero_state = jnp.zeros_like(out_state)
-    zero_norm = jnp.zeros_like(out_norm)
-    zero_flag = jnp.zeros_like(reset_flag)
-    in_state, in_norm, flag_seen = prefix(
-        (out_state, out_norm, reset_flag),
-        "seq",
-        chain_states,
-        (zero_state, zero_norm, zero_flag),
-        False,
-    )
+    passing = 1.0 - reset_flag
+    in_state, in_norm = carried((out_state, out_norm), passing, "seq", 1)
     group_state = carry_in[..., None, None, None] * in_state[:, None] + jnp.einsum(
         "bcd,bdhme->bchme", link_mask, local_state, precision=HIGH
     )
@@ -220,13 +304,31 @@
     output = (inputs_wide + attn_out + mlp_out).astype(narrow)
     cot_wide = cotangent.astype(wide_type)
     bias_grad = jnp.sum(cot_wide, axis=(0, 1))
-    dense_grad = jnp.einsum("bti,btj->ij", attn_low, cotangent, preferred_element_type=wide_type)
-    down_grad = jnp.einsum("bti,btj->ij", act_low, cotangent, preferred_element_type=wide_type)
+    down_parts = []
+    rows_each = 4 * D // owners
+    for part, bits in enumerate(orders):
+        mine, other = owner_blocks(
+            act_low.reshape(-1, 4 * D),
+            rows_each,
+            owner_order(bits),
+            part * rows_each // 2,
+            rows_each // 2,
+        )
+        down_parts.append(grad_scatter(pair_gather(mine, other), cot_pair, bits))
+    down_total = jnp.concatenate(down_parts, axis=0)
+    mine, other = owner_blocks(attn_low.reshape(flat), D // owners, owner_order(orders[0]))
+    dense_total = grad_scatter(pair_gather(mine, other), cot_pair, orders[0])
     attn_grad = jnp.einsum("btj,ij->bti", cotangent, dense_weight, preferred_element_type=wide_type)
     act_grad = jnp.einsum("btj,ij->bti", cotangent, down_weight, preferred_element_type=wide_type)
     up_grad_low = gelu_back(act_grad)[0].astype(narrow)
-    up_weight_grad = jnp.einsum(
-        "bti,btj->ij", mlp_in, up_grad_low, preferred_element_type=wide_type
+    up_grad_flat = up_grad_low.reshape(-1, 4 * D)
+    up_pair = pair_gather(up_grad_flat, up_grad_flat)
+    up_total = jnp.concatenate(
+        [
+            grad_scatter(norm_pairs[part][1], piece, bits)
+            for part, (bits, piece) in enumerate(zip(orders, jnp.split(up_pair, 2, axis=1)))
+        ],
+        axis=1,
     )
     up_bias_grad = jnp.sum(up_grad_low.astype(wide_type), axis=(0, 1))
     mlp_norm_grad = jnp.einsum(
@@ -259,13 +361,7 @@
     norm_grad = jnp.einsum("bcthm,bcth->bchm", query_wide, denom_used, precision=HIGH)
     in_state_grad = jnp.einsum("bc,bchme->bhme", carry_in, state_grad, precision=HIGH)
     in_norm_grad = jnp.einsum("bc,bchm->bhm", carry_in, norm_grad, precision=HIGH)
-    out_state_grad, out_norm_grad, flag_after = prefix(
-        (in_state_grad, in_norm_grad, reset_flag),
-        "seq",
-        chain_states,
-        (zero_state, zero_norm, zero_flag),
-        True,
-    )
+    out_state_grad, out_norm_grad = carried((in_state_grad, in_norm_grad), passing, "seq", -1)
     local_grad = (
         jnp.einsum("bcd,bchme->bdhme", link_mask, state_grad, precision=HIGH)
         + to_end[..., None, None, None] * out_state_grad[:, None]
@@ -293,58 +389,52 @@
         .reshape(seqs_here, context, 3 * D)
         .astype(narrow)
     )
-    qkv_weight_grad = jnp.einsum("bti,btj->ij", attn_in, qkv_grad, preferred_element_type=wide_type)
+    qkv_grad_flat = qkv_grad.reshape(-1, 3 * D)
+    qkv_pair = pair_gather(qkv_grad_flat, qkv_grad_flat)
+    qkv_total = jnp.concatenate(
+        [
+            grad_scatter(norm_pairs[part][0], piece, bits)
+            for part, (bits, piece) in enumerate(zip(orders, jnp.split(qkv_pair, 2, axis=1)))
+        ],
+        axis=1,
+    )
     qkv_bias_grad = jnp.sum(qkv_grad.astype(wide_type), axis=(0, 1))
     attn_norm_grad = jnp.einsum(
         "btj,ij->bti", qkv_grad, qkv_weight, preferred_element_type=wide_type
     )
-    input_from_attn, attn_gain_grad, attn_shift_grad = attn_norm_back(attn_norm_grad)
-    input_from_mlp, mlp_gain_grad, mlp_shift_grad = mlp_norm_back(mlp_norm_grad)
-    input_grad = cot_wide + input_from_attn + input_from_mlp
-    shared = (
-        lax.psum_scatter(attn_gain_grad, "batch", scatter_dimension=0, tiled=True),
-        lax.psum_scatter(attn_shift_grad, "batch", scatter_dimension=0, tiled=True),
-        lax.psum_scatter(mlp_gain_grad, "batch", scatter_dimension=0, tiled=True),
-        lax.psum_scatter(mlp_shift_grad, "batch", scatter_dimension=0, tiled=True),
-        lax.psum_scatter(qkv_weight_grad, "batch", scatter_dimension=0, tiled=True),
-        lax.psum_scatter(qkv_bias_grad, "batch", scatter_dimension=0, tiled=True),
-        lax.psum_scatter(dense_grad, "batch", scatter_dimension=0, tiled=True),
-        lax.psum_scatter(bias_grad, "batch", scatter_dimension=0, tiled=True),
-        lax.psum_scatter(up_weight_grad, "batch", scatter_dimension=0, tiled=True),
-        lax.psum_scatter(up_bias_grad, "batch", scatter_dimension=0, tiled=True),
-        lax.psum_scatter(down_grad, "batch", scatter_dimension=0, tiled=True),
-    )
-    totals = lax.psum(
-        (
-            shared[0],
-            shared[1],
-            shared[2],
-            shared[3],
-            shared[4],
-            shared[5],
-            shared[6],
-            shared[7],
-            shared[8],
-            shared[9],
-            shared[10],
-        ),
-        "seq",
+    attn_gain_grad = jnp.sum(attn_norm_grad * normed, axis=(0, 1))
+    attn_shift_grad = jnp.sum(attn_norm_grad, axis=(0, 1))
+    mlp_gain_grad = jnp.sum(mlp_norm_grad * normed, axis=(0, 1))
+    mlp_shift_grad = jnp.sum(mlp_norm_grad, axis=(0, 1))
+    normed_grad = attn_norm_grad * ln1_gain.astype(wide_type) + mlp_norm_grad * ln2_gain.astype(
+        wide_type
+    )
+    input_grad = cot_wide + inv_spread * (
+        normed_grad
+        - jnp.mean(normed_grad, axis=-1, keepdims=True)
+        - normed * jnp.mean(normed_grad * normed, axis=-1, keepdims=True)
+    )
+    mlp_gain_total, mlp_shift_total, up_bias_total, bias_total = scatter_vectors(
+        (mlp_gain_grad, mlp_shift_grad, up_bias_grad, bias_grad)
+    )
+    attn_gain_total, attn_shift_total, qkv_bias_total = scatter_vectors(
+        (attn_gain_grad, attn_shift_grad, qkv_bias_grad)
     )
     return (
         output,
         input_grad,
-        totals[0],
-        totals[1],
-        totals[2],
-        totals[3],
-        totals[4],
-        totals[5],
-        totals[6],
-        totals[7],
-        totals[8],
-        totals[9],
-        totals[10],
-        totals[7],
+        attn_gain_total,
+        attn_shift_total,
+        mlp_gain_total,
+        mlp_shift_total,
+        qkv_total,
+        qkv_bias_total,
+        dense_total,
+        bias_total,
+        up_total,
+        up_bias_total,
+        down_total,
+        bias_total,
     )
 
 

time: 889 us -> 753 us (0.85)
  waiting for transfers between devices: 500 us -> 341 us
  starting transfers between devices: 0.46 us -> 104 us
  blocking collectives: 97.2 us -> 0 us
  other arithmetic: 39.5 us -> 68.8 us
  matrix products: 152 us -> 129 us
  local copies, waits for them, and re-layouts: 77.1 us -> 94.7 us
  between operations: 18.1 us -> 3.87 us
    ppermute x0 -> x63, waiting for transfers between devices: none -> 341 us  [the longest x9 104 us: line_sum(): lax.ppermute(part, 'seq', [(k + 1, k), (count - 2 - k, count - 1 - k)])]
    reduce_scatter x4 -> x0, waiting for transfers between devices: 287 us -> none  [the longest x1 120 us: shards(): lax.psum_scatter(down_grad, 'batch', scatter_dimension=0, tiled=True)]
    psum x1 -> x0, waiting for transfers between devices: 160 us -> none  [shards(): lax.psum((shared[0], shared[1], shared[2], shared[3], shared[4], shared[5...]
    ppermute x0 -> x63, starting transfers between devices: none -> 104 us  [the longest x9 41.7 us: line_sum(): lax.ppermute(part, 'seq', [(k, k + 1), (count - 1 - k, count - 2 - k)])]
    all_gather x2 -> x0, waiting for transfers between devices: 52.5 us -> none  [prefix(): gathered = jax.tree.map(lambda a: lax.all_gather(a, axis), part)]
    unnamed x2 -> x0, blocking collectives: 49.5 us -> none
    all_gather x2 -> x0, blocking collectives: 32.8 us -> none  [prefix(): gathered = jax.tree.map(lambda a: lax.all_gather(a, axis), part)]
    convert_element_type x1 -> x17, other arithmetic: 0.18 us -> 20.7 us  [the longest x8 9.55 us: pair_gather(): return jnp.concatenate([mine, arrived.astype(jnp.bfloat16)], axis=0)]
  transfers between devices with their start and end apart: 7 -> 63, of which waited for: 6 -> 28; matrix products, arithmetic and copies ran while one was open for 20% -> 35% of each run, Pallas kernels for 0% -> 0%
where the time goes in v1:
time: 753 us; the launch traced here: 742 us
  waiting for transfers between devices  341 us (45%)
  matrix products  129 us (17%)
  starting transfers between devices  104 us (14%)
  local copies, waits for them, and re-layouts  94.7 us (13%)
  other arithmetic  68.8 us (9%)
    ppermute x9, waiting for transfers between devices, line_sum(): lax.ppermute(part, 'seq', [(k + 1, k), (count - 2 - k, count - 1 - k)])  104 us
    ppermute x28, waiting for transfers between devices, swap(): lax.ppermute(value, 'batch', [(i, i ^ 1 << bit) for i in range(count)])  99.4 us
    ppermute x8, waiting for transfers between devices, shift_rows(): lax.ppermute(value, axis, [(i, i + by) for i in range(count) if 0 <= i +...  70.4 us
    ppermute x9, waiting for transfers between devices, line_sum(): lax.ppermute(part, 'seq', [(k, k + 1), (count - 1 - k, count - 2 - k)])  67.8 us
    ppermute x9, starting transfers between devices, line_sum(): lax.ppermute(part, 'seq', [(k, k + 1), (count - 1 - k, count - 2 - k)])  41.7 us
    unnamed x288, local copies, waits for them, and re-layouts  24.3 us
    ppermute x8, starting transfers between devices, shift_rows(): lax.ppermute(value, axis, [(i, i + by) for i in range(count) if 0 <= i +...  21.8 us
    ppermute x28, starting transfers between devices, swap(): lax.ppermute(value, 'batch', [(i, i ^ 1 << bit) for i in range(count)])  21.1 us
  transfers between devices with their start and end apart: 63, of which 28 were waited for; matrix products, arithmetic and copies ran while one was open for 35% of the time, Pallas kernels for 0%

profile of v1, /device:TPU:0, one launch (start us, length us, event | category | flops | bytes accessed | tf_op | source)
XLA Modules:
  0.0 741.8 jit_solution(17098941617970125953)
XLA Ops:
  29.0 6.3 fusion.23
  35.3 3.6 copy.180
  57.4 4.7 collective-permute-start.2
  73.0 5.5 fusion.35
  78.5 4.6 collective-permute-start
  83.2 3.7 copy.186
  91.7 3.2 reshape.428
  99.8 7.0 fusion.79
  106.9 10.6 %multiply_convert_fusion.1 = (bf16[2,128,4096]{2,1,0:T(8,128)(2,1)}, f32[2,128,4096]{2,1,0:T(8,128)S(1)}) fusion(f32[2,128,4096]{2,1,0:T(8,128)S(1)} %get-tuple-element.144, u8[128,4096]{1,0:T(8,128)(4,1)S(1)} %get-tuple-element.15, u8[128,4096]{1,0:T(8,128)(4,1)S(1)} %get-tuple-element.14), kind=kLoop, calls=%fused_computation.25 | loop fusion | flops 73400320 | bytes 11534336 | tf_op jit(solution)/shard_map/convert_element_type | solution.py:300
  117.6 7.3 convert_reduce_fusion
  146.5 3.9 collective-permute-start.1
  151.7 20.4 %collective-permute-done.1 = f32[2,16,64,64]{3,2,1,0:T(8,128)S(1)} collective-permute-done((f32[2,16,64,64]{3,2,1,0:T(8,128)S(1)}, f32[2,16,64,64]{3,2,1,0:T(8,128)S(1)}, u32[]{:S(2)}, u32[]{:S(2)}) %collective-permute-start.1) | collective-permute-done | bytes 524320 | tf_op jit(solution)/shard_map/ppermute | solution.py:23
  172.1 7.0 add_convert_fusion.2
  195.0 3.3 reshape.431
  218.6 4.7 fusion.31
  226.2 26.0 %collective-permute-done.7 = f32[2,16,64]{2,1,0:T(8,128)S(1)} collective-permute-done((f32[2,16,64]{2,1,0:T(8,128)S(1)}, f32[2,16,64]{2,1,0:T(8,128)S(1)}, u32[]{:S(2)}, u32[]{:S(2)}) %collective-permute-start.7) | collective-permute-done | bytes 8224 | tf_op jit(solution)/shard_map/ppermute | solution.py:23
  257.4 24.0 %collective-permute-done.5 = f32[2,16,64,64]{3,2,1,0:T(8,128)S(1)} collective-permute-done((f32[2,16,64,64]{3,2,1,0:T(8,128)S(1)}, f32[2,16,64,64]{3,2,1,0:T(8,128)S(1)}, u32[]{:S(2)}, u32[]{:S(2)}) %collective-permute-start.5) | collective-permute-done | bytes 524320 | tf_op jit(solution)/shard_map/ppermute | solution.py:23
  281.4 6.2 add_convert_fusion.1
  287.6 3.7 copy.220
  297.5 3.9 reshape.432
  313.9 3.2 reshape.433
  321.4 5.2 fusion.8
  326.7 6.3 fusion.234
  352.3 3.6 collective-permute-start.11
  357.2 4.1 collective-permute-start.17
  365.6 10.9 %collective-permute-done.35 = f32[256,1024]{1,0:T(8,128)S(1)} collective-permute-done((f32[256,1024]{1,0:T(8,128)S(1)}, f32[256,1024]{1,0:T(8,128)S(1)}, u32[]{:S(2)}, u32[]{:S(2)}) %collective-permute-start.35) | collective-permute-done | bytes 1048608 | tf_op jit(solution)/shard_map/ppermute | solution.py:44
  381.0 15.0 %collective-permute-done.58 = f32[512,1024]{1,0:T(8,128)S(1)} collective-permute-done((f32[512,1024]{1,0:T(8,128)S(1)}, f32[512,1024]{1,0:T(8,128)S(1)}, u32[]{:S(2)}, u32[]{:S(2)}) %collective-permute-start.58) | collective-permute-done | bytes 2097184 | tf_op jit(solution)/shard_map/ppermute | solution.py:44
  404.3 15.1 %collective-permute-done.53 = f32[256,1024]{1,0:T(8,128)S(1)} collective-permute-done((f32[256,1024]{1,0:T(8,128)S(1)}, f32[256,1024]{1,0:T(8,128)S(1)}, u32[]{:S(2)}, u32[]{:S(2)}) %collective-permute-start.53) | collective-permute-done | bytes 1048608 | tf_op jit(solution)/shard_map/ppermute | solution.py:44
  420.0 3.7 collective-permute-start.54
  435.5 11.7 %collective-permute-done.54 = f32[256,1024]{1,0:T(8,128)S(1)} collective-permute-done((f32[256,1024]{1,0:T(8,128)S(1)}, f32[256,1024]{1,0:T(8,128)S(1)}, u32[]{:S(2)}, u32[]{:S(2)}) %collective-permute-start.54) | collective-permute-done | bytes 1048608 | tf_op jit(solution)/shard_map/ppermute | solution.py:56
  447.2 4.4 collective-permute-start.37
  454.6 17.5 %collective-permute-done.37 = f32[128,1024]{1,0:T(8,128)S(1)} collective-permute-done((f32[128,1024]{1,0:T(8,128)S(1)}, f32[128,1024]{1,0:T(8,128)S(1)}, u32[]{:S(2)}, u32[]{:S(2)}) %collective-permute-start.37) | collective-permute-done | bytes 524320 | tf_op jit(solution)/shard_map/ppermute | solution.py:56
  476.0 3.3 fusion.52
  485.1 21.8 %collective-permute-done.28 = f32[256,1536]{1,0:T(8,128)} collective-permute-done((f32[256,1536]{1,0:T(8,128)}, f32[256,1536]{1,0:T(8,128)}, u32[]{:S(2)}, u32[]{:S(2)}) %collective-permute-start.28) | collective-permute-done | bytes 1572896 | tf_op jit(solution)/shard_map/ppermute | solution.py:44
  523.7 7.4 collective-permute-done.29
  531.7 14.8 %collective-permute-done.47 = f32[128,2048]{1,0:T(8,128)S(1)} collective-permute-done((f32[128,2048]{1,0:T(8,128)S(1)}, f32[128,2048]{1,0:T(8,128)S(1)}, u32[]{:S(2)}, u32[]{:S(2)}) %collective-permute-start.47) | collective-permute-done | bytes 1048608 | tf_op jit(solution)/shard_map/ppermute | solution.py:44
  546.5 4.3 collective-permute-start.30
  552.7 3.6 collective-permute-done.23
  556.3 4.3 collective-permute-start.48
  560.7 7.4 collective-permute-done.30
  568.1 4.4 collective-permute-start.43
  574.1 11.4 %collective-permute-start.24 = (f32[128,1536]{1,0:T(8,128)S(1)}, f32[128,1536]{1,0:T(8,128)S(1)}, u32[]{:S(2)}, u32[]{:S(2)}) collective-permute-start(f32[128,1536]{1,0:T(8,128)S(1)} %slice_add_fusion.5), channel_id=1, source_target_pairs={{0,8},{24,16},{1,9},{25,17},{2,10},{26,18},{3,11},{27,19},{4,12},{... | collective-permute-start | bytes 2359304 | tf_op jit(solution)/shard_map/ppermute | solution.py:56
  592.5 20.5 %collective-permute-done.43 = f32[128,2048]{1,0:T(8,128)S(1)} collective-permute-done((f32[128,2048]{1,0:T(8,128)S(1)}, f32[128,2048]{1,0:T(8,128)S(1)}, u32[]{:S(2)}, u32[]{:S(2)}) %collective-permute-start.43) | collective-permute-done | bytes 1048608 | tf_op jit(solution)/shard_map/ppermute | solution.py:56
  615.2 7.1 collective-permute-done.24
  634.9 11.7 %collective-permute-done.32 = f32[128,1536]{1,0:T(8,128)S(1)} collective-permute-done((f32[128,1536]{1,0:T(8,128)S(1)}, f32[128,1536]{1,0:T(8,128)S(1)}, u32[]{:S(2)}, u32[]{:S(2)}) %collective-permute-start.32) | collective-permute-done | bytes 786464 | tf_op jit(solution)/shard_map/ppermute | solution.py:59
  646.6 56.8 %collective-permute-done.26 = f32[128,1536]{1,0:T(8,128)S(1)} collective-permute-done((f32[128,1536]{1,0:T(8,128)S(1)}, f32[128,1536]{1,0:T(8,128)S(1)}, u32[]{:S(2)}, u32[]{:S(2)}) %collective-permute-start.26) | collective-permute-done | bytes 786464 | tf_op jit(solution)/shard_map/ppermute | solution.py:59
  704.8 21.1 %collective-permute-done.50 = f32[128,2048]{1,0:T(8,128)S(1)} collective-permute-done((f32[128,2048]{1,0:T(8,128)S(1)}, f32[128,2048]{1,0:T(8,128)S(1)}, u32[]{:S(2)}, u32[]{:S(2)}) %collective-permute-start.50) | collective-permute-done | bytes 1048608 | tf_op jit(solution)/shard_map/ppermute | solution.py:59
  726.1 13.2 %collective-permute-done.45 = f32[128,2048]{1,0:T(8,128)S(1)} collective-permute-done((f32[128,2048]{1,0:T(8,128)S(1)}, f32[128,2048]{1,0:T(8,128)S(1)}, u32[]{:S(2)}, u32[]{:S(2)}) %collective-permute-start.45) | collective-permute-done | bytes 1048608 | tf_op jit(solution)/shard_map/ppermute | solution.py:59
  (603 shorter events, 264.5 us)
Async XLA Ops:
  24.9 325.2 %collective-permute-start.27 = (f32[256,1024]{1,0:T(8,128)}, f32[256,1024]{1,0:T(8,128)}, u32[]{:S(2)}, u32[]{:S(2)}) collective-permute-start(f32[256,1024]{1,0:T(8,128)} %convert_element_type.286), channel_id=1, source_target_pairs={{0,1},{1,0},{2,3},{3,2},{4,5},{5,4},{6,7},{7,6},{8,9},{9,8},{10,11... | collective-permute-start | bytes 3145736 | tf_op jit(solution)/shard_map/ppermute | solution.py:44
  26.5 329.4 %collective-permute-start.20 = (f32[256,1024]{1,0:T(8,128)}, f32[256,1024]{1,0:T(8,128)}, u32[]{:S(2)}, u32[]{:S(2)}) collective-permute-start(f32[256,1024]{1,0:T(8,128)} %convert_element_type.281), channel_id=1, source_target_pairs={{0,1},{1,0},{2,3},{3,2},{4,5},{5,4},{6,7},{7,6},{8,9},{9,8},{10,11... | collective-permute-start | bytes 3145736 | tf_op jit(solution)/shard_map/ppermute | solution.py:44
  27.8 173.8 %collective-permute-start.34 = (f32[256,1024]{1,0:T(8,128)}, f32[256,1024]{1,0:T(8,128)}, u32[]{:S(2)}, u32[]{:S(2)}) collective-permute-start(f32[256,1024]{1,0:T(8,128)} %bitcast_convert_fusion.1), channel_id=1, source_target_pairs={{0,1},{1,0},{2,3},{3,2},{4,5},{5,4},{6,7},{7,6},{8,9},{9,8},{10,11... | collective-permute-start | bytes 3145736 | tf_op jit(solution)/shard_map/ppermute | solution.py:44
  57.4 84.4 %collective-permute-start.2 = (f32[2,16,64]{2,1,0:T(8,128)S(1)}, f32[2,16,64]{2,1,0:T(8,128)S(1)}, u32[]{:S(2)}, u32[]{:S(2)}) collective-permute-start(f32[2,16,64]{2,1,0:T(8,128)S(1)} %bitcast.264), channel_id=1, source_target_pairs={{0,8},{8,16},{16,24},{1,9},{9,17},{17,25},{2,10},{10,18},{18,26},{... | collective-permute-start | bytes 24584 | tf_op jit(solution)/shard_map/ppermute | solution.py:23
  78.5 63.4 %collective-permute-start = (f32[2,16,64,64]{3,2,1,0:T(8,128)}, f32[2,16,64,64]{3,2,1,0:T(8,128)}, u32[]{:S(2)}, u32[]{:S(2)}) collective-permute-start(f32[2,16,64,64]{3,2,1,0:T(8,128)} %bitcast.9), channel_id=1, source_target_pairs={{0,8},{8,16},{16,24},{1,9},{9,17},{17,25},{2,10},{10,18},{18,26},{... | collective-permute-start | bytes 1572872 | tf_op jit(solution)/shard_map/ppermute | solution.py:23
  141.7 70.6 %collective-permute-start.51 = (f32[256,1024]{1,0:T(8,128)}, f32[256,1024]{1,0:T(8,128)}, u32[]{:S(2)}, u32[]{:S(2)}) collective-permute-start(f32[256,1024]{1,0:T(8,128)} %maximum_convert_fusion.1), channel_id=1, source_target_pairs={{0,1},{1,0},{2,3},{3,2},{4,5},{5,4},{6,7},{7,6},{8,9},{9,8},{10,11... | collective-permute-start | bytes 3145736 | tf_op jit(solution)/shard_map/ppermute | solution.py:44
  146.5 25.6 %collective-permute-start.1 = (f32[2,16,64,64]{3,2,1,0:T(8,128)S(1)}, f32[2,16,64,64]{3,2,1,0:T(8,128)S(1)}, u32[]{:S(2)}, u32[]{:S(2)}) collective-permute-start(f32[2,16,64,64]{3,2,1,0:T(8,128)S(1)} %multiply_add_fusion.2), channel_id=1, source_target_pairs={{0,8},{8,16},{16,24},{1,9},{9,17},{17,25},{2,10},{10,18},{18,26},{... | collective-permute-start | bytes 1572872 | tf_op jit(solution)/shard_map/ppermute | solution.py:23
  172.1 31.4 %collective-permute-start.57 = (f32[256,1024]{1,0:T(8,128)}, f32[256,1024]{1,0:T(8,128)}, u32[]{:S(2)}, u32[]{:S(2)}) collective-permute-start(f32[256,1024]{1,0:T(8,128)} %maximum_convert_fusion.2), channel_id=1, source_target_pairs={{0,1},{1,0},{2,3},{3,2},{4,5},{5,4},{6,7},{7,6},{8,9},{9,8},{10,11... | collective-permute-start | bytes 3145736 | tf_op jit(solution)/shard_map/ppermute | solution.py:44
  201.6 195.8 %collective-permute-start.40 = (f32[256,4096]{1,0:T(8,128)}, f32[256,4096]{1,0:T(8,128)}, u32[]{:S(2)}, u32[]{:S(2)}) collective-permute-start(f32[256,4096]{1,0:T(8,128)} %bitcast_convert_fusion), channel_id=1, source_target_pairs={{0,1},{1,0},{2,3},{3,2},{4,5},{5,4},{6,7},{7,6},{8,9},{9,8},{10,11... | collective-permute-start | bytes 12582920 | tf_op jit(solution)/shard_map/ppermute | solution.py:44
  203.5 21.3 %collective-permute-start.6 = (f32[2,16,64]{2,1,0:T(8,128)S(1)}, f32[2,16,64]{2,1,0:T(8,128)S(1)}, u32[]{:S(2)}, u32[]{:S(2)}) collective-permute-start(f32[2,16,64]{2,1,0:T(8,128)S(1)} %bitcast.266), channel_id=1, source_target_pairs={{8,0},{16,8},{24,16},{9,1},{17,9},{25,17},{10,2},{18,10},{26,18},{... | collective-permute-start | bytes 24584 | tf_op jit(solution)/shard_map/ppermute | solution.py:23
  223.5 28.9 %collective-permute-start.4 = (f32[2,16,64,64]{3,2,1,0:T(8,128)S(1)}, f32[2,16,64,64]{3,2,1,0:T(8,128)S(1)}, u32[]{:S(2)}, u32[]{:S(2)}) collective-permute-start(f32[2,16,64,64]{3,2,1,0:T(8,128)S(1)} %bitcast.257), channel_id=1, source_target_pairs={{8,0},{16,8},{24,16},{9,1},{17,9},{25,17},{10,2},{18,10},{26,18},{... | collective-permute-start | bytes 1572872 | tf_op jit(solution)/shard_map/ppermute | solution.py:23
  224.9 27.3 %collective-permute-start.7 = (f32[2,16,64]{2,1,0:T(8,128)S(1)}, f32[2,16,64]{2,1,0:T(8,128)S(1)}, u32[]{:S(2)}, u32[]{:S(2)}) collective-permute-start(f32[2,16,64]{2,1,0:T(8,128)S(1)} %multiply_add_fusion.6), channel_id=1, source_target_pairs={{8,0},{16,8},{24,16},{9,1},{17,9},{25,17},{10,2},{18,10},{26,18},{... | collective-permute-start | bytes 24584 | tf_op jit(solution)/shard_map/ppermute | solution.py:23
  252.4 125.2 %collective-permute-start.52 = (f32[512,1024]{1,0:T(8,128)}, f32[512,1024]{1,0:T(8,128)}, u32[]{:S(2)}, u32[]{:S(2)}) collective-permute-start(f32[512,1024]{1,0:T(8,128)} %fusion.100), channel_id=1, source_target_pairs={{0,2},{1,3},{2,0},{3,1},{4,6},{5,7},{6,4},{7,5},{8,10},{9,11},{10,... | collective-permute-start | bytes 6291464 | tf_op jit(solution)/shard_map/ppermute | solution.py:44
  254.2 27.2 %collective-permute-start.5 = (f32[2,16,64,64]{3,2,1,0:T(8,128)S(1)}, f32[2,16,64,64]{3,2,1,0:T(8,128)S(1)}, u32[]{:S(2)}, u32[]{:S(2)}) collective-permute-start(f32[2,16,64,64]{3,2,1,0:T(8,128)S(1)} %multiply_add_fusion.1), channel_id=1, source_target_pairs={{8,0},{16,8},{24,16},{9,1},{17,9},{25,17},{10,2},{18,10},{26,18},{... | collective-permute-start | bytes 1572872 | tf_op jit(solution)/shard_map/ppermute | solution.py:23
  350.1 45.9 %collective-permute-start.58 = (f32[512,1024]{1,0:T(8,128)S(1)}, f32[512,1024]{1,0:T(8,128)S(1)}, u32[]{:S(2)}, u32[]{:S(2)}) collective-permute-start(f32[512,1024]{1,0:T(8,128)S(1)} %copy-done.130), channel_id=1, source_target_pairs={{0,4},{1,5},{2,6},{3,7},{4,0},{5,1},{6,2},{7,3},{8,12},{9,13},{10,... | collective-permute-start | bytes 6291464 | tf_op jit(solution)/shard_map/ppermute | solution.py:44
  356.0 20.5 %collective-permute-start.35 = (f32[256,1024]{1,0:T(8,128)S(1)}, f32[256,1024]{1,0:T(8,128)S(1)}, u32[]{:S(2)}, u32[]{:S(2)}) collective-permute-start(f32[256,1024]{1,0:T(8,128)S(1)} %copy-done.131), channel_id=1, source_target_pairs={{0,2},{1,3},{2,0},{3,1},{4,6},{5,7},{6,4},{7,5},{8,10},{9,11},{10,... | collective-permute-start | bytes 3145736 | tf_op jit(solution)/shard_map/ppermute | solution.py:44
  362.7 61.2 %collective-permute-start.21 = (f32[256,3072]{0,1:T(8,128)S(1)}, f32[256,3072]{0,1:T(8,128)S(1)}, u32[]{:S(2)}, u32[]{:S(2)}) collective-permute-start(f32[256,3072]{0,1:T(8,128)S(1)} %get-tuple-element.69), channel_id=1, source_target_pairs={{0,1},{1,0},{2,3},{3,2},{4,5},{5,4},{6,7},{7,6},{8,9},{9,8},{10,11... | collective-permute-start | bytes 9437192 | tf_op jit(solution)/shard_map/ppermute | solution.py:44
  376.5 49.1 %collective-permute-start.12 = (f32[1,640]{1,0:T(1,128)S(1)}, f32[1,640]{1,0:T(1,128)S(1)}, u32[]{:S(2)}, u32[]{:S(2)}) collective-permute-start(f32[1,640]{1,0:T(1,128)S(1)} %add.588), channel_id=1, source_target_pairs={{8,16},{16,8},{9,17},{17,9},{10,18},{18,10},{11,19},{19,11},{12,20... | collective-permute-start | bytes 7688 | tf_op jit(solution)/shard_map/ppermute | solution.py:57
  377.7 52.3 %collective-permute-start.18 = (f32[1,896]{1,0:T(1,128)S(1)}, f32[1,896]{1,0:T(1,128)S(1)}, u32[]{:S(2)}, u32[]{:S(2)}) collective-permute-start(f32[1,896]{1,0:T(1,128)S(1)} %add.593), channel_id=1, source_target_pairs={{8,16},{16,8},{9,17},{17,9},{10,18},{18,10},{11,19},{19,11},{12,20... | collective-permute-start | bytes 10760 | tf_op jit(solution)/shard_map/ppermute | solution.py:57
  396.0 23.3 %collective-permute-start.53 = (f32[256,1024]{1,0:T(8,128)S(1)}, f32[256,1024]{1,0:T(8,128)S(1)}, u32[]{:S(2)}, u32[]{:S(2)}) collective-permute-start(f32[256,1024]{1,0:T(8,128)S(1)} %slice.326), channel_id=1, source_target_pairs={{0,4},{1,5},{2,6},{3,7},{4,0},{5,1},{6,2},{7,3},{8,12},{9,13},{10,... | collective-permute-start | bytes 3145736 | tf_op jit(solution)/shard_map/ppermute | solution.py:44
  397.4 22.6 %collective-permute-start.59 = (f32[256,1024]{1,0:T(8,128)S(1)}, f32[256,1024]{1,0:T(8,128)S(1)}, u32[]{:S(2)}, u32[]{:S(2)}) collective-permute-start(f32[256,1024]{1,0:T(8,128)S(1)} %slice.330), channel_id=1, source_target_pairs={{0,2},{1,3},{2,0},{3,1},{4,6},{5,7},{6,4},{7,5},{8,10},{9,11},{10,... | collective-permute-start | bytes 3145736 | tf_op jit(solution)/shard_map/ppermute | solution.py:44
  420.0 27.2 %collective-permute-start.54 = (f32[256,1024]{1,0:T(8,128)S(1)}, f32[256,1024]{1,0:T(8,128)S(1)}, u32[]{:S(2)}, u32[]{:S(2)}) collective-permute-start(f32[256,1024]{1,0:T(8,128)S(1)} %slice_add_fusion.1), channel_id=1, source_target_pairs={{0,8},{24,16},{1,9},{25,17},{2,10},{26,18},{3,11},{27,19},{4,12},{... | collective-permute-start | bytes 3145736 | tf_op jit(solution)/shard_map/ppermute | solution.py:56
  423.9 49.4 %collective-permute-start.60 = (f32[256,1024]{1,0:T(8,128)S(1)}, f32[256,1024]{1,0:T(8,128)S(1)}, u32[]{:S(2)}, u32[]{:S(2)}) collective-permute-start(f32[256,1024]{1,0:T(8,128)S(1)} %slice_add_fusion), channel_id=1, source_target_pairs={{0,8},{24,16},{1,9},{25,17},{2,10},{26,18},{3,11},{27,19},{4,12},{... | collective-permute-start | bytes 3145736 | tf_op jit(solution)/shard_map/ppermute | solution.py:56
  425.5 85.0 %collective-permute-start.46 = (f32[256,2048]{1,0:T(8,128)}, f32[256,2048]{1,0:T(8,128)}, u32[]{:S(2)}, u32[]{:S(2)}) collective-permute-start(f32[256,2048]{1,0:T(8,128)} %fusion.117), channel_id=1, source_target_pairs={{0,4},{1,5},{2,6},{3,7},{4,0},{5,1},{6,2},{7,3},{8,12},{9,13},{10,... | collective-permute-start | bytes 6291464 | tf_op jit(solution)/shard_map/ppermute | solution.py:44
  430.0 76.9 %collective-permute-start.28 = (f32[256,1536]{1,0:T(8,128)}, f32[256,1536]{1,0:T(8,128)}, u32[]{:S(2)}, u32[]{:S(2)}) collective-permute-start(f32[256,1536]{1,0:T(8,128)} %fusion.123), channel_id=1, source_target_pairs={{0,4},{1,5},{2,6},{3,7},{4,0},{5,1},{6,2},{7,3},{8,12},{9,13},{10,... | collective-permute-start | bytes 4718600 | tf_op jit(solution)/shard_map/ppermute | solution.py:44
  434.2 80.1 %collective-permute-start.41 = (f32[256,2048]{1,0:T(8,128)}, f32[256,2048]{1,0:T(8,128)}, u32[]{:S(2)}, u32[]{:S(2)}) collective-permute-start(f32[256,2048]{1,0:T(8,128)} %fusion.133), channel_id=1, source_target_pairs={{0,2},{1,3},{2,0},{3,1},{4,6},{5,7},{6,4},{7,5},{8,10},{9,11},{10,... | collective-permute-start | bytes 6291464 | tf_op jit(solution)/shard_map/ppermute | solution.py:44
  447.2 24.9 %collective-permute-start.37 = (f32[128,1024]{1,0:T(8,128)S(1)}, f32[128,1024]{1,0:T(8,128)S(1)}, u32[]{:S(2)}, u32[]{:S(2)}) collective-permute-start(f32[128,1024]{1,0:T(8,128)S(1)} %slice_add_fusion.6), channel_id=1, source_target_pairs={{0,8},{24,16},{1,9},{25,17},{2,10},{26,18},{3,11},{27,19},{4,12},{... | collective-permute-start | bytes 1572872 | tf_op jit(solution)/shard_map/ppermute | solution.py:56
  472.1 48.8 %collective-permute-start.22 = (f32[256,1536]{1,0:T(8,128)}, f32[256,1536]{1,0:T(8,128)}, u32[]{:S(2)}, u32[]{:S(2)}) collective-permute-start(f32[256,1536]{1,0:T(8,128)} %fusion.130), channel_id=1, source_target_pairs={{0,2},{1,3},{2,0},{3,1},{4,6},{5,7},{6,4},{7,5},{8,10},{9,11},{10,... | collective-permute-start | bytes 4718600 | tf_op jit(solution)/shard_map/ppermute | solution.py:44
  474.3 43.4 %collective-permute-start.55 = (f32[256,1024]{1,0:T(8,128)}, f32[256,1024]{1,0:T(8,128)}, u32[]{:S(2)}, u32[]{:S(2)}) collective-permute-start(f32[256,1024]{1,0:T(8,128)} %add.633), channel_id=1, source_target_pairs={{8,16},{16,8},{9,17},{17,9},{10,18},{18,10},{11,19},{19,11},{12,20... | collective-permute-start | bytes 3145736 | tf_op jit(solution)/shard_map/ppermute | solution.py:57
  506.8 45.0 %collective-permute-start.13 = (f32[1,640]{1,0:T(1,128)S(1)}, f32[1,640]{1,0:T(1,128)S(1)}, u32[]{:S(2)}, u32[]{:S(2)}) collective-permute-start(f32[1,640]{1,0:T(1,128)S(1)} %add.589), channel_id=1, source_target_pairs={{8,0},{16,24},{9,1},{17,25},{10,2},{18,26},{11,3},{19,27},{12,4},{... | collective-permute-start | bytes 7688 | tf_op jit(solution)/shard_map/ppermute | solution.py:59
  510.5 20.5 %collective-permute-start.29 = (f32[128,1536]{1,0:T(8,128)S(1)}, f32[128,1536]{1,0:T(8,128)S(1)}, u32[]{:S(2)}, u32[]{:S(2)}) collective-permute-start(f32[128,1536]{1,0:T(8,128)S(1)} %slice.307), channel_id=1, source_target_pairs={{0,2},{1,3},{2,0},{3,1},{4,6},{5,7},{6,4},{7,5},{8,10},{9,11},{10,... | collective-permute-start | bytes 2359304 | tf_op jit(solution)/shard_map/ppermute | solution.py:44
  514.4 32.2 %collective-permute-start.47 = (f32[128,2048]{1,0:T(8,128)S(1)}, f32[128,2048]{1,0:T(8,128)S(1)}, u32[]{:S(2)}, u32[]{:S(2)}) collective-permute-start(f32[128,2048]{1,0:T(8,128)S(1)} %slice.321), channel_id=1, source_target_pairs={{0,2},{1,3},{2,0},{3,1},{4,6},{5,7},{6,4},{7,5},{8,10},{9,11},{10,... | collective-permute-start | bytes 3145736 | tf_op jit(solution)/shard_map/ppermute | solution.py:44
  517.7 55.1 %collective-permute-start.19 = (f32[1,896]{1,0:T(1,128)S(1)}, f32[1,896]{1,0:T(1,128)S(1)}, u32[]{:S(2)}, u32[]{:S(2)}) collective-permute-start(f32[1,896]{1,0:T(1,128)S(1)} %add.594), channel_id=1, source_target_pairs={{8,0},{16,24},{9,1},{17,25},{10,2},{18,26},{11,3},{19,27},{12,4},{... | collective-permute-start | bytes 10760 | tf_op jit(solution)/shard_map/ppermute | solution.py:59
  520.9 30.0 %collective-permute-start.42 = (f32[128,2048]{1,0:T(8,128)S(1)}, f32[128,2048]{1,0:T(8,128)S(1)}, u32[]{:S(2)}, u32[]{:S(2)}) collective-permute-start(f32[128,2048]{1,0:T(8,128)S(1)} %slice.317), channel_id=1, source_target_pairs={{0,4},{1,5},{2,6},{3,7},{4,0},{5,1},{6,2},{7,3},{8,12},{9,13},{10,... | collective-permute-start | bytes 3145736 | tf_op jit(solution)/shard_map/ppermute | solution.py:44
  531.1 25.3 %collective-permute-start.23 = (f32[128,1536]{1,0:T(8,128)S(1)}, f32[128,1536]{1,0:T(8,128)S(1)}, u32[]{:S(2)}, u32[]{:S(2)}) collective-permute-start(f32[128,1536]{1,0:T(8,128)S(1)} %slice.301), channel_id=1, source_target_pairs={{0,4},{1,5},{2,6},{3,7},{4,0},{5,1},{6,2},{7,3},{8,12},{9,13},{10,... | collective-permute-start | bytes 2359304 | tf_op jit(solution)/shard_map/ppermute | solution.py:44
  546.5 21.6 %collective-permute-start.30 = (f32[128,1536]{1,0:T(8,128)S(1)}, f32[128,1536]{1,0:T(8,128)S(1)}, u32[]{:S(2)}, u32[]{:S(2)}) collective-permute-start(f32[128,1536]{1,0:T(8,128)S(1)} %slice_add_fusion.4), channel_id=1, source_target_pairs={{0,8},{24,16},{1,9},{25,17},{2,10},{26,18},{3,11},{27,19},{4,12},{... | collective-permute-start | bytes 2359304 | tf_op jit(solution)/shard_map/ppermute | solution.py:56
  551.0 34.6 %collective-permute-start.61 = (f32[256,1024]{1,0:T(8,128)S(1)}, f32[256,1024]{1,0:T(8,128)S(1)}, u32[]{:S(2)}, u32[]{:S(2)}) collective-permute-start(f32[256,1024]{1,0:T(8,128)S(1)} %add.653), channel_id=1, source_target_pairs={{8,16},{16,8},{9,17},{17,9},{10,18},{18,10},{11,19},{19,11},{12,20... | collective-permute-start | bytes 3145736 | tf_op jit(solution)/shard_map/ppermute | solution.py:57
  551.9 22.2 %collective-permute-start.38 = (f32[128,1024]{1,0:T(8,128)S(1)}, f32[128,1024]{1,0:T(8,128)S(1)}, u32[]{:S(2)}, u32[]{:S(2)}) collective-permute-start(f32[128,1024]{1,0:T(8,128)S(1)} %add.613), channel_id=1, source_target_pairs={{8,16},{16,8},{9,17},{17,9},{10,18},{18,10},{11,19},{19,11},{12,20... | collective-permute-start | bytes 1572872 | tf_op jit(solution)/shard_map/ppermute | solution.py:57
  556.3 34.2 %collective-permute-start.48 = (f32[128,2048]{1,0:T(8,128)S(1)}, f32[128,2048]{1,0:T(8,128)S(1)}, u32[]{:S(2)}, u32[]{:S(2)}) collective-permute-start(f32[128,2048]{1,0:T(8,128)S(1)} %slice_add_fusion.2), channel_id=1, source_target_pairs={{0,8},{24,16},{1,9},{25,17},{2,10},{26,18},{3,11},{27,19},{4,12},{... | collective-permute-start | bytes 3145736 | tf_op jit(solution)/shard_map/ppermute | solution.py:56
  568.1 44.9 %collective-permute-start.43 = (f32[128,2048]{1,0:T(8,128)S(1)}, f32[128,2048]{1,0:T(8,128)S(1)}, u32[]{:S(2)}, u32[]{:S(2)}) collective-permute-start(f32[128,2048]{1,0:T(8,128)S(1)} %slice_add_fusion.3), channel_id=1, source_target_pairs={{0,8},{24,16},{1,9},{25,17},{2,10},{26,18},{3,11},{27,19},{4,12},{... | collective-permute-start | bytes 3145736 | tf_op jit(solution)/shard_map/ppermute | solution.py:56
  572.8 53.0 %collective-permute-start.56 = (f32[256,1024]{1,0:T(8,128)S(1)}, f32[256,1024]{1,0:T(8,128)S(1)}, u32[]{:S(2)}, u32[]{:S(2)}) collective-permute-start(f32[256,1024]{1,0:T(8,128)S(1)} %add.634), channel_id=1, source_target_pairs={{8,0},{16,24},{9,1},{17,25},{10,2},{18,26},{11,3},{19,27},{12,4},{... | collective-permute-start | bytes 3145736 | tf_op jit(solution)/shard_map/ppermute | solution.py:59
  574.1 48.2 %collective-permute-start.24 = (f32[128,1536]{1,0:T(8,128)S(1)}, f32[128,1536]{1,0:T(8,128)S(1)}, u32[]{:S(2)}, u32[]{:S(2)}) collective-permute-start(f32[128,1536]{1,0:T(8,128)S(1)} %slice_add_fusion.5), channel_id=1, source_target_pairs={{0,8},{24,16},{1,9},{25,17},{2,10},{26,18},{3,11},{27,19},{4,12},{... | collective-permute-start | bytes 2359304 | tf_op jit(solution)/shard_map/ppermute | solution.py:56
  585.5 38.3 %collective-permute-start.31 = (f32[128,1536]{1,0:T(8,128)S(1)}, f32[128,1536]{1,0:T(8,128)S(1)}, u32[]{:S(2)}, u32[]{:S(2)}) collective-permute-start(f32[128,1536]{1,0:T(8,128)S(1)} %add.609), channel_id=1, source_target_pairs={{8,16},{16,8},{9,17},{17,9},{10,18},{18,10},{11,19},{19,11},{12,20... | collective-permute-start | bytes 2359304 | tf_op jit(solution)/shard_map/ppermute | solution.py:57
  590.5 32.6 %collective-permute-start.39 = (f32[128,1024]{1,0:T(8,128)S(1)}, f32[128,1024]{1,0:T(8,128)S(1)}, u32[]{:S(2)}, u32[]{:S(2)}) collective-permute-start(f32[128,1024]{1,0:T(8,128)S(1)} %add.614), channel_id=1, source_target_pairs={{8,0},{16,24},{9,1},{17,25},{10,2},{18,26},{11,3},{19,27},{12,4},{... | collective-permute-start | bytes 1572872 | tf_op jit(solution)/shard_map/ppermute | solution.py:59
  625.8 20.7 %collective-permute-start.32 = (f32[128,1536]{1,0:T(8,128)S(1)}, f32[128,1536]{1,0:T(8,128)S(1)}, u32[]{:S(2)}, u32[]{:S(2)}) collective-permute-start(f32[128,1536]{1,0:T(8,128)S(1)} %add.610), channel_id=1, source_target_pairs={{8,0},{16,24},{9,1},{17,25},{10,2},{18,26},{11,3},{19,27},{12,4},{... | collective-permute-start | bytes 2359304 | tf_op jit(solution)/shard_map/ppermute | solution.py:59
  628.3 75.2 %collective-permute-start.26 = (f32[128,1536]{1,0:T(8,128)S(1)}, f32[128,1536]{1,0:T(8,128)S(1)}, u32[]{:S(2)}, u32[]{:S(2)}) collective-permute-start(f32[128,1536]{1,0:T(8,128)S(1)} %add.606), channel_id=1, source_target_pairs={{8,0},{16,24},{9,1},{17,25},{10,2},{18,26},{11,3},{19,27},{12,4},{... | collective-permute-start | bytes 2359304 | tf_op jit(solution)/shard_map/ppermute | solution.py:59
  632.1 93.8 %collective-permute-start.50 = (f32[128,2048]{1,0:T(8,128)S(1)}, f32[128,2048]{1,0:T(8,128)S(1)}, u32[]{:S(2)}, u32[]{:S(2)}) collective-permute-start(f32[128,2048]{1,0:T(8,128)S(1)} %add.622), channel_id=1, source_target_pairs={{8,0},{16,24},{9,1},{17,25},{10,2},{18,26},{11,3},{19,27},{12,4},{... | collective-permute-start | bytes 3145736 | tf_op jit(solution)/shard_map/ppermute | solution.py:59
  633.6 105.7 %collective-permute-start.45 = (f32[128,2048]{1,0:T(8,128)S(1)}, f32[128,2048]{1,0:T(8,128)S(1)}, u32[]{:S(2)}, u32[]{:S(2)}) collective-permute-start(f32[128,2048]{1,0:T(8,128)S(1)} %add.618), channel_id=1, source_target_pairs={{8,0},{16,24},{9,1},{17,25},{10,2},{18,26},{11,3},{19,27},{12,4},{... | collective-permute-start | bytes 3145736 | tf_op jit(solution)/shard_map/ppermute | solution.py:59
  (153 other events, 1747.4 us)

commit v2 on v0

v2 whole, which is shorter than its diff:
```python
import math
from functools import partial

import jax
import jax.numpy as jnp
import numpy as np
from jax import lax
from jax.experimental import pallas as pl
from jax.experimental.pallas import tpu as pltpu
from jax.sharding import PartitionSpec as P

D = 1024
HEADS = 16
HEAD = 64
ROT = 16
FF = 4096
PAIR = 2 * HEAD
BLOCK = 128
COLUMNS = 512

EPSILON = 1e-05
ROTARY_BASE = 10000.0

ROWS_COLS = ((1,), (0,))
ROWS_ROWS = ((1,), (1,))
COLS_COLS = ((0,), (0,))
NARROW = jnp.bfloat16
WIDE = jnp.float32


def plain_dot(left, right, dims):
    return lax.dot_general(left, right, (dims, ((), ())), preferred_element_type=WIDE)


def whole_spec(shape):
    return pl.BlockSpec(shape, lambda *_: (0,) * len(shape))


def shift_rows(value, axis, by):
    count = lax.axis_size(axis)
    return lax.ppermute(
        value, axis, [(i, i + by) for i in range(count) if 0 <= i + by < count]
    )


def swap(value, bit):
    count = lax.axis_size("batch")
    return lax.ppermute(value, "batch", [(i, i ^ (1 << bit)) for i in range(count)])


def owner_order(bits):
    return sorted(
        range(1 << len(bits)), key=lambda r: tuple(-((r >> bit) & 1) for bit in bits)
    )


def line_rounds(count):
    half = count // 2
    rounds = [("in", [(k, k + 1), (count - 1 - k, count - 2 - k)], k) for k in range(half - 1)]
    rounds.append(("in", [(half - 1, half), (half, half - 1)], -1))
    for k in range(half - 2, -1, -1):
        rounds.append(("out", [(k + 1, k), (count - 2 - k, count - 1 - k)], k))
    return rounds


class Line:
    def __init__(self):
        self.last = None

    def wait(self, *values):
        if self.last is not None:
            values, _ = lax.optimization_barrier((values, self.last))
        return values

    def send(self, value, how):
        return how(*self.wait(value))

    def step(self, function, *values):
        out = function(*self.wait(*values))
        self.last = jax.tree.leaves(out)[0]
        return out


class Vectors:
    def __init__(self, line, vectors):
        owners = lax.axis_size("batch")
        me = lax.axis_index("batch")
        self.line = line
        self.sizes = [v.shape[0] // owners for v in vectors]
        pieces = jnp.concatenate([v.reshape(owners, -1) for v in vectors], axis=1)
        bits = list(range(owners.bit_length() - 1))
        rows = [lax.dynamic_slice_in_dim(pieces, r ^ me, 1, 0) for r in owner_order(bits)]
        self.held = jnp.concatenate(rows)
        count = lax.axis_size("seq")
        self.steps = [("swap", bit, 0) for bit in bits]
        self.steps += line_rounds(count) if count % 2 == 0 else []
        self.moving = None
        self.now = None
        self.send()

    def send(self):
        if self.moving is not None or not self.steps:
            return
        self.now = kind, what, _ = self.steps.pop(0)
        if kind == "swap":
            half = self.held.shape[0] // 2
            self.moving = self.line.send(self.held[:half], lambda a: swap(a, what))
            self.held = self.held[half:]
        else:
            self.moving = self.line.send(self.held, lambda a: lax.ppermute(a, "seq", what))

    def take(self):
        if self.moving is None:
            return
        kind, _, at = self.now
        if kind == "out":
            place, count = lax.axis_index("seq"), lax.axis_size("seq")
            edge = (place == at) | (place == count - 1 - at)
            self.held = self.line.step(
                lambda a, b: jnp.where(edge, b, a), self.held, self.moving
            )
        else:
            self.held = self.line.step(lambda a, b: a + b, self.held, self.moving)
        self.moving = None

    def results(self):
        while self.moving is not None or self.steps:
            self.take()
            self.send()
        if lax.axis_size("seq") % 2 and lax.axis_size("seq") > 1:
            self.held = lax.psum(self.held, "seq")
        out, at = [], 0
        for size in self.sizes:
            out.append(self.held[0, at : at + size])
            at += size
        return out


class Reduction:
    def __init__(self, line, left, right, bits):
        self.line = line
        half = left.shape[1] // 2
        send = line.step(lambda a, b: plain_dot(a, b, COLS_COLS), left[:, :half], right)
        self.held = line.step(lambda a, b: plain_dot(a, b, COLS_COLS), left[:, half:], right)
        count = lax.axis_size("seq")
        self.steps = [("swap", bit + 1, 0) for bit in bits]
        self.steps += line_rounds(count) if count % 2 == 0 else []
        self.moving = swap(send, bits[0] + 1)

    def finish(self):
        place, count = lax.axis_index("seq"), lax.axis_size("seq")
        for i, (kind, _, at) in enumerate(self.steps):
            if kind == "out":
                edge = (place == at) | (place == count - 1 - at)
                self.held = self.line.step(
                    lambda a, b: jnp.where(edge, b, a), self.held, self.moving
                )
            else:
                self.held = self.line.step(lambda a, b: a + b, self.held, self.moving)
            if i + 1 == len(self.steps):
                break
            kind, what, _ = self.steps[i + 1]
            if kind == "swap":
                half = self.held.shape[0] // 2
                self.moving = swap(self.held[:half], what)
                self.held = self.held[half:]
            else:
                self.moving = lax.ppermute(self.held, "seq", what)
        return self.held if count % 2 == 0 or count == 1 else lax.psum(self.held, "seq")


class Singly:
    def __init__(self, line, bits):
        self.line, self.bits = line, bits
        self.pieces = []

    def prepare(self, pairs):
        for piece in (one for pair in pairs for one in pair):
            left, left_in, block, right, right_in, column = piece
            columns = slice(column * COLUMNS, (column + 1) * COLUMNS)
            left = jnp.concatenate([left[block], rounded(left_in[block])], axis=0)
            right = jnp.concatenate([right[:, columns], rounded(right_in[:, columns])], axis=0)
            self.pieces.append(Reduction(self.line, left, right, self.bits))

    def step(self):
        pass

    def finished(self):
        return True

    def results(self):
        return [one.finish() for one in self.pieces]


def rounded(arrived):
    one = jnp.where(lax.axis_index("seq") < lax.axis_size("seq"), 1.0, 0.5)
    return (arrived * one).astype(NARROW)


def product_kernel(count, *refs):
    ins, (to_x, to_y, hold_a, hold_b) = refs[: 8 * count], refs[-4:]
    for p in range(count):
        for i, (to, hold) in enumerate(((to_x, hold_a), (to_y, hold_b))):
            left, left_in, right, right_in = ins[8 * p + 4 * i : 8 * p + 4 * i + 4]
            whole = jnp.concatenate([left[0], left_in[0].astype(NARROW)], axis=0)
            right = jnp.concatenate([right[...], right_in[...].astype(NARROW)], axis=0)

            def product(first, second):
                rows = [whole[:, k * BLOCK : (k + 1) * BLOCK] for k in (first, second)]
                return plain_dot(jnp.concatenate(rows, axis=1), right, COLS_COLS)

            out = pl.ds(p * 2 * BLOCK, 2 * BLOCK)
            to[out, :] = product(0, 1 if i else 2)
            hold[out, :] = product(2 if i else 1, 3)


def round_kernel(counts, *refs):
    first, second, inward, middle, outward = counts
    refs = list(refs)
    edge = refs.pop(0)[0] != 0

    def take(flag, count):
        return [refs.pop(0) for _ in range(count)] if flag else [None] * count

    from_x, from_y = take(first or second, 2)
    hold_a, hold_b = take(first, 2)
    kept_a, kept_b = take(second, 2)
    (sums,) = take(inward, 1)
    (from_end,) = take(inward or outward, 1)
    inner, from_middle = take(middle, 2)
    (whole,) = take(outward, 1)
    to_x, to_y, keep_a, keep_b = take(first, 4)
    (new_sums,) = take(second, 1)
    (to_end,) = take(second or middle, 1)
    (new_inner,) = take(inward, 1)
    (new_whole,) = take(middle, 1)
    (final,) = take(outward, 1)
    for p in range(first):
        low = pl.ds(2 * p * BLOCK, BLOCK)
        high = pl.ds((2 * p + 1) * BLOCK, BLOCK)
        out = pl.ds(p * BLOCK, BLOCK)
        to_y[out, :] = hold_a[low, :] + from_x[low, :]
        to_x[out, :] = hold_b[low, :] + from_y[low, :]
        keep_a[out, :] = hold_a[high, :] + from_x[high, :]
        keep_b[out, :] = hold_b[high, :] + from_y[high, :]
    for p in range(max(second, middle)):
        for i, (kept, arrived) in enumerate(((kept_a, from_y), (kept_b, from_x))):
            out = pl.ds((2 * p + i) * BLOCK, BLOCK)
            ends = inners = None
            if p < second:
                come = pl.ds((2 * first + p) * BLOCK, BLOCK)
                ends = kept[pl.ds(p * BLOCK, BLOCK), :] + arrived[come, :]
                new_sums[out, :] = ends
            if p < middle:
                inners = inner[out, :] + from_middle[out, :]
                new_whole[out, :] = inners
            if ends is None:
                to_end[out, :] = inners
            elif inners is None:
                to_end[out, :] = ends
            else:
                to_end[out, :] = jnp.where(edge, ends, inners)
    if inward:
        new_inner[...] = sums[...] + from_end[: 2 * inward * BLOCK, :]
    if outward:
        final[...] = jnp.where(edge, from_end[: 2 * outward * BLOCK, :], whole[...])


class Rounds:
    PARTS = 2

    def __init__(self, line, edge, counts):
        self.line, self.edge, self.counts = line, edge, counts
        self.made = self.at = 0
        self.buffers, self.moving, self.hold, self.kept = {}, {}, {}, {}
        self.sums, self.inner, self.whole, self.finals = {}, {}, {}, []
        self.end = self.middle = None
        self.wide = COLUMNS // self.PARTS

    def count(self, group):
        return self.counts[group] if 0 <= group < len(self.counts) else 0

    def rows_spec(self, rows, at=0):
        return pl.BlockSpec((rows, self.wide), lambda i: (at, i))

    def prepare(self, pairs):
        r = self.made
        self.made += 1
        count = len(pairs)
        args, specs = [], []
        for left, left_in, block, right, right_in, column in (
            one for pair in pairs for one in pair
        ):
            for value in (left, left_in):
                args.append(value)
                specs.append(
                    pl.BlockSpec((1, *value.shape[1:]), lambda i, block=block: (block, 0, 0))
                )
            for value in (right, right_in):
                args.append(value)
                specs.append(
                    pl.BlockSpec(
                        (value.shape[0], self.wide),
                        lambda i, c=column: (0, c * self.PARTS + i),
                    )
                )
        rows = 2 * count * BLOCK
        total = rows + self.count(r - 2) * BLOCK
        aliases = {}
        if r in self.buffers:
            aliases = {len(args) + i: i for i in range(2)}
            args += list(self.buffers.pop(r))
            specs += [pl.BlockSpec(memory_space=pl.ANY)] * 2
        call = pl.pallas_call(
            partial(product_kernel, count),
            grid=(self.PARTS,),
            in_specs=specs,
            out_specs=[self.rows_spec(rows)] * 4,
            out_shape=[jax.ShapeDtypeStruct((total, COLUMNS), WIDE)] * 2
            + [jax.ShapeDtypeStruct((rows, COLUMNS), WIDE)] * 2,
            input_output_aliases=aliases,
            name="piece_products",
        )
        to_x, to_y, hold_a, hold_b = self.line.step(call, *args)
        self.hold[r] = (hold_a, hold_b)
        self.moving[r] = (swap(to_x, 1), swap(to_y, 2))

    def step(self):
        r = self.at
        self.at += 1
        counts = [self.count(r - back) for back in (0, 2, 3, 4, 5)]
        first, second, inward, middle, outward = counts
        args, specs = [self.edge], [pl.BlockSpec(memory_space=pltpu.SMEM)]

        def add(value):
            args.append(value)
            specs.append(self.rows_spec(value.shape[0]))

        if first or second:
            for value in self.moving.pop(r):
                add(value)
        if first:
            for value in self.hold.pop(r):
                add(value)
        if second:
            for value in self.kept.pop(r - 2):
                add(value)
        if inward:
            add(self.sums.pop(r - 3))
        if inward or outward:
            add(self.end)
        if middle:
            add(self.inner.pop(r - 4))
            add(self.middle)
        if outward:
            add(self.whole.pop(r - 5))
        outs, out_specs = [], []

        def out(rows, at=0, of=None):
            outs.append(jax.ShapeDtypeStruct((of or rows, COLUMNS), WIDE))
            out_specs.append(self.rows_spec(rows, at))

        ahead = self.count(r + 2)
        if first:
            for _ in range(2):
                out(first * BLOCK, 2 * ahead // first, (2 * ahead + first) * BLOCK)
            out(first * BLOCK)
            out(first * BLOCK)
        if second:
            out(2 * second * BLOCK)
        if second or middle:
            out(2 * max(second, middle) * BLOCK)
        for count in (inward, middle, outward):
            if count:
                out(2 * count * BLOCK)
        call = pl.pallas_call(
            partial(round_kernel, counts),
            grid=(self.PARTS,),
            in_specs=specs,
            out_specs=out_specs,
            out_shape=outs,
            name="reduce_round",
        )
        got = list(self.line.step(call, *args))
        if first:
            to = (got.pop(0), got.pop(0))
            if ahead:
                self.buffers[r + 2] = to
            else:
                self.moving[r + 2] = (swap(to[0], 1), swap(to[1], 2))
            self.kept[r] = (got.pop(0), got.pop(0))
        if second:
            self.sums[r - 2] = got.pop(0)
        if second or middle:
            self.end = lax.ppermute(got.pop(0), "seq", [(0, 1), (1, 0), (2, 3), (3, 2)])
        if inward:
            self.inner[r - 3] = got.pop(0)
            self.middle = lax.ppermute(self.inner[r - 3], "seq", [(1, 2), (2, 1)])
        if middle:
            self.whole[r - 4] = got.pop(0)
        if outward:
            self.finals.append(got.pop(0))

    def finished(self):
        return len(self.finals) == len(self.counts)

    def results(self):
        return [
            final[k * BLOCK : (k + 1) * BLOCK]
            for final in self.finals
            for k in range(final.shape[0] // BLOCK)
        ]


def pick_kernel(me_ref, *refs):
    ins, (keep_ref, send_ref) = refs[:-2], refs[-2:]
    half = keep_ref.shape[2] // BLOCK
    for i, ref in enumerate(ins):
        for p in range(half):
            for core in range(2):
                owner = (2 * (half - 1 - p) + core) ^ me_ref[0]
                columns = ref[:, pl.ds(pl.multiple_of(owner * BLOCK, BLOCK), BLOCK)]
                at = slice(p * BLOCK, (p + 1) * BLOCK)
                if core:
                    send_ref[i, :, at] = columns.astype(WIDE)
                else:
                    keep_ref[i, :, at] = columns


def pick(arrays, me):
    owners = lax.axis_size("batch")
    half = owners // 2
    tokens, features = arrays[0].shape
    size = features // owners
    if size != BLOCK:

        def columns(value, core):
            return jnp.concatenate(
                [
                    lax.dynamic_slice_in_dim(value, ((2 * r + core) ^ me[0]) * size, size, 1)
                    for r in range(half)[::-1]
                ],
                axis=1,
            )

        return (
            jnp.stack([columns(a, 0) for a in arrays]),
            jnp.stack([columns(a, 1) for a in arrays]).astype(WIDE),
        )
    shape = (len(arrays), tokens, half * size)
    return pl.pallas_call(
        pick_kernel,
        in_specs=[pl.BlockSpec(memory_space=pltpu.SMEM)]
        + [pl.BlockSpec(memory_space=pltpu.VMEM)] * len(arrays),
        out_specs=[pl.BlockSpec(memory_space=pltpu.VMEM)] * 2,
        out_shape=[jax.ShapeDtypeStruct(shape, NARROW), jax.ShapeDtypeStruct(shape, WIDE)],
        name="pick_columns",
    )(me, *arrays)


def norm_kernel(x_ref, gain1, bias1, gain2, bias2, attn_ref, mlp_ref, unit_ref, rate_ref):
    x = x_ref[...].astype(WIDE)
    centered = x - jnp.mean(x, axis=-1, keepdims=True)
    rate = lax.rsqrt(jnp.mean(centered * centered, axis=-1, keepdims=True) + EPSILON)
    unit = centered * rate
    unit_ref[...] = unit
    rate_ref[...] = jnp.broadcast_to(rate, rate_ref.shape)
    for gain, bias, out in ((gain1, bias1, attn_ref), (gain2, bias2, mlp_ref)):
        out[...] = (unit * gain[...].astype(WIDE) + bias[...].astype(WIDE)).astype(NARROW)


def two_norms(inputs, *gains):
    tokens = inputs.shape[0]
    rows = tokens // 4
    by_rows = pl.BlockSpec((rows, D), lambda i: (i, 0))
    return pl.pallas_call(
        norm_kernel,
        grid=(4,),
        in_specs=[by_rows] + [whole_spec((1, D))] * 4,
        out_specs=[by_rows, by_rows, by_rows, pl.BlockSpec((rows, 128), lambda i: (i, 0))],
        out_shape=[
            jax.ShapeDtypeStruct((tokens, D), NARROW),
            jax.ShapeDtypeStruct((tokens, D), NARROW),
            jax.ShapeDtypeStruct((tokens, D), WIDE),
            jax.ShapeDtypeStruct((tokens, 128), WIDE),
        ],
        name="two_norms",
    )(inputs, *gains)


def up_kernel(
    half, me_ref, x_ref, weight_ref, bias_ref, act_ref, slope_ref, keep_ref, send_ref
):
    step = pl.program_id(0)
    up = plain_dot(x_ref[...], weight_ref[...], ROWS_COLS) + bias_ref[...].astype(WIDE)
    below = 0.5 * (1.0 + lax.erf(up * (0.5**0.5)))
    act = (up * below).astype(NARROW)
    act_ref[...] = act
    slope_ref[...] = below + up * jnp.exp(-0.5 * up * up) * ((2.0 * math.pi) ** -0.5)

    @pl.when(step < half)
    def _():
        for i in range(keep_ref.shape[0]):
            keep_ref[i] = act[:, i * BLOCK : (i + 1) * BLOCK]

    @pl.when(step >= half)
    def _():
        wide = act.astype(WIDE)
        for i in range(send_ref.shape[0]):
            send_ref[i] = wide[:, i * BLOCK : (i + 1) * BLOCK]


def mlp_up(mlp_in, up_weight, up_bias, me):
    owners = lax.axis_size("batch")
    tokens = mlp_in.shape[0]
    half = owners // 2
    each = FF // owners
    subs = each // BLOCK

    def natural(i, me):
        return (0, (2 * (i % half) + i // half) ^ me[0])

    return pl.pallas_call(
        partial(up_kernel, half),
        grid_spec=pltpu.PrefetchScalarGridSpec(
            num_scalar_prefetch=1,
            grid=(owners,),
            in_specs=[
                pl.BlockSpec((tokens, D), lambda i, me: (0, 0)),
                pl.BlockSpec((D, each), natural),
                pl.BlockSpec((1, each), natural),
            ],
            out_specs=[
                pl.BlockSpec((tokens, each), natural),
                pl.BlockSpec((tokens, each), natural),
                pl.BlockSpec(
                    (subs, tokens, BLOCK),
                    lambda i, me: (0, 0, half - 1 - jnp.minimum(i, half - 1)),
                ),
                pl.BlockSpec(
                    (subs, tokens, BLOCK),
                    lambda i, me: (0, 0, half - 1 - jnp.maximum(i - half, 0)),
                ),
            ],
        ),
        out_shape=[
            jax.ShapeDtypeStruct((tokens, FF), NARROW),
            jax.ShapeDtypeStruct((tokens, FF), WIDE),
            jax.ShapeDtypeStruct((subs, tokens, half * BLOCK), NARROW),
            jax.ShapeDtypeStruct((subs, tokens, half * BLOCK), WIDE),
        ],
        name="mlp_up",
    )(me, mlp_in, up_weight, up_bias)


def back_kernel(
    cot_ref, down_ref, up_ref, act_ref, slope_ref, grad_ref, send_ref, sums_ref, out_ref, norm_ref
):
    step = pl.program_id(0)
    down = down_ref[...]
    grad = plain_dot(cot_ref[...], down, ROWS_ROWS) * slope_ref[...]
    grad = grad.astype(NARROW)
    grad_ref[...] = grad
    wide = grad.astype(WIDE)
    send_ref[...] = wide
    sums_ref[...] = jnp.sum(wide, axis=0, keepdims=True)
    out = plain_dot(act_ref[...], down, ROWS_COLS)
    norm = plain_dot(grad, up_ref[...], ROWS_ROWS)

    @pl.when(step == 0)
    def _():
        out_ref[...] = out
        norm_ref[...] = norm

    @pl.when(step > 0)
    def _():
        out_ref[...] += out
        norm_ref[...] += norm


def mlp_back(cot, down_weight, up_weight, act, slope):
    tokens = cot.shape[0]
    each = 1024
    by_column = pl.BlockSpec((tokens, each), lambda i: (0, i))
    total = whole_spec((tokens, D))
    return pl.pallas_call(
        back_kernel,
        grid=(FF // each,),
        in_specs=[
            total,
            pl.BlockSpec((each, D), lambda i: (i, 0)),
            pl.BlockSpec((D, each), lambda i: (0, i)),
            by_column,
            by_column,
        ],
        out_specs=[
            by_column,
            by_column,
            pl.BlockSpec((1, each), lambda i: (0, i)),
            total,
            total,
        ],
        out_shape=[
            jax.ShapeDtypeStruct((tokens, FF), NARROW),
            jax.ShapeDtypeStruct((tokens, FF), WIDE),
            jax.ShapeDtypeStruct((1, FF), WIDE),
            jax.ShapeDtypeStruct((tokens, D), WIDE),
            jax.ShapeDtypeStruct((tokens, D), WIDE),
        ],
        name="mlp_back",
    )(cot, down_weight, up_weight, act, slope)


def output_kernel(low_ref, weight_ref, x_ref, mlp_ref, dense_ref, down_ref, out_ref):
    attn = plain_dot(low_ref[...], weight_ref[...], ROWS_COLS) + dense_ref[...].astype(WIDE)
    mlp = mlp_ref[...] + down_ref[...].astype(WIDE)
    out_ref[...] = (x_ref[...].astype(WIDE) + attn + mlp).astype(NARROW)


def layer_output(low, dense_weight, inputs, mlp_out, *biases):
    tokens = inputs.shape[0]
    each = 512
    by_column = pl.BlockSpec((tokens, each), lambda i: (0, i))
    return pl.pallas_call(
        output_kernel,
        grid=(D // each,),
        in_specs=[
            whole_spec((tokens, D)),
            pl.BlockSpec((D, each), lambda i: (0, i)),
            by_column,
            by_column,
            pl.BlockSpec((1, each), lambda i: (0, i)),
            pl.BlockSpec((1, each), lambda i: (0, i)),
        ],
        out_specs=by_column,
        out_shape=jax.ShapeDtypeStruct((tokens, D), NARROW),
        name="layer_output",
    )(low, dense_weight, inputs, mlp_out, *biases)


def norm_back_kernel(
    qkv_ref,
    weight_ref,
    mlp_ref,
    unit_ref,
    rate_ref,
    cot_ref,
    gain1,
    gain2,
    grad_ref,
    sums_ref,
    qkv_sums,
):
    step = pl.program_id(0)
    qkv = qkv_ref[...]
    qkv_sums[...] = jnp.sum(qkv.astype(WIDE), axis=0, keepdims=True)
    part = plain_dot(qkv, weight_ref[...], ROWS_ROWS)

    @pl.when(step == 0)
    def _():
        grad_ref[...] = part

    @pl.when(step > 0)
    def _():
        grad_ref[...] += part

    @pl.when(step == pl.num_programs(0) - 1)
    def _():
        size = 64
        gain_attn, gain_mlp = gain1[...].astype(WIDE), gain2[...].astype(WIDE)
        totals = [jnp.zeros((1, D), WIDE)] * 5
        for k in range(grad_ref.shape[0] // size):
            rows = pl.ds(k * size, size)
            attn, mlp, unit = grad_ref[rows, :], mlp_ref[rows, :], unit_ref[rows, :]
            cot = cot_ref[rows, :].astype(WIDE)
            together = attn * gain_attn + mlp * gain_mlp
            grad_ref[rows, :] = cot + rate_ref[rows, 0:1] * (
                together
                - jnp.mean(together, axis=-1, keepdims=True)
                - unit * jnp.mean(together * unit, axis=-1, keepdims=True)
            )
            for i, value in enumerate((attn * unit, attn, mlp * unit, mlp, cot)):
                totals[i] = totals[i] + jnp.sum(value, axis=0, keepdims=True)
        for i, value in enumerate(totals):
            sums_ref[i : i + 1, :] = value
        sums_ref[5:8, :] = jnp.zeros((3, D), WIDE)


def norm_back(qkv_grad, qkv_weight, mlp_norm_grad, unit, rate, cot, gain1, gain2):
    tokens = cot.shape[0]
    each = 512
    total = whole_spec((tokens, D))
    return pl.pallas_call(
        norm_back_kernel,
        grid=(3 * D // each,),
        in_specs=[
            pl.BlockSpec((tokens, each), lambda i: (0, i)),
            pl.BlockSpec((D, each), lambda i: (0, i)),
            total,
            total,
            whole_spec(rate.shape),
            total,
            whole_spec((1, D)),
            whole_spec((1, D)),
        ],
        out_specs=[total, whole_spec((8, D)), pl.BlockSpec((1, each), lambda i: (0, i))],
        out_shape=[
            jax.ShapeDtypeStruct((tokens, D), WIDE),
            jax.ShapeDtypeStruct((8, D), WIDE),
            jax.ShapeDtypeStruct((1, 3 * D), WIDE),
        ],
        name="norm_back",
    )(qkv_grad, qkv_weight, mlp_norm_grad, unit, rate, cot, gain1, gain2)


def dct_matrix():
    rows = np.arange(HEAD)[:, None]
    columns = np.arange(HEAD)[None, :]
    cosines = np.cos(np.pi * (columns + 0.5) * rows / HEAD) * np.sqrt(2.0 / HEAD)
    return np.where(rows == 0, cosines * np.sqrt(0.5), cosines).astype(np.float32)


def attention_tables(positions, points, weights):
    half_rot = ROT // 2
    lane = jnp.arange(PAIR) % HEAD
    freq = ROTARY_BASE ** (-2.0 * (lane % half_rot).astype(WIDE) / ROT)
    angles = positions.astype(WIDE)[:, None] * freq[None, :]
    sin = jnp.sin(angles)
    tables = jnp.stack(
        [
            jnp.where(lane < ROT, jnp.cos(angles), 1.0),
            jnp.where(lane < half_rot, -sin, 0.0),
            jnp.where((lane >= half_rot) & (lane < ROT), sin, 0.0),
        ]
    )
    mix = HEAD ** (-0.25) * jnp.einsum(
        "kn,km->nm", dct_matrix(), points, precision=lax.Precision.HIGHEST
    )
    side = jnp.arange(PAIR) // HEAD
    mix = jnp.where(side[:, None] == side[None, :], jnp.tile(mix, (2, 2)), 0.0)
    return tables, mix, jnp.tile(weights, 2)[None, :]


def lane_is_low(shape):
    return lax.broadcasted_iota(jnp.int32, shape, len(shape) - 1) % PAIR < HEAD


def halves(full):
    return jnp.where(lane_is_low((HEAD, PAIR)), full[:HEAD], full[HEAD:])


def spread_pair(block):
    low = lane_is_low(block.shape)
    zero = jnp.zeros_like(block)
    return jnp.concatenate([jnp.where(low, block, zero), jnp.where(low, zero, block)], axis=0)


def one_head(tile, head):
    low = lane_is_low(tile.shape)
    zero = jnp.zeros_like(tile)
    return jnp.where(low, tile, zero) if head == 0 else jnp.where(low, zero, tile)


def in_two(value):
    high = value.astype(NARROW)
    return high, (value - high.astype(WIDE)).astype(NARROW)


def fine_dot(left, right, dims):
    left_high, left_low = in_two(left)
    right_high, right_low = in_two(right)
    return (
        plain_dot(left_high, right_high, dims)
        + plain_dot(left_low, right_high, dims)
        + plain_dot(left_high, right_low, dims)
    )


def head_sums(tile):
    rows = lax.broadcasted_iota(jnp.int32, (PAIR, PAIR), 0) // HEAD
    columns = lax.broadcasted_iota(jnp.int32, (PAIR, PAIR), 1) // HEAD
    ones = (rows == columns).astype(WIDE).astype(NARROW)
    high, low = in_two(tile)
    return plain_dot(
        jnp.concatenate([high, low], axis=1), jnp.concatenate([ones, ones], axis=0), ROWS_COLS
    )


def turn(tile, cos, sin_up, sin_down):
    half_rot = ROT // 2
    return (
        tile * cos
        + pltpu.roll(tile, PAIR - half_rot, 1) * sin_up
        + pltpu.roll(tile, half_rot, 1) * sin_down
    )


def turn_back(tile, cos, sin_up, sin_down):
    half_rot = ROT // 2
    return (
        tile * cos
        + pltpu.roll(tile * sin_up, half_rot, 1)
        + pltpu.roll(tile * sin_down, PAIR - half_rot, 1)
    )


def all_rows(tables_ref, seqs):
    return [jnp.concatenate([tables_ref[k]] * seqs, axis=0) for k in range(3)]


def feature_grad(grad, phi, turned, mix, tables):
    weighted = grad * phi
    back = fine_dot(weighted, mix, ROWS_ROWS) - (HEAD**-0.5) * turned * head_sums(weighted)
    return turn_back(back, *tables)


def doc_at(where, lengths_ref, b):
    start, found = 0, jnp.zeros_like(where) - 1
    for k in range(lengths_ref.shape[1]):
        found = found + jnp.where(start <= where, 1, 0)
        start = start + lengths_ref[b, k]
    return found


def same_doc_before(lengths_ref, b, first, context):
    query = first + lax.broadcasted_iota(jnp.int32, (context, context), 0)
    key = first + lax.broadcasted_iota(jnp.int32, (context, context), 1)
    same = doc_at(query, lengths_ref, b) == doc_at(key, lengths_ref, b)
    return jnp.where(same & (key <= query), 1.0, 0.0)


def in_doc_of(lengths_ref, b, first, context, where):
    rows = first + lax.broadcasted_iota(jnp.int32, (context, PAIR), 0)
    return jnp.where(doc_at(rows, lengths_ref, b) == doc_at(where, lengths_ref, b), 1.0, 0.0)


def local_kernel(
    seqs,
    lengths_ref,
    first_ref,
    attn_ref,
    weight_ref,
    bias_ref,
    tables_ref,
    mix_ref,
    wrow_ref,
    fq_ref,
    fk_ref,
    val_ref,
    phiq_ref,
    phik_ref,
    rotq_ref,
    rotk_ref,
    num_ref,
    den_ref,
    score_ref,
    carry_ref,
):
    context = tables_ref.shape[1]
    first = first_ref[0]
    mix, wrow = mix_ref[...], wrow_ref[...]
    tables = all_rows(tables_ref, seqs)
    low = lane_is_low((seqs * context, PAIR))
    block = plain_dot(attn_ref[...], weight_ref[...], ROWS_COLS) + bias_ref[...].astype(WIDE)
    one, two, three = block[:, :PAIR], block[:, PAIR : 2 * PAIR], block[:, 2 * PAIR :]
    query = jnp.where(low, one, two)
    key = pltpu.roll(jnp.where(low, three, one), HEAD, 1)
    value_all = jnp.where(low, two, three).astype(NARROW)
    val_ref[...] = value_all

    def features(raw):
        turned = turn(raw, *tables)
        power = fine_dot(turned, mix, ROWS_COLS) - (0.5 * HEAD**-0.5) * head_sums(turned * turned)
        return turned, wrow * jnp.exp(power)

    turned_q, phi_q = features(query)
    turned_k, phi_k = features(key)
    rotq_ref[...], rotk_ref[...] = turned_q, turned_k
    phiq_ref[...], phik_ref[...] = phi_q, phi_k
    fq_all, fk_all = phi_q.astype(NARROW), phi_k.astype(NARROW)
    fq_ref[...], fk_ref[...] = fq_all, fk_all
    low = lane_is_low((context, PAIR))
    for b in range(seqs):
        rows = slice(b * context, (b + 1) * context)
        fq, fk, value = fq_all[rows], fk_all[rows], value_all[rows]
        mask = same_doc_before(lengths_ref, b, first, context)
        keep = in_doc_of(lengths_ref, b, first, context, first + context - 1)
        wide_value = jnp.concatenate([value, jnp.ones_like(value)], axis=1)
        sums = []
        for h in range(2):
            scores = (plain_dot(one_head(fq, h), fk, ROWS_ROWS) * mask).astype(NARROW)
            score_ref[0, b, h] = scores
            sums.append(plain_dot(scores, wide_value, ROWS_COLS))
        num_ref[rows, :] = jnp.where(low, sums[0][:, :PAIR], sums[1][:, :PAIR])
        den_ref[rows, :] = jnp.where(low, sums[0][:, PAIR:], sums[1][:, PAIR:])
        kept = fk * keep.astype(NARROW)
        carry_ref[b, 0, :HEAD, :] = halves(plain_dot(kept, value, COLS_COLS))
        norm = jnp.sum(kept.astype(WIDE), axis=0, keepdims=True)
        carry_ref[b, 0, HEAD:, :] = jnp.broadcast_to(norm, (8, PAIR))


def middle_kernel(
    seqs,
    lengths_ref,
    first_ref,
    cot_ref,
    dense_ref,
    fq_ref,
    fk_ref,
    val_ref,
    phiq_ref,
    rotq_ref,
    num_ref,
    den_ref,
    score_ref,
    carry_ref,
    tables_ref,
    mix_ref,
    low_ref,
    gradq_ref,
    gradk_ref,
    gradv_ref,
    out_ref,
):
    context = tables_ref.shape[1]
    first = first_ref[0]
    mix = mix_ref[...]
    tables = all_rows(tables_ref, seqs)
    low = lane_is_low((context, PAIR))
    back_all = plain_dot(cot_ref[...], dense_ref[...], ROWS_ROWS)
    grads_q = []
    for b in range(seqs):
        rows = pl.ds(b * context, context)
        fq, fk, value = fq_ref[rows, :], fk_ref[rows, :], val_ref[rows, :]
        use = in_doc_of(lengths_ref, b, first, context, first - 1)
        state = spread_pair(carry_ref[b, 0, :HEAD, :].astype(NARROW))
        norm = carry_ref[b, 0, HEAD : HEAD + 1, :]
        wide_fq = fq.astype(WIDE)
        num = num_ref[rows, :] + use * plain_dot(fq, state, ROWS_COLS)
        den = den_ref[rows, :] + use * head_sums(wide_fq * norm)
        heads_out = num / den
        low_ref[rows, :] = heads_out.astype(NARROW)
        back = back_all[b * context : (b + 1) * context]
        num_grad = (back / den).astype(NARROW)
        den_grad = -head_sums(back * heads_out) / den
        mask = same_doc_before(lengths_ref, b, first, context)
        parts_q, parts_k, parts_v = [], [], []
        for h in range(2):
            column = den_grad[:, h * HEAD : h * HEAD + 1]
            score_grad = plain_dot(one_head(num_grad, h), value, ROWS_ROWS) + column
            score_grad = (score_grad * mask).astype(NARROW)
            parts_q.append(plain_dot(score_grad, fk, ROWS_COLS))
            parts_k.append(plain_dot(score_grad, fq, COLS_COLS))
            parts_v.append(plain_dot(score_ref[0, b, h], num_grad, COLS_COLS))
        gradk_ref[rows, :] = jnp.where(low, parts_k[0], parts_k[1])
        gradv_ref[rows, :] = jnp.where(low, parts_v[0], parts_v[1])
        num_used = num_grad * use.astype(NARROW)
        den_used = den_grad * use
        grads_q.append(
            jnp.where(low, parts_q[0], parts_q[1])
            + plain_dot(num_used, state, ROWS_ROWS)
            + den_used * norm
        )
        out_ref[b, 0, :HEAD, :] = halves(plain_dot(fq, num_used, COLS_COLS))
        norm_grad = jnp.sum(den_used * wide_fq, axis=0, keepdims=True)
        out_ref[b, 0, HEAD:, :] = jnp.broadcast_to(norm_grad, (8, PAIR))
    gradq_ref[...] = feature_grad(
        jnp.concatenate(grads_q, axis=0), phiq_ref[...], rotq_ref[...], mix, tables
    ).astype(NARROW)


def last_kernel(
    seqs,
    lengths_ref,
    first_ref,
    gradq_ref,
    gradk_ref,
    gradv_ref,
    fk_ref,
    val_ref,
    phik_ref,
    rotk_ref,
    carry_ref,
    tables_ref,
    mix_ref,
    out_ref,
    send_ref,
):
    context = tables_ref.shape[1]
    first = first_ref[0]
    tables = all_rows(tables_ref, seqs)
    grads_k, grads_v = [], []
    for b in range(seqs):
        rows = pl.ds(b * context, context)
        keep = in_doc_of(lengths_ref, b, first, context, first + context - 1)
        state = spread_pair(carry_ref[b, 0, :HEAD, :].astype(NARROW))
        norm = carry_ref[b, 0, HEAD : HEAD + 1, :]
        grads_k.append(
            gradk_ref[rows, :] + keep * (plain_dot(val_ref[rows, :], state, ROWS_ROWS) + norm)
        )
        grads_v.append(gradv_ref[rows, :] + keep * plain_dot(fk_ref[rows, :], state, ROWS_COLS))
    grad_k = feature_grad(
        jnp.concatenate(grads_k, axis=0), phik_ref[...], rotk_ref[...], mix_ref[...], tables
    )
    grad_k = pltpu.roll(grad_k, HEAD, 1)
    grad_v = jnp.concatenate(grads_v, axis=0)
    grad_q = gradq_ref[...].astype(WIDE)
    low = lane_is_low(grad_q.shape)
    grad = jnp.concatenate(
        [
            jnp.where(low, grad_q, grad_k),
            jnp.where(low, grad_v, grad_q),
            jnp.where(low, grad_k, grad_v),
        ],
        axis=1,
    ).astype(NARROW)
    out_ref[...] = grad
    send_ref[...] = grad.astype(WIDE)


def pass_kernel(lengths_ref, first_ref, own_ref, arrived_ref, out_ref):
    context = first_ref[1]
    for b in range(own_ref.shape[0]):
        last = doc_at(first_ref[0] + context - 1, lengths_ref, b)
        through = last == doc_at(first_ref[0] - 1, lengths_ref, b)
        out_ref[b] = own_ref[b] + jnp.where(through, arrived_ref[b], 0.0)


SMEM_SPEC = pl.BlockSpec(memory_space=pltpu.SMEM)


def pass_on(own, arrived, lengths, first):
    seqs, pairs = own.shape[:2]
    spec = pl.BlockSpec((seqs, pairs // 2, *own.shape[2:]), lambda i: (0, i, 0, 0))
    return pl.pallas_call(
        pass_kernel,
        grid=(2,),
        in_specs=[SMEM_SPEC, SMEM_SPEC, spec, spec],
        out_specs=spec,
        out_shape=jax.ShapeDtypeStruct(own.shape, WIDE),
        name="pass_carry",
    )(lengths, first, own, arrived)


def pair_spec(rows):
    return pl.BlockSpec((None, rows, PAIR), lambda i: (i, 0, 0))


def pair_shapes(tokens):
    shape = (HEADS // 2, tokens, PAIR)
    return jax.ShapeDtypeStruct(shape, NARROW), jax.ShapeDtypeStruct(shape, WIDE)


def attention_specs(seqs, context):
    carry = pl.BlockSpec((seqs, 1, HEAD + 8, PAIR), lambda i: (0, i, 0, 0))
    scores = pl.BlockSpec((1, seqs, 2, context, context), lambda i: (i, 0, 0, 0, 0))
    return carry, scores, [whole_spec((3, context, PAIR)), whole_spec((PAIR, PAIR))]


def attention_local(lengths, first, attn_in, weight, bias, tables, mix, wrow):
    seqs, context, tokens = lengths.shape[0], tables.shape[1], attn_in.shape[0]
    pairs = HEADS // 2
    carry, scores, shared = attention_specs(seqs, context)
    narrow, wide = pair_shapes(tokens)
    return pl.pallas_call(
        partial(local_kernel, seqs),
        grid=(pairs,),
        in_specs=[
            SMEM_SPEC,
            SMEM_SPEC,
            whole_spec((tokens, D)),
            pl.BlockSpec((D, 3 * PAIR), lambda i: (0, i)),
            pl.BlockSpec((1, 3 * PAIR), lambda i: (0, i)),
            *shared,
            whole_spec((1, PAIR)),
        ],
        out_specs=[pair_spec(tokens)] * 9 + [scores, carry],
        out_shape=[narrow] * 3
        + [wide] * 6
        + [
            jax.ShapeDtypeStruct((pairs, seqs, 2, context, context), NARROW),
            jax.ShapeDtypeStruct((seqs, pairs, HEAD + 8, PAIR), WIDE),
        ],
        name="attention_local",
    )(lengths, first, attn_in, weight, bias, tables, mix, wrow)


def attention_middle(lengths, first, cot, dense_weight, *rest):
    seqs, context, tokens = lengths.shape[0], rest[-2].shape[1], cot.shape[0]
    pairs = HEADS // 2
    carry, scores, shared = attention_specs(seqs, context)
    narrow, wide = pair_shapes(tokens)
    return pl.pallas_call(
        partial(middle_kernel, seqs),
        grid=(pairs,),
        in_specs=[
            SMEM_SPEC,
            SMEM_SPEC,
            whole_spec((tokens, D)),
            pl.BlockSpec((PAIR, D), lambda i: (i, 0)),
        ]
        + [pair_spec(tokens)] * 7
        + [scores, carry, *shared],
        out_specs=[pl.BlockSpec((tokens, PAIR), lambda i: (0, i))]
        + [pair_spec(tokens)] * 3
        + [carry],
        out_shape=[jax.ShapeDtypeStruct((tokens, D), NARROW), narrow, wide, wide]
        + [jax.ShapeDtypeStruct((seqs, pairs, HEAD + 8, PAIR), WIDE)],
        name="attention_middle",
    )(lengths, first, cot, dense_weight, *rest)


def attention_last(lengths, first, *rest):
    seqs, context, tokens = lengths.shape[0], rest[-2].shape[1], rest[0].shape[1]
    carry, _, shared = attention_specs(seqs, context)
    return pl.pallas_call(
        partial(last_kernel, seqs),
        grid=(HEADS // 2,),
        in_specs=[SMEM_SPEC, SMEM_SPEC] + [pair_spec(tokens)] * 7 + [carry, *shared],
        out_specs=[pl.BlockSpec((tokens, 3 * PAIR), lambda i: (0, i))] * 2,
        out_shape=[
            jax.ShapeDtypeStruct((tokens, 3 * D), NARROW),
            jax.ShapeDtypeStruct((tokens, 3 * D), WIDE),
        ],
        name="attention_last",
    )(lengths, first, *rest)


def shards(
    inputs,
    lengths,
    ln1_gain,
    ln1_bias,
    ln2_gain,
    ln2_bias,
    qkv_weight,
    qkv_bias,
    dense_weight,
    dense_bias,
    up_weight,
    up_bias,
    down_weight,
    down_bias,
    qmc_points,
    qmc_weights,
    cotangent,
):
    seqs, context = inputs.shape[:2]
    tokens = seqs * context
    owners, count, place = lax.axis_size("batch"), lax.axis_size("seq"), lax.axis_index("seq")
    bits = list(range(owners.bit_length() - 2))[::-1]
    across = D // COLUMNS
    hops = max(1, count // 2)

    line = Line()
    me = lax.axis_index("batch").astype(jnp.int32)[None]
    edge = ((place == 0) | (place == count - 1)).astype(jnp.int32)[None]
    if owners == 8 and count == 4:
        reduction = Rounds(line, edge, [2, 2, 2, 2, 1, 1, 1, 1])
    else:
        reduction = Singly(line, bits)

    def pieces(left, left_in, blocks, right, right_in, columns):
        return [
            (left, left_in, block, right, right_in, column)
            for column in columns
            for block in blocks
        ]

    def pairs(parts):
        return list(zip(parts[::2], parts[1::2]))

    inputs_flat = inputs.reshape(tokens, D)
    cot = cotangent.reshape(tokens, D)
    cot_in = swap(cot.astype(WIDE), 0)
    gains = [v[None, :] for v in (ln1_gain, ln1_bias, ln2_gain, ln2_bias)]
    attn_in, mlp_in, unit, rate = line.step(two_norms, inputs_flat, *gains)
    act, slope, act_own, act_send = line.step(mlp_up, mlp_in, up_weight, up_bias[None, :], me)
    act_in = swap(act_send, 0)
    norm_own, norm_send = line.step(lambda *a: pick(a[:2], a[2]), attn_in, mlp_in, me)
    subs = act_own.shape[0]
    down_parts = [
        pieces(act_own, act_in, range(sub, sub + 2), cot, cot_in, range(across))
        for sub in range(0, subs, 2)
    ]
    reduction.prepare(pairs(down_parts[0]))
    up_grad, up_send, up_sums, mlp_out, mlp_norm_grad = line.step(
        mlp_back, cot, down_weight, up_weight, act, slope
    )
    for part in down_parts[1:]:
        reduction.prepare(pairs(part))
    reduction.step()
    up_in = line.send(up_send, lambda a: swap(a, 0))
    norm_in = line.send(norm_send, lambda a: swap(a, 0))

    start, lengths_here = line.wait(place * context, lengths)
    first = jnp.stack([start, jnp.full((), context, jnp.int32)])
    positions = start + jnp.arange(context, dtype=jnp.int32)
    tables, mix, wrow = attention_tables(positions, qmc_points, qmc_weights)
    fq, fk, value, phi_q, phi_k, rot_q, rot_k, num, den, scores, carry = line.step(
        attention_local,
        lengths_here,
        first,
        attn_in,
        qkv_weight,
        qkv_bias[None, :],
        tables,
        mix,
        wrow,
    )
    arrived = shift_rows(carry, "seq", 1)
    up_pieces = pieces(norm_own, norm_in, [1], up_grad, up_in, range(FF // COLUMNS))
    up_pairs = pairs(up_pieces)
    reduction.prepare(up_pairs[:2])
    reduction.step()
    reduction.prepare(up_pairs[2:])
    for _ in range(hops - 1):
        passed = line.step(pass_on, carry, arrived, lengths_here, first)
        arrived = shift_rows(passed, "seq", 1)
    attn_low, grad_q, grad_k, grad_v, carry_back = line.step(
        attention_middle,
        lengths_here,
        first,
        cot,
        dense_weight,
        fq,
        fk,
        value,
        phi_q,
        rot_q,
        num,
        den,
        scores,
        arrived,
        tables,
        mix,
    )
    arrived_back = shift_rows(carry_back, "seq", -1)
    low_own, low_send = line.step(lambda *a: pick(a[:1], a[1]), attn_low, me)
    low_in = swap(low_send, 0)
    output = line.step(
        layer_output,
        attn_low,
        dense_weight,
        inputs_flat,
        mlp_out,
        dense_bias[None, :],
        down_bias[None, :],
    )
    reduction.step()
    for _ in range(hops - 1):
        passed = line.step(pass_on, carry_back, arrived_back, lengths_here, first)
        arrived_back = shift_rows(passed, "seq", -1)
    dense_pieces = pieces(low_own, low_in, [0], cot, cot_in, range(across))
    reduction.prepare(pairs(dense_pieces))
    qkv_grad, qkv_send = line.step(
        attention_last,
        lengths_here,
        first,
        grad_q,
        grad_k,
        grad_v,
        fk,
        value,
        phi_k,
        rot_k,
        arrived_back,
        tables,
        mix,
    )
    reduction.step()
    qkv_in = line.send(qkv_send, lambda a: swap(a, 0))
    input_grad, sums, qkv_sums = line.step(
        norm_back, qkv_grad, qkv_weight, mlp_norm_grad, unit, rate, cot, gains[0], gains[2]
    )
    qkv_pieces = pieces(norm_own, norm_in, [0], qkv_grad, qkv_in, range(3 * D // COLUMNS))
    qkv_pairs = pairs(qkv_pieces)
    reduction.prepare(qkv_pairs[:1])
    vectors = Vectors(
        line, (sums[0], sums[1], sums[2], sums[3], qkv_sums[0], sums[4], up_sums[0])
    )
    for pair in qkv_pairs[1:]:
        vectors.take()
        reduction.step()
        reduction.prepare([pair])
        vectors.send()
    while not reduction.finished():
        vectors.take()
        reduction.step()
        vectors.send()
    totals = reduction.results()
    (
        attn_gain_total,
        attn_shift_total,
        mlp_gain_total,
        mlp_shift_total,
        qkv_bias_total,
        bias_total,
        up_bias_total,
    ) = vectors.results()

    def next_totals(parts):
        taken = totals[: len(parts)]
        del totals[: len(parts)]
        return taken

    down_total = []
    for part in down_parts:
        taken = next_totals(part)
        each = len(part) // across
        down_total += [jnp.concatenate(taken[block::each], axis=1) for block in range(each)]
    down_total = jnp.concatenate(down_total, axis=0)
    up_total, dense_total, qkv_total = (
        jnp.concatenate(next_totals(part), axis=1)
        for part in (up_pieces, dense_pieces, qkv_pieces)
    )
    return (
        output.reshape(inputs.shape),
        input_grad.reshape(inputs.shape),
        attn_gain_total,
        attn_shift_total,
        mlp_gain_total,
        mlp_shift_total,
        qkv_total,
        qkv_bias_total,
        dense_total,
        bias_total,
        up_total,
        up_bias_total,
        down_total,
        bias_total,
    )


def solution(mesh):
    placed = (
        P("batch", "seq", None),
        P("batch", None),
        P(),
        P(),
        P(),
        P(),
        P(),
        P(),
        P(),
        P(),
        P(),
        P(),
        P(),
        P(),
        P(),
        P(),
        P("batch", "seq", None),
    )
    return jax.shard_map(
        shards,
        mesh=mesh,
        in_specs=placed,
        out_specs=(
            P("batch", "seq", None),
            P("batch", "seq", None),
            P("batch"),
            P("batch"),
            P("batch"),
            P("batch"),
            P("batch", None),
            P("batch"),
            P("batch", None),
            P("batch"),
            P("batch", None),
            P("batch"),
            P("batch", None),
            P("batch"),
        ),
        check_vma=False,
    )
```

time: 889 us -> 443 us (0.50)
  waiting for transfers between devices: 500 us -> 113 us
  Pallas kernels: 0 us -> 186 us
  matrix products: 152 us -> 0.24 us
  blocking collectives: 97.2 us -> 0 us
  starting transfers between devices: 0.46 us -> 81.9 us
  other arithmetic: 39.5 us -> 9.22 us
  local copies, waits for them, and re-layouts: 77.1 us -> 48.8 us
  between operations: 18.1 us -> 1.58 us
    reduce_scatter x4 -> x0, waiting for transfers between devices: 287 us -> none  [the longest x1 120 us: shards(): lax.psum_scatter(down_grad, 'batch', scatter_dimension=0, tiled=True)]
    pallas_call x0 -> x33, Pallas kernels: none -> 186 us  [the longest x21 90.6 us: step(): out = function(*self.wait(*values))]
    psum x1 -> x0, waiting for transfers between devices: 160 us -> none  [shards(): lax.psum((shared[0], shared[1], shared[2], shared[3], shared[4], shared[5...]
    dot_general x43 -> x1, matrix products: 152 us -> 0.24 us  [attention_tables(): jnp.einsum('kn,km->nm', dct_matrix(), points, precision=lax.Precision.HIG...]
    ppermute x0 -> x54, waiting for transfers between devices: none -> 113 us  [the longest x4 35.5 us: shift_rows(): lax.ppermute(value, axis, [(i, i + by) for i in range(count) if 0 <= i +...]
    ppermute x0 -> x54, starting transfers between devices: none -> 81.9 us  [the longest x10 28.4 us: step(): self.end = lax.ppermute(got.pop(0), 'seq', [(0, 1), (1, 0), (2, 3), (3, 2)])]
    all_gather x2 -> x0, waiting for transfers between devices: 52.5 us -> none  [prefix(): gathered = jax.tree.map(lambda a: lax.all_gather(a, axis), part)]
    unnamed x2 -> x0, blocking collectives: 49.5 us -> none
  transfers between devices with their start and end apart: 7 -> 54, of which waited for: 6 -> 21; matrix products, arithmetic and copies ran while one was open for 20% -> 7% of each run, Pallas kernels for 0% -> 31%
where the time goes in v2:
time: 443 us; the launch traced here: 441 us
  Pallas kernels  186 us (42%)
  waiting for transfers between devices  113 us (26%)
  starting transfers between devices  81.9 us (18%)
  local copies, waits for them, and re-layouts  48.8 us (11%)
  other arithmetic  9.22 us (2%)
    pallas_call x21, Pallas kernels, step(): out = function(*self.wait(*values))  90.6 us
    ppermute x4, waiting for transfers between devices, shift_rows(): lax.ppermute(value, axis, [(i, i + by) for i in range(count) if 0 <= i +...  35.5 us
    ppermute x10, waiting for transfers between devices, step(): self.end = lax.ppermute(got.pop(0), 'seq', [(0, 1), (1, 0), (2, 3), (3, 2)])  34.1 us
    unnamed x131, local copies, waits for them, and re-layouts  31.3 us
    ppermute x10, starting transfers between devices, step(): self.end = lax.ppermute(got.pop(0), 'seq', [(0, 1), (1, 0), (2, 3), (3, 2)])  28.4 us
    ppermute x29, starting transfers between devices, swap(): lax.ppermute(value, 'batch', [(i, i ^ 1 << bit) for i in range(count)])  28.4 us
    ppermute x29, waiting for transfers between devices, swap(): lax.ppermute(value, 'batch', [(i, i ^ 1 << bit) for i in range(count)])  28.3 us
    pallas_call x1, Pallas kernels, attention_middle(): pl.pallas_call(partial(middle_kernel, seqs), grid=(pairs,), in_specs=[SME...  20 us
  transfers between devices with their start and end apart: 54, of which 21 were waited for; matrix products, arithmetic and copies ran while one was open for 7% of the time, Pallas kernels for 31%

profile of v2, /device:TPU:0, one launch (start us, length us, event | category | flops | bytes accessed | tf_op | source)
XLA Modules:
  0.0 440.7 jit_solution(3815719822340509007)
XLA Ops:
  7.1 3.9 two_norms.1
  11.0 11.1 %mlp_up.1 = (bf16[256,4096]{1,0:T(8,128)(2,1)}, f32[256,4096]{1,0:T(8,128)}, bf16[4,256,512]{2,1,0:T(8,128)(2,1)}, f32[4,256,512]{2,1,0:T(8,128)}) custom-call(s32[1]{0:T(128)} %bitcast.2.me_ref, bf16[256,1024]{1,0:T(8,128)(2,1)} %get-tuple-element.477.x_ref.refs_1_, bf16[1024,4096]{1,0:T(8,128)(2,1)} %up_ref, bf16[1,4096]{1,0:T(2,128)(2,1)} %broadcast_in_dim.65.bias_ref), custom_call_target="tpu_custom_call" | custom-call | tf_op jit(solution)/shard_map/mlp_up/pallas_call | solution.py:523
  29.7 5.7 %piece_products.8 = (f32[512,512]{1,0:T(8,128)}, f32[512,512]{1,0:T(8,128)}, f32[512,512]{1,0:T(8,128)}, f32[512,512]{1,0:T(8,128)}) custom-call(bf16[4,256,512]{2,1,0:T(8,128)(2,1)} %get-tuple-element.518.refs_0_.refs_4_.refs_8_.refs_12_, f32[4,256,512]{2,1,0:T(8,128)} %copy-done.3, bf16[256,1024]{1,0:T(8,128)(2,1)} %bitcast.26, f32[256,1024]{1,0:T(8,128)} %copy-done.5, ...), custom_call_target="tpu_custom_call" | custom-call | tf_op jit(solution)/shard_map/piece_products/pallas_call | solution.py:79
  35.4 2.9 collective-permute-start.2
  39.8 15.9 %mlp_back.1 = (bf16[256,4096]{1,0:T(8,128)(2,1)}, f32[256,4096]{1,0:T(8,128)}, f32[1,4096]{1,0:T(1,128)}, f32[256,1024]{1,0:T(8,128)}, f32[256,1024]{1,0:T(8,128)}) custom-call(bf16[256,1024]{1,0:T(8,128)(2,1)} %bitcast.30, bf16[4096,1024]{1,0:T(8,128)(2,1)} %down_ref, bf16[1024,4096]{1,0:T(8,128)(2,1)} %up_ref, ...), custom_call_target="tpu_custom_call" | custom-call | tf_op jit(solution)/shard_map/mlp_back/pallas_call | solution.py:586
  55.7 5.7 %piece_products.9 = (f32[512,512]{1,0:T(8,128)}, f32[512,512]{1,0:T(8,128)}, f32[512,512]{1,0:T(8,128)}, f32[512,512]{1,0:T(8,128)}) custom-call(bf16[4,256,512]{2,1,0:T(8,128)(2,1)} %get-tuple-element.518.refs_0_.refs_4_.refs_8_.refs_12_, f32[4,256,512]{2,1,0:T(8,128)} %copy-done.3, bf16[256,1024]{1,0:T(8,128)(2,1)} %bitcast.31, f32[256,1024]{1,0:T(8,128)} %copy-done.5, ...), custom_call_target="tpu_custom_call" | custom-call | tf_op jit(solution)/shard_map/piece_products/pallas_call | solution.py:79
  64.4 3.3 reduce_round.13
  74.4 13.9 %attention_local.1 = (bf16[8,256,128]{2,1,0:T(8,128)(2,1)}, bf16[8,256,128]{2,1,0:T(8,128)(2,1)}, bf16[8,256,128]{2,1,0:T(8,128)(2,1)}, f32[8,256,128]{2,1,0:T(8...) custom-call(s32[2,3]{1,0:T(2,128)} %lengths_ref.4, ...), custom_call_target="tpu_custom_call" | custom-call | tf_op jit(solution)/shard_map/attention_local/pallas_call | solution.py:1065
  89.3 5.8 %piece_products.10 = (f32[768,512]{1,0:T(8,128)}, f32[768,512]{1,0:T(8,128)}, f32[512,512]{1,0:T(8,128)}, f32[512,512]{1,0:T(8,128)}) custom-call(bf16[2,256,512]{2,1,0:T(8,128)(2,1)} %get-tuple-element.791.refs_0_.refs_4_.refs_8_.refs_12_, f32[2,256,512]{2,1,0:T(8,128)} %copy-done.2, ...), custom_call_target="tpu_custom_call", output_to_operand_aliasing={{0}: (16, {}), {1}: (17, {})} | custom-call | tf_op jit(solution)/shard_map/piece_products/pallas_call | solution.py:79
  97.0 3.5 collective-permute-start.4
  101.9 3.2 reduce_round.14
  105.1 5.7 %piece_products.11 = (f32[768,512]{1,0:T(8,128)}, f32[768,512]{1,0:T(8,128)}, f32[512,512]{1,0:T(8,128)}, f32[512,512]{1,0:T(8,128)}) custom-call(bf16[2,256,512]{2,1,0:T(8,128)(2,1)} %get-tuple-element.791.refs_0_.refs_4_.refs_8_.refs_12_, f32[2,256,512]{2,1,0:T(8,128)} %copy-done.2, ...), custom_call_target="tpu_custom_call", output_to_operand_aliasing={{0}: (16, {}), {1}: (17, {})} | custom-call | tf_op jit(solution)/shard_map/piece_products/pallas_call | solution.py:79
  115.3 4.3 collective-permute-start.9
  121.8 8.9 %collective-permute-done.9.carry_ref = f32[2,8,72,128]{3,2,1,0:T(8,128)S(1)} collective-permute-done((f32[2,8,72,128]{3,2,1,0:T(8,128)}, f32[2,8,72,128]{3,2,1,0:T(8,128)S(1)}, u32[]{:S(2)}, u32[]{:S(2)}) %collective-permute-start.9) | collective-permute-done | bytes 589856 | tf_op jit(solution)/shard_map/ppermute | solution.py:41
  131.6 20.0 %attention_middle.1 = (bf16[256,1024]{1,0:T(8,128)(2,1)}, bf16[8,256,128]{2,1,0:T(8,128)(2,1)}, f32[8,256,128]{2,1,0:T(8,128)}, f32[8,256,128]{2,1,0:T(8,128)}, f32[2,8,72,128]{3,2,1,0:T(8,128)}) custom-call(s32[2,3]{1,0:T(2,128)} %lengths_ref.4, s32[2]{0:T(128)} %pad_add_fusion.first_ref, bf16[256,1024]{1,0:T(8,128)(2,1)} %bitcast.35, ...), custom_call_target="tpu_custom_call" | custom-call | tf_op jit(solution)/shard_map/attention_middle/pallas_call | solution.py:1093
  156.3 3.4 layer_output.1
  159.7 4.3 reduce_round.15
  163.9 3.1 collective-permute-start.17
  174.5 3.8 piece_products.12
  178.3 23.7 %collective-permute-done.13.carry_ref = f32[2,8,72,128]{3,2,1,0:T(8,128)} collective-permute-done((f32[2,8,72,128]{3,2,1,0:T(8,128)}, f32[2,8,72,128]{3,2,1,0:T(8,128)}, u32[]{:S(2)}, u32[]{:S(2)}) %collective-permute-start.13) | collective-permute-done | bytes 589856 | tf_op jit(solution)/shard_map/ppermute | solution.py:41
  202.0 9.6 %attention_last.1 = (bf16[256,3072]{1,0:T(8,128)(2,1)}, f32[256,3072]{1,0:T(8,128)}) custom-call(s32[2,3]{1,0:T(2,128)} %lengths_ref.4, s32[2]{0:T(128)} %pad_add_fusion.first_ref, bf16[8,256,128]{2,1,0:T(8,128)(2,1)} %get-tuple-element.669.gradq_ref, f32[8,256,128]{2,1,0:T(8,128)} %get-tuple-element.670.gradk_ref, ...), custom_call_target="tpu_custom_call" | custom-call | tf_op jit(solution)/shard_map/attention_last/pallas_call | solution.py:1116
  213.1 5.5 %reduce_round.16 = (f32[512,512]{1,0:T(8,128)}, f32[512,512]{1,0:T(8,128)}, f32[256,512]{1,0:T(8,128)}, f32[256,512]{1,0:T(8,128)}, f32[512,512]{1,0:T(8,128)}, /*index=5*/f32[512,512]{1,0:T(8,128)}, f32[512,512]{1,0:T(8,128)}) custom-call(s32[1]{0:T(128)} %bitcast.refs_0_, f32[768,512]{1,0:T(8,128)} %copy-done.8, ...), custom_call_target="tpu_custom_call" | custom-call | tf_op jit(solution)/shard_map/reduce_round/pallas_call | solution.py:79
  223.8 9.2 %norm_back.1 = (f32[256,1024]{1,0:T(8,128)}, f32[8,1024]{1,0:T(8,128)}, f32[1,3072]{1,0:T(1,128)}) custom-call(bf16[256,3072]{1,0:T(8,128)(2,1)} %get-tuple-element.793.qkv_ref.refs_2_.refs_6_, bf16[1024,3072]{1,0:T(8,128)(2,1)} %weight_ref.3, f32[256,1024]{1,0:T(8,128)} %get-tuple-element.702.mlp_ref, f32[256,1024]{1,0:T(8,128)} %get-tuple-element.703.unit_ref, ...), custom_call_target="tpu_custom_call" | custom-call | tf_op jit(solution)/shard_map/norm_back/pallas_call | solution.py:693
  237.2 3.8 piece_products.13
  247.8 5.4 %reduce_round.17 = (f32[384,512]{1,0:T(8,128)}, f32[384,512]{1,0:T(8,128)}, f32[128,512]{1,0:T(8,128)}, f32[128,512]{1,0:T(8,128)}, f32[512,512]{1,0:T(8,128)}, ...) custom-call(s32[1]{0:T(128)} %bitcast.refs_0_, f32[512,512]{1,0:T(8,128)} %collective-permute-done.20.refs_1_, ...), custom_call_target="tpu_custom_call" | custom-call | tf_op jit(solution)/shard_map/reduce_round/pallas_call | solution.py:79
  253.2 3.3 collective-permute-start.27
  258.2 3.7 piece_products.14
  263.4 5.1 %collective-permute-done.24 = f32[2,1536]{1,0:T(2,128)S(1)} collective-permute-done((f32[2,1536]{1,0:T(2,128)S(1)}, f32[2,1536]{1,0:T(2,128)S(1)}, u32[]{:S(2)}, u32[]{:S(2)}) %collective-permute-start.24) | collective-permute-done | bytes 12320 | tf_op jit(solution)/shard_map/ppermute | solution.py:48
  270.8 8.0 %collective-permute-done.27.refs_8_ = f32[512,512]{1,0:T(8,128)S(1)} collective-permute-done((f32[512,512]{1,0:T(8,128)}, f32[512,512]{1,0:T(8,128)S(1)}, u32[]{:S(2)}, u32[]{:S(2)}) %collective-permute-start.27) | collective-permute-done | bytes 1048608 | tf_op jit(solution)/shard_map/ppermute | solution.py:395
  279.8 6.2 %reduce_round.18 = (f32[384,512]{1,0:T(8,128)}, f32[384,512]{1,0:T(8,128)}, f32[128,512]{1,0:T(8,128)}, f32[128,512]{1,0:T(8,128)}, f32[512,512]{1,0:T(8,128)}, ...) custom-call(s32[1]{0:T(128)} %bitcast.refs_0_, f32[512,512]{1,0:T(8,128)} %copy-done.9, ...), custom_call_target="tpu_custom_call" | custom-call | tf_op jit(solution)/shard_map/reduce_round/pallas_call | solution.py:79
  286.0 2.9 collective-permute-start.32
  291.7 3.7 piece_products.15
  297.0 11.4 %collective-permute-done.29 = f32[1,1536]{1,0:T(1,128)S(1)} collective-permute-done((f32[1,1536]{1,0:T(1,128)S(1)}, f32[1,1536]{1,0:T(1,128)S(1)}, u32[]{:S(2)}, u32[]{:S(2)}) %collective-permute-start.29) | collective-permute-done | bytes 6176 | tf_op jit(solution)/shard_map/ppermute | solution.py:48
  311.8 5.5 %reduce_round.19 = (f32[128,512]{1,0:T(8,128)}, f32[128,512]{1,0:T(8,128)}, f32[128,512]{1,0:T(8,128)}, f32[128,512]{1,0:T(8,128)}, f32[256,512]{1,0:T(8,128)}, ...) custom-call(s32[1]{0:T(128)} %bitcast.refs_0_, f32[384,512]{1,0:T(8,128)} %copy-done.28, ...), custom_call_target="tpu_custom_call" | custom-call | tf_op jit(solution)/shard_map/reduce_round/pallas_call | solution.py:79
  317.3 3.5 collective-permute-start.37
  324.5 5.0 %collective-permute-start.34 = (f32[1,1536]{1,0:T(1,128)S(1)}, f32[1,1536]{1,0:T(1,128)S(1)}, u32[]{:S(2)}, u32[]{:S(2)}) collective-permute-start(f32[1,1536]{1,0:T(1,128)S(1)} %add.96), channel_id=1, source_target_pairs={{0,8},{24,16},{1,9},{25,17},{2,10},{26,18},{3,11},{27,19},{4,12},{... | collective-permute-start | bytes 18440 | tf_op jit(solution)/shard_map/ppermute | solution.py:110
  330.4 10.7 %collective-permute-done.34 = f32[1,1536]{1,0:T(1,128)S(1)} collective-permute-done((f32[1,1536]{1,0:T(1,128)S(1)}, f32[1,1536]{1,0:T(1,128)S(1)}, u32[]{:S(2)}, u32[]{:S(2)}) %collective-permute-start.34) | collective-permute-done | bytes 6176 | tf_op jit(solution)/shard_map/ppermute | solution.py:110
  344.6 5.1 %reduce_round.20 = (f32[128,512]{1,0:T(8,128)}, f32[128,512]{1,0:T(8,128)}, f32[128,512]{1,0:T(8,128)}, f32[128,512]{1,0:T(8,128)}, f32[256,512]{1,0:T(8,128)}, ...) custom-call(s32[1]{0:T(128)} %bitcast.refs_0_, f32[384,512]{1,0:T(8,128)} %copy-done.29, ...), custom_call_target="tpu_custom_call" | custom-call | tf_op jit(solution)/shard_map/reduce_round/pallas_call | solution.py:79
  359.0 12.4 %collective-permute-done.42.refs_6_ = f32[512,512]{1,0:T(8,128)S(1)} collective-permute-done((f32[512,512]{1,0:T(8,128)}, f32[512,512]{1,0:T(8,128)S(1)}, u32[]{:S(2)}, u32[]{:S(2)}) %collective-permute-start.42) | collective-permute-done | bytes 1048608 | tf_op jit(solution)/shard_map/ppermute | solution.py:395
  372.4 3.7 reduce_round.21
  384.9 4.1 collective-permute-done.44
  390.1 3.3 reduce_round.22
  393.4 3.5 collective-permute-start.49
  401.0 3.3 collective-permute-done.49.refs_2_
  408.1 3.9 collective-permute-start.51
  414.3 5.1 %collective-permute-done.51.refs_1_ = f32[256,512]{1,0:T(8,128)S(1)} collective-permute-done((f32[256,512]{1,0:T(8,128)}, f32[256,512]{1,0:T(8,128)S(1)}, u32[]{:S(2)}, u32[]{:S(2)}) %collective-permute-start.51) | collective-permute-done | bytes 524320 | tf_op jit(solution)/shard_map/ppermute | solution.py:395
  422.9 3.9 collective-permute-start.53
  430.8 3.3 collective-permute-done.53.refs_1_
  (275 shorter events, 133.0 us)
Async XLA Ops:
  35.4 26.6 %collective-permute-start.2 = (f32[512,512]{1,0:T(8,128)}, f32[512,512]{1,0:T(8,128)S(1)}, u32[]{:S(2)}, u32[]{:S(2)}) collective-permute-start(f32[512,512]{1,0:T(8,128)} %get-tuple-element.495), channel_id=1, source_target_pairs={{0,2},{1,3},{2,0},{3,1},{4,6},{5,7},{6,4},{7,5},{8,10},{9,11},{10,... | collective-permute-start | bytes 3145736 | tf_op jit(solution)/shard_map/ppermute | solution.py:48
  38.3 25.1 %collective-permute-start.3 = (f32[512,512]{1,0:T(8,128)}, f32[512,512]{1,0:T(8,128)S(1)}, u32[]{:S(2)}, u32[]{:S(2)}) collective-permute-start(f32[512,512]{1,0:T(8,128)} %get-tuple-element.496), channel_id=1, source_target_pairs={{0,4},{1,5},{2,6},{3,7},{4,0},{5,1},{6,2},{7,3},{8,12},{9,13},{10,... | collective-permute-start | bytes 3145736 | tf_op jit(solution)/shard_map/ppermute | solution.py:48
  67.7 20.6 %collective-permute-start.6 = (f32[256,4096]{1,0:T(8,128)}, f32[256,4096]{1,0:T(8,128)}, u32[]{:S(2)}, u32[]{:S(2)}) collective-permute-start(f32[256,4096]{1,0:T(8,128)} %get-tuple-element.551), channel_id=1, source_target_pairs={{0,1},{1,0},{2,3},{3,2},{4,5},{5,4},{6,7},{7,6},{8,9},{9,8},{10,11... | collective-permute-start | bytes 12582920 | tf_op jit(solution)/shard_map/ppermute | solution.py:48
  68.0 20.3 %collective-permute-start.5 = (f32[2,256,512]{2,1,0:T(8,128)}, f32[2,256,512]{2,1,0:T(8,128)S(1)}, u32[]{:S(2)}, u32[]{:S(2)}) collective-permute-start(f32[2,256,512]{2,1,0:T(8,128)} %get-tuple-element.549), channel_id=1, source_target_pairs={{0,1},{1,0},{2,3},{3,2},{4,5},{5,4},{6,7},{7,6},{8,9},{9,8},{10,11... | collective-permute-start | bytes 3145736 | tf_op jit(solution)/shard_map/ppermute | solution.py:48
  70.6 29.9 %collective-permute-start.7 = (f32[512,512]{1,0:T(8,128)}, f32[512,512]{1,0:T(8,128)S(1)}, u32[]{:S(2)}, u32[]{:S(2)}) collective-permute-start(f32[512,512]{1,0:T(8,128)} %get-tuple-element.522), channel_id=1, source_target_pairs={{0,2},{1,3},{2,0},{3,1},{4,6},{5,7},{6,4},{7,5},{8,10},{9,11},{10,... | collective-permute-start | bytes 3145736 | tf_op jit(solution)/shard_map/ppermute | solution.py:48
  71.3 29.3 %collective-permute-start.8 = (f32[512,512]{1,0:T(8,128)}, f32[512,512]{1,0:T(8,128)S(1)}, u32[]{:S(2)}, u32[]{:S(2)}) collective-permute-start(f32[512,512]{1,0:T(8,128)} %get-tuple-element.552), channel_id=1, source_target_pairs={{0,4},{1,5},{2,6},{3,7},{4,0},{5,1},{6,2},{7,3},{8,12},{9,13},{10,... | collective-permute-start | bytes 3145736 | tf_op jit(solution)/shard_map/ppermute | solution.py:48
  95.1 64.6 %collective-permute-start.11 = (f32[768,512]{1,0:T(8,128)}, f32[768,512]{1,0:T(8,128)}, u32[]{:S(2)}, u32[]{:S(2)}) collective-permute-start(f32[768,512]{1,0:T(8,128)} %get-tuple-element.574), channel_id=1, source_target_pairs={{0,2},{1,3},{2,0},{3,1},{4,6},{5,7},{6,4},{7,5},{8,10},{9,11},{10,... | collective-permute-start | bytes 4718600 | tf_op jit(solution)/shard_map/ppermute | solution.py:48
  96.5 63.1 %collective-permute-start.12 = (f32[768,512]{1,0:T(8,128)}, f32[768,512]{1,0:T(8,128)}, u32[]{:S(2)}, u32[]{:S(2)}) collective-permute-start(f32[768,512]{1,0:T(8,128)} %get-tuple-element.637), channel_id=1, source_target_pairs={{0,4},{1,5},{2,6},{3,7},{4,0},{5,1},{6,2},{7,3},{8,12},{9,13},{10,... | collective-permute-start | bytes 4718600 | tf_op jit(solution)/shard_map/ppermute | solution.py:48
  97.0 15.4 %collective-permute-start.4 = (f32[2,8,72,128]{3,2,1,0:T(8,128)}, f32[2,8,72,128]{3,2,1,0:T(8,128)S(1)}, u32[]{:S(2)}, u32[]{:S(2)}) collective-permute-start(f32[2,8,72,128]{3,2,1,0:T(8,128)} %get-tuple-element.603.own_ref), channel_id=1, source_target_pairs={{0,8},{8,16},{16,24},{1,9},{9,17},{17,25},{2,10},{10,18},{18,26},{... | collective-permute-start | bytes 1769480 | tf_op jit(solution)/shard_map/ppermute | solution.py:41
  115.3 15.4 %collective-permute-start.9 = (f32[2,8,72,128]{3,2,1,0:T(8,128)}, f32[2,8,72,128]{3,2,1,0:T(8,128)S(1)}, u32[]{:S(2)}, u32[]{:S(2)}) collective-permute-start(f32[2,8,72,128]{3,2,1,0:T(8,128)} %pass_carry.2), channel_id=1, source_target_pairs={{0,8},{8,16},{16,24},{1,9},{9,17},{17,25},{2,10},{10,18},{18,26},{... | collective-permute-start | bytes 1769480 | tf_op jit(solution)/shard_map/ppermute | solution.py:41
  119.6 92.0 %collective-permute-start.15 = (f32[768,512]{1,0:T(8,128)}, f32[768,512]{1,0:T(8,128)S(1)}, u32[]{:S(2)}, u32[]{:S(2)}) collective-permute-start(f32[768,512]{1,0:T(8,128)} %get-tuple-element.600), channel_id=1, source_target_pairs={{0,2},{1,3},{2,0},{3,1},{4,6},{5,7},{6,4},{7,5},{8,10},{9,11},{10,... | collective-permute-start | bytes 4718600 | tf_op jit(solution)/shard_map/ppermute | solution.py:48
  120.3 91.3 %collective-permute-start.16 = (f32[768,512]{1,0:T(8,128)}, f32[768,512]{1,0:T(8,128)}, u32[]{:S(2)}, u32[]{:S(2)}) collective-permute-start(f32[768,512]{1,0:T(8,128)} %get-tuple-element.683), channel_id=1, source_target_pairs={{0,4},{1,5},{2,6},{3,7},{4,0},{5,1},{6,2},{7,3},{8,12},{9,13},{10,... | collective-permute-start | bytes 4718600 | tf_op jit(solution)/shard_map/ppermute | solution.py:48
  151.5 16.7 %collective-permute-start.10 = (f32[2,8,72,128]{3,2,1,0:T(8,128)}, f32[2,8,72,128]{3,2,1,0:T(8,128)}, u32[]{:S(2)}, u32[]{:S(2)}) collective-permute-start(f32[2,8,72,128]{3,2,1,0:T(8,128)} %get-tuple-element.652.own_ref), channel_id=1, source_target_pairs={{8,0},{16,8},{24,16},{9,1},{17,9},{25,17},{10,2},{18,10},{26,18},{... | collective-permute-start | bytes 1769480 | tf_op jit(solution)/shard_map/ppermute | solution.py:41
  163.9 47.7 %collective-permute-start.17 = (f32[512,512]{1,0:T(8,128)}, f32[512,512]{1,0:T(8,128)S(1)}, u32[]{:S(2)}, u32[]{:S(2)}) collective-permute-start(f32[512,512]{1,0:T(8,128)} %get-tuple-element.689), channel_id=1, source_target_pairs={{0,8},{8,0},{16,24},{24,16},{1,9},{9,1},{17,25},{25,17},{2,10},{10... | collective-permute-start | bytes 3145736 | tf_op jit(solution)/shard_map/ppermute | solution.py:395
  170.2 31.8 %collective-permute-start.13 = (f32[2,8,72,128]{3,2,1,0:T(8,128)}, f32[2,8,72,128]{3,2,1,0:T(8,128)}, u32[]{:S(2)}, u32[]{:S(2)}) collective-permute-start(f32[2,8,72,128]{3,2,1,0:T(8,128)} %pass_carry.3), channel_id=1, source_target_pairs={{8,0},{16,8},{24,16},{9,1},{17,9},{25,17},{10,2},{18,10},{26,18},{... | collective-permute-start | bytes 1769480 | tf_op jit(solution)/shard_map/ppermute | solution.py:41
  218.6 16.9 %collective-permute-start.18 = (f32[256,3072]{1,0:T(8,128)}, f32[256,3072]{1,0:T(8,128)S(1)}, u32[]{:S(2)}, u32[]{:S(2)}) collective-permute-start(f32[256,3072]{1,0:T(8,128)} %get-tuple-element.713), channel_id=1, source_target_pairs={{0,1},{1,0},{2,3},{3,2},{4,5},{5,4},{6,7},{7,6},{8,9},{9,8},{10,11... | collective-permute-start | bytes 9437192 | tf_op jit(solution)/shard_map/ppermute | solution.py:48
  219.9 26.3 %collective-permute-start.20 = (f32[512,512]{1,0:T(8,128)}, f32[512,512]{1,0:T(8,128)}, u32[]{:S(2)}, u32[]{:S(2)}) collective-permute-start(f32[512,512]{1,0:T(8,128)} %get-tuple-element.666), channel_id=1, source_target_pairs={{0,2},{1,3},{2,0},{3,1},{4,6},{5,7},{6,4},{7,5},{8,10},{9,11},{10,... | collective-permute-start | bytes 3145736 | tf_op jit(solution)/shard_map/ppermute | solution.py:48
  220.6 27.2 %collective-permute-start.21 = (f32[512,512]{1,0:T(8,128)}, f32[512,512]{1,0:T(8,128)}, u32[]{:S(2)}, u32[]{:S(2)}) collective-permute-start(f32[512,512]{1,0:T(8,128)} %get-tuple-element.729), channel_id=1, source_target_pairs={{0,4},{1,5},{2,6},{3,7},{4,0},{5,1},{6,2},{7,3},{8,12},{9,13},{10,... | collective-permute-start | bytes 3145736 | tf_op jit(solution)/shard_map/ppermute | solution.py:48
  222.1 25.7 %collective-permute-start.22 = (f32[512,512]{1,0:T(8,128)}, f32[512,512]{1,0:T(8,128)}, u32[]{:S(2)}, u32[]{:S(2)}) collective-permute-start(f32[512,512]{1,0:T(8,128)} %get-tuple-element.735), channel_id=1, source_target_pairs={{0,8},{8,0},{16,24},{24,16},{1,9},{9,1},{17,25},{25,17},{2,10},{10... | collective-permute-start | bytes 3145736 | tf_op jit(solution)/shard_map/ppermute | solution.py:395
  222.1 25.7 %collective-permute-start.23 = (f32[512,512]{1,0:T(8,128)}, f32[512,512]{1,0:T(8,128)}, u32[]{:S(2)}, u32[]{:S(2)}) collective-permute-start(f32[512,512]{1,0:T(8,128)} %get-tuple-element.746.refs_9_), channel_id=1, source_target_pairs={{8,16},{16,8},{9,17},{17,9},{10,18},{18,10},{11,19},{19,11},{12,20... | collective-permute-start | bytes 3145736 | tf_op jit(solution)/shard_map/ppermute | solution.py:398
  242.2 26.2 %collective-permute-start.25 = (f32[512,512]{1,0:T(8,128)}, f32[512,512]{1,0:T(8,128)S(1)}, u32[]{:S(2)}, u32[]{:S(2)}) collective-permute-start(f32[512,512]{1,0:T(8,128)} %get-tuple-element.725), channel_id=1, source_target_pairs={{0,2},{1,3},{2,0},{3,1},{4,6},{5,7},{6,4},{7,5},{8,10},{9,11},{10,... | collective-permute-start | bytes 3145736 | tf_op jit(solution)/shard_map/ppermute | solution.py:48
  246.3 24.5 %collective-permute-start.26 = (f32[512,512]{1,0:T(8,128)}, f32[512,512]{1,0:T(8,128)S(1)}, u32[]{:S(2)}, u32[]{:S(2)}) collective-permute-start(f32[512,512]{1,0:T(8,128)} %get-tuple-element.764), channel_id=1, source_target_pairs={{0,4},{1,5},{2,6},{3,7},{4,0},{5,1},{6,2},{7,3},{8,12},{9,13},{10,... | collective-permute-start | bytes 3145736 | tf_op jit(solution)/shard_map/ppermute | solution.py:48
  253.2 25.5 %collective-permute-start.27 = (f32[512,512]{1,0:T(8,128)}, f32[512,512]{1,0:T(8,128)S(1)}, u32[]{:S(2)}, u32[]{:S(2)}) collective-permute-start(f32[512,512]{1,0:T(8,128)} %get-tuple-element.770), channel_id=1, source_target_pairs={{0,8},{8,0},{16,24},{24,16},{1,9},{9,1},{17,25},{25,17},{2,10},{10... | collective-permute-start | bytes 3145736 | tf_op jit(solution)/shard_map/ppermute | solution.py:395
  256.5 22.2 %collective-permute-start.28 = (f32[512,512]{1,0:T(8,128)}, f32[512,512]{1,0:T(8,128)}, u32[]{:S(2)}, u32[]{:S(2)}) collective-permute-start(f32[512,512]{1,0:T(8,128)} %get-tuple-element.782.refs_9_), channel_id=1, source_target_pairs={{8,16},{16,8},{9,17},{17,9},{10,18},{18,10},{11,19},{19,11},{12,20... | collective-permute-start | bytes 3145736 | tf_op jit(solution)/shard_map/ppermute | solution.py:398
  261.9 6.5 %collective-permute-start.24 = (f32[2,1536]{1,0:T(2,128)S(1)}, f32[2,1536]{1,0:T(2,128)S(1)}, u32[]{:S(2)}, u32[]{:S(2)}) collective-permute-start(f32[2,1536]{1,0:T(2,128)S(1)} %get-tuple-element.761), channel_id=1, source_target_pairs={{0,2},{1,3},{2,0},{3,1},{4,6},{5,7},{6,4},{7,5},{8,10},{9,11},{10,... | collective-permute-start | bytes 36872 | tf_op jit(solution)/shard_map/ppermute | solution.py:48
  286.0 24.4 %collective-permute-start.32 = (f32[512,512]{1,0:T(8,128)}, f32[512,512]{1,0:T(8,128)S(1)}, u32[]{:S(2)}, u32[]{:S(2)}) collective-permute-start(f32[512,512]{1,0:T(8,128)} %get-tuple-element.807), channel_id=1, source_target_pairs={{0,8},{8,0},{16,24},{24,16},{1,9},{9,1},{17,25},{25,17},{2,10},{10... | collective-permute-start | bytes 3145736 | tf_op jit(solution)/shard_map/ppermute | solution.py:395
  289.0 21.5 %collective-permute-start.33 = (f32[512,512]{1,0:T(8,128)}, f32[512,512]{1,0:T(8,128)S(1)}, u32[]{:S(2)}, u32[]{:S(2)}) collective-permute-start(f32[512,512]{1,0:T(8,128)} %get-tuple-element.819.refs_9_), channel_id=1, source_target_pairs={{8,16},{16,8},{9,17},{17,9},{10,18},{18,10},{11,19},{19,11},{12,20... | collective-permute-start | bytes 3145736 | tf_op jit(solution)/shard_map/ppermute | solution.py:398
  289.7 18.7 %collective-permute-start.30 = (f32[384,512]{1,0:T(8,128)}, f32[384,512]{1,0:T(8,128)S(1)}, u32[]{:S(2)}, u32[]{:S(2)}) collective-permute-start(f32[384,512]{1,0:T(8,128)} %get-tuple-element.760), channel_id=1, source_target_pairs={{0,2},{1,3},{2,0},{3,1},{4,6},{5,7},{6,4},{7,5},{8,10},{9,11},{10,... | collective-permute-start | bytes 2359304 | tf_op jit(solution)/shard_map/ppermute | solution.py:48
  291.2 17.2 %collective-permute-start.31 = (f32[384,512]{1,0:T(8,128)}, f32[384,512]{1,0:T(8,128)}, u32[]{:S(2)}, u32[]{:S(2)}) collective-permute-start(f32[384,512]{1,0:T(8,128)} %get-tuple-element.801), channel_id=1, source_target_pairs={{0,4},{1,5},{2,6},{3,7},{4,0},{5,1},{6,2},{7,3},{8,12},{9,13},{10,... | collective-permute-start | bytes 2359304 | tf_op jit(solution)/shard_map/ppermute | solution.py:48
  295.4 13.0 %collective-permute-start.29 = (f32[1,1536]{1,0:T(1,128)S(1)}, f32[1,1536]{1,0:T(1,128)S(1)}, u32[]{:S(2)}, u32[]{:S(2)}) collective-permute-start(f32[1,1536]{1,0:T(1,128)S(1)} %get-tuple-element.798), channel_id=1, source_target_pairs={{0,4},{1,5},{2,6},{3,7},{4,0},{5,1},{6,2},{7,3},{8,12},{9,13},{10,... | collective-permute-start | bytes 18440 | tf_op jit(solution)/shard_map/ppermute | solution.py:48
  317.3 25.7 %collective-permute-start.37 = (f32[512,512]{1,0:T(8,128)}, f32[512,512]{1,0:T(8,128)S(1)}, u32[]{:S(2)}, u32[]{:S(2)}) collective-permute-start(f32[512,512]{1,0:T(8,128)} %get-tuple-element.832), channel_id=1, source_target_pairs={{0,8},{8,0},{16,24},{24,16},{1,9},{9,1},{17,25},{25,17},{2,10},{10... | collective-permute-start | bytes 3145736 | tf_op jit(solution)/shard_map/ppermute | solution.py:395
  320.9 22.2 %collective-permute-start.38 = (f32[512,512]{1,0:T(8,128)}, f32[512,512]{1,0:T(8,128)S(1)}, u32[]{:S(2)}, u32[]{:S(2)}) collective-permute-start(f32[512,512]{1,0:T(8,128)} %get-tuple-element.844.refs_9_), channel_id=1, source_target_pairs={{8,16},{16,8},{9,17},{17,9},{10,18},{18,10},{11,19},{19,11},{12,20... | collective-permute-start | bytes 3145736 | tf_op jit(solution)/shard_map/ppermute | solution.py:398
  321.6 20.8 %collective-permute-start.35 = (f32[384,512]{1,0:T(8,128)}, f32[384,512]{1,0:T(8,128)S(1)}, u32[]{:S(2)}, u32[]{:S(2)}) collective-permute-start(f32[384,512]{1,0:T(8,128)} %get-tuple-element.797), channel_id=1, source_target_pairs={{0,2},{1,3},{2,0},{3,1},{4,6},{5,7},{6,4},{7,5},{8,10},{9,11},{10,... | collective-permute-start | bytes 2359304 | tf_op jit(solution)/shard_map/ppermute | solution.py:48
  323.0 20.0 %collective-permute-start.36 = (f32[384,512]{1,0:T(8,128)}, f32[384,512]{1,0:T(8,128)S(1)}, u32[]{:S(2)}, u32[]{:S(2)}) collective-permute-start(f32[384,512]{1,0:T(8,128)} %get-tuple-element.826), channel_id=1, source_target_pairs={{0,4},{1,5},{2,6},{3,7},{4,0},{5,1},{6,2},{7,3},{8,12},{9,13},{10,... | collective-permute-start | bytes 2359304 | tf_op jit(solution)/shard_map/ppermute | solution.py:48
  324.5 16.6 %collective-permute-start.34 = (f32[1,1536]{1,0:T(1,128)S(1)}, f32[1,1536]{1,0:T(1,128)S(1)}, u32[]{:S(2)}, u32[]{:S(2)}) collective-permute-start(f32[1,1536]{1,0:T(1,128)S(1)} %add.96), channel_id=1, source_target_pairs={{0,8},{24,16},{1,9},{25,17},{2,10},{26,18},{3,11},{27,19},{4,12},{... | collective-permute-start | bytes 18440 | tf_op jit(solution)/shard_map/ppermute | solution.py:110
  341.1 16.3 %collective-permute-start.40 = (f32[128,512]{1,0:T(8,128)}, f32[128,512]{1,0:T(8,128)}, u32[]{:S(2)}, u32[]{:S(2)}) collective-permute-start(f32[128,512]{1,0:T(8,128)} %get-tuple-element.822), channel_id=1, source_target_pairs={{0,2},{1,3},{2,0},{3,1},{4,6},{5,7},{6,4},{7,5},{8,10},{9,11},{10,... | collective-permute-start | bytes 786440 | tf_op jit(solution)/shard_map/ppermute | solution.py:48
  342.4 16.6 %collective-permute-start.41 = (f32[128,512]{1,0:T(8,128)}, f32[128,512]{1,0:T(8,128)}, u32[]{:S(2)}, u32[]{:S(2)}) collective-permute-start(f32[128,512]{1,0:T(8,128)} %get-tuple-element.851), channel_id=1, source_target_pairs={{0,4},{1,5},{2,6},{3,7},{4,0},{5,1},{6,2},{7,3},{8,12},{9,13},{10,... | collective-permute-start | bytes 786440 | tf_op jit(solution)/shard_map/ppermute | solution.py:48
  349.6 21.8 %collective-permute-start.42 = (f32[512,512]{1,0:T(8,128)}, f32[512,512]{1,0:T(8,128)S(1)}, u32[]{:S(2)}, u32[]{:S(2)}) collective-permute-start(f32[512,512]{1,0:T(8,128)} %get-tuple-element.855), channel_id=1, source_target_pairs={{0,8},{8,0},{16,24},{24,16},{1,9},{9,1},{17,25},{25,17},{2,10},{10... | collective-permute-start | bytes 3145736 | tf_op jit(solution)/shard_map/ppermute | solution.py:395
  356.6 32.4 %collective-permute-start.45 = (f32[128,512]{1,0:T(8,128)S(1)}, f32[128,512]{1,0:T(8,128)S(1)}, u32[]{:S(2)}, u32[]{:S(2)}) collective-permute-start(f32[128,512]{1,0:T(8,128)S(1)} %copy-done.54), channel_id=1, source_target_pairs={{0,2},{1,3},{2,0},{3,1},{4,6},{5,7},{6,4},{7,5},{8,10},{9,11},{10,... | collective-permute-start | bytes 786440 | tf_op jit(solution)/shard_map/ppermute | solution.py:48
  357.4 31.5 %collective-permute-start.46 = (f32[128,512]{1,0:T(8,128)S(1)}, f32[128,512]{1,0:T(8,128)S(1)}, u32[]{:S(2)}, u32[]{:S(2)}) collective-permute-start(f32[128,512]{1,0:T(8,128)S(1)} %copy-done.53), channel_id=1, source_target_pairs={{0,4},{1,5},{2,6},{3,7},{4,0},{5,1},{6,2},{7,3},{8,12},{9,13},{10,... | collective-permute-start | bytes 786440 | tf_op jit(solution)/shard_map/ppermute | solution.py:48
  379.5 9.5 %collective-permute-start.47 = (f32[256,512]{1,0:T(8,128)}, f32[256,512]{1,0:T(8,128)S(1)}, u32[]{:S(2)}, u32[]{:S(2)}) collective-permute-start(f32[256,512]{1,0:T(8,128)} %get-tuple-element.875), channel_id=1, source_target_pairs={{0,8},{8,0},{16,24},{24,16},{1,9},{9,1},{17,25},{25,17},{2,10},{10... | collective-permute-start | bytes 1572872 | tf_op jit(solution)/shard_map/ppermute | solution.py:395
  381.2 7.8 %collective-permute-start.48 = (f32[256,512]{1,0:T(8,128)}, f32[256,512]{1,0:T(8,128)S(1)}, u32[]{:S(2)}, u32[]{:S(2)}) collective-permute-start(f32[256,512]{1,0:T(8,128)} %get-tuple-element.885.refs_7_), channel_id=1, source_target_pairs={{8,16},{16,8},{9,17},{17,9},{10,18},{18,10},{11,19},{19,11},{12,20... | collective-permute-start | bytes 1572872 | tf_op jit(solution)/shard_map/ppermute | solution.py:398
  381.9 7.0 %collective-permute-start.44 = (f32[1,1536]{1,0:T(1,128)S(1)}, f32[1,1536]{1,0:T(1,128)S(1)}, u32[]{:S(2)}, u32[]{:S(2)}) collective-permute-start(f32[1,1536]{1,0:T(1,128)S(1)} %add.98), channel_id=1, source_target_pairs={{8,0},{16,24},{9,1},{17,25},{10,2},{18,26},{11,3},{19,27},{12,4},{... | collective-permute-start | bytes 18440 | tf_op jit(solution)/shard_map/ppermute | solution.py:110
  393.4 10.9 %collective-permute-start.49 = (f32[256,512]{1,0:T(8,128)}, f32[256,512]{1,0:T(8,128)S(1)}, u32[]{:S(2)}, u32[]{:S(2)}) collective-permute-start(f32[256,512]{1,0:T(8,128)} %get-tuple-element.889), channel_id=1, source_target_pairs={{0,8},{8,0},{16,24},{24,16},{1,9},{9,1},{17,25},{25,17},{2,10},{10... | collective-permute-start | bytes 1572872 | tf_op jit(solution)/shard_map/ppermute | solution.py:395
  396.9 7.4 %collective-permute-start.50 = (f32[256,512]{1,0:T(8,128)}, f32[256,512]{1,0:T(8,128)S(1)}, u32[]{:S(2)}, u32[]{:S(2)}) collective-permute-start(f32[256,512]{1,0:T(8,128)} %get-tuple-element.895.refs_3_), channel_id=1, source_target_pairs={{8,16},{16,8},{9,17},{17,9},{10,18},{18,10},{11,19},{19,11},{12,20... | collective-permute-start | bytes 1572872 | tf_op jit(solution)/shard_map/ppermute | solution.py:398
  408.1 11.3 %collective-permute-start.51 = (f32[256,512]{1,0:T(8,128)}, f32[256,512]{1,0:T(8,128)S(1)}, u32[]{:S(2)}, u32[]{:S(2)}) collective-permute-start(f32[256,512]{1,0:T(8,128)} %get-tuple-element.899), channel_id=1, source_target_pairs={{0,8},{8,0},{16,24},{24,16},{1,9},{9,1},{17,25},{25,17},{2,10},{10... | collective-permute-start | bytes 1572872 | tf_op jit(solution)/shard_map/ppermute | solution.py:395
  412.0 7.4 %collective-permute-start.52 = (f32[256,512]{1,0:T(8,128)}, f32[256,512]{1,0:T(8,128)S(1)}, u32[]{:S(2)}, u32[]{:S(2)}) collective-permute-start(f32[256,512]{1,0:T(8,128)} %get-tuple-element.904.refs_2_), channel_id=1, source_target_pairs={{8,16},{16,8},{9,17},{17,9},{10,18},{18,10},{11,19},{19,11},{12,20... | collective-permute-start | bytes 1572872 | tf_op jit(solution)/shard_map/ppermute | solution.py:398
  422.9 11.2 %collective-permute-start.53 = (f32[256,512]{1,0:T(8,128)}, f32[256,512]{1,0:T(8,128)S(1)}, u32[]{:S(2)}, u32[]{:S(2)}) collective-permute-start(f32[256,512]{1,0:T(8,128)} %get-tuple-element.908), channel_id=1, source_target_pairs={{0,8},{8,0},{16,24},{24,16},{1,9},{9,1},{17,25},{25,17},{2,10},{10... | collective-permute-start | bytes 1572872 | tf_op jit(solution)/shard_map/ppermute | solution.py:395
  (62 other events, 378.2 us)

commit v3 on v2

--- a/solution.py
+++ b/solution.py
@@ -20,6 +20,15 @@
 
 EPSILON = 1e-05
 ROTARY_BASE = 10000.0
+
+UP_AT = 3 * D
+LN1_GAIN, LN1_BIAS, LN2_GAIN, LN2_BIAS, DENSE, DOWN = range((UP_AT + FF) // D, (UP_AT + FF) // D + 6)
+
+def lasting(microseconds):
+    return pl.CostEstimate(
+        flops=int(microseconds * 1.15e9), transcendentals=0, bytes_accessed=0
+    )
+
 
 ROWS_COLS = ((1,), (0,))
 ROWS_ROWS = ((1,), (1,))
@@ -172,15 +181,22 @@
 class Singly:
     def __init__(self, line, bits):
         self.line, self.bits = line, bits
-        self.pieces = []
-
-    def prepare(self, pairs):
-        for piece in (one for pair in pairs for one in pair):
-            left, left_in, block, right, right_in, column = piece
-            columns = slice(column * COLUMNS, (column + 1) * COLUMNS)
+        self.pieces, self.outputs = [], {}
+
+    def prepare(self, target, pieces):
+        _, _, at, size = target
+        for left, left_in, block, right, right_in, (row, column) in pieces:
+            wide = COLUMNS // Rounds.PARTS
+            across = size[1] // wide
+            starts = [((at[1] + i) * across + column) * wide for i in range(Rounds.PARTS)]
+            right, right_in = (
+                jnp.concatenate([value[:, k : k + wide] for k in starts], axis=1)
+                for value in (right, right_in)
+            )
             left = jnp.concatenate([left[block], rounded(left_in[block])], axis=0)
-            right = jnp.concatenate([right[:, columns], rounded(right_in[:, columns])], axis=0)
-            self.pieces.append(Reduction(self.line, left, right, self.bits))
+            right = jnp.concatenate([right, rounded(right_in)], axis=0)
+            done = Reduction(self.line, left, right, self.bits)
+            self.pieces.append((target, row, starts, wide, done))
 
     def step(self):
         pass
@@ -189,7 +205,16 @@
         return True
 
     def results(self):
-        return [one.finish() for one in self.pieces]
+        for (name, shape, at, size), row, starts, wide, piece in self.pieces:
+            whole = self.outputs.get(name, jnp.zeros(shape, WIDE))
+            total = piece.finish()
+            top = at[0] * size[0] + row * total.shape[0]
+            for i, k in enumerate(starts):
+                whole = lax.dynamic_update_slice(
+                    whole, total[:, i * wide : (i + 1) * wide], (top, k)
+                )
+            self.outputs[name] = whole
+        return self.outputs
 
 
 def rounded(arrived):
@@ -214,7 +239,7 @@
             hold[out, :] = product(2 if i else 1, 3)
 
 
-def round_kernel(counts, *refs):
+def round_kernel(counts, places, skip, *refs):
     first, second, inward, middle, outward = counts
     refs = list(refs)
     edge = refs.pop(0)[0] != 0
@@ -229,6 +254,7 @@
     (from_end,) = take(inward or outward, 1)
     inner, from_middle = take(middle, 2)
     (whole,) = take(outward, 1)
+    take(True, skip)
     to_x, to_y, keep_a, keep_b = take(first, 4)
     (new_sums,) = take(second, 1)
     (to_end,) = take(second or middle, 1)
@@ -262,8 +288,11 @@
                 to_end[out, :] = jnp.where(edge, ends, inners)
     if inward:
         new_inner[...] = sums[...] + from_end[: 2 * inward * BLOCK, :]
-    if outward:
-        final[...] = jnp.where(edge, from_end[: 2 * outward * BLOCK, :], whole[...])
+    for k, (row, column) in enumerate(places):
+        rows = pl.ds(k * BLOCK, BLOCK)
+        wide = whole.shape[1]
+        total = jnp.where(edge, from_end[rows, :], whole[rows, :])
+        final[row * BLOCK : (row + 1) * BLOCK, column * wide : (column + 1) * wide] = total
 
 
 class Rounds:
@@ -273,7 +302,8 @@
         self.line, self.edge, self.counts = line, edge, counts
         self.made = self.at = 0
         self.buffers, self.moving, self.hold, self.kept = {}, {}, {}, {}
-        self.sums, self.inner, self.whole, self.finals = {}, {}, {}, []
+        self.sums, self.inner, self.whole, self.targets = {}, {}, {}, []
+        self.outputs = {}
         self.end = self.middle = None
         self.wide = COLUMNS // self.PARTS
 
@@ -283,14 +313,15 @@
     def rows_spec(self, rows, at=0):
         return pl.BlockSpec((rows, self.wide), lambda i: (at, i))
 
-    def prepare(self, pairs):
+    def prepare(self, target, pieces):
         r = self.made
         self.made += 1
-        count = len(pairs)
+        self.targets.append((target, [piece[5] for piece in pieces]))
+        count = len(pieces) // 2
+        name, shape, at, size = target
+        across = size[1] // self.wide
         args, specs = [], []
-        for left, left_in, block, right, right_in, column in (
-            one for pair in pairs for one in pair
-        ):
+        for left, left_in, block, right, right_in, (_, column) in pieces:
             for value in (left, left_in):
                 args.append(value)
                 specs.append(
@@ -301,16 +332,11 @@
                 specs.append(
                     pl.BlockSpec(
                         (value.shape[0], self.wide),
-                        lambda i, c=column: (0, c * self.PARTS + i),
+                        lambda i, c=column: (0, (at[1] + i) * across + c),
                     )
                 )
         rows = 2 * count * BLOCK
-        total = rows + self.count(r - 2) * BLOCK
-        aliases = {}
-        if r in self.buffers:
-            aliases = {len(args) + i: i for i in range(2)}
-            args += list(self.buffers.pop(r))
-            specs += [pl.BlockSpec(memory_space=pl.ANY)] * 2
+        total = rows + self.count(r - 1) * BLOCK
         call = pl.pallas_call(
             partial(product_kernel, count),
             grid=(self.PARTS,),
@@ -318,18 +344,22 @@
             out_specs=[self.rows_spec(rows)] * 4,
             out_shape=[jax.ShapeDtypeStruct((total, COLUMNS), WIDE)] * 2
             + [jax.ShapeDtypeStruct((rows, COLUMNS), WIDE)] * 2,
-            input_output_aliases=aliases,
-            name="piece_products",
+            cost_estimate=lasting(5.0),
+        name="piece_products",
         )
         to_x, to_y, hold_a, hold_b = self.line.step(call, *args)
         self.hold[r] = (hold_a, hold_b)
-        self.moving[r] = (swap(to_x, 1), swap(to_y, 2))
+        if r:
+            self.buffers[r] = (to_x, to_y)
+        else:
+            self.moving[r] = (swap(to_x, 1), swap(to_y, 2))
 
     def step(self):
         r = self.at
         self.at += 1
-        counts = [self.count(r - back) for back in (0, 2, 3, 4, 5)]
+        counts = [self.count(r - back) for back in (0, 1, 2, 3, 4)]
         first, second, inward, middle, outward = counts
+        aliases = {}
         args, specs = [self.edge], [pl.BlockSpec(memory_space=pltpu.SMEM)]
 
         def add(value):
@@ -343,24 +373,28 @@
             for value in self.hold.pop(r):
                 add(value)
         if second:
-            for value in self.kept.pop(r - 2):
+            for value in self.kept.pop(r - 1):
                 add(value)
         if inward:
-            add(self.sums.pop(r - 3))
+            add(self.sums.pop(r - 2))
         if inward or outward:
             add(self.end)
         if middle:
-            add(self.inner.pop(r - 4))
+            add(self.inner.pop(r - 3))
             add(self.middle)
         if outward:
-            add(self.whole.pop(r - 5))
+            add(self.whole.pop(r - 4))
         outs, out_specs = [], []
 
         def out(rows, at=0, of=None):
             outs.append(jax.ShapeDtypeStruct((of or rows, COLUMNS), WIDE))
             out_specs.append(self.rows_spec(rows, at))
 
-        ahead = self.count(r + 2)
+        ahead = self.count(r + 1)
+        if ahead:
+            aliases = {len(args): 0, len(args) + 1: 1}
+            args += list(self.buffers.pop(r + 1))
+            specs += [pl.BlockSpec(memory_space=pl.ANY)] * 2
         if first:
             for _ in range(2):
                 out(first * BLOCK, 2 * ahead // first, (2 * ahead + first) * BLOCK)
@@ -370,46 +404,49 @@
             out(2 * second * BLOCK)
         if second or middle:
             out(2 * max(second, middle) * BLOCK)
-        for count in (inward, middle, outward):
+        for count in (inward, middle):
             if count:
                 out(2 * count * BLOCK)
+        places = ()
+        if outward:
+            (name, shape, at, size), places = self.targets[r - 4]
+            if name in self.outputs:
+                aliases[len(args)] = len(outs)
+                args.append(self.outputs[name])
+                specs.append(pl.BlockSpec(memory_space=pl.ANY))
+            outs.append(jax.ShapeDtypeStruct(shape, WIDE))
+            out_specs.append(pl.BlockSpec(size, lambda i: (at[0], at[1] + i)))
         call = pl.pallas_call(
-            partial(round_kernel, counts),
+            partial(round_kernel, counts, places, len(aliases)),
             grid=(self.PARTS,),
             in_specs=specs,
             out_specs=out_specs,
             out_shape=outs,
+            input_output_aliases=aliases,
+            cost_estimate=lasting(5.0),
             name="reduce_round",
         )
         got = list(self.line.step(call, *args))
         if first:
-            to = (got.pop(0), got.pop(0))
-            if ahead:
-                self.buffers[r + 2] = to
-            else:
-                self.moving[r + 2] = (swap(to[0], 1), swap(to[1], 2))
+            self.moving[r + 1] = (swap(got.pop(0), 1), swap(got.pop(0), 2))
             self.kept[r] = (got.pop(0), got.pop(0))
         if second:
-            self.sums[r - 2] = got.pop(0)
+            self.sums[r - 1] = got.pop(0)
         if second or middle:
             self.end = lax.ppermute(got.pop(0), "seq", [(0, 1), (1, 0), (2, 3), (3, 2)])
         if inward:
-            self.inner[r - 3] = got.pop(0)
-            self.middle = lax.ppermute(self.inner[r - 3], "seq", [(1, 2), (2, 1)])
+            self.inner[r - 2] = got.pop(0)
+            self.middle = lax.ppermute(self.inner[r - 2], "seq", [(1, 2), (2, 1)])
         if middle:
-            self.whole[r - 4] = got.pop(0)
+            self.whole[r - 3] = got.pop(0)
         if outward:
-            self.finals.append(got.pop(0))
+            self.outputs[name] = got.pop(0)
 
     def finished(self):
-        return len(self.finals) == len(self.counts)
+        return self.at == len(self.counts) + 4
 
     def results(self):
-        return [
-            final[k * BLOCK : (k + 1) * BLOCK]
-            for final in self.finals
-            for k in range(final.shape[0] // BLOCK)
-        ]
+        return self.outputs
 
 
 def pick_kernel(me_ref, *refs):
@@ -454,6 +491,7 @@
         + [pl.BlockSpec(memory_space=pltpu.VMEM)] * len(arrays),
         out_specs=[pl.BlockSpec(memory_space=pltpu.VMEM)] * 2,
         out_shape=[jax.ShapeDtypeStruct(shape, NARROW), jax.ShapeDtypeStruct(shape, WIDE)],
+        cost_estimate=lasting(2.0),
         name="pick_columns",
     )(me, *arrays)
 
@@ -466,17 +504,17 @@
     unit_ref[...] = unit
     rate_ref[...] = jnp.broadcast_to(rate, rate_ref.shape)
     for gain, bias, out in ((gain1, bias1, attn_ref), (gain2, bias2, mlp_ref)):
-        out[...] = (unit * gain[...].astype(WIDE) + bias[...].astype(WIDE)).astype(NARROW)
-
-
-def two_norms(inputs, *gains):
+        out[...] = (unit * gain[...] + bias[...]).astype(NARROW)
+
+
+def two_norms(inputs, row, gains):
     tokens = inputs.shape[0]
     rows = tokens // 4
     by_rows = pl.BlockSpec((rows, D), lambda i: (i, 0))
     return pl.pallas_call(
         norm_kernel,
         grid=(4,),
-        in_specs=[by_rows] + [whole_spec((1, D))] * 4,
+        in_specs=[by_rows] + [pl.BlockSpec((1, D), lambda i, k=k: (0, k)) for k in gains],
         out_specs=[by_rows, by_rows, by_rows, pl.BlockSpec((rows, 128), lambda i: (i, 0))],
         out_shape=[
             jax.ShapeDtypeStruct((tokens, D), NARROW),
@@ -484,15 +522,16 @@
             jax.ShapeDtypeStruct((tokens, D), WIDE),
             jax.ShapeDtypeStruct((tokens, 128), WIDE),
         ],
+        cost_estimate=lasting(4.0),
         name="two_norms",
-    )(inputs, *gains)
+    )(inputs, *[row] * 4)
 
 
 def up_kernel(
     half, me_ref, x_ref, weight_ref, bias_ref, act_ref, slope_ref, keep_ref, send_ref
 ):
     step = pl.program_id(0)
-    up = plain_dot(x_ref[...], weight_ref[...], ROWS_COLS) + bias_ref[...].astype(WIDE)
+    up = plain_dot(x_ref[...], weight_ref[...], ROWS_COLS) + bias_ref[...]
     below = 0.5 * (1.0 + lax.erf(up * (0.5**0.5)))
     act = (up * below).astype(NARROW)
     act_ref[...] = act
@@ -510,7 +549,7 @@
             send_ref[i] = wide[:, i * BLOCK : (i + 1) * BLOCK]
 
 
-def mlp_up(mlp_in, up_weight, up_bias, me):
+def mlp_up(mlp_in, up_weight, row, me):
     owners = lax.axis_size("batch")
     tokens = mlp_in.shape[0]
     half = owners // 2
@@ -528,7 +567,9 @@
             in_specs=[
                 pl.BlockSpec((tokens, D), lambda i, me: (0, 0)),
                 pl.BlockSpec((D, each), natural),
-                pl.BlockSpec((1, each), natural),
+                pl.BlockSpec(
+                    (1, each), lambda i, me: (0, UP_AT // each + natural(i, me)[1])
+                ),
             ],
             out_specs=[
                 pl.BlockSpec((tokens, each), natural),
@@ -549,8 +590,9 @@
             jax.ShapeDtypeStruct((subs, tokens, half * BLOCK), NARROW),
             jax.ShapeDtypeStruct((subs, tokens, half * BLOCK), WIDE),
         ],
+        cost_estimate=lasting(11.0),
         name="mlp_up",
-    )(me, mlp_in, up_weight, up_bias)
+    )(me, mlp_in, up_weight, row)
 
 
 def back_kernel(
@@ -607,17 +649,18 @@
             jax.ShapeDtypeStruct((tokens, D), WIDE),
             jax.ShapeDtypeStruct((tokens, D), WIDE),
         ],
+        cost_estimate=lasting(16.0),
         name="mlp_back",
     )(cot, down_weight, up_weight, act, slope)
 
 
 def output_kernel(low_ref, weight_ref, x_ref, mlp_ref, dense_ref, down_ref, out_ref):
-    attn = plain_dot(low_ref[...], weight_ref[...], ROWS_COLS) + dense_ref[...].astype(WIDE)
-    mlp = mlp_ref[...] + down_ref[...].astype(WIDE)
+    attn = plain_dot(low_ref[...], weight_ref[...], ROWS_COLS) + dense_ref[...]
+    mlp = mlp_ref[...] + down_ref[...]
     out_ref[...] = (x_ref[...].astype(WIDE) + attn + mlp).astype(NARROW)
 
 
-def layer_output(low, dense_weight, inputs, mlp_out, *biases):
+def layer_output(low, dense_weight, inputs, mlp_out, row, biases):
     tokens = inputs.shape[0]
     each = 512
     by_column = pl.BlockSpec((tokens, each), lambda i: (0, i))
@@ -629,13 +672,13 @@
             pl.BlockSpec((D, each), lambda i: (0, i)),
             by_column,
             by_column,
-            pl.BlockSpec((1, each), lambda i: (0, i)),
-            pl.BlockSpec((1, each), lambda i: (0, i)),
-        ],
+        ]
+        + [pl.BlockSpec((1, each), lambda i, k=k: (0, k * (D // each) + i)) for k in biases],
         out_specs=by_column,
         out_shape=jax.ShapeDtypeStruct((tokens, D), NARROW),
+        cost_estimate=lasting(3.0),
         name="layer_output",
-    )(low, dense_weight, inputs, mlp_out, *biases)
+    )(low, dense_weight, inputs, mlp_out, row, row)
 
 
 def norm_back_kernel(
@@ -667,7 +710,7 @@
     @pl.when(step == pl.num_programs(0) - 1)
     def _():
         size = 64
-        gain_attn, gain_mlp = gain1[...].astype(WIDE), gain2[...].astype(WIDE)
+        gain_attn, gain_mlp = gain1[...], gain2[...]
         totals = [jnp.zeros((1, D), WIDE)] * 5
         for k in range(grad_ref.shape[0] // size):
             rows = pl.ds(k * size, size)
@@ -686,7 +729,7 @@
         sums_ref[5:8, :] = jnp.zeros((3, D), WIDE)
 
 
-def norm_back(qkv_grad, qkv_weight, mlp_norm_grad, unit, rate, cot, gain1, gain2):
+def norm_back(qkv_grad, qkv_weight, mlp_norm_grad, unit, rate, cot, row, gains):
     tokens = cot.shape[0]
     each = 512
     total = whole_spec((tokens, D))
@@ -700,17 +743,17 @@
             total,
             whole_spec(rate.shape),
             total,
-            whole_spec((1, D)),
-            whole_spec((1, D)),
-        ],
+        ]
+        + [pl.BlockSpec((1, D), lambda i, k=k: (0, k)) for k in gains],
         out_specs=[total, whole_spec((8, D)), pl.BlockSpec((1, each), lambda i: (0, i))],
         out_shape=[
             jax.ShapeDtypeStruct((tokens, D), WIDE),
             jax.ShapeDtypeStruct((8, D), WIDE),
             jax.ShapeDtypeStruct((1, 3 * D), WIDE),
         ],
+        cost_estimate=lasting(9.0),
         name="norm_back",
-    )(qkv_grad, qkv_weight, mlp_norm_grad, unit, rate, cot, gain1, gain2)
+    )(qkv_grad, qkv_weight, mlp_norm_grad, unit, rate, cot, row, row)
 
 
 def dct_matrix():
@@ -861,7 +904,7 @@
     mix, wrow = mix_ref[...], wrow_ref[...]
     tables = all_rows(tables_ref, seqs)
     low = lane_is_low((seqs * context, PAIR))
-    block = plain_dot(attn_ref[...], weight_ref[...], ROWS_COLS) + bias_ref[...].astype(WIDE)
+    block = plain_dot(attn_ref[...], weight_ref[...], ROWS_COLS) + bias_ref[...]
     one, two, three = block[:, :PAIR], block[:, PAIR : 2 * PAIR], block[:, 2 * PAIR :]
     query = jnp.where(low, one, two)
     key = pltpu.roll(jnp.where(low, three, one), HEAD, 1)
@@ -1038,6 +1081,7 @@
         in_specs=[SMEM_SPEC, SMEM_SPEC, spec, spec],
         out_specs=spec,
         out_shape=jax.ShapeDtypeStruct(own.shape, WIDE),
+        cost_estimate=lasting(2.0),
         name="pass_carry",
     )(lengths, first, own, arrived)
 
@@ -1081,6 +1125,7 @@
             jax.ShapeDtypeStruct((pairs, seqs, 2, context, context), NARROW),
             jax.ShapeDtypeStruct((seqs, pairs, HEAD + 8, PAIR), WIDE),
         ],
+        cost_estimate=lasting(14.0),
         name="attention_local",
     )(lengths, first, attn_in, weight, bias, tables, mix, wrow)
 
@@ -1106,6 +1151,7 @@
         + [carry],
         out_shape=[jax.ShapeDtypeStruct((tokens, D), NARROW), narrow, wide, wide]
         + [jax.ShapeDtypeStruct((seqs, pairs, HEAD + 8, PAIR), WIDE)],
+        cost_estimate=lasting(20.0),
         name="attention_middle",
     )(lengths, first, cot, dense_weight, *rest)
 
@@ -1122,6 +1168,7 @@
             jax.ShapeDtypeStruct((tokens, 3 * D), NARROW),
             jax.ShapeDtypeStruct((tokens, 3 * D), WIDE),
         ],
+        cost_estimate=lasting(10.0),
         name="attention_last",
     )(lengths, first, *rest)
 
@@ -1160,35 +1207,41 @@
     else:
         reduction = Singly(line, bits)
 
-    def pieces(left, left_in, blocks, right, right_in, columns):
-        return [
-            (left, left_in, block, right, right_in, column)
-            for column in columns
-            for block in blocks
+    def group(name, shape, at, left, blocks, right, columns):
+        pieces = [
+            (*left, block, *right, (row, column))
+            for column in range(columns)
+            for row, block in enumerate(blocks)
         ]
-
-    def pairs(parts):
-        return list(zip(parts[::2], parts[1::2]))
-
+        size = (len(blocks) * BLOCK_ROWS, columns * COLUMNS // Rounds.PARTS)
+        reduction.prepare((name, shape, at, size), pieces)
+
+    BLOCK_ROWS = min(BLOCK, D // owners)
     inputs_flat = inputs.reshape(tokens, D)
     cot = cotangent.reshape(tokens, D)
     cot_in = swap(cot.astype(WIDE), 0)
-    gains = [v[None, :] for v in (ln1_gain, ln1_bias, ln2_gain, ln2_bias)]
-    attn_in, mlp_in, unit, rate = line.step(two_norms, inputs_flat, *gains)
-    act, slope, act_own, act_send = line.step(mlp_up, mlp_in, up_weight, up_bias[None, :], me)
+    row = jnp.concatenate(
+        [qkv_bias, up_bias, ln1_gain, ln1_bias, ln2_gain, ln2_bias, dense_bias, down_bias]
+    ).astype(WIDE)[None, :]
+    attn_in, mlp_in, unit, rate = line.step(
+        lambda *a: two_norms(*a, (LN1_GAIN, LN1_BIAS, LN2_GAIN, LN2_BIAS)), inputs_flat, row
+    )
+    act, slope, act_own, act_send = line.step(mlp_up, mlp_in, up_weight, row, me)
     act_in = swap(act_send, 0)
     norm_own, norm_send = line.step(lambda *a: pick(a[:2], a[2]), attn_in, mlp_in, me)
     subs = act_own.shape[0]
-    down_parts = [
-        pieces(act_own, act_in, range(sub, sub + 2), cot, cot_in, range(across))
-        for sub in range(0, subs, 2)
-    ]
-    reduction.prepare(pairs(down_parts[0]))
+
+    def down_group(sub):
+        shape = (FF // owners, D)
+        at = (sub // 2, 0)
+        group("down", shape, at, (act_own, act_in), (sub, sub + 1), (cot, cot_in), across)
+
+    down_group(0)
     up_grad, up_send, up_sums, mlp_out, mlp_norm_grad = line.step(
         mlp_back, cot, down_weight, up_weight, act, slope
     )
-    for part in down_parts[1:]:
-        reduction.prepare(pairs(part))
+    for sub in range(2, subs, 2):
+        down_group(sub)
     reduction.step()
     up_in = line.send(up_send, lambda a: swap(a, 0))
     norm_in = line.send(norm_send, lambda a: swap(a, 0))
@@ -1203,20 +1256,25 @@
         first,
         attn_in,
         qkv_weight,
-        qkv_bias[None, :],
+        row,
         tables,
         mix,
         wrow,
     )
     arrived = shift_rows(carry, "seq", 1)
-    up_pieces = pieces(norm_own, norm_in, [1], up_grad, up_in, range(FF // COLUMNS))
-    up_pairs = pairs(up_pieces)
-    reduction.prepare(up_pairs[:2])
-    reduction.step()
-    reduction.prepare(up_pairs[2:])
+
+    def up_group(part):
+        shape = (D // owners, FF)
+        at = (0, part * Rounds.PARTS)
+        columns = FF // COLUMNS // 2
+        group("up", shape, at, (norm_own, norm_in), (1,), (up_grad, up_in), columns)
+
+    up_group(0)
     for _ in range(hops - 1):
         passed = line.step(pass_on, carry, arrived, lengths_here, first)
         arrived = shift_rows(passed, "seq", 1)
+    reduction.step()
+    up_group(1)
     attn_low, grad_q, grad_k, grad_v, carry_back = line.step(
         attention_middle,
         lengths_here,
@@ -1238,21 +1296,20 @@
     arrived_back = shift_rows(carry_back, "seq", -1)
     low_own, low_send = line.step(lambda *a: pick(a[:1], a[1]), attn_low, me)
     low_in = swap(low_send, 0)
+    reduction.step()
     output = line.step(
-        layer_output,
+        lambda *a: layer_output(*a, (DENSE, DOWN)),
         attn_low,
         dense_weight,
         inputs_flat,
         mlp_out,
-        dense_bias[None, :],
-        down_bias[None, :],
-    )
-    reduction.step()
+        row,
+    )
     for _ in range(hops - 1):
         passed = line.step(pass_on, carry_back, arrived_back, lengths_here, first)
         arrived_back = shift_rows(passed, "seq", -1)
-    dense_pieces = pieces(low_own, low_in, [0], cot, cot_in, range(across))
-    reduction.prepare(pairs(dense_pieces))
+    shape = (D // owners, D)
+    group("dense", shape, (0, 0), (low_own, low_in), (0,), (cot, cot_in), across)
     qkv_grad, qkv_send = line.step(
         attention_last,
         lengths_here,
@@ -1271,18 +1328,30 @@
     reduction.step()
     qkv_in = line.send(qkv_send, lambda a: swap(a, 0))
     input_grad, sums, qkv_sums = line.step(
-        norm_back, qkv_grad, qkv_weight, mlp_norm_grad, unit, rate, cot, gains[0], gains[2]
-    )
-    qkv_pieces = pieces(norm_own, norm_in, [0], qkv_grad, qkv_in, range(3 * D // COLUMNS))
-    qkv_pairs = pairs(qkv_pieces)
-    reduction.prepare(qkv_pairs[:1])
+        lambda *a: norm_back(*a, (LN1_GAIN, LN2_GAIN)),
+        qkv_grad,
+        qkv_weight,
+        mlp_norm_grad,
+        unit,
+        rate,
+        cot,
+        row,
+    )
+
+    def qkv_group(part):
+        shape = (D // owners, 3 * D)
+        at = (0, part * Rounds.PARTS)
+        group("qkv", shape, at, (norm_own, norm_in), (0,), (qkv_grad, qkv_in), 2)
+
+    qkv_group(0)
+    reduction.step()
     vectors = Vectors(
         line, (sums[0], sums[1], sums[2], sums[3], qkv_sums[0], sums[4], up_sums[0])
     )
-    for pair in qkv_pairs[1:]:
+    for part in range(1, 3):
+        qkv_group(part)
         vectors.take()
         reduction.step()
-        reduction.prepare([pair])
         vectors.send()
     while not reduction.finished():
         vectors.take()
@@ -1299,21 +1368,6 @@
         up_bias_total,
     ) = vectors.results()
 
-    def next_totals(parts):
-        taken = totals[: len(parts)]
-        del totals[: len(parts)]
-        return taken
-
-    down_total = []
-    for part in down_parts:
-        taken = next_totals(part)
-        each = len(part) // across
-        down_total += [jnp.concatenate(taken[block::each], axis=1) for block in range(each)]
-    down_total = jnp.concatenate(down_total, axis=0)
-    up_total, dense_total, qkv_total = (
-        jnp.concatenate(next_totals(part), axis=1)
-        for part in (up_pieces, dense_pieces, qkv_pieces)
-    )
     return (
         output.reshape(inputs.shape),
         input_grad.reshape(inputs.shape),
@@ -1321,13 +1375,13 @@
         attn_shift_total,
         mlp_gain_total,
         mlp_shift_total,
-        qkv_total,
+        totals["qkv"],
         qkv_bias_total,
-        dense_total,
+        totals["dense"],
         bias_total,
-        up_total,
+        totals["up"],
         up_bias_total,
-        down_total,
+        totals["down"],
         bias_total,
     )
 

time: 443 us -> 401 us (0.905)
  local copies, waits for them, and re-layouts: 48.8 us -> 27 us
  waiting for transfers between devices: 113 us -> 102 us
    ppermute x29 -> x27, waiting for transfers between devices: 28.3 us -> 51.1 us  [swap(): lax.ppermute(value, 'batch', [(i, i ^ 1 << bit) for i in range(count)])]
    ppermute x4, waiting for transfers between devices: 35.5 us -> 13.9 us  [shift_rows(): lax.ppermute(value, axis, [(i, i + by) for i in range(count) if 0 <= i +...]
    unnamed x131 -> x88, local copies, waits for them, and re-layouts: 31.3 us -> 22.3 us
    broadcast_in_dim x8 -> x0, local copies, waits for them, and re-layouts: 8.21 us -> none  [the longest x4 5.1 us: shards(): gains = [v[None, :] for v in (ln1_gain, ln1_bias, ln2_gain, ln2_bias)]]
    ppermute x3, waiting for transfers between devices: 14.8 us -> 6.78 us  [send(): lax.ppermute(a, 'seq', what)]
    ppermute x29 -> x27, starting transfers between devices: 28.4 us -> 24.4 us  [swap(): lax.ppermute(value, 'batch', [(i, i ^ 1 << bit) for i in range(count)])]
    pallas_call x21 -> x20, Pallas kernels: 90.6 us -> 89.2 us  [step(): out = function(*self.wait(*values))]
  transfers between devices with their start and end apart: 54 -> 52, of which waited for: 21 -> 23; matrix products, arithmetic and copies ran while one was open for 7% -> 2% of each run, Pallas kernels for 31% -> 31%
where the time goes in v3:
time: 401 us; the launch traced here: 399 us
  Pallas kernels  185 us (46%)
  waiting for transfers between devices  102 us (25%)
  starting transfers between devices  78.3 us (20%)
  local copies, waits for them, and re-layouts  27 us (7%)
  other arithmetic  5.31 us (1%)
    pallas_call x20, Pallas kernels, step(): out = function(*self.wait(*values))  89.2 us
    ppermute x27, waiting for transfers between devices, swap(): lax.ppermute(value, 'batch', [(i, i ^ 1 << bit) for i in range(count)])  51.1 us
    ppermute x10, waiting for transfers between devices, step(): self.end = lax.ppermute(got.pop(0), 'seq', [(0, 1), (1, 0), (2, 3), (3, 2)])  29.8 us
    ppermute x10, starting transfers between devices, step(): self.end = lax.ppermute(got.pop(0), 'seq', [(0, 1), (1, 0), (2, 3), (3, 2)])  28.9 us
    ppermute x27, starting transfers between devices, swap(): lax.ppermute(value, 'batch', [(i, i ^ 1 << bit) for i in range(count)])  24.4 us
    unnamed x88, local copies, waits for them, and re-layouts  22.3 us
    pallas_call x1, Pallas kernels, attention_middle(): pl.pallas_call(partial(middle_kernel, seqs), grid=(pairs,), in_specs=[SME...  20 us
    pallas_call x1, Pallas kernels, mlp_back(): pl.pallas_call(back_kernel, grid=(FF // each,), in_specs=[total, pl.Block...  15.9 us
  transfers between devices with their start and end apart: 52, of which 23 were waited for; matrix products, arithmetic and copies ran while one was open for 2% of the time, Pallas kernels for 31%

profile of v3, /device:TPU:0, one launch (start us, length us, event | category | flops | bytes accessed | tf_op | source)
XLA Modules:
  0.0 398.9 jit_solution(10996747770675213714)
XLA Ops:
  6.9 3.9 two_norms.1
  10.8 11.0 %mlp_up.1 = (bf16[256,4096]{1,0:T(8,128)(2,1)}, f32[256,4096]{1,0:T(8,128)}, bf16[4,256,512]{2,1,0:T(8,128)(2,1)}, f32[4,256,512]{2,1,0:T(8,128)}) custom-call(s32[1]{0:T(128)} %bitcast.2.me_ref, bf16[256,1024]{1,0:T(8,128)(2,1)} %get-tuple-element.478.x_ref.refs_1_, bf16[1024,4096]{1,0:T(8,128)(2,1)} %up_ref, ...), custom_call_target="tpu_custom_call" | custom-call | flops 12650000384 | tf_op jit(solution)/shard_map/mlp_up/pallas_call | solution.py:562
  28.6 6.0 %piece_products.8 = (f32[512,512]{1,0:T(8,128)}, f32[512,512]{1,0:T(8,128)}, f32[512,512]{1,0:T(8,128)}, f32[512,512]{1,0:T(8,128)}) custom-call(bf16[4,256,512]{2,1,0:T(8,128)(2,1)} %get-tuple-element.519.refs_0_.refs_4_.refs_8_.refs_12_, f32[4,256,512]{2,1,0:T(8,128)} %collective-permute-done.refs_1_.refs_5_.refs_9_.refs_13_, bf16[256,1024]{1,0:T(8,128)(2,1)} %bitcast.26, ...), custom_call_target="tpu_custom_call" | custom-call | flops 5750000128 | tf_op jit(solution)/shard_map/piece_products/pallas_call | solution.py:88
  34.6 2.9 collective-permute-start.2
  39.0 15.9 %mlp_back.1 = (bf16[256,4096]{1,0:T(8,128)(2,1)}, f32[256,4096]{1,0:T(8,128)}, f32[1,4096]{1,0:T(1,128)}, f32[256,1024]{1,0:T(8,128)}, f32[256,1024]{1,0:T(8,128)}) custom-call(bf16[256,1024]{1,0:T(8,128)(2,1)} %bitcast.30, bf16[4096,1024]{1,0:T(8,128)(2,1)} %down_ref, bf16[1024,4096]{1,0:T(8,128)(2,1)} %up_ref, ...), custom_call_target="tpu_custom_call" | custom-call | flops 18400000000 | tf_op jit(solution)/shard_map/mlp_back/pallas_call | solution.py:628
  55.0 5.8 %piece_products.9 = (f32[768,512]{1,0:T(8,128)}, f32[768,512]{1,0:T(8,128)}, f32[512,512]{1,0:T(8,128)}, f32[512,512]{1,0:T(8,128)}) custom-call(bf16[4,256,512]{2,1,0:T(8,128)(2,1)} %get-tuple-element.519.refs_0_.refs_4_.refs_8_.refs_12_, f32[4,256,512]{2,1,0:T(8,128)} %collective-permute-done.refs_1_.refs_5_.refs_9_.refs_13_, bf16[256,1024]{1,0:T(8,128)(2,1)} %bitcast.31, ...), custom_call_target="tpu_custom_call" | custom-call | flops 5750000128 | tf_op jit(solution)/shard_map/piece_products/pallas_call | solution.py:88
  63.7 3.3 reduce_round.12
  72.7 14.0 %attention_local.1 = (bf16[8,256,128]{2,1,0:T(8,128)(2,1)}, bf16[8,256,128]{2,1,0:T(8,128)(2,1)}, bf16[8,256,128]{2,1,0:T(8,128)(2,1)}, f32[8,256,128]{2,1,0:T(8...) custom-call(s32[2,3]{1,0:T(2,128)} %lengths_ref.4, ...), custom_call_target="tpu_custom_call" | custom-call | flops 16099999744 | tf_op jit(solution)/shard_map/attention_local/pallas_call | solution.py:1109
  86.7 3.5 collective-permute-start.4
  91.2 5.9 %piece_products.10 = (f32[768,512]{1,0:T(8,128)}, f32[768,512]{1,0:T(8,128)}, f32[512,512]{1,0:T(8,128)}, f32[512,512]{1,0:T(8,128)}) custom-call(bf16[2,256,512]{2,1,0:T(8,128)(2,1)} %get-tuple-element.805.refs_0_.refs_4_.refs_8_.refs_12_, f32[2,256,512]{2,1,0:T(8,128)} %copy-done.2, bf16[256,4096]{1,0:T(8,128)(2,1)} %get-tuple-element.607.refs_2_.refs_6_.refs_10_.refs_14_, ...), custom_call_target="tpu_custom_call" | custom-call | flops 5750000128 | tf_op jit(solution)/shard_map/piece_products/pallas_call | solution.py:88
  97.1 6.2 %collective-permute-done.4.arrived_ref = f32[2,8,72,128]{3,2,1,0:T(8,128)S(1)} collective-permute-done((f32[2,8,72,128]{3,2,1,0:T(8,128)}, f32[2,8,72,128]{3,2,1,0:T(8,128)S(1)}, u32[]{:S(2)}, u32[]{:S(2)}) %collective-permute-start.4) | collective-permute-done | bytes 589856 | tf_op jit(solution)/shard_map/ppermute | solution.py:50
  106.1 5.1 %collective-permute-start.7 = (f32[2,8,72,128]{3,2,1,0:T(8,128)}, f32[2,8,72,128]{3,2,1,0:T(8,128)}, u32[]{:S(2)}, u32[]{:S(2)}) collective-permute-start(f32[2,8,72,128]{3,2,1,0:T(8,128)} %pass_carry.2), channel_id=1, source_target_pairs={{0,8},{8,16},{16,24},{1,9},{9,17},{17,25},{2,10},{10,18},{18,26},{... | collective-permute-start | bytes 1769480 | tf_op jit(solution)/shard_map/ppermute | solution.py:50
  112.3 4.3 %reduce_round.13 = (f32[768,512]{1,0:T(8,128)}, f32[768,512]{1,0:T(8,128)}, f32[256,512]{1,0:T(8,128)}, f32[256,512]{1,0:T(8,128)}, f32[512,512]{1,0:T(8,128)}, /*index=5*/f32[512,512]{1,0:T(8,128)}) custom-call(s32[1]{0:T(128)} %bitcast.refs_0_, f32[768,512]{1,0:T(8,128)} %copy-done.8, ...), custom_call_target="tpu_custom_call", output_to_operand_aliasing={{0}: (7, {}), {1}: (8, {})} | custom-call | flops 5750000128 | tf_op jit(solution)/shard_map/reduce_round/pallas_call | solution.py:88
  119.3 5.6 %piece_products.11 = (f32[768,512]{1,0:T(8,128)}, f32[768,512]{1,0:T(8,128)}, f32[512,512]{1,0:T(8,128)}, f32[512,512]{1,0:T(8,128)}) custom-call(bf16[2,256,512]{2,1,0:T(8,128)(2,1)} %get-tuple-element.805.refs_0_.refs_4_.refs_8_.refs_12_, f32[2,256,512]{2,1,0:T(8,128)} %copy-done.2, bf16[256,4096]{1,0:T(8,128)(2,1)} %get-tuple-element.607.refs_2_.refs_6_.refs_10_.refs_14_, ...), custom_call_target="tpu_custom_call" | custom-call | flops 5750000128 | tf_op jit(solution)/shard_map/piece_products/pallas_call | solution.py:88
  125.0 20.0 %attention_middle.1 = (bf16[256,1024]{1,0:T(8,128)(2,1)}, bf16[8,256,128]{2,1,0:T(8,128)(2,1)}, f32[8,256,128]{2,1,0:T(8,128)}, f32[8,256,128]{2,1,0:T(8,128)}, f32[2,8,72,128]{3,2,1,0:T(8,128)}) custom-call(s32[2,3]{1,0:T(2,128)} %lengths_ref.4, s32[2]{0:T(128)} %pad_add_fusion.first_ref, bf16[256,1024]{1,0:T(8,128)(2,1)} %bitcast.35, ...), custom_call_target="tpu_custom_call" | custom-call | flops 23000000512 | tf_op jit(solution)/shard_map/attention_middle/pallas_call | solution.py:1138
  148.5 3.6 collective-permute-done.10.refs_1_
  154.4 5.3 %reduce_round.14 = (f32[768,512]{1,0:T(8,128)}, f32[768,512]{1,0:T(8,128)}, f32[256,512]{1,0:T(8,128)}, f32[256,512]{1,0:T(8,128)}, f32[512,512]{1,0:T(8,128)}, /*index=5*/f32[512,512]{1,0:T(8,128)}, f32[512,512]{1,0:T(8,128)}) custom-call(s32[1]{0:T(128)} %bitcast.refs_0_, f32[768,512]{1,0:T(8,128)} %copy-done.10, ...), custom_call_target="tpu_custom_call", output_to_operand_aliasing={{0}: (9, {}), {1}: (10, {})} | custom-call | flops 5750000128 | tf_op jit(solution)/shard_map/reduce_round/pallas_call | solution.py:88
  159.7 3.4 layer_output.1
  172.1 3.8 piece_products.12
  176.0 7.7 %collective-permute-done.14.carry_ref = f32[2,8,72,128]{3,2,1,0:T(8,128)} collective-permute-done((f32[2,8,72,128]{3,2,1,0:T(8,128)}, f32[2,8,72,128]{3,2,1,0:T(8,128)}, u32[]{:S(2)}, u32[]{:S(2)}) %collective-permute-start.14) | collective-permute-done | bytes 589856 | tf_op jit(solution)/shard_map/ppermute | solution.py:50
  183.7 9.7 %attention_last.1 = (bf16[256,3072]{1,0:T(8,128)(2,1)}, f32[256,3072]{1,0:T(8,128)}) custom-call(s32[2,3]{1,0:T(2,128)} %lengths_ref.4, s32[2]{0:T(128)} %pad_add_fusion.first_ref, bf16[8,256,128]{2,1,0:T(8,128)(2,1)} %get-tuple-element.677.gradq_ref, f32[8,256,128]{2,1,0:T(8,128)} %get-tuple-element.678.gradk_ref, ...), custom_call_target="tpu_custom_call" | custom-call | flops 11500000256 | tf_op jit(solution)/shard_map/attention_last/pallas_call | solution.py:1162
  193.3 9.7 %collective-permute-done.18.refs_8_ = f32[512,512]{1,0:T(8,128)} collective-permute-done((f32[512,512]{1,0:T(8,128)}, f32[512,512]{1,0:T(8,128)}, u32[]{:S(2)}, u32[]{:S(2)}) %collective-permute-start.18) | collective-permute-done | bytes 1048608 | tf_op jit(solution)/shard_map/ppermute | solution.py:436
  204.7 6.8 %reduce_round.15 = (f32[512,512]{1,0:T(8,128)}, f32[512,512]{1,0:T(8,128)}, f32[256,512]{1,0:T(8,128)}, f32[256,512]{1,0:T(8,128)}, f32[512,512]{1,0:T(8,128)}, ...) custom-call(s32[1]{0:T(128)} %bitcast.refs_0_, ...), custom_call_target="tpu_custom_call", output_to_operand_aliasing={{0}: (11, {}), {1}: (12, {})} | custom-call | flops 5750000128 | tf_op jit(solution)/shard_map/reduce_round/pallas_call | solution.py:88
  217.7 9.2 %norm_back.1 = (f32[256,1024]{1,0:T(8,128)}, f32[8,1024]{1,0:T(8,128)}, f32[1,3072]{1,0:T(1,128)}) custom-call(bf16[256,3072]{1,0:T(8,128)(2,1)} %get-tuple-element.807.qkv_ref.refs_2_.refs_6_, bf16[1024,3072]{1,0:T(8,128)(2,1)} %weight_ref.3, f32[256,1024]{1,0:T(8,128)} %get-tuple-element.716.mlp_ref, f32[256,1024]{1,0:T(8,128)} %get-tuple-element.717.unit_ref, ...), custom_call_target="tpu_custom_call" | custom-call | flops 10350000128 | tf_op jit(solution)/shard_map/norm_back/pallas_call | solution.py:736
  231.0 3.8 piece_products.13
  234.8 3.8 collective-permute-done.20.refs_1_
  239.6 6.0 %reduce_round.16 = (f32[384,512]{1,0:T(8,128)}, f32[384,512]{1,0:T(8,128)}, f32[128,512]{1,0:T(8,128)}, f32[128,512]{1,0:T(8,128)}, f32[512,512]{1,0:T(8,128)}, ...) custom-call(s32[1]{0:T(128)} %bitcast.refs_0_, ...), custom_call_target="tpu_custom_call", output_to_operand_aliasing={{0}: (12, {}), {1}: (13, {})} | custom-call | flops 5750000128 | tf_op jit(solution)/shard_map/reduce_round/pallas_call | solution.py:88
  245.7 4.5 %collective-permute-start.28 = (f32[512,512]{1,0:T(8,128)}, f32[512,512]{1,0:T(8,128)S(1)}, u32[]{:S(2)}, u32[]{:S(2)}) collective-permute-start(f32[512,512]{1,0:T(8,128)} %get-tuple-element.779), channel_id=1, source_target_pairs={{0,8},{8,0},{16,24},{24,16},{1,9},{9,1},{17,25},{25,17},{2,10},{10... | collective-permute-start | bytes 3145736 | tf_op jit(solution)/shard_map/ppermute | solution.py:436
  253.8 3.8 piece_products.14
  257.6 11.9 %collective-permute-done.26.refs_1_ = f32[384,512]{1,0:T(8,128)S(1)} collective-permute-done((f32[384,512]{1,0:T(8,128)}, f32[384,512]{1,0:T(8,128)S(1)}, u32[]{:S(2)}, u32[]{:S(2)}) %collective-permute-start.26) | collective-permute-done | bytes 786464 | tf_op jit(solution)/shard_map/ppermute | solution.py:57
  274.0 5.3 %reduce_round.17 = (f32[384,512]{1,0:T(8,128)}, f32[384,512]{1,0:T(8,128)}, f32[128,512]{1,0:T(8,128)}, f32[128,512]{1,0:T(8,128)}, f32[256,512]{1,0:T(8,128)}, ...) custom-call(s32[1]{0:T(128)} %bitcast.refs_0_, ...), custom_call_target="tpu_custom_call", output_to_operand_aliasing={{0}: (12, {}), {1}: (13, {}), {8}: (14, {})} | custom-call | flops 5750000128 | tf_op jit(solution)/shard_map/reduce_round/pallas_call | solution.py:88
  279.4 3.4 collective-permute-start.33
  287.0 3.8 piece_products.15
  290.8 10.5 %collective-permute-done.30 = f32[2,1536]{1,0:T(2,128)S(1)} collective-permute-done((f32[2,1536]{1,0:T(2,128)S(1)}, f32[2,1536]{1,0:T(2,128)S(1)}, u32[]{:S(2)}, u32[]{:S(2)}) %collective-permute-start.30) | collective-permute-done | bytes 12320 | tf_op jit(solution)/shard_map/ppermute | solution.py:57
  305.7 5.1 %reduce_round.18 = (f32[384,512]{1,0:T(8,128)}, f32[384,512]{1,0:T(8,128)}, f32[128,512]{1,0:T(8,128)}, f32[128,512]{1,0:T(8,128)}, f32[256,512]{1,0:T(8,128)}, ...) custom-call(s32[1]{0:T(128)} %bitcast.refs_0_, ...), custom_call_target="tpu_custom_call", output_to_operand_aliasing={{0}: (12, {}), {1}: (13, {})} | custom-call | flops 5750000128 | tf_op jit(solution)/shard_map/reduce_round/pallas_call | solution.py:88
  310.8 3.4 collective-permute-start.38
  318.0 13.6 %collective-permute-done.35 = f32[1,1536]{1,0:T(1,128)S(1)} collective-permute-done((f32[1,1536]{1,0:T(1,128)S(1)}, f32[1,1536]{1,0:T(1,128)S(1)}, u32[]{:S(2)}, u32[]{:S(2)}) %collective-permute-start.35) | collective-permute-done | bytes 6176 | tf_op jit(solution)/shard_map/ppermute | solution.py:57
  331.7 3.2 collective-permute-done.38.refs_8_
  335.8 4.5 %reduce_round.19 = (f32[128,512]{1,0:T(8,128)}, f32[128,512]{1,0:T(8,128)}, f32[128,512]{1,0:T(8,128)}, f32[128,512]{1,0:T(8,128)}, f32[256,512]{1,0:T(8,128)}, ...) custom-call(s32[1]{0:T(128)} %bitcast.refs_0_, ...), custom_call_target="tpu_custom_call", output_to_operand_aliasing={{8}: (12, {})} | custom-call | flops 5750000128 | tf_op jit(solution)/shard_map/reduce_round/pallas_call | solution.py:88
  345.5 4.2 %collective-permute-start.40 = (f32[1,1536]{1,0:T(1,128)S(1)}, f32[1,1536]{1,0:T(1,128)S(1)}, u32[]{:S(2)}, u32[]{:S(2)}) collective-permute-start(f32[1,1536]{1,0:T(1,128)S(1)} %add.96), channel_id=1, source_target_pairs={{0,8},{24,16},{1,9},{25,17},{2,10},{26,18},{3,11},{27,19},{4,12},{... | collective-permute-start | bytes 18440 | tf_op jit(solution)/shard_map/ppermute | solution.py:119
  352.1 3.2 reduce_round.20
  355.3 3.3 collective-permute-start.46
  360.0 6.2 %collective-permute-done.46.refs_2_ = f32[256,512]{1,0:T(8,128)S(1)} collective-permute-done((f32[256,512]{1,0:T(8,128)}, f32[256,512]{1,0:T(8,128)S(1)}, u32[]{:S(2)}, u32[]{:S(2)}) %collective-permute-start.46) | collective-permute-done | bytes 524320 | tf_op jit(solution)/shard_map/ppermute | solution.py:436
  367.2 2.7 reduce_round.21
  370.0 3.8 collective-permute-start.49
  375.8 5.4 %collective-permute-done.48 = f32[1,1536]{1,0:T(1,128)S(1)} collective-permute-done((f32[1,1536]{1,0:T(1,128)S(1)}, f32[1,1536]{1,0:T(1,128)S(1)}, u32[]{:S(2)}, u32[]{:S(2)}) %collective-permute-start.48) | collective-permute-done | bytes 6176 | tf_op jit(solution)/shard_map/ppermute | solution.py:119
  384.7 3.6 collective-permute-start.51
  390.0 5.7 %collective-permute-done.51.refs_1_ = f32[256,512]{1,0:T(8,128)S(1)} collective-permute-done((f32[256,512]{1,0:T(8,128)}, f32[256,512]{1,0:T(8,128)S(1)}, u32[]{:S(2)}, u32[]{:S(2)}) %collective-permute-start.51) | collective-permute-done | bytes 524320 | tf_op jit(solution)/shard_map/ppermute | solution.py:436
  (214 shorter events, 100.4 us)
Async XLA Ops:
  21.8 5.7 %collective-permute-start = (f32[4,256,512]{2,1,0:T(8,128)}, f32[4,256,512]{2,1,0:T(8,128)}, u32[]{:S(2)}, u32[]{:S(2)}) collective-permute-start(f32[4,256,512]{2,1,0:T(8,128)} %get-tuple-element.474), channel_id=1, source_target_pairs={{0,1},{1,0},{2,3},{3,2},{4,5},{5,4},{6,7},{7,6},{8,9},{9,8},{10,11... | collective-permute-start | bytes 6291464 | tf_op jit(solution)/shard_map/ppermute | solution.py:57
  34.6 26.6 %collective-permute-start.2 = (f32[512,512]{1,0:T(8,128)}, f32[512,512]{1,0:T(8,128)S(1)}, u32[]{:S(2)}, u32[]{:S(2)}) collective-permute-start(f32[512,512]{1,0:T(8,128)} %get-tuple-element.496), channel_id=1, source_target_pairs={{0,2},{1,3},{2,0},{3,1},{4,6},{5,7},{6,4},{7,5},{8,10},{9,11},{10,... | collective-permute-start | bytes 3145736 | tf_op jit(solution)/shard_map/ppermute | solution.py:57
  37.5 25.1 %collective-permute-start.3 = (f32[512,512]{1,0:T(8,128)}, f32[512,512]{1,0:T(8,128)S(1)}, u32[]{:S(2)}, u32[]{:S(2)}) collective-permute-start(f32[512,512]{1,0:T(8,128)} %get-tuple-element.497), channel_id=1, source_target_pairs={{0,4},{1,5},{2,6},{3,7},{4,0},{5,1},{6,2},{7,3},{8,12},{9,13},{10,... | collective-permute-start | bytes 3145736 | tf_op jit(solution)/shard_map/ppermute | solution.py:57
  67.0 23.3 %collective-permute-start.6 = (f32[256,4096]{1,0:T(8,128)}, f32[256,4096]{1,0:T(8,128)}, u32[]{:S(2)}, u32[]{:S(2)}) collective-permute-start(f32[256,4096]{1,0:T(8,128)} %get-tuple-element.555), channel_id=1, source_target_pairs={{0,1},{1,0},{2,3},{3,2},{4,5},{5,4},{6,7},{7,6},{8,9},{9,8},{10,11... | collective-permute-start | bytes 12582920 | tf_op jit(solution)/shard_map/ppermute | solution.py:57
  68.8 42.4 %collective-permute-start.8 = (f32[768,512]{1,0:T(8,128)}, f32[768,512]{1,0:T(8,128)S(1)}, u32[]{:S(2)}, u32[]{:S(2)}) collective-permute-start(f32[768,512]{1,0:T(8,128)} %get-tuple-element.532), channel_id=1, source_target_pairs={{0,2},{1,3},{2,0},{3,1},{4,6},{5,7},{6,4},{7,5},{8,10},{9,11},{10,... | collective-permute-start | bytes 4718600 | tf_op jit(solution)/shard_map/ppermute | solution.py:57
  69.4 20.8 %collective-permute-start.5 = (f32[2,256,512]{2,1,0:T(8,128)}, f32[2,256,512]{2,1,0:T(8,128)S(1)}, u32[]{:S(2)}, u32[]{:S(2)}) collective-permute-start(f32[2,256,512]{2,1,0:T(8,128)} %get-tuple-element.553), channel_id=1, source_target_pairs={{0,1},{1,0},{2,3},{3,2},{4,5},{5,4},{6,7},{7,6},{8,9},{9,8},{10,11... | collective-permute-start | bytes 3145736 | tf_op jit(solution)/shard_map/ppermute | solution.py:57
  71.2 40.0 %collective-permute-start.9 = (f32[768,512]{1,0:T(8,128)}, f32[768,512]{1,0:T(8,128)}, u32[]{:S(2)}, u32[]{:S(2)}) collective-permute-start(f32[768,512]{1,0:T(8,128)} %get-tuple-element.577), channel_id=1, source_target_pairs={{0,4},{1,5},{2,6},{3,7},{4,0},{5,1},{6,2},{7,3},{8,12},{9,13},{10,... | collective-permute-start | bytes 4718600 | tf_op jit(solution)/shard_map/ppermute | solution.py:57
  86.7 16.6 %collective-permute-start.4 = (f32[2,8,72,128]{3,2,1,0:T(8,128)}, f32[2,8,72,128]{3,2,1,0:T(8,128)S(1)}, u32[]{:S(2)}, u32[]{:S(2)}) collective-permute-start(f32[2,8,72,128]{3,2,1,0:T(8,128)} %get-tuple-element.575.own_ref), channel_id=1, source_target_pairs={{0,8},{8,16},{16,24},{1,9},{9,17},{17,25},{2,10},{10,18},{18,26},{... | collective-permute-start | bytes 1769480 | tf_op jit(solution)/shard_map/ppermute | solution.py:50
  106.1 18.9 %collective-permute-start.7 = (f32[2,8,72,128]{3,2,1,0:T(8,128)}, f32[2,8,72,128]{3,2,1,0:T(8,128)}, u32[]{:S(2)}, u32[]{:S(2)}) collective-permute-start(f32[2,8,72,128]{3,2,1,0:T(8,128)} %pass_carry.2), channel_id=1, source_target_pairs={{0,8},{8,16},{16,24},{1,9},{9,17},{17,25},{2,10},{10,18},{18,26},{... | collective-permute-start | bytes 1769480 | tf_op jit(solution)/shard_map/ppermute | solution.py:50
  116.6 35.6 %collective-permute-start.10 = (f32[768,512]{1,0:T(8,128)}, f32[768,512]{1,0:T(8,128)S(1)}, u32[]{:S(2)}, u32[]{:S(2)}) collective-permute-start(f32[768,512]{1,0:T(8,128)} %get-tuple-element.592), channel_id=1, source_target_pairs={{0,2},{1,3},{2,0},{3,1},{4,6},{5,7},{6,4},{7,5},{8,10},{9,11},{10,... | collective-permute-start | bytes 4718600 | tf_op jit(solution)/shard_map/ppermute | solution.py:57
  118.1 35.2 %collective-permute-start.11 = (f32[768,512]{1,0:T(8,128)}, f32[768,512]{1,0:T(8,128)S(1)}, u32[]{:S(2)}, u32[]{:S(2)}) collective-permute-start(f32[768,512]{1,0:T(8,128)} %get-tuple-element.627), channel_id=1, source_target_pairs={{0,4},{1,5},{2,6},{3,7},{4,0},{5,1},{6,2},{7,3},{8,12},{9,13},{10,... | collective-permute-start | bytes 4718600 | tf_op jit(solution)/shard_map/ppermute | solution.py:57
  118.6 30.0 %collective-permute-start.12 = (f32[512,512]{1,0:T(8,128)}, f32[512,512]{1,0:T(8,128)}, u32[]{:S(2)}, u32[]{:S(2)}) collective-permute-start(f32[512,512]{1,0:T(8,128)} %get-tuple-element.633), channel_id=1, source_target_pairs={{0,8},{8,0},{16,24},{24,16},{1,9},{9,1},{17,25},{25,17},{2,10},{10... | collective-permute-start | bytes 3145736 | tf_op jit(solution)/shard_map/ppermute | solution.py:436
  145.0 18.2 %collective-permute-start.13 = (f32[2,8,72,128]{3,2,1,0:T(8,128)}, f32[2,8,72,128]{3,2,1,0:T(8,128)}, u32[]{:S(2)}, u32[]{:S(2)}) collective-permute-start(f32[2,8,72,128]{3,2,1,0:T(8,128)} %get-tuple-element.663.own_ref), channel_id=1, source_target_pairs={{8,0},{16,8},{24,16},{9,1},{17,9},{25,17},{10,2},{18,10},{26,18},{... | collective-permute-start | bytes 1769480 | tf_op jit(solution)/shard_map/ppermute | solution.py:50
  148.5 18.8 %collective-permute-start.15 = (f32[1,256,512]{2,1,0:T(8,128)}, f32[1,256,512]{2,1,0:T(8,128)}, u32[]{:S(2)}, u32[]{:S(2)}) collective-permute-start(f32[1,256,512]{2,1,0:T(8,128)} %get-tuple-element.665), channel_id=1, source_target_pairs={{0,1},{1,0},{2,3},{3,2},{4,5},{5,4},{6,7},{7,6},{8,9},{9,8},{10,11... | collective-permute-start | bytes 1572872 | tf_op jit(solution)/shard_map/ppermute | solution.py:57
  165.2 18.5 %collective-permute-start.14 = (f32[2,8,72,128]{3,2,1,0:T(8,128)}, f32[2,8,72,128]{3,2,1,0:T(8,128)}, u32[]{:S(2)}, u32[]{:S(2)}) collective-permute-start(f32[2,8,72,128]{3,2,1,0:T(8,128)} %pass_carry.3), channel_id=1, source_target_pairs={{8,0},{16,8},{24,16},{9,1},{17,9},{25,17},{10,2},{18,10},{26,18},{... | collective-permute-start | bytes 1769480 | tf_op jit(solution)/shard_map/ppermute | solution.py:50
  166.5 36.5 %collective-permute-start.16 = (f32[768,512]{1,0:T(8,128)}, f32[768,512]{1,0:T(8,128)S(1)}, u32[]{:S(2)}, u32[]{:S(2)}) collective-permute-start(f32[768,512]{1,0:T(8,128)} %get-tuple-element.649), channel_id=1, source_target_pairs={{0,2},{1,3},{2,0},{3,1},{4,6},{5,7},{6,4},{7,5},{8,10},{9,11},{10,... | collective-permute-start | bytes 4718600 | tf_op jit(solution)/shard_map/ppermute | solution.py:57
  167.3 35.7 %collective-permute-start.17 = (f32[768,512]{1,0:T(8,128)}, f32[768,512]{1,0:T(8,128)S(1)}, u32[]{:S(2)}, u32[]{:S(2)}) collective-permute-start(f32[768,512]{1,0:T(8,128)} %get-tuple-element.691), channel_id=1, source_target_pairs={{0,4},{1,5},{2,6},{3,7},{4,0},{5,1},{6,2},{7,3},{8,12},{9,13},{10,... | collective-permute-start | bytes 4718600 | tf_op jit(solution)/shard_map/ppermute | solution.py:57
  167.9 35.1 %collective-permute-start.18 = (f32[512,512]{1,0:T(8,128)}, f32[512,512]{1,0:T(8,128)}, u32[]{:S(2)}, u32[]{:S(2)}) collective-permute-start(f32[512,512]{1,0:T(8,128)} %get-tuple-element.697), channel_id=1, source_target_pairs={{0,8},{8,0},{16,24},{24,16},{1,9},{9,1},{17,25},{25,17},{2,10},{10... | collective-permute-start | bytes 3145736 | tf_op jit(solution)/shard_map/ppermute | solution.py:436
  170.5 32.5 %collective-permute-start.19 = (f32[512,512]{1,0:T(8,128)}, f32[512,512]{1,0:T(8,128)}, u32[]{:S(2)}, u32[]{:S(2)}) collective-permute-start(f32[512,512]{1,0:T(8,128)} %get-tuple-element.709.refs_9_), channel_id=1, source_target_pairs={{8,16},{16,8},{9,17},{17,9},{10,18},{18,10},{11,19},{19,11},{12,20... | collective-permute-start | bytes 3145736 | tf_op jit(solution)/shard_map/ppermute | solution.py:439
  211.4 17.9 %collective-permute-start.24 = (f32[256,3072]{1,0:T(8,128)}, f32[256,3072]{1,0:T(8,128)S(1)}, u32[]{:S(2)}, u32[]{:S(2)}) collective-permute-start(f32[256,3072]{1,0:T(8,128)} %get-tuple-element.735), channel_id=1, source_target_pairs={{0,1},{1,0},{2,3},{3,2},{4,5},{5,4},{6,7},{7,6},{8,9},{9,8},{10,11... | collective-permute-start | bytes 9437192 | tf_op jit(solution)/shard_map/ppermute | solution.py:57
  212.8 25.9 %collective-permute-start.20 = (f32[512,512]{1,0:T(8,128)}, f32[512,512]{1,0:T(8,128)}, u32[]{:S(2)}, u32[]{:S(2)}) collective-permute-start(f32[512,512]{1,0:T(8,128)} %get-tuple-element.713), channel_id=1, source_target_pairs={{0,2},{1,3},{2,0},{3,1},{4,6},{5,7},{6,4},{7,5},{8,10},{9,11},{10,... | collective-permute-start | bytes 3145736 | tf_op jit(solution)/shard_map/ppermute | solution.py:57
  213.8 25.6 %collective-permute-start.21 = (f32[512,512]{1,0:T(8,128)}, f32[512,512]{1,0:T(8,128)}, u32[]{:S(2)}, u32[]{:S(2)}) collective-permute-start(f32[512,512]{1,0:T(8,128)} %get-tuple-element.725), channel_id=1, source_target_pairs={{0,4},{1,5},{2,6},{3,7},{4,0},{5,1},{6,2},{7,3},{8,12},{9,13},{10,... | collective-permute-start | bytes 3145736 | tf_op jit(solution)/shard_map/ppermute | solution.py:57
  214.3 25.3 %collective-permute-start.22 = (f32[512,512]{1,0:T(8,128)}, f32[512,512]{1,0:T(8,128)}, u32[]{:S(2)}, u32[]{:S(2)}) collective-permute-start(f32[512,512]{1,0:T(8,128)} %get-tuple-element.731), channel_id=1, source_target_pairs={{0,8},{8,0},{16,24},{24,16},{1,9},{9,1},{17,25},{25,17},{2,10},{10... | collective-permute-start | bytes 3145736 | tf_op jit(solution)/shard_map/ppermute | solution.py:436
  216.0 23.6 %collective-permute-start.23 = (f32[512,512]{1,0:T(8,128)}, f32[512,512]{1,0:T(8,128)}, u32[]{:S(2)}, u32[]{:S(2)}) collective-permute-start(f32[512,512]{1,0:T(8,128)} %get-tuple-element.755.refs_9_), channel_id=1, source_target_pairs={{8,16},{16,8},{9,17},{17,9},{10,18},{18,10},{11,19},{19,11},{12,20... | collective-permute-start | bytes 3145736 | tf_op jit(solution)/shard_map/ppermute | solution.py:439
  245.7 27.1 %collective-permute-start.28 = (f32[512,512]{1,0:T(8,128)}, f32[512,512]{1,0:T(8,128)S(1)}, u32[]{:S(2)}, u32[]{:S(2)}) collective-permute-start(f32[512,512]{1,0:T(8,128)} %get-tuple-element.779), channel_id=1, source_target_pairs={{0,8},{8,0},{16,24},{24,16},{1,9},{9,1},{17,25},{25,17},{2,10},{10... | collective-permute-start | bytes 3145736 | tf_op jit(solution)/shard_map/ppermute | solution.py:436
  250.2 22.6 %collective-permute-start.29 = (f32[512,512]{1,0:T(8,128)}, f32[512,512]{1,0:T(8,128)S(1)}, u32[]{:S(2)}, u32[]{:S(2)}) collective-permute-start(f32[512,512]{1,0:T(8,128)} %get-tuple-element.793.refs_9_), channel_id=1, source_target_pairs={{8,16},{16,8},{9,17},{17,9},{10,18},{18,10},{11,19},{19,11},{12,20... | collective-permute-start | bytes 3145736 | tf_op jit(solution)/shard_map/ppermute | solution.py:439
  251.0 18.5 %collective-permute-start.26 = (f32[384,512]{1,0:T(8,128)}, f32[384,512]{1,0:T(8,128)S(1)}, u32[]{:S(2)}, u32[]{:S(2)}) collective-permute-start(f32[384,512]{1,0:T(8,128)} %get-tuple-element.760), channel_id=1, source_target_pairs={{0,2},{1,3},{2,0},{3,1},{4,6},{5,7},{6,4},{7,5},{8,10},{9,11},{10,... | collective-permute-start | bytes 2359304 | tf_op jit(solution)/shard_map/ppermute | solution.py:57
  252.1 18.2 %collective-permute-start.27 = (f32[384,512]{1,0:T(8,128)}, f32[384,512]{1,0:T(8,128)}, u32[]{:S(2)}, u32[]{:S(2)}) collective-permute-start(f32[384,512]{1,0:T(8,128)} %get-tuple-element.773), channel_id=1, source_target_pairs={{0,4},{1,5},{2,6},{3,7},{4,0},{5,1},{6,2},{7,3},{8,12},{9,13},{10,... | collective-permute-start | bytes 2359304 | tf_op jit(solution)/shard_map/ppermute | solution.py:57
  279.4 25.0 %collective-permute-start.33 = (f32[512,512]{1,0:T(8,128)}, f32[512,512]{1,0:T(8,128)S(1)}, u32[]{:S(2)}, u32[]{:S(2)}) collective-permute-start(f32[512,512]{1,0:T(8,128)} %get-tuple-element.818), channel_id=1, source_target_pairs={{0,8},{8,0},{16,24},{24,16},{1,9},{9,1},{17,25},{25,17},{2,10},{10... | collective-permute-start | bytes 3145736 | tf_op jit(solution)/shard_map/ppermute | solution.py:436
  282.8 21.6 %collective-permute-start.34 = (f32[512,512]{1,0:T(8,128)}, f32[512,512]{1,0:T(8,128)S(1)}, u32[]{:S(2)}, u32[]{:S(2)}) collective-permute-start(f32[512,512]{1,0:T(8,128)} %get-tuple-element.831.refs_9_), channel_id=1, source_target_pairs={{8,16},{16,8},{9,17},{17,9},{10,18},{18,10},{11,19},{19,11},{12,20... | collective-permute-start | bytes 3145736 | tf_op jit(solution)/shard_map/ppermute | solution.py:439
  283.5 17.8 %collective-permute-start.31 = (f32[384,512]{1,0:T(8,128)}, f32[384,512]{1,0:T(8,128)S(1)}, u32[]{:S(2)}, u32[]{:S(2)}) collective-permute-start(f32[384,512]{1,0:T(8,128)} %get-tuple-element.799), channel_id=1, source_target_pairs={{0,2},{1,3},{2,0},{3,1},{4,6},{5,7},{6,4},{7,5},{8,10},{9,11},{10,... | collective-permute-start | bytes 2359304 | tf_op jit(solution)/shard_map/ppermute | solution.py:57
  284.6 17.3 %collective-permute-start.32 = (f32[384,512]{1,0:T(8,128)}, f32[384,512]{1,0:T(8,128)}, u32[]{:S(2)}, u32[]{:S(2)}) collective-permute-start(f32[384,512]{1,0:T(8,128)} %get-tuple-element.812), channel_id=1, source_target_pairs={{0,4},{1,5},{2,6},{3,7},{4,0},{5,1},{6,2},{7,3},{8,12},{9,13},{10,... | collective-permute-start | bytes 2359304 | tf_op jit(solution)/shard_map/ppermute | solution.py:57
  286.2 15.1 %collective-permute-start.30 = (f32[2,1536]{1,0:T(2,128)S(1)}, f32[2,1536]{1,0:T(2,128)S(1)}, u32[]{:S(2)}, u32[]{:S(2)}) collective-permute-start(f32[2,1536]{1,0:T(2,128)S(1)} %get-tuple-element.800), channel_id=1, source_target_pairs={{0,2},{1,3},{2,0},{3,1},{4,6},{5,7},{6,4},{7,5},{8,10},{9,11},{10,... | collective-permute-start | bytes 36872 | tf_op jit(solution)/shard_map/ppermute | solution.py:57
  310.8 24.1 %collective-permute-start.38 = (f32[512,512]{1,0:T(8,128)}, f32[512,512]{1,0:T(8,128)S(1)}, u32[]{:S(2)}, u32[]{:S(2)}) collective-permute-start(f32[512,512]{1,0:T(8,128)} %get-tuple-element.846), channel_id=1, source_target_pairs={{0,8},{8,0},{16,24},{24,16},{1,9},{9,1},{17,25},{25,17},{2,10},{10... | collective-permute-start | bytes 3145736 | tf_op jit(solution)/shard_map/ppermute | solution.py:436
  314.1 17.5 %collective-permute-start.36 = (f32[384,512]{1,0:T(8,128)}, f32[384,512]{1,0:T(8,128)S(1)}, u32[]{:S(2)}, u32[]{:S(2)}) collective-permute-start(f32[384,512]{1,0:T(8,128)} %get-tuple-element.836), channel_id=1, source_target_pairs={{0,2},{1,3},{2,0},{3,1},{4,6},{5,7},{6,4},{7,5},{8,10},{9,11},{10,... | collective-permute-start | bytes 2359304 | tf_op jit(solution)/shard_map/ppermute | solution.py:57
  315.2 16.5 %collective-permute-start.37 = (f32[384,512]{1,0:T(8,128)}, f32[384,512]{1,0:T(8,128)S(1)}, u32[]{:S(2)}, u32[]{:S(2)}) collective-permute-start(f32[384,512]{1,0:T(8,128)} %get-tuple-element.840), channel_id=1, source_target_pairs={{0,4},{1,5},{2,6},{3,7},{4,0},{5,1},{6,2},{7,3},{8,12},{9,13},{10,... | collective-permute-start | bytes 2359304 | tf_op jit(solution)/shard_map/ppermute | solution.py:57
  316.7 14.9 %collective-permute-start.39 = (f32[256,512]{1,0:T(8,128)}, f32[256,512]{1,0:T(8,128)S(1)}, u32[]{:S(2)}, u32[]{:S(2)}) collective-permute-start(f32[256,512]{1,0:T(8,128)} %get-tuple-element.859.refs_9_), channel_id=1, source_target_pairs={{8,16},{16,8},{9,17},{17,9},{10,18},{18,10},{11,19},{19,11},{12,20... | collective-permute-start | bytes 1572872 | tf_op jit(solution)/shard_map/ppermute | solution.py:439
  317.4 14.2 %collective-permute-start.35 = (f32[1,1536]{1,0:T(1,128)S(1)}, f32[1,1536]{1,0:T(1,128)S(1)}, u32[]{:S(2)}, u32[]{:S(2)}) collective-permute-start(f32[1,1536]{1,0:T(1,128)S(1)} %get-tuple-element.837), channel_id=1, source_target_pairs={{0,4},{1,5},{2,6},{3,7},{4,0},{5,1},{6,2},{7,3},{8,12},{9,13},{10,... | collective-permute-start | bytes 18440 | tf_op jit(solution)/shard_map/ppermute | solution.py:57
  340.3 10.7 %collective-permute-start.43 = (f32[256,512]{1,0:T(8,128)}, f32[256,512]{1,0:T(8,128)S(1)}, u32[]{:S(2)}, u32[]{:S(2)}) collective-permute-start(f32[256,512]{1,0:T(8,128)} %get-tuple-element.871), channel_id=1, source_target_pairs={{0,8},{8,0},{16,24},{24,16},{1,9},{9,1},{17,25},{25,17},{2,10},{10... | collective-permute-start | bytes 1572872 | tf_op jit(solution)/shard_map/ppermute | solution.py:436
  342.1 8.9 %collective-permute-start.44 = (f32[256,512]{1,0:T(8,128)}, f32[256,512]{1,0:T(8,128)S(1)}, u32[]{:S(2)}, u32[]{:S(2)}) collective-permute-start(f32[256,512]{1,0:T(8,128)} %get-tuple-element.881.refs_7_), channel_id=1, source_target_pairs={{8,16},{16,8},{9,17},{17,9},{10,18},{18,10},{11,19},{19,11},{12,20... | collective-permute-start | bytes 1572872 | tf_op jit(solution)/shard_map/ppermute | solution.py:439
  342.8 8.2 %collective-permute-start.41 = (f32[128,512]{1,0:T(8,128)}, f32[128,512]{1,0:T(8,128)S(1)}, u32[]{:S(2)}, u32[]{:S(2)}) collective-permute-start(f32[128,512]{1,0:T(8,128)} %get-tuple-element.863), channel_id=1, source_target_pairs={{0,2},{1,3},{2,0},{3,1},{4,6},{5,7},{6,4},{7,5},{8,10},{9,11},{10,... | collective-permute-start | bytes 786440 | tf_op jit(solution)/shard_map/ppermute | solution.py:57
  343.9 7.1 %collective-permute-start.42 = (f32[128,512]{1,0:T(8,128)}, f32[128,512]{1,0:T(8,128)S(1)}, u32[]{:S(2)}, u32[]{:S(2)}) collective-permute-start(f32[128,512]{1,0:T(8,128)} %get-tuple-element.867), channel_id=1, source_target_pairs={{0,4},{1,5},{2,6},{3,7},{4,0},{5,1},{6,2},{7,3},{8,12},{9,13},{10,... | collective-permute-start | bytes 786440 | tf_op jit(solution)/shard_map/ppermute | solution.py:57
  355.3 10.9 %collective-permute-start.46 = (f32[256,512]{1,0:T(8,128)}, f32[256,512]{1,0:T(8,128)S(1)}, u32[]{:S(2)}, u32[]{:S(2)}) collective-permute-start(f32[256,512]{1,0:T(8,128)} %get-tuple-element.888), channel_id=1, source_target_pairs={{0,8},{8,0},{16,24},{24,16},{1,9},{9,1},{17,25},{25,17},{2,10},{10... | collective-permute-start | bytes 1572872 | tf_op jit(solution)/shard_map/ppermute | solution.py:436
  358.6 7.6 %collective-permute-start.47 = (f32[256,512]{1,0:T(8,128)}, f32[256,512]{1,0:T(8,128)S(1)}, u32[]{:S(2)}, u32[]{:S(2)}) collective-permute-start(f32[256,512]{1,0:T(8,128)} %get-tuple-element.894.refs_3_), channel_id=1, source_target_pairs={{8,16},{16,8},{9,17},{17,9},{10,18},{18,10},{11,19},{19,11},{12,20... | collective-permute-start | bytes 1572872 | tf_op jit(solution)/shard_map/ppermute | solution.py:439
  370.0 11.2 %collective-permute-start.49 = (f32[256,512]{1,0:T(8,128)}, f32[256,512]{1,0:T(8,128)S(1)}, u32[]{:S(2)}, u32[]{:S(2)}) collective-permute-start(f32[256,512]{1,0:T(8,128)} %get-tuple-element.897), channel_id=1, source_target_pairs={{0,8},{8,0},{16,24},{24,16},{1,9},{9,1},{17,25},{25,17},{2,10},{10... | collective-permute-start | bytes 1572872 | tf_op jit(solution)/shard_map/ppermute | solution.py:436
  373.8 7.5 %collective-permute-start.50 = (f32[256,512]{1,0:T(8,128)}, f32[256,512]{1,0:T(8,128)S(1)}, u32[]{:S(2)}, u32[]{:S(2)}) collective-permute-start(f32[256,512]{1,0:T(8,128)} %get-tuple-element.906.refs_2_), channel_id=1, source_target_pairs={{8,16},{16,8},{9,17},{17,9},{10,18},{18,10},{11,19},{19,11},{12,20... | collective-permute-start | bytes 1572872 | tf_op jit(solution)/shard_map/ppermute | solution.py:439
  374.5 6.7 %collective-permute-start.48 = (f32[1,1536]{1,0:T(1,128)S(1)}, f32[1,1536]{1,0:T(1,128)S(1)}, u32[]{:S(2)}, u32[]{:S(2)}) collective-permute-start(f32[1,1536]{1,0:T(1,128)S(1)} %add.98), channel_id=1, source_target_pairs={{8,0},{16,24},{9,1},{17,25},{10,2},{18,26},{11,3},{19,27},{12,4},{... | collective-permute-start | bytes 18440 | tf_op jit(solution)/shard_map/ppermute | solution.py:119
  384.7 11.0 %collective-permute-start.51 = (f32[256,512]{1,0:T(8,128)}, f32[256,512]{1,0:T(8,128)S(1)}, u32[]{:S(2)}, u32[]{:S(2)}) collective-permute-start(f32[256,512]{1,0:T(8,128)} %get-tuple-element.910), channel_id=1, source_target_pairs={{0,8},{8,0},{16,24},{24,16},{1,9},{9,1},{17,25},{25,17},{2,10},{10... | collective-permute-start | bytes 1572872 | tf_op jit(solution)/shard_map/ppermute | solution.py:436
  (41 other events, 161.5 us)

commit v4 on v3

--- a/solution.py
+++ b/solution.py
@@ -20,9 +20,6 @@
 
 EPSILON = 1e-05
 ROTARY_BASE = 10000.0
-
-UP_AT = 3 * D
-LN1_GAIN, LN1_BIAS, LN2_GAIN, LN2_BIAS, DENSE, DOWN = range((UP_AT + FF) // D, (UP_AT + FF) // D + 6)
 
 def lasting(microseconds):
     return pl.CostEstimate(
@@ -345,6 +342,7 @@
             out_shape=[jax.ShapeDtypeStruct((total, COLUMNS), WIDE)] * 2
             + [jax.ShapeDtypeStruct((rows, COLUMNS), WIDE)] * 2,
             cost_estimate=lasting(5.0),
+        compiler_params=pltpu.CompilerParams(vmem_limit_bytes=67108864),
         name="piece_products",
         )
         to_x, to_y, hold_a, hold_b = self.line.step(call, *args)
@@ -424,6 +422,7 @@
             out_shape=outs,
             input_output_aliases=aliases,
             cost_estimate=lasting(5.0),
+            compiler_params=pltpu.CompilerParams(vmem_limit_bytes=67108864),
             name="reduce_round",
         )
         got = list(self.line.step(call, *args))
@@ -496,6 +495,10 @@
     )(me, *arrays)
 
 
+def as_row(ref):
+    return ref[...].astype(WIDE)[None, :]
+
+
 def norm_kernel(x_ref, gain1, bias1, gain2, bias2, attn_ref, mlp_ref, unit_ref, rate_ref):
     x = x_ref[...].astype(WIDE)
     centered = x - jnp.mean(x, axis=-1, keepdims=True)
@@ -504,17 +507,17 @@
     unit_ref[...] = unit
     rate_ref[...] = jnp.broadcast_to(rate, rate_ref.shape)
     for gain, bias, out in ((gain1, bias1, attn_ref), (gain2, bias2, mlp_ref)):
-        out[...] = (unit * gain[...] + bias[...]).astype(NARROW)
-
-
-def two_norms(inputs, row, gains):
+        out[...] = (unit * as_row(gain) + as_row(bias)).astype(NARROW)
+
+
+def two_norms(inputs, *gains):
     tokens = inputs.shape[0]
     rows = tokens // 4
     by_rows = pl.BlockSpec((rows, D), lambda i: (i, 0))
     return pl.pallas_call(
         norm_kernel,
         grid=(4,),
-        in_specs=[by_rows] + [pl.BlockSpec((1, D), lambda i, k=k: (0, k)) for k in gains],
+        in_specs=[by_rows] + [whole_spec((D,))] * len(gains),
         out_specs=[by_rows, by_rows, by_rows, pl.BlockSpec((rows, 128), lambda i: (i, 0))],
         out_shape=[
             jax.ShapeDtypeStruct((tokens, D), NARROW),
@@ -524,14 +527,14 @@
         ],
         cost_estimate=lasting(4.0),
         name="two_norms",
-    )(inputs, *[row] * 4)
+    )(inputs, *gains)
 
 
 def up_kernel(
     half, me_ref, x_ref, weight_ref, bias_ref, act_ref, slope_ref, keep_ref, send_ref
 ):
     step = pl.program_id(0)
-    up = plain_dot(x_ref[...], weight_ref[...], ROWS_COLS) + bias_ref[...]
+    up = plain_dot(x_ref[...], weight_ref[...], ROWS_COLS) + as_row(bias_ref)
     below = 0.5 * (1.0 + lax.erf(up * (0.5**0.5)))
     act = (up * below).astype(NARROW)
     act_ref[...] = act
@@ -549,7 +552,7 @@
             send_ref[i] = wide[:, i * BLOCK : (i + 1) * BLOCK]
 
 
-def mlp_up(mlp_in, up_weight, row, me):
+def mlp_up(mlp_in, up_weight, up_bias, me):
     owners = lax.axis_size("batch")
     tokens = mlp_in.shape[0]
     half = owners // 2
@@ -567,9 +570,7 @@
             in_specs=[
                 pl.BlockSpec((tokens, D), lambda i, me: (0, 0)),
                 pl.BlockSpec((D, each), natural),
-                pl.BlockSpec(
-                    (1, each), lambda i, me: (0, UP_AT // each + natural(i, me)[1])
-                ),
+                pl.BlockSpec((each,), lambda i, me: natural(i, me)[1:]),
             ],
             out_specs=[
                 pl.BlockSpec((tokens, each), natural),
@@ -592,7 +593,7 @@
         ],
         cost_estimate=lasting(11.0),
         name="mlp_up",
-    )(me, mlp_in, up_weight, row)
+    )(me, mlp_in, up_weight, up_bias)
 
 
 def back_kernel(
@@ -650,17 +651,18 @@
             jax.ShapeDtypeStruct((tokens, D), WIDE),
         ],
         cost_estimate=lasting(16.0),
+        compiler_params=pltpu.CompilerParams(vmem_limit_bytes=67108864),
         name="mlp_back",
     )(cot, down_weight, up_weight, act, slope)
 
 
 def output_kernel(low_ref, weight_ref, x_ref, mlp_ref, dense_ref, down_ref, out_ref):
-    attn = plain_dot(low_ref[...], weight_ref[...], ROWS_COLS) + dense_ref[...]
-    mlp = mlp_ref[...] + down_ref[...]
+    attn = plain_dot(low_ref[...], weight_ref[...], ROWS_COLS) + as_row(dense_ref)
+    mlp = mlp_ref[...] + as_row(down_ref)
     out_ref[...] = (x_ref[...].astype(WIDE) + attn + mlp).astype(NARROW)
 
 
-def layer_output(low, dense_weight, inputs, mlp_out, row, biases):
+def layer_output(low, dense_weight, inputs, mlp_out, *biases):
     tokens = inputs.shape[0]
     each = 512
     by_column = pl.BlockSpec((tokens, each), lambda i: (0, i))
@@ -673,12 +675,12 @@
             by_column,
             by_column,
         ]
-        + [pl.BlockSpec((1, each), lambda i, k=k: (0, k * (D // each) + i)) for k in biases],
+        + [pl.BlockSpec((each,), lambda i: (i,))] * len(biases),
         out_specs=by_column,
         out_shape=jax.ShapeDtypeStruct((tokens, D), NARROW),
         cost_estimate=lasting(3.0),
         name="layer_output",
-    )(low, dense_weight, inputs, mlp_out, row, row)
+    )(low, dense_weight, inputs, mlp_out, *biases)
 
 
 def norm_back_kernel(
@@ -710,7 +712,7 @@
     @pl.when(step == pl.num_programs(0) - 1)
     def _():
         size = 64
-        gain_attn, gain_mlp = gain1[...], gain2[...]
+        gain_attn, gain_mlp = as_row(gain1), as_row(gain2)
         totals = [jnp.zeros((1, D), WIDE)] * 5
         for k in range(grad_ref.shape[0] // size):
             rows = pl.ds(k * size, size)
@@ -729,7 +731,7 @@
         sums_ref[5:8, :] = jnp.zeros((3, D), WIDE)
 
 
-def norm_back(qkv_grad, qkv_weight, mlp_norm_grad, unit, rate, cot, row, gains):
+def norm_back(qkv_grad, qkv_weight, mlp_norm_grad, unit, rate, cot, *gains):
     tokens = cot.shape[0]
     each = 512
     total = whole_spec((tokens, D))
@@ -744,7 +746,7 @@
             whole_spec(rate.shape),
             total,
         ]
-        + [pl.BlockSpec((1, D), lambda i, k=k: (0, k)) for k in gains],
+        + [whole_spec((D,))] * len(gains),
         out_specs=[total, whole_spec((8, D)), pl.BlockSpec((1, each), lambda i: (0, i))],
         out_shape=[
             jax.ShapeDtypeStruct((tokens, D), WIDE),
@@ -752,8 +754,9 @@
             jax.ShapeDtypeStruct((1, 3 * D), WIDE),
         ],
         cost_estimate=lasting(9.0),
+        compiler_params=pltpu.CompilerParams(vmem_limit_bytes=67108864),
         name="norm_back",
-    )(qkv_grad, qkv_weight, mlp_norm_grad, unit, rate, cot, row, row)
+    )(qkv_grad, qkv_weight, mlp_norm_grad, unit, rate, cot, *gains)
 
 
 def dct_matrix():
@@ -1126,6 +1129,7 @@
             jax.ShapeDtypeStruct((seqs, pairs, HEAD + 8, PAIR), WIDE),
         ],
         cost_estimate=lasting(14.0),
+        compiler_params=pltpu.CompilerParams(vmem_limit_bytes=67108864),
         name="attention_local",
     )(lengths, first, attn_in, weight, bias, tables, mix, wrow)
 
@@ -1152,6 +1156,7 @@
         out_shape=[jax.ShapeDtypeStruct((tokens, D), NARROW), narrow, wide, wide]
         + [jax.ShapeDtypeStruct((seqs, pairs, HEAD + 8, PAIR), WIDE)],
         cost_estimate=lasting(20.0),
+        compiler_params=pltpu.CompilerParams(vmem_limit_bytes=67108864),
         name="attention_middle",
     )(lengths, first, cot, dense_weight, *rest)
 
@@ -1169,6 +1174,7 @@
             jax.ShapeDtypeStruct((tokens, 3 * D), WIDE),
         ],
         cost_estimate=lasting(10.0),
+        compiler_params=pltpu.CompilerParams(vmem_limit_bytes=67108864),
         name="attention_last",
     )(lengths, first, *rest)
 
@@ -1220,13 +1226,10 @@
     inputs_flat = inputs.reshape(tokens, D)
     cot = cotangent.reshape(tokens, D)
     cot_in = swap(cot.astype(WIDE), 0)
-    row = jnp.concatenate(
-        [qkv_bias, up_bias, ln1_gain, ln1_bias, ln2_gain, ln2_bias, dense_bias, down_bias]
-    ).astype(WIDE)[None, :]
     attn_in, mlp_in, unit, rate = line.step(
-        lambda *a: two_norms(*a, (LN1_GAIN, LN1_BIAS, LN2_GAIN, LN2_BIAS)), inputs_flat, row
-    )
-    act, slope, act_own, act_send = line.step(mlp_up, mlp_in, up_weight, row, me)
+        two_norms, inputs_flat, ln1_gain, ln1_bias, ln2_gain, ln2_bias
+    )
+    act, slope, act_own, act_send = line.step(mlp_up, mlp_in, up_weight, up_bias, me)
     act_in = swap(act_send, 0)
     norm_own, norm_send = line.step(lambda *a: pick(a[:2], a[2]), attn_in, mlp_in, me)
     subs = act_own.shape[0]
@@ -1256,7 +1259,7 @@
         first,
         attn_in,
         qkv_weight,
-        row,
+        qkv_bias.astype(WIDE)[None, :],
         tables,
         mix,
         wrow,
@@ -1298,12 +1301,13 @@
     low_in = swap(low_send, 0)
     reduction.step()
     output = line.step(
-        lambda *a: layer_output(*a, (DENSE, DOWN)),
+        layer_output,
         attn_low,
         dense_weight,
         inputs_flat,
         mlp_out,
-        row,
+        dense_bias,
+        down_bias,
     )
     for _ in range(hops - 1):
         passed = line.step(pass_on, carry_back, arrived_back, lengths_here, first)
@@ -1328,14 +1332,15 @@
     reduction.step()
     qkv_in = line.send(qkv_send, lambda a: swap(a, 0))
     input_grad, sums, qkv_sums = line.step(
-        lambda *a: norm_back(*a, (LN1_GAIN, LN2_GAIN)),
+        norm_back,
         qkv_grad,
         qkv_weight,
         mlp_norm_grad,
         unit,
         rate,
         cot,
-        row,
+        ln1_gain,
+        ln2_gain,
     )
 
     def qkv_group(part):

time: 401 us -> 391 us (0.975)
  waiting for transfers between devices: 102 us -> 83.4 us
  local copies, waits for them, and re-layouts: 27 us -> 17.8 us
  other arithmetic: 5.31 us -> 14.3 us
  starting transfers between devices: 78.3 us -> 86.2 us
    unnamed x88 -> x11, local copies, waits for them, and re-layouts: 22.3 us -> 5.71 us
    ppermute x27, waiting for transfers between devices: 51.1 us -> 41.3 us  [swap(): lax.ppermute(value, 'batch', [(i, i ^ 1 << bit) for i in range(count)])]
    ppermute x10, waiting for transfers between devices: 29.8 us -> 20.9 us  [step(): self.end = lax.ppermute(got.pop(0), 'seq', [(0, 1), (1, 0), (2, 3), (3, 2)])]
    add x5, other arithmetic: 0.04 us -> 5.87 us  [take(): self.held = self.line.step(lambda a, b: a + b, self.held, self.moving)]
    ppermute x8, starting transfers between devices: 7.46 us -> 12.5 us  [step(): self.middle = lax.ppermute(self.inner[r - 2], 'seq', [(1, 2), (2, 1)])]
  transfers between devices with their start and end apart: 52 -> 52, of which waited for: 23 -> 21; matrix products, arithmetic and copies ran while one was open for 2% -> 8% of each run, Pallas kernels for 31% -> 32%
where the time goes in v4:
time: 391 us; the launch traced here: 388 us
  Pallas kernels  185 us (47%)
  starting transfers between devices  86.2 us (22%)
  waiting for transfers between devices  83.4 us (21%)
  local copies, waits for them, and re-layouts  17.8 us (5%)
  other arithmetic  14.3 us (4%)
    pallas_call x20, Pallas kernels, step(): out = function(*self.wait(*values))  88.9 us
    ppermute x27, waiting for transfers between devices, swap(): lax.ppermute(value, 'batch', [(i, i ^ 1 << bit) for i in range(count)])  41.3 us
    ppermute x10, starting transfers between devices, step(): self.end = lax.ppermute(got.pop(0), 'seq', [(0, 1), (1, 0), (2, 3), (3, 2)])  30.3 us
    ppermute x27, starting transfers between devices, swap(): lax.ppermute(value, 'batch', [(i, i ^ 1 << bit) for i in range(count)])  25.7 us
    ppermute x10, waiting for transfers between devices, step(): self.end = lax.ppermute(got.pop(0), 'seq', [(0, 1), (1, 0), (2, 3), (3, 2)])  20.9 us
    pallas_call x1, Pallas kernels, attention_middle(): pl.pallas_call(partial(middle_kernel, seqs), grid=(pairs,), in_specs=[SME...  19.9 us
    pallas_call x1, Pallas kernels, mlp_back(): pl.pallas_call(back_kernel, grid=(FF // each,), in_specs=[total, pl.Block...  15.9 us
    ppermute x4, waiting for transfers between devices, shift_rows(): lax.ppermute(value, axis, [(i, i + by) for i in range(count) if 0 <= i +...  14.9 us
  transfers between devices with their start and end apart: 52, of which 21 were waited for; matrix products, arithmetic and copies ran while one was open for 8% of the time, Pallas kernels for 32%

profile of v4, /device:TPU:0, one launch (start us, length us, event | category | flops | bytes accessed | tf_op | source)
XLA Modules:
  0.0 388.4 jit_solution(9567345754790531751)
XLA Ops:
  0.7 3.9 %two_norms.1 = (bf16[256,1024]{1,0:T(8,128)(2,1)}, bf16[256,1024]{1,0:T(8,128)(2,1)}, f32[256,1024]{1,0:T(8,128)}, f32[256,128]{1,0:T(8,128)}) custom-call(bf16[256,1024]{1,0:T(8,128)(2,1)} %bitcast.47, bf16[1024]{0:T(1024)(128)(2,1)} %gain1.2, bf16[1024]{0:T(1024)(128)(2,1)} %bias1.1, bf16[1024]{0:T(1024)(128)(2,1)} %gain2.2, bf16[1024]{0:T(1024)(128)(2,1)} %bias2.1), custom_call_target="tpu_custom_call" | custom-call | flops 4600000000 | tf_op jit(solution)/shard_map/two_norms/pallas_call | solution.py:517
  4.6 11.1 %mlp_up.1 = (bf16[256,4096]{1,0:T(8,128)(2,1)}, f32[256,4096]{1,0:T(8,128)}, bf16[4,256,512]{2,1,0:T(8,128)(2,1)}, f32[4,256,512]{2,1,0:T(8,128)}) custom-call(s32[1]{0:T(128)} %bitcast.2.me_ref, bf16[256,1024]{1,0:T(8,128)(2,1)} %get-tuple-element.480.x_ref.refs_1_, bf16[1024,4096]{1,0:T(8,128)(2,1)} %up_ref, bf16[4096]{0:T(1024)(128)(2,1)} %bias_ref), custom_call_target="tpu_custom_call" | custom-call | flops 12650000384 | tf_op jit(solution)/shard_map/mlp_up/pallas_call | solution.py:565
  16.4 2.6 pick_columns.2
  22.4 6.0 %piece_products.8 = (f32[512,512]{1,0:T(8,128)}, f32[512,512]{1,0:T(8,128)}, f32[512,512]{1,0:T(8,128)}, f32[512,512]{1,0:T(8,128)}) custom-call(bf16[4,256,512]{2,1,0:T(8,128)(2,1)} %get-tuple-element.521.refs_0_.refs_4_.refs_8_.refs_12_, f32[4,256,512]{2,1,0:T(8,128)} %collective-permute-done.refs_1_.refs_5_.refs_9_.refs_13_, bf16[256,1024]{1,0:T(8,128)(2,1)} %bitcast.27, ...), custom_call_target="tpu_custom_call" | custom-call | flops 5750000128 | tf_op jit(solution)/shard_map/piece_products/pallas_call | solution.py:85
  28.3 2.9 collective-permute-start.2
  32.8 15.9 %mlp_back.1 = (bf16[256,4096]{1,0:T(8,128)(2,1)}, f32[256,4096]{1,0:T(8,128)}, f32[1,4096]{1,0:T(1,128)}, f32[256,1024]{1,0:T(8,128)}, f32[256,1024]{1,0:T(8,128)}) custom-call(bf16[256,1024]{1,0:T(8,128)(2,1)} %bitcast.31, bf16[4096,1024]{1,0:T(8,128)(2,1)} %down_ref, bf16[1024,4096]{1,0:T(8,128)(2,1)} %up_ref, ...), custom_call_target="tpu_custom_call" | custom-call | flops 18400000000 | tf_op jit(solution)/shard_map/mlp_back/pallas_call | solution.py:629
  48.7 5.9 %piece_products.9 = (f32[768,512]{1,0:T(8,128)}, f32[768,512]{1,0:T(8,128)}, f32[512,512]{1,0:T(8,128)}, f32[512,512]{1,0:T(8,128)}) custom-call(bf16[4,256,512]{2,1,0:T(8,128)(2,1)} %get-tuple-element.521.refs_0_.refs_4_.refs_8_.refs_12_, f32[4,256,512]{2,1,0:T(8,128)} %collective-permute-done.refs_1_.refs_5_.refs_9_.refs_13_, bf16[256,1024]{1,0:T(8,128)(2,1)} %bitcast.32, ...), custom_call_target="tpu_custom_call" | custom-call | flops 5750000128 | tf_op jit(solution)/shard_map/piece_products/pallas_call | solution.py:85
  56.5 3.2 reduce_round.12
  68.1 13.9 %attention_local.1 = (bf16[8,256,128]{2,1,0:T(8,128)(2,1)}, bf16[8,256,128]{2,1,0:T(8,128)(2,1)}, bf16[8,256,128]{2,1,0:T(8,128)(2,1)}, f32[8,256,128]{2,1,0:T(8...) custom-call(s32[2,3]{1,0:T(2,128)} %lengths_ref.4, ...), custom_call_target="tpu_custom_call" | custom-call | flops 16099999744 | tf_op jit(solution)/shard_map/attention_local/pallas_call | solution.py:1112
  82.1 4.3 %collective-permute-start.4 = (f32[2,8,72,128]{3,2,1,0:T(8,128)}, f32[2,8,72,128]{3,2,1,0:T(8,128)}, u32[]{:S(2)}, u32[]{:S(2)}) collective-permute-start(f32[2,8,72,128]{3,2,1,0:T(8,128)} %get-tuple-element.577.own_ref), channel_id=1, source_target_pairs={{0,8},{8,16},{16,24},{1,9},{9,17},{17,25},{2,10},{10,18},{18,26},{... | collective-permute-start | bytes 1769480 | tf_op jit(solution)/shard_map/ppermute | solution.py:47
  86.4 5.7 %piece_products.10 = (f32[768,512]{1,0:T(8,128)}, f32[768,512]{1,0:T(8,128)}, f32[512,512]{1,0:T(8,128)}, f32[512,512]{1,0:T(8,128)}) custom-call(bf16[2,256,512]{2,1,0:T(8,128)(2,1)} %get-tuple-element.809.refs_0_.refs_4_.refs_8_.refs_12_, f32[2,256,512]{2,1,0:T(8,128)} %collective-permute-done.5.refs_1_.refs_5_.refs_9_.refs_13_, ...), custom_call_target="tpu_custom_call" | custom-call | flops 5750000128 | tf_op jit(solution)/shard_map/piece_products/pallas_call | solution.py:85
  92.1 6.5 %collective-permute-done.4.arrived_ref = f32[2,8,72,128]{3,2,1,0:T(8,128)} collective-permute-done((f32[2,8,72,128]{3,2,1,0:T(8,128)}, f32[2,8,72,128]{3,2,1,0:T(8,128)}, u32[]{:S(2)}, u32[]{:S(2)}) %collective-permute-start.4) | collective-permute-done | bytes 589856 | tf_op jit(solution)/shard_map/ppermute | solution.py:47
  100.6 5.2 %collective-permute-start.7 = (f32[2,8,72,128]{3,2,1,0:T(8,128)}, f32[2,8,72,128]{3,2,1,0:T(8,128)}, u32[]{:S(2)}, u32[]{:S(2)}) collective-permute-start(f32[2,8,72,128]{3,2,1,0:T(8,128)} %pass_carry.2), channel_id=1, source_target_pairs={{0,8},{8,16},{16,24},{1,9},{9,17},{17,25},{2,10},{10,18},{18,26},{... | collective-permute-start | bytes 1769480 | tf_op jit(solution)/shard_map/ppermute | solution.py:47
  105.8 4.3 %reduce_round.13 = (f32[768,512]{1,0:T(8,128)}, f32[768,512]{1,0:T(8,128)}, f32[256,512]{1,0:T(8,128)}, f32[256,512]{1,0:T(8,128)}, f32[512,512]{1,0:T(8,128)}, /*index=5*/f32[512,512]{1,0:T(8,128)}) custom-call(s32[1]{0:T(128)} %bitcast.refs_0_, f32[768,512]{1,0:T(8,128)} %collective-permute-done.8.refs_1_, ...), custom_call_target="tpu_custom_call", output_to_operand_aliasing={{0}: (7, {}), {1}: (8, {})} | custom-call | flops 5750000128 | tf_op jit(solution)/shard_map/reduce_round/pallas_call | solution.py:85
  113.0 5.7 %piece_products.11 = (f32[768,512]{1,0:T(8,128)}, f32[768,512]{1,0:T(8,128)}, f32[512,512]{1,0:T(8,128)}, f32[512,512]{1,0:T(8,128)}) custom-call(bf16[2,256,512]{2,1,0:T(8,128)(2,1)} %get-tuple-element.809.refs_0_.refs_4_.refs_8_.refs_12_, f32[2,256,512]{2,1,0:T(8,128)} %collective-permute-done.5.refs_1_.refs_5_.refs_9_.refs_13_, ...), custom_call_target="tpu_custom_call" | custom-call | flops 5750000128 | tf_op jit(solution)/shard_map/piece_products/pallas_call | solution.py:85
  119.1 19.9 %attention_middle.1 = (bf16[256,1024]{1,0:T(8,128)(2,1)}, bf16[8,256,128]{2,1,0:T(8,128)(2,1)}, f32[8,256,128]{2,1,0:T(8,128)}, f32[8,256,128]{2,1,0:T(8,128)}, f32[2,8,72,128]{3,2,1,0:T(8,128)}) custom-call(s32[2,3]{1,0:T(2,128)} %lengths_ref.4, s32[2]{0:T(128)} %pad_add_fusion.first_ref, bf16[256,1024]{1,0:T(8,128)(2,1)} %bitcast.36, ...), custom_call_target="tpu_custom_call" | custom-call | flops 23000000512 | tf_op jit(solution)/shard_map/attention_middle/pallas_call | solution.py:1142
  142.6 3.1 collective-permute-done.10.refs_1_
  146.9 5.2 %reduce_round.14 = (f32[768,512]{1,0:T(8,128)}, f32[768,512]{1,0:T(8,128)}, f32[256,512]{1,0:T(8,128)}, f32[256,512]{1,0:T(8,128)}, f32[512,512]{1,0:T(8,128)}, /*index=5*/f32[512,512]{1,0:T(8,128)}, f32[512,512]{1,0:T(8,128)}) custom-call(s32[1]{0:T(128)} %bitcast.refs_0_, ...), custom_call_target="tpu_custom_call", output_to_operand_aliasing={{0}: (9, {}), {1}: (10, {})} | custom-call | flops 5750000128 | tf_op jit(solution)/shard_map/reduce_round/pallas_call | solution.py:85
  152.1 3.4 layer_output.1
  160.0 2.6 collective-permute-start.18
  164.3 3.7 piece_products.12
  168.0 8.1 %collective-permute-done.14.carry_ref = f32[2,8,72,128]{3,2,1,0:T(8,128)} collective-permute-done((f32[2,8,72,128]{3,2,1,0:T(8,128)}, f32[2,8,72,128]{3,2,1,0:T(8,128)}, u32[]{:S(2)}, u32[]{:S(2)}) %collective-permute-start.14) | collective-permute-done | bytes 589856 | tf_op jit(solution)/shard_map/ppermute | solution.py:47
  176.0 9.6 %attention_last.1 = (bf16[256,3072]{1,0:T(8,128)(2,1)}, f32[256,3072]{1,0:T(8,128)}) custom-call(s32[2,3]{1,0:T(2,128)} %lengths_ref.4, s32[2]{0:T(128)} %pad_add_fusion.first_ref, bf16[8,256,128]{2,1,0:T(8,128)(2,1)} %get-tuple-element.680.gradq_ref, f32[8,256,128]{2,1,0:T(8,128)} %get-tuple-element.681.gradk_ref, ...), custom_call_target="tpu_custom_call" | custom-call | flops 11500000256 | tf_op jit(solution)/shard_map/attention_last/pallas_call | solution.py:1167
  185.7 9.5 %collective-permute-done.18.refs_8_ = f32[512,512]{1,0:T(8,128)} collective-permute-done((f32[512,512]{1,0:T(8,128)}, f32[512,512]{1,0:T(8,128)}, u32[]{:S(2)}, u32[]{:S(2)}) %collective-permute-start.18) | collective-permute-done | bytes 1048608 | tf_op jit(solution)/shard_map/ppermute | solution.py:435
  195.2 6.7 %reduce_round.15 = (f32[512,512]{1,0:T(8,128)}, f32[512,512]{1,0:T(8,128)}, f32[256,512]{1,0:T(8,128)}, f32[256,512]{1,0:T(8,128)}, f32[512,512]{1,0:T(8,128)}, ...) custom-call(s32[1]{0:T(128)} %bitcast.refs_0_, ...), custom_call_target="tpu_custom_call", output_to_operand_aliasing={{0}: (11, {}), {1}: (12, {})} | custom-call | flops 5750000128 | tf_op jit(solution)/shard_map/reduce_round/pallas_call | solution.py:85
  210.1 9.2 %norm_back.1 = (f32[256,1024]{1,0:T(8,128)}, f32[8,1024]{1,0:T(8,128)}, f32[1,3072]{1,0:T(1,128)}) custom-call(bf16[256,3072]{1,0:T(8,128)(2,1)} %get-tuple-element.811.qkv_ref.refs_2_.refs_6_, bf16[1024,3072]{1,0:T(8,128)(2,1)} %weight_ref.3, f32[256,1024]{1,0:T(8,128)} %get-tuple-element.719.mlp_ref, f32[256,1024]{1,0:T(8,128)} %get-tuple-element.720.unit_ref, ...), custom_call_target="tpu_custom_call" | custom-call | flops 10350000128 | tf_op jit(solution)/shard_map/norm_back/pallas_call | solution.py:738
  226.7 3.8 piece_products.13
  232.0 6.1 %reduce_round.16 = (f32[384,512]{1,0:T(8,128)}, f32[384,512]{1,0:T(8,128)}, f32[128,512]{1,0:T(8,128)}, f32[128,512]{1,0:T(8,128)}, f32[512,512]{1,0:T(8,128)}, ...) custom-call(s32[1]{0:T(128)} %bitcast.refs_0_, ...), custom_call_target="tpu_custom_call", output_to_operand_aliasing={{0}: (12, {}), {1}: (13, {})} | custom-call | flops 5750000128 | tf_op jit(solution)/shard_map/reduce_round/pallas_call | solution.py:85
  238.1 4.8 %collective-permute-start.28 = (f32[512,512]{1,0:T(8,128)}, f32[512,512]{1,0:T(8,128)}, u32[]{:S(2)}, u32[]{:S(2)}) collective-permute-start(f32[512,512]{1,0:T(8,128)} %get-tuple-element.783), channel_id=1, source_target_pairs={{0,8},{8,0},{16,24},{24,16},{1,9},{9,1},{17,25},{25,17},{2,10},{10... | collective-permute-start | bytes 3145736 | tf_op jit(solution)/shard_map/ppermute | solution.py:435
  250.2 3.8 piece_products.14
  255.3 9.1 %collective-permute-done.26.refs_1_ = f32[384,512]{1,0:T(8,128)} collective-permute-done((f32[384,512]{1,0:T(8,128)}, f32[384,512]{1,0:T(8,128)}, u32[]{:S(2)}, u32[]{:S(2)}) %collective-permute-start.26) | collective-permute-done | bytes 786464 | tf_op jit(solution)/shard_map/ppermute | solution.py:54
  265.6 5.3 %reduce_round.17 = (f32[384,512]{1,0:T(8,128)}, f32[384,512]{1,0:T(8,128)}, f32[128,512]{1,0:T(8,128)}, f32[128,512]{1,0:T(8,128)}, f32[256,512]{1,0:T(8,128)}, ...) custom-call(s32[1]{0:T(128)} %bitcast.refs_0_, ...), custom_call_target="tpu_custom_call", output_to_operand_aliasing={{0}: (12, {}), {1}: (13, {}), {8}: (14, {})} | custom-call | flops 5750000128 | tf_op jit(solution)/shard_map/reduce_round/pallas_call | solution.py:85
  271.0 3.7 collective-permute-start.33
  281.3 3.7 piece_products.15
  285.0 9.2 %collective-permute-done.30 = f32[2,1536]{1,0:T(2,128)} collective-permute-done((f32[2,1536]{1,0:T(2,128)}, f32[2,1536]{1,0:T(2,128)}, u32[]{:S(2)}, u32[]{:S(2)}) %collective-permute-start.30) | collective-permute-done | bytes 12320 | tf_op jit(solution)/shard_map/ppermute | solution.py:54
  296.4 5.0 %reduce_round.18 = (f32[384,512]{1,0:T(8,128)}, f32[384,512]{1,0:T(8,128)}, f32[128,512]{1,0:T(8,128)}, f32[128,512]{1,0:T(8,128)}, f32[256,512]{1,0:T(8,128)}, ...) custom-call(s32[1]{0:T(128)} %bitcast.refs_0_, ...), custom_call_target="tpu_custom_call", output_to_operand_aliasing={{0}: (12, {}), {1}: (13, {})} | custom-call | flops 5750000128 | tf_op jit(solution)/shard_map/reduce_round/pallas_call | solution.py:85
  301.4 3.7 collective-permute-start.38
  311.0 12.1 %collective-permute-done.35 = f32[1,1536]{1,0:T(1,128)S(1)} collective-permute-done((f32[1,1536]{1,0:T(1,128)S(1)}, f32[1,1536]{1,0:T(1,128)S(1)}, u32[]{:S(2)}, u32[]{:S(2)}) %collective-permute-start.35) | collective-permute-done | bytes 6176 | tf_op jit(solution)/shard_map/ppermute | solution.py:54
  325.9 4.5 %reduce_round.19 = (f32[128,512]{1,0:T(8,128)}, f32[128,512]{1,0:T(8,128)}, f32[128,512]{1,0:T(8,128)}, f32[128,512]{1,0:T(8,128)}, f32[256,512]{1,0:T(8,128)}, ...) custom-call(s32[1]{0:T(128)} %bitcast.refs_0_, ...), custom_call_target="tpu_custom_call", output_to_operand_aliasing={{8}: (12, {})} | custom-call | flops 5750000128 | tf_op jit(solution)/shard_map/reduce_round/pallas_call | solution.py:85
  336.7 3.5 collective-permute-start.40
  343.0 3.2 reduce_round.20
  352.0 4.1 %collective-permute-done.46.refs_2_ = f32[256,512]{1,0:T(8,128)} collective-permute-done((f32[256,512]{1,0:T(8,128)}, f32[256,512]{1,0:T(8,128)}, u32[]{:S(2)}, u32[]{:S(2)}) %collective-permute-start.46) | collective-permute-done | bytes 524320 | tf_op jit(solution)/shard_map/ppermute | solution.py:435
  356.1 2.7 reduce_round.21
  358.8 5.2 %collective-permute-start.49 = (f32[256,512]{1,0:T(8,128)}, f32[256,512]{1,0:T(8,128)}, u32[]{:S(2)}, u32[]{:S(2)}) collective-permute-start(f32[256,512]{1,0:T(8,128)} %get-tuple-element.901), channel_id=1, source_target_pairs={{0,8},{8,0},{16,24},{24,16},{1,9},{9,1},{17,25},{25,17},{2,10},{10... | collective-permute-start | bytes 1572872 | tf_op jit(solution)/shard_map/ppermute | solution.py:435
  366.8 4.7 %collective-permute-done.48 = f32[1,1536]{1,0:T(1,128)S(1)} collective-permute-done((f32[1,1536]{1,0:T(1,128)}, f32[1,1536]{1,0:T(1,128)S(1)}, u32[]{:S(2)}, u32[]{:S(2)}) %collective-permute-start.48) | collective-permute-done | bytes 6176 | tf_op jit(solution)/shard_map/ppermute | solution.py:116
  372.1 2.5 reduce_round.22
  374.6 3.3 collective-permute-start.51
  381.6 3.7 collective-permute-done.51.refs_1_
  (136 shorter events, 101.6 us)
Async XLA Ops:
  15.6 6.7 %collective-permute-start = (f32[4,256,512]{2,1,0:T(8,128)}, f32[4,256,512]{2,1,0:T(8,128)}, u32[]{:S(2)}, u32[]{:S(2)}) collective-permute-start(f32[4,256,512]{2,1,0:T(8,128)} %get-tuple-element.476), channel_id=1, source_target_pairs={{0,1},{1,0},{2,3},{3,2},{4,5},{5,4},{6,7},{7,6},{8,9},{9,8},{10,11... | collective-permute-start | bytes 6291464 | tf_op jit(solution)/shard_map/ppermute | solution.py:54
  28.3 26.7 %collective-permute-start.2 = (f32[512,512]{1,0:T(8,128)}, f32[512,512]{1,0:T(8,128)}, u32[]{:S(2)}, u32[]{:S(2)}) collective-permute-start(f32[512,512]{1,0:T(8,128)} %get-tuple-element.498), channel_id=1, source_target_pairs={{0,2},{1,3},{2,0},{3,1},{4,6},{5,7},{6,4},{7,5},{8,10},{9,11},{10,... | collective-permute-start | bytes 3145736 | tf_op jit(solution)/shard_map/ppermute | solution.py:54
  31.3 25.2 %collective-permute-start.3 = (f32[512,512]{1,0:T(8,128)}, f32[512,512]{1,0:T(8,128)}, u32[]{:S(2)}, u32[]{:S(2)}) collective-permute-start(f32[512,512]{1,0:T(8,128)} %get-tuple-element.499), channel_id=1, source_target_pairs={{0,4},{1,5},{2,6},{3,7},{4,0},{5,1},{6,2},{7,3},{8,12},{9,13},{10,... | collective-permute-start | bytes 3145736 | tf_op jit(solution)/shard_map/ppermute | solution.py:54
  59.8 26.7 %collective-permute-start.6 = (f32[256,4096]{1,0:T(8,128)}, f32[256,4096]{1,0:T(8,128)}, u32[]{:S(2)}, u32[]{:S(2)}) collective-permute-start(f32[256,4096]{1,0:T(8,128)} %get-tuple-element.557), channel_id=1, source_target_pairs={{0,1},{1,0},{2,3},{3,2},{4,5},{5,4},{6,7},{7,6},{8,9},{9,8},{10,11... | collective-permute-start | bytes 12582920 | tf_op jit(solution)/shard_map/ppermute | solution.py:54
  64.3 41.6 %collective-permute-start.8 = (f32[768,512]{1,0:T(8,128)}, f32[768,512]{1,0:T(8,128)}, u32[]{:S(2)}, u32[]{:S(2)}) collective-permute-start(f32[768,512]{1,0:T(8,128)} %get-tuple-element.534), channel_id=1, source_target_pairs={{0,2},{1,3},{2,0},{3,1},{4,6},{5,7},{6,4},{7,5},{8,10},{9,11},{10,... | collective-permute-start | bytes 4718600 | tf_op jit(solution)/shard_map/ppermute | solution.py:54
  64.6 21.8 %collective-permute-start.5 = (f32[2,256,512]{2,1,0:T(8,128)}, f32[2,256,512]{2,1,0:T(8,128)}, u32[]{:S(2)}, u32[]{:S(2)}) collective-permute-start(f32[2,256,512]{2,1,0:T(8,128)} %get-tuple-element.555), channel_id=1, source_target_pairs={{0,1},{1,0},{2,3},{3,2},{4,5},{5,4},{6,7},{7,6},{8,9},{9,8},{10,11... | collective-permute-start | bytes 3145736 | tf_op jit(solution)/shard_map/ppermute | solution.py:54
  66.4 39.4 %collective-permute-start.9 = (f32[768,512]{1,0:T(8,128)}, f32[768,512]{1,0:T(8,128)}, u32[]{:S(2)}, u32[]{:S(2)}) collective-permute-start(f32[768,512]{1,0:T(8,128)} %get-tuple-element.579), channel_id=1, source_target_pairs={{0,4},{1,5},{2,6},{3,7},{4,0},{5,1},{6,2},{7,3},{8,12},{9,13},{10,... | collective-permute-start | bytes 4718600 | tf_op jit(solution)/shard_map/ppermute | solution.py:54
  82.1 16.6 %collective-permute-start.4 = (f32[2,8,72,128]{3,2,1,0:T(8,128)}, f32[2,8,72,128]{3,2,1,0:T(8,128)}, u32[]{:S(2)}, u32[]{:S(2)}) collective-permute-start(f32[2,8,72,128]{3,2,1,0:T(8,128)} %get-tuple-element.577.own_ref), channel_id=1, source_target_pairs={{0,8},{8,16},{16,24},{1,9},{9,17},{17,25},{2,10},{10,18},{18,26},{... | collective-permute-start | bytes 1769480 | tf_op jit(solution)/shard_map/ppermute | solution.py:47
  100.6 18.5 %collective-permute-start.7 = (f32[2,8,72,128]{3,2,1,0:T(8,128)}, f32[2,8,72,128]{3,2,1,0:T(8,128)}, u32[]{:S(2)}, u32[]{:S(2)}) collective-permute-start(f32[2,8,72,128]{3,2,1,0:T(8,128)} %pass_carry.2), channel_id=1, source_target_pairs={{0,8},{8,16},{16,24},{1,9},{9,17},{17,25},{2,10},{10,18},{18,26},{... | collective-permute-start | bytes 1769480 | tf_op jit(solution)/shard_map/ppermute | solution.py:47
  110.1 35.6 %collective-permute-start.10 = (f32[768,512]{1,0:T(8,128)}, f32[768,512]{1,0:T(8,128)}, u32[]{:S(2)}, u32[]{:S(2)}) collective-permute-start(f32[768,512]{1,0:T(8,128)} %get-tuple-element.594), channel_id=1, source_target_pairs={{0,2},{1,3},{2,0},{3,1},{4,6},{5,7},{6,4},{7,5},{8,10},{9,11},{10,... | collective-permute-start | bytes 4718600 | tf_op jit(solution)/shard_map/ppermute | solution.py:54
  111.7 35.2 %collective-permute-start.11 = (f32[768,512]{1,0:T(8,128)}, f32[768,512]{1,0:T(8,128)}, u32[]{:S(2)}, u32[]{:S(2)}) collective-permute-start(f32[768,512]{1,0:T(8,128)} %get-tuple-element.629), channel_id=1, source_target_pairs={{0,4},{1,5},{2,6},{3,7},{4,0},{5,1},{6,2},{7,3},{8,12},{9,13},{10,... | collective-permute-start | bytes 4718600 | tf_op jit(solution)/shard_map/ppermute | solution.py:54
  112.2 30.4 %collective-permute-start.12 = (f32[512,512]{1,0:T(8,128)}, f32[512,512]{1,0:T(8,128)}, u32[]{:S(2)}, u32[]{:S(2)}) collective-permute-start(f32[512,512]{1,0:T(8,128)} %get-tuple-element.635), channel_id=1, source_target_pairs={{0,8},{8,0},{16,24},{24,16},{1,9},{9,1},{17,25},{25,17},{2,10},{10... | collective-permute-start | bytes 3145736 | tf_op jit(solution)/shard_map/ppermute | solution.py:435
  139.0 16.5 %collective-permute-start.13 = (f32[2,8,72,128]{3,2,1,0:T(8,128)}, f32[2,8,72,128]{3,2,1,0:T(8,128)}, u32[]{:S(2)}, u32[]{:S(2)}) collective-permute-start(f32[2,8,72,128]{3,2,1,0:T(8,128)} %get-tuple-element.666.own_ref), channel_id=1, source_target_pairs={{8,0},{16,8},{24,16},{9,1},{17,9},{25,17},{10,2},{18,10},{26,18},{... | collective-permute-start | bytes 1769480 | tf_op jit(solution)/shard_map/ppermute | solution.py:47
  142.6 16.9 %collective-permute-start.15 = (f32[1,256,512]{2,1,0:T(8,128)}, f32[1,256,512]{2,1,0:T(8,128)}, u32[]{:S(2)}, u32[]{:S(2)}) collective-permute-start(f32[1,256,512]{2,1,0:T(8,128)} %get-tuple-element.668), channel_id=1, source_target_pairs={{0,1},{1,0},{2,3},{3,2},{4,5},{5,4},{6,7},{7,6},{8,9},{9,8},{10,11... | collective-permute-start | bytes 1572872 | tf_op jit(solution)/shard_map/ppermute | solution.py:54
  157.6 18.5 %collective-permute-start.14 = (f32[2,8,72,128]{3,2,1,0:T(8,128)}, f32[2,8,72,128]{3,2,1,0:T(8,128)}, u32[]{:S(2)}, u32[]{:S(2)}) collective-permute-start(f32[2,8,72,128]{3,2,1,0:T(8,128)} %pass_carry.3), channel_id=1, source_target_pairs={{8,0},{16,8},{24,16},{9,1},{17,9},{25,17},{10,2},{18,10},{26,18},{... | collective-permute-start | bytes 1769480 | tf_op jit(solution)/shard_map/ppermute | solution.py:47
  158.9 36.3 %collective-permute-start.16 = (f32[768,512]{1,0:T(8,128)}, f32[768,512]{1,0:T(8,128)}, u32[]{:S(2)}, u32[]{:S(2)}) collective-permute-start(f32[768,512]{1,0:T(8,128)} %get-tuple-element.651), channel_id=1, source_target_pairs={{0,2},{1,3},{2,0},{3,1},{4,6},{5,7},{6,4},{7,5},{8,10},{9,11},{10,... | collective-permute-start | bytes 4718600 | tf_op jit(solution)/shard_map/ppermute | solution.py:54
  159.5 35.7 %collective-permute-start.17 = (f32[768,512]{1,0:T(8,128)}, f32[768,512]{1,0:T(8,128)}, u32[]{:S(2)}, u32[]{:S(2)}) collective-permute-start(f32[768,512]{1,0:T(8,128)} %get-tuple-element.694), channel_id=1, source_target_pairs={{0,4},{1,5},{2,6},{3,7},{4,0},{5,1},{6,2},{7,3},{8,12},{9,13},{10,... | collective-permute-start | bytes 4718600 | tf_op jit(solution)/shard_map/ppermute | solution.py:54
  160.0 35.2 %collective-permute-start.18 = (f32[512,512]{1,0:T(8,128)}, f32[512,512]{1,0:T(8,128)}, u32[]{:S(2)}, u32[]{:S(2)}) collective-permute-start(f32[512,512]{1,0:T(8,128)} %get-tuple-element.700), channel_id=1, source_target_pairs={{0,8},{8,0},{16,24},{24,16},{1,9},{9,1},{17,25},{25,17},{2,10},{10... | collective-permute-start | bytes 3145736 | tf_op jit(solution)/shard_map/ppermute | solution.py:435
  162.6 32.5 %collective-permute-start.19 = (f32[512,512]{1,0:T(8,128)}, f32[512,512]{1,0:T(8,128)}, u32[]{:S(2)}, u32[]{:S(2)}) collective-permute-start(f32[512,512]{1,0:T(8,128)} %get-tuple-element.712.refs_9_), channel_id=1, source_target_pairs={{8,16},{16,8},{9,17},{17,9},{10,18},{18,10},{11,19},{19,11},{12,20... | collective-permute-start | bytes 3145736 | tf_op jit(solution)/shard_map/ppermute | solution.py:438
  201.9 24.8 %collective-permute-start.24 = (f32[256,3072]{1,0:T(8,128)}, f32[256,3072]{1,0:T(8,128)}, u32[]{:S(2)}, u32[]{:S(2)}) collective-permute-start(f32[256,3072]{1,0:T(8,128)} %get-tuple-element.739), channel_id=1, source_target_pairs={{0,1},{1,0},{2,3},{3,2},{4,5},{5,4},{6,7},{7,6},{8,9},{9,8},{10,11... | collective-permute-start | bytes 9437192 | tf_op jit(solution)/shard_map/ppermute | solution.py:54
  204.5 25.9 %collective-permute-start.20 = (f32[512,512]{1,0:T(8,128)}, f32[512,512]{1,0:T(8,128)}, u32[]{:S(2)}, u32[]{:S(2)}) collective-permute-start(f32[512,512]{1,0:T(8,128)} %get-tuple-element.716), channel_id=1, source_target_pairs={{0,2},{1,3},{2,0},{3,1},{4,6},{5,7},{6,4},{7,5},{8,10},{9,11},{10,... | collective-permute-start | bytes 3145736 | tf_op jit(solution)/shard_map/ppermute | solution.py:54
  206.0 25.6 %collective-permute-start.21 = (f32[512,512]{1,0:T(8,128)}, f32[512,512]{1,0:T(8,128)}, u32[]{:S(2)}, u32[]{:S(2)}) collective-permute-start(f32[512,512]{1,0:T(8,128)} %get-tuple-element.729), channel_id=1, source_target_pairs={{0,4},{1,5},{2,6},{3,7},{4,0},{5,1},{6,2},{7,3},{8,12},{9,13},{10,... | collective-permute-start | bytes 3145736 | tf_op jit(solution)/shard_map/ppermute | solution.py:54
  206.5 25.5 %collective-permute-start.22 = (f32[512,512]{1,0:T(8,128)}, f32[512,512]{1,0:T(8,128)}, u32[]{:S(2)}, u32[]{:S(2)}) collective-permute-start(f32[512,512]{1,0:T(8,128)} %get-tuple-element.735), channel_id=1, source_target_pairs={{0,8},{8,0},{16,24},{24,16},{1,9},{9,1},{17,25},{25,17},{2,10},{10... | collective-permute-start | bytes 3145736 | tf_op jit(solution)/shard_map/ppermute | solution.py:435
  208.5 23.5 %collective-permute-start.23 = (f32[512,512]{1,0:T(8,128)}, f32[512,512]{1,0:T(8,128)}, u32[]{:S(2)}, u32[]{:S(2)}) collective-permute-start(f32[512,512]{1,0:T(8,128)} %get-tuple-element.759.refs_9_), channel_id=1, source_target_pairs={{8,16},{16,8},{9,17},{17,9},{10,18},{18,10},{11,19},{19,11},{12,20... | collective-permute-start | bytes 3145736 | tf_op jit(solution)/shard_map/ppermute | solution.py:438
  238.1 27.5 %collective-permute-start.28 = (f32[512,512]{1,0:T(8,128)}, f32[512,512]{1,0:T(8,128)}, u32[]{:S(2)}, u32[]{:S(2)}) collective-permute-start(f32[512,512]{1,0:T(8,128)} %get-tuple-element.783), channel_id=1, source_target_pairs={{0,8},{8,0},{16,24},{24,16},{1,9},{9,1},{17,25},{25,17},{2,10},{10... | collective-permute-start | bytes 3145736 | tf_op jit(solution)/shard_map/ppermute | solution.py:435
  242.9 22.7 %collective-permute-start.29 = (f32[512,512]{1,0:T(8,128)}, f32[512,512]{1,0:T(8,128)}, u32[]{:S(2)}, u32[]{:S(2)}) collective-permute-start(f32[512,512]{1,0:T(8,128)} %get-tuple-element.797.refs_9_), channel_id=1, source_target_pairs={{8,16},{16,8},{9,17},{17,9},{10,18},{18,10},{11,19},{19,11},{12,20... | collective-permute-start | bytes 3145736 | tf_op jit(solution)/shard_map/ppermute | solution.py:438
  245.8 18.6 %collective-permute-start.26 = (f32[384,512]{1,0:T(8,128)}, f32[384,512]{1,0:T(8,128)}, u32[]{:S(2)}, u32[]{:S(2)}) collective-permute-start(f32[384,512]{1,0:T(8,128)} %get-tuple-element.764), channel_id=1, source_target_pairs={{0,2},{1,3},{2,0},{3,1},{4,6},{5,7},{6,4},{7,5},{8,10},{9,11},{10,... | collective-permute-start | bytes 2359304 | tf_op jit(solution)/shard_map/ppermute | solution.py:54
  247.4 18.2 %collective-permute-start.27 = (f32[384,512]{1,0:T(8,128)}, f32[384,512]{1,0:T(8,128)}, u32[]{:S(2)}, u32[]{:S(2)}) collective-permute-start(f32[384,512]{1,0:T(8,128)} %get-tuple-element.777), channel_id=1, source_target_pairs={{0,4},{1,5},{2,6},{3,7},{4,0},{5,1},{6,2},{7,3},{8,12},{9,13},{10,... | collective-permute-start | bytes 2359304 | tf_op jit(solution)/shard_map/ppermute | solution.py:54
  271.0 25.4 %collective-permute-start.33 = (f32[512,512]{1,0:T(8,128)}, f32[512,512]{1,0:T(8,128)}, u32[]{:S(2)}, u32[]{:S(2)}) collective-permute-start(f32[512,512]{1,0:T(8,128)} %get-tuple-element.822), channel_id=1, source_target_pairs={{0,8},{8,0},{16,24},{24,16},{1,9},{9,1},{17,25},{25,17},{2,10},{10... | collective-permute-start | bytes 3145736 | tf_op jit(solution)/shard_map/ppermute | solution.py:435
  274.7 21.7 %collective-permute-start.34 = (f32[512,512]{1,0:T(8,128)}, f32[512,512]{1,0:T(8,128)}, u32[]{:S(2)}, u32[]{:S(2)}) collective-permute-start(f32[512,512]{1,0:T(8,128)} %get-tuple-element.835.refs_9_), channel_id=1, source_target_pairs={{8,16},{16,8},{9,17},{17,9},{10,18},{18,10},{11,19},{19,11},{12,20... | collective-permute-start | bytes 3145736 | tf_op jit(solution)/shard_map/ppermute | solution.py:438
  276.3 19.2 %collective-permute-start.31 = (f32[384,512]{1,0:T(8,128)}, f32[384,512]{1,0:T(8,128)}, u32[]{:S(2)}, u32[]{:S(2)}) collective-permute-start(f32[384,512]{1,0:T(8,128)} %get-tuple-element.803), channel_id=1, source_target_pairs={{0,2},{1,3},{2,0},{3,1},{4,6},{5,7},{6,4},{7,5},{8,10},{9,11},{10,... | collective-permute-start | bytes 2359304 | tf_op jit(solution)/shard_map/ppermute | solution.py:54
  277.8 17.7 %collective-permute-start.32 = (f32[384,512]{1,0:T(8,128)}, f32[384,512]{1,0:T(8,128)}, u32[]{:S(2)}, u32[]{:S(2)}) collective-permute-start(f32[384,512]{1,0:T(8,128)} %get-tuple-element.816), channel_id=1, source_target_pairs={{0,4},{1,5},{2,6},{3,7},{4,0},{5,1},{6,2},{7,3},{8,12},{9,13},{10,... | collective-permute-start | bytes 2359304 | tf_op jit(solution)/shard_map/ppermute | solution.py:54
  280.8 13.4 %collective-permute-start.30 = (f32[2,1536]{1,0:T(2,128)}, f32[2,1536]{1,0:T(2,128)}, u32[]{:S(2)}, u32[]{:S(2)}) collective-permute-start(f32[2,1536]{1,0:T(2,128)} %get-tuple-element.804), channel_id=1, source_target_pairs={{0,2},{1,3},{2,0},{3,1},{4,6},{5,7},{6,4},{7,5},{8,10},{9,11},{10,... | collective-permute-start | bytes 36872 | tf_op jit(solution)/shard_map/ppermute | solution.py:54
  301.4 24.5 %collective-permute-start.38 = (f32[512,512]{1,0:T(8,128)}, f32[512,512]{1,0:T(8,128)}, u32[]{:S(2)}, u32[]{:S(2)}) collective-permute-start(f32[512,512]{1,0:T(8,128)} %get-tuple-element.850), channel_id=1, source_target_pairs={{0,8},{8,0},{16,24},{24,16},{1,9},{9,1},{17,25},{25,17},{2,10},{10... | collective-permute-start | bytes 3145736 | tf_op jit(solution)/shard_map/ppermute | solution.py:435
  305.1 18.5 %collective-permute-start.36 = (f32[384,512]{1,0:T(8,128)}, f32[384,512]{1,0:T(8,128)}, u32[]{:S(2)}, u32[]{:S(2)}) collective-permute-start(f32[384,512]{1,0:T(8,128)} %get-tuple-element.840), channel_id=1, source_target_pairs={{0,2},{1,3},{2,0},{3,1},{4,6},{5,7},{6,4},{7,5},{8,10},{9,11},{10,... | collective-permute-start | bytes 2359304 | tf_op jit(solution)/shard_map/ppermute | solution.py:54
  306.6 17.1 %collective-permute-start.37 = (f32[384,512]{1,0:T(8,128)}, f32[384,512]{1,0:T(8,128)}, u32[]{:S(2)}, u32[]{:S(2)}) collective-permute-start(f32[384,512]{1,0:T(8,128)} %get-tuple-element.844), channel_id=1, source_target_pairs={{0,4},{1,5},{2,6},{3,7},{4,0},{5,1},{6,2},{7,3},{8,12},{9,13},{10,... | collective-permute-start | bytes 2359304 | tf_op jit(solution)/shard_map/ppermute | solution.py:54
  308.1 15.5 %collective-permute-start.39 = (f32[256,512]{1,0:T(8,128)}, f32[256,512]{1,0:T(8,128)}, u32[]{:S(2)}, u32[]{:S(2)}) collective-permute-start(f32[256,512]{1,0:T(8,128)} %get-tuple-element.863.refs_9_), channel_id=1, source_target_pairs={{8,16},{16,8},{9,17},{17,9},{10,18},{18,10},{11,19},{19,11},{12,20... | collective-permute-start | bytes 1572872 | tf_op jit(solution)/shard_map/ppermute | solution.py:438
  310.4 12.6 %collective-permute-start.35 = (f32[1,1536]{1,0:T(1,128)S(1)}, f32[1,1536]{1,0:T(1,128)S(1)}, u32[]{:S(2)}, u32[]{:S(2)}) collective-permute-start(f32[1,1536]{1,0:T(1,128)S(1)} %get-tuple-element.841), channel_id=1, source_target_pairs={{0,4},{1,5},{2,6},{3,7},{4,0},{5,1},{6,2},{7,3},{8,12},{9,13},{10,... | collective-permute-start | bytes 18440 | tf_op jit(solution)/shard_map/ppermute | solution.py:54
  330.4 12.6 %collective-permute-start.43 = (f32[256,512]{1,0:T(8,128)}, f32[256,512]{1,0:T(8,128)}, u32[]{:S(2)}, u32[]{:S(2)}) collective-permute-start(f32[256,512]{1,0:T(8,128)} %get-tuple-element.875), channel_id=1, source_target_pairs={{0,8},{8,0},{16,24},{24,16},{1,9},{9,1},{17,25},{25,17},{2,10},{10... | collective-permute-start | bytes 1572872 | tf_op jit(solution)/shard_map/ppermute | solution.py:435
  332.2 10.8 %collective-permute-start.44 = (f32[256,512]{1,0:T(8,128)}, f32[256,512]{1,0:T(8,128)}, u32[]{:S(2)}, u32[]{:S(2)}) collective-permute-start(f32[256,512]{1,0:T(8,128)} %get-tuple-element.885.refs_7_), channel_id=1, source_target_pairs={{8,16},{16,8},{9,17},{17,9},{10,18},{18,10},{11,19},{19,11},{12,20... | collective-permute-start | bytes 1572872 | tf_op jit(solution)/shard_map/ppermute | solution.py:438
  333.7 9.3 %collective-permute-start.41 = (f32[128,512]{1,0:T(8,128)}, f32[128,512]{1,0:T(8,128)}, u32[]{:S(2)}, u32[]{:S(2)}) collective-permute-start(f32[128,512]{1,0:T(8,128)} %get-tuple-element.867), channel_id=1, source_target_pairs={{0,2},{1,3},{2,0},{3,1},{4,6},{5,7},{6,4},{7,5},{8,10},{9,11},{10,... | collective-permute-start | bytes 786440 | tf_op jit(solution)/shard_map/ppermute | solution.py:54
  335.1 7.8 %collective-permute-start.42 = (f32[128,512]{1,0:T(8,128)}, f32[128,512]{1,0:T(8,128)}, u32[]{:S(2)}, u32[]{:S(2)}) collective-permute-start(f32[128,512]{1,0:T(8,128)} %get-tuple-element.871), channel_id=1, source_target_pairs={{0,4},{1,5},{2,6},{3,7},{4,0},{5,1},{6,2},{7,3},{8,12},{9,13},{10,... | collective-permute-start | bytes 786440 | tf_op jit(solution)/shard_map/ppermute | solution.py:54
  346.2 9.8 %collective-permute-start.46 = (f32[256,512]{1,0:T(8,128)}, f32[256,512]{1,0:T(8,128)}, u32[]{:S(2)}, u32[]{:S(2)}) collective-permute-start(f32[256,512]{1,0:T(8,128)} %get-tuple-element.892), channel_id=1, source_target_pairs={{0,8},{8,0},{16,24},{24,16},{1,9},{9,1},{17,25},{25,17},{2,10},{10... | collective-permute-start | bytes 1572872 | tf_op jit(solution)/shard_map/ppermute | solution.py:435
  348.6 7.5 %collective-permute-start.47 = (f32[256,512]{1,0:T(8,128)}, f32[256,512]{1,0:T(8,128)}, u32[]{:S(2)}, u32[]{:S(2)}) collective-permute-start(f32[256,512]{1,0:T(8,128)} %get-tuple-element.898.refs_3_), channel_id=1, source_target_pairs={{8,16},{16,8},{9,17},{17,9},{10,18},{18,10},{11,19},{19,11},{12,20... | collective-permute-start | bytes 1572872 | tf_op jit(solution)/shard_map/ppermute | solution.py:438
  358.8 13.3 %collective-permute-start.49 = (f32[256,512]{1,0:T(8,128)}, f32[256,512]{1,0:T(8,128)}, u32[]{:S(2)}, u32[]{:S(2)}) collective-permute-start(f32[256,512]{1,0:T(8,128)} %get-tuple-element.901), channel_id=1, source_target_pairs={{0,8},{8,0},{16,24},{24,16},{1,9},{9,1},{17,25},{25,17},{2,10},{10... | collective-permute-start | bytes 1572872 | tf_op jit(solution)/shard_map/ppermute | solution.py:435
  364.0 8.1 %collective-permute-start.50 = (f32[256,512]{1,0:T(8,128)}, f32[256,512]{1,0:T(8,128)}, u32[]{:S(2)}, u32[]{:S(2)}) collective-permute-start(f32[256,512]{1,0:T(8,128)} %get-tuple-element.910.refs_2_), channel_id=1, source_target_pairs={{8,16},{16,8},{9,17},{17,9},{10,18},{18,10},{11,19},{19,11},{12,20... | collective-permute-start | bytes 1572872 | tf_op jit(solution)/shard_map/ppermute | solution.py:438
  365.5 6.0 %collective-permute-start.48 = (f32[1,1536]{1,0:T(1,128)}, f32[1,1536]{1,0:T(1,128)S(1)}, u32[]{:S(2)}, u32[]{:S(2)}) collective-permute-start(f32[1,1536]{1,0:T(1,128)} %add.98), channel_id=1, source_target_pairs={{8,0},{16,24},{9,1},{17,25},{10,2},{18,26},{11,3},{19,27},{12,4},{... | collective-permute-start | bytes 18440 | tf_op jit(solution)/shard_map/ppermute | solution.py:116
  374.6 10.8 %collective-permute-start.51 = (f32[256,512]{1,0:T(8,128)}, f32[256,512]{1,0:T(8,128)}, u32[]{:S(2)}, u32[]{:S(2)}) collective-permute-start(f32[256,512]{1,0:T(8,128)} %get-tuple-element.914), channel_id=1, source_target_pairs={{0,8},{8,0},{16,24},{24,16},{1,9},{9,1},{17,25},{25,17},{2,10},{10... | collective-permute-start | bytes 1572872 | tf_op jit(solution)/shard_map/ppermute | solution.py:435
  (6 other events, 27.1 us)

commit v5 on v4

--- a/solution.py
+++ b/solution.py
@@ -49,6 +49,15 @@
     )
 
 
+def in_hbm(*values):
+    return [
+        pltpu.with_memory_space_constraint(v, pltpu.HBM)
+        if v.size * v.dtype.itemsize >= 1 << 16
+        else v
+        for v in values
+    ]
+
+
 def swap(value, bit):
     count = lax.axis_size("batch")
     return lax.ppermute(value, "batch", [(i, i ^ (1 << bit)) for i in range(count)])
@@ -87,16 +96,46 @@
         return out
 
 
+def pack_kernel(order, sizes, me_ref, *refs):
+    ins, out_ref = refs[:-1], refs[-1]
+    at, sizes = 0, list(sizes)
+    for ref in ins:
+        count = ref.shape[0]
+        size, sizes = sizes[0], sizes[count:]
+        for k, relative in enumerate(order):
+            start = pl.multiple_of((relative ^ me_ref[0]) * size, BLOCK)
+            block = ref[:, pl.ds(start, size)]
+            for j in range(count):
+                out_ref[k : k + 1, at + j * size : at + (j + 1) * size] = block[j : j + 1]
+        at += count * size
+
+
+def pack(order, sizes, me, *blocks):
+    return pl.pallas_call(
+        partial(pack_kernel, order, sizes),
+        in_specs=[pl.BlockSpec(memory_space=pltpu.SMEM)]
+        + [pl.BlockSpec(memory_space=pltpu.VMEM)] * len(blocks),
+        out_specs=pl.BlockSpec(memory_space=pltpu.VMEM),
+        out_shape=jax.ShapeDtypeStruct((len(order), sum(sizes)), WIDE),
+        name="pack_vectors",
+    )(me, *blocks)
+
+
 class Vectors:
-    def __init__(self, line, vectors):
+    def __init__(self, line, blocks):
         owners = lax.axis_size("batch")
-        me = lax.axis_index("batch")
+        me = lax.axis_index("batch").astype(jnp.int32)
         self.line = line
+        vectors = [v for block in blocks for v in block]
         self.sizes = [v.shape[0] // owners for v in vectors]
-        pieces = jnp.concatenate([v.reshape(owners, -1) for v in vectors], axis=1)
         bits = list(range(owners.bit_length() - 1))
-        rows = [lax.dynamic_slice_in_dim(pieces, r ^ me, 1, 0) for r in owner_order(bits)]
-        self.held = jnp.concatenate(rows)
+        order = owner_order(bits)
+        if any(size % BLOCK for size in self.sizes):
+            pieces = jnp.concatenate([v.reshape(owners, -1) for v in vectors], axis=1)
+            rows = [lax.dynamic_slice_in_dim(pieces, r ^ me, 1, 0) for r in order]
+            self.held = jnp.concatenate(rows)
+        else:
+            self.held = line.step(lambda *a: pack(order, self.sizes, *a), me[None], *blocks)
         count = lax.axis_size("seq")
         self.steps = [("swap", bit, 0) for bit in bits]
         self.steps += line_rounds(count) if count % 2 == 0 else []
@@ -195,7 +234,7 @@
             done = Reduction(self.line, left, right, self.bits)
             self.pieces.append((target, row, starts, wide, done))
 
-    def step(self):
+    def step(self, *arrived):
         pass
 
     def finished(self):
@@ -256,7 +295,6 @@
     (new_sums,) = take(second, 1)
     (to_end,) = take(second or middle, 1)
     (new_inner,) = take(inward, 1)
-    (new_whole,) = take(middle, 1)
     (final,) = take(outward, 1)
     for p in range(first):
         low = pl.ds(2 * p * BLOCK, BLOCK)
@@ -276,7 +314,6 @@
                 new_sums[out, :] = ends
             if p < middle:
                 inners = inner[out, :] + from_middle[out, :]
-                new_whole[out, :] = inners
             if ends is None:
                 to_end[out, :] = inners
             elif inners is None:
@@ -287,7 +324,7 @@
         new_inner[...] = sums[...] + from_end[: 2 * inward * BLOCK, :]
     for k, (row, column) in enumerate(places):
         rows = pl.ds(k * BLOCK, BLOCK)
-        wide = whole.shape[1]
+        wide = final.shape[1] // (1 + max(column for _, column in places))
         total = jnp.where(edge, from_end[rows, :], whole[rows, :])
         final[row * BLOCK : (row + 1) * BLOCK, column * wide : (column + 1) * wide] = total
 
@@ -299,13 +336,18 @@
         self.line, self.edge, self.counts = line, edge, counts
         self.made = self.at = 0
         self.buffers, self.moving, self.hold, self.kept = {}, {}, {}, {}
-        self.sums, self.inner, self.whole, self.targets = {}, {}, {}, []
+        self.sums, self.inner, self.whole, self.targets = {}, {}, None, []
         self.outputs = {}
         self.end = self.middle = None
         self.wide = COLUMNS // self.PARTS
 
     def count(self, group):
         return self.counts[group] if 0 <= group < len(self.counts) else 0
+
+    def place(self, value, local, sent):
+        if local:
+            return pltpu.with_memory_space_constraint(value, pltpu.HBM)
+        return pltpu.with_memory_space_constraint(value, pltpu.HBM) if sent else value
 
     def rows_spec(self, rows, at=0):
         return pl.BlockSpec((rows, self.wide), lambda i: (at, i))
@@ -320,12 +362,12 @@
         args, specs = [], []
         for left, left_in, block, right, right_in, (_, column) in pieces:
             for value in (left, left_in):
-                args.append(value)
+                args += in_hbm(value) if value is left else [value]
                 specs.append(
                     pl.BlockSpec((1, *value.shape[1:]), lambda i, block=block: (block, 0, 0))
                 )
             for value in (right, right_in):
-                args.append(value)
+                args += in_hbm(value) if value is right else [value]
                 specs.append(
                     pl.BlockSpec(
                         (value.shape[0], self.wide),
@@ -339,10 +381,10 @@
             grid=(self.PARTS,),
             in_specs=specs,
             out_specs=[self.rows_spec(rows)] * 4,
-            out_shape=[jax.ShapeDtypeStruct((total, COLUMNS), WIDE)] * 2
-            + [jax.ShapeDtypeStruct((rows, COLUMNS), WIDE)] * 2,
+            out_shape=[pltpu.HBM((total, COLUMNS), WIDE)] * 2
+            + [pltpu.HBM((rows, COLUMNS), WIDE)] * 2,
             cost_estimate=lasting(5.0),
-        compiler_params=pltpu.CompilerParams(vmem_limit_bytes=67108864),
+        compiler_params=pltpu.CompilerParams(vmem_limit_bytes=25165824),
         name="piece_products",
         )
         to_x, to_y, hold_a, hold_b = self.line.step(call, *args)
@@ -352,7 +394,7 @@
         else:
             self.moving[r] = (swap(to_x, 1), swap(to_y, 2))
 
-    def step(self):
+    def step(self, *arrived):
         r = self.at
         self.at += 1
         counts = [self.count(r - back) for back in (0, 1, 2, 3, 4)]
@@ -360,8 +402,8 @@
         aliases = {}
         args, specs = [self.edge], [pl.BlockSpec(memory_space=pltpu.SMEM)]
 
-        def add(value):
-            args.append(value)
+        def add(value, local=False, sent=False):
+            args.append(self.place(value, local, sent))
             specs.append(self.rows_spec(value.shape[0]))
 
         if first or second:
@@ -369,23 +411,24 @@
                 add(value)
         if first:
             for value in self.hold.pop(r):
-                add(value)
+                add(value, local=True)
         if second:
             for value in self.kept.pop(r - 1):
-                add(value)
+                add(value, local=True)
         if inward:
-            add(self.sums.pop(r - 2))
+            add(self.sums.pop(r - 2), local=True)
         if inward or outward:
             add(self.end)
         if middle:
-            add(self.inner.pop(r - 3))
+            add(self.inner.pop(r - 3), sent=True)
             add(self.middle)
         if outward:
-            add(self.whole.pop(r - 4))
+            add(self.whole, sent=True)
         outs, out_specs = [], []
 
-        def out(rows, at=0, of=None):
-            outs.append(jax.ShapeDtypeStruct((of or rows, COLUMNS), WIDE))
+        def out(rows, at=0, of=None, sent=False):
+            kind = pltpu.HBM if sent else pltpu.HBM
+            outs.append(kind((of or rows, COLUMNS), WIDE))
             out_specs.append(self.rows_spec(rows, at))
 
         ahead = self.count(r + 1)
@@ -395,16 +438,15 @@
             specs += [pl.BlockSpec(memory_space=pl.ANY)] * 2
         if first:
             for _ in range(2):
-                out(first * BLOCK, 2 * ahead // first, (2 * ahead + first) * BLOCK)
+                out(first * BLOCK, 2 * ahead // first, (2 * ahead + first) * BLOCK, sent=True)
             out(first * BLOCK)
             out(first * BLOCK)
         if second:
             out(2 * second * BLOCK)
         if second or middle:
-            out(2 * max(second, middle) * BLOCK)
-        for count in (inward, middle):
-            if count:
-                out(2 * count * BLOCK)
+            out(2 * max(second, middle) * BLOCK, sent=True)
+        if inward:
+            out(2 * inward * BLOCK, sent=True)
         places = ()
         if outward:
             (name, shape, at, size), places = self.targets[r - 4]
@@ -412,17 +454,19 @@
                 aliases[len(args)] = len(outs)
                 args.append(self.outputs[name])
                 specs.append(pl.BlockSpec(memory_space=pl.ANY))
-            outs.append(jax.ShapeDtypeStruct(shape, WIDE))
+            outs.append(pltpu.HBM(shape, WIDE))
             out_specs.append(pl.BlockSpec(size, lambda i: (at[0], at[1] + i)))
+        args += arrived
+        specs += [pl.BlockSpec(memory_space=pl.ANY)] * len(arrived)
         call = pl.pallas_call(
-            partial(round_kernel, counts, places, len(aliases)),
+            partial(round_kernel, counts, places, len(aliases) + len(arrived)),
             grid=(self.PARTS,),
             in_specs=specs,
             out_specs=out_specs,
             out_shape=outs,
             input_output_aliases=aliases,
             cost_estimate=lasting(5.0),
-            compiler_params=pltpu.CompilerParams(vmem_limit_bytes=67108864),
+            compiler_params=pltpu.CompilerParams(vmem_limit_bytes=25165824),
             name="reduce_round",
         )
         got = list(self.line.step(call, *args))
@@ -431,13 +475,13 @@
             self.kept[r] = (got.pop(0), got.pop(0))
         if second:
             self.sums[r - 1] = got.pop(0)
+        self.whole = None
         if second or middle:
-            self.end = lax.ppermute(got.pop(0), "seq", [(0, 1), (1, 0), (2, 3), (3, 2)])
+            self.whole = got.pop(0)
+            self.end = lax.ppermute(self.whole, "seq", [(0, 1), (1, 0), (2, 3), (3, 2)])
         if inward:
             self.inner[r - 2] = got.pop(0)
             self.middle = lax.ppermute(self.inner[r - 2], "seq", [(1, 2), (2, 1)])
-        if middle:
-            self.whole[r - 3] = got.pop(0)
         if outward:
             self.outputs[name] = got.pop(0)
 
@@ -489,10 +533,10 @@
         in_specs=[pl.BlockSpec(memory_space=pltpu.SMEM)]
         + [pl.BlockSpec(memory_space=pltpu.VMEM)] * len(arrays),
         out_specs=[pl.BlockSpec(memory_space=pltpu.VMEM)] * 2,
-        out_shape=[jax.ShapeDtypeStruct(shape, NARROW), jax.ShapeDtypeStruct(shape, WIDE)],
+        out_shape=[pltpu.HBM(shape, NARROW), pltpu.HBM(shape, WIDE)],
         cost_estimate=lasting(2.0),
         name="pick_columns",
-    )(me, *arrays)
+    )(*in_hbm(me, *arrays))
 
 
 def as_row(ref):
@@ -520,14 +564,14 @@
         in_specs=[by_rows] + [whole_spec((D,))] * len(gains),
         out_specs=[by_rows, by_rows, by_rows, pl.BlockSpec((rows, 128), lambda i: (i, 0))],
         out_shape=[
-            jax.ShapeDtypeStruct((tokens, D), NARROW),
-            jax.ShapeDtypeStruct((tokens, D), NARROW),
-            jax.ShapeDtypeStruct((tokens, D), WIDE),
-            jax.ShapeDtypeStruct((tokens, 128), WIDE),
+            pltpu.HBM((tokens, D), NARROW),
+            pltpu.HBM((tokens, D), NARROW),
+            pltpu.HBM((tokens, D), WIDE),
+            pltpu.HBM((tokens, 128), WIDE),
         ],
         cost_estimate=lasting(4.0),
         name="two_norms",
-    )(inputs, *gains)
+    )(*in_hbm(inputs, *gains))
 
 
 def up_kernel(
@@ -586,14 +630,14 @@
             ],
         ),
         out_shape=[
-            jax.ShapeDtypeStruct((tokens, FF), NARROW),
-            jax.ShapeDtypeStruct((tokens, FF), WIDE),
-            jax.ShapeDtypeStruct((subs, tokens, half * BLOCK), NARROW),
-            jax.ShapeDtypeStruct((subs, tokens, half * BLOCK), WIDE),
+            pltpu.HBM((tokens, FF), NARROW),
+            pltpu.HBM((tokens, FF), WIDE),
+            pltpu.HBM((subs, tokens, half * BLOCK), NARROW),
+            pltpu.HBM((subs, tokens, half * BLOCK), WIDE),
         ],
         cost_estimate=lasting(11.0),
         name="mlp_up",
-    )(me, mlp_in, up_weight, up_bias)
+    )(*in_hbm(me, mlp_in, up_weight, up_bias))
 
 
 def back_kernel(
@@ -644,16 +688,16 @@
             total,
         ],
         out_shape=[
-            jax.ShapeDtypeStruct((tokens, FF), NARROW),
-            jax.ShapeDtypeStruct((tokens, FF), WIDE),
-            jax.ShapeDtypeStruct((1, FF), WIDE),
-            jax.ShapeDtypeStruct((tokens, D), WIDE),
-            jax.ShapeDtypeStruct((tokens, D), WIDE),
+            pltpu.HBM((tokens, FF), NARROW),
+            pltpu.HBM((tokens, FF), WIDE),
+            pltpu.HBM((1, FF), WIDE),
+            pltpu.HBM((tokens, D), WIDE),
+            pltpu.HBM((tokens, D), WIDE),
         ],
         cost_estimate=lasting(16.0),
-        compiler_params=pltpu.CompilerParams(vmem_limit_bytes=67108864),
+        compiler_params=pltpu.CompilerParams(vmem_limit_bytes=25165824),
         name="mlp_back",
-    )(cot, down_weight, up_weight, act, slope)
+    )(*in_hbm(cot, down_weight, up_weight, act, slope))
 
 
 def output_kernel(low_ref, weight_ref, x_ref, mlp_ref, dense_ref, down_ref, out_ref):
@@ -677,10 +721,10 @@
         ]
         + [pl.BlockSpec((each,), lambda i: (i,))] * len(biases),
         out_specs=by_column,
-        out_shape=jax.ShapeDtypeStruct((tokens, D), NARROW),
+        out_shape=pltpu.HBM((tokens, D), NARROW),
         cost_estimate=lasting(3.0),
         name="layer_output",
-    )(low, dense_weight, inputs, mlp_out, *biases)
+    )(*in_hbm(low, dense_weight, inputs, mlp_out, *biases))
 
 
 def norm_back_kernel(
@@ -728,7 +772,6 @@
                 totals[i] = totals[i] + jnp.sum(value, axis=0, keepdims=True)
         for i, value in enumerate(totals):
             sums_ref[i : i + 1, :] = value
-        sums_ref[5:8, :] = jnp.zeros((3, D), WIDE)
 
 
 def norm_back(qkv_grad, qkv_weight, mlp_norm_grad, unit, rate, cot, *gains):
@@ -747,16 +790,16 @@
             total,
         ]
         + [whole_spec((D,))] * len(gains),
-        out_specs=[total, whole_spec((8, D)), pl.BlockSpec((1, each), lambda i: (0, i))],
+        out_specs=[total, whole_spec((5, D)), pl.BlockSpec((1, each), lambda i: (0, i))],
         out_shape=[
-            jax.ShapeDtypeStruct((tokens, D), WIDE),
-            jax.ShapeDtypeStruct((8, D), WIDE),
-            jax.ShapeDtypeStruct((1, 3 * D), WIDE),
+            pltpu.HBM((tokens, D), WIDE),
+            pltpu.HBM((5, D), WIDE),
+            pltpu.HBM((1, 3 * D), WIDE),
         ],
         cost_estimate=lasting(9.0),
-        compiler_params=pltpu.CompilerParams(vmem_limit_bytes=67108864),
+        compiler_params=pltpu.CompilerParams(vmem_limit_bytes=25165824),
         name="norm_back",
-    )(qkv_grad, qkv_weight, mlp_norm_grad, unit, rate, cot, *gains)
+    )(*in_hbm(qkv_grad, qkv_weight, mlp_norm_grad, unit, rate, cot, *gains))
 
 
 def dct_matrix():
@@ -766,25 +809,21 @@
     return np.where(rows == 0, cosines * np.sqrt(0.5), cosines).astype(np.float32)
 
 
-def attention_tables(positions, points, weights):
+def attention_tables(place, context, count):
     half_rot = ROT // 2
-    lane = jnp.arange(PAIR) % HEAD
-    freq = ROTARY_BASE ** (-2.0 * (lane % half_rot).astype(WIDE) / ROT)
-    angles = positions.astype(WIDE)[:, None] * freq[None, :]
-    sin = jnp.sin(angles)
-    tables = jnp.stack(
+    lane = np.arange(PAIR) % HEAD
+    freq = ROTARY_BASE ** (-2.0 * (lane % half_rot) / ROT)
+    angles = np.arange(count * context)[:, None] * freq[None, :]
+    tables = np.stack(
         [
-            jnp.where(lane < ROT, jnp.cos(angles), 1.0),
-            jnp.where(lane < half_rot, -sin, 0.0),
-            jnp.where((lane >= half_rot) & (lane < ROT), sin, 0.0),
+            np.where(lane < ROT, np.cos(angles), 1.0),
+            np.where(lane < half_rot, -np.sin(angles), 0.0),
+            np.where((lane >= half_rot) & (lane < ROT), np.sin(angles), 0.0),
         ]
     )
-    mix = HEAD ** (-0.25) * jnp.einsum(
-        "kn,km->nm", dct_matrix(), points, precision=lax.Precision.HIGHEST
-    )
-    side = jnp.arange(PAIR) // HEAD
-    mix = jnp.where(side[:, None] == side[None, :], jnp.tile(mix, (2, 2)), 0.0)
-    return tables, mix, jnp.tile(weights, 2)[None, :]
+    return lax.dynamic_slice_in_dim(
+        jnp.asarray(tables.astype(np.float32)), place * context, context, 1
+    )
 
 
 def lane_is_low(shape):
@@ -888,8 +927,9 @@
     weight_ref,
     bias_ref,
     tables_ref,
-    mix_ref,
-    wrow_ref,
+    dct_ref,
+    points_ref,
+    weights_ref,
     fq_ref,
     fk_ref,
     val_ref,
@@ -901,10 +941,25 @@
     den_ref,
     score_ref,
     carry_ref,
+    mix_ref,
 ):
     context = tables_ref.shape[1]
     first = first_ref[0]
-    mix, wrow = mix_ref[...], wrow_ref[...]
+
+    @pl.when(pl.program_id(0) == 0)
+    def _():
+        both = lax.dot_general(
+            dct_ref[...],
+            points_ref[...],
+            (COLS_COLS, ((), ())),
+            precision=lax.Precision.HIGHEST,
+            preferred_element_type=WIDE,
+        )
+        mix_ref[...] = spread_pair(jnp.concatenate([both, both], axis=1) * HEAD ** (-0.25))
+
+    mix = mix_ref[...]
+    weights = as_row(weights_ref)
+    wrow = jnp.concatenate([weights, weights], axis=1)
     tables = all_rows(tables_ref, seqs)
     low = lane_is_low((seqs * context, PAIR))
     block = plain_dot(attn_ref[...], weight_ref[...], ROWS_COLS) + bias_ref[...]
@@ -1083,10 +1138,10 @@
         grid=(2,),
         in_specs=[SMEM_SPEC, SMEM_SPEC, spec, spec],
         out_specs=spec,
-        out_shape=jax.ShapeDtypeStruct(own.shape, WIDE),
+        out_shape=pltpu.HBM(own.shape, WIDE),
         cost_estimate=lasting(2.0),
         name="pass_carry",
-    )(lengths, first, own, arrived)
+    )(*in_hbm(lengths, first, own, arrived))
 
 
 def pair_spec(rows):
@@ -1095,7 +1150,7 @@
 
 def pair_shapes(tokens):
     shape = (HEADS // 2, tokens, PAIR)
-    return jax.ShapeDtypeStruct(shape, NARROW), jax.ShapeDtypeStruct(shape, WIDE)
+    return pltpu.HBM(shape, NARROW), pltpu.HBM(shape, WIDE)
 
 
 def attention_specs(seqs, context):
@@ -1104,7 +1159,7 @@
     return carry, scores, [whole_spec((3, context, PAIR)), whole_spec((PAIR, PAIR))]
 
 
-def attention_local(lengths, first, attn_in, weight, bias, tables, mix, wrow):
+def attention_local(lengths, first, attn_in, weight, bias, tables, points, weights):
     seqs, context, tokens = lengths.shape[0], tables.shape[1], attn_in.shape[0]
     pairs = HEADS // 2
     carry, scores, shared = attention_specs(seqs, context)
@@ -1118,20 +1173,23 @@
             whole_spec((tokens, D)),
             pl.BlockSpec((D, 3 * PAIR), lambda i: (0, i)),
             pl.BlockSpec((1, 3 * PAIR), lambda i: (0, i)),
-            *shared,
-            whole_spec((1, PAIR)),
+            shared[0],
+            whole_spec((HEAD, HEAD)),
+            whole_spec((HEAD, HEAD)),
+            whole_spec((HEAD,)),
         ],
-        out_specs=[pair_spec(tokens)] * 9 + [scores, carry],
+        out_specs=[pair_spec(tokens)] * 9 + [scores, carry, shared[1]],
         out_shape=[narrow] * 3
         + [wide] * 6
         + [
-            jax.ShapeDtypeStruct((pairs, seqs, 2, context, context), NARROW),
-            jax.ShapeDtypeStruct((seqs, pairs, HEAD + 8, PAIR), WIDE),
+            pltpu.HBM((pairs, seqs, 2, context, context), NARROW),
+            pltpu.HBM((seqs, pairs, HEAD + 8, PAIR), WIDE),
+            pltpu.HBM((PAIR, PAIR), WIDE),
         ],
         cost_estimate=lasting(14.0),
-        compiler_params=pltpu.CompilerParams(vmem_limit_bytes=67108864),
+        compiler_params=pltpu.CompilerParams(vmem_limit_bytes=25165824),
         name="attention_local",
-    )(lengths, first, attn_in, weight, bias, tables, mix, wrow)
+    )(*in_hbm(lengths, first, attn_in, weight, bias, tables, dct_matrix(), points, weights))
 
 
 def attention_middle(lengths, first, cot, dense_weight, *rest):
@@ -1153,12 +1211,12 @@
         out_specs=[pl.BlockSpec((tokens, PAIR), lambda i: (0, i))]
         + [pair_spec(tokens)] * 3
         + [carry],
-        out_shape=[jax.ShapeDtypeStruct((tokens, D), NARROW), narrow, wide, wide]
-        + [jax.ShapeDtypeStruct((seqs, pairs, HEAD + 8, PAIR), WIDE)],
+        out_shape=[pltpu.HBM((tokens, D), NARROW), narrow, wide, wide]
+        + [pltpu.HBM((seqs, pairs, HEAD + 8, PAIR), WIDE)],
         cost_estimate=lasting(20.0),
-        compiler_params=pltpu.CompilerParams(vmem_limit_bytes=67108864),
+        compiler_params=pltpu.CompilerParams(vmem_limit_bytes=25165824),
         name="attention_middle",
-    )(lengths, first, cot, dense_weight, *rest)
+    )(*in_hbm(lengths, first, cot, dense_weight, *rest))
 
 
 def attention_last(lengths, first, *rest):
@@ -1170,13 +1228,13 @@
         in_specs=[SMEM_SPEC, SMEM_SPEC] + [pair_spec(tokens)] * 7 + [carry, *shared],
         out_specs=[pl.BlockSpec((tokens, 3 * PAIR), lambda i: (0, i))] * 2,
         out_shape=[
-            jax.ShapeDtypeStruct((tokens, 3 * D), NARROW),
-            jax.ShapeDtypeStruct((tokens, 3 * D), WIDE),
+            pltpu.HBM((tokens, 3 * D), NARROW),
+            pltpu.HBM((tokens, 3 * D), WIDE),
         ],
         cost_estimate=lasting(10.0),
-        compiler_params=pltpu.CompilerParams(vmem_limit_bytes=67108864),
+        compiler_params=pltpu.CompilerParams(vmem_limit_bytes=25165824),
         name="attention_last",
-    )(lengths, first, *rest)
+    )(*in_hbm(lengths, first, *rest))
 
 
 def shards(
@@ -1226,6 +1284,10 @@
     inputs_flat = inputs.reshape(tokens, D)
     cot = cotangent.reshape(tokens, D)
     cot_in = swap(cot.astype(WIDE), 0)
+    start = place * context
+    first = jnp.stack([start, jnp.full((), context, jnp.int32)])
+    qkv_row = qkv_bias.astype(WIDE)[None, :]
+    tables = attention_tables(place, context, count)
     attn_in, mlp_in, unit, rate = line.step(
         two_norms, inputs_flat, ln1_gain, ln1_bias, ln2_gain, ln2_bias
     )
@@ -1245,24 +1307,20 @@
     )
     for sub in range(2, subs, 2):
         down_group(sub)
-    reduction.step()
+    reduction.step(tables, qkv_row, first)
     up_in = line.send(up_send, lambda a: swap(a, 0))
     norm_in = line.send(norm_send, lambda a: swap(a, 0))
 
-    start, lengths_here = line.wait(place * context, lengths)
-    first = jnp.stack([start, jnp.full((), context, jnp.int32)])
-    positions = start + jnp.arange(context, dtype=jnp.int32)
-    tables, mix, wrow = attention_tables(positions, qmc_points, qmc_weights)
-    fq, fk, value, phi_q, phi_k, rot_q, rot_k, num, den, scores, carry = line.step(
+    fq, fk, value, phi_q, phi_k, rot_q, rot_k, num, den, scores, carry, mix = line.step(
         attention_local,
-        lengths_here,
+        lengths,
         first,
         attn_in,
         qkv_weight,
-        qkv_bias.astype(WIDE)[None, :],
+        qkv_row,
         tables,
-        mix,
-        wrow,
+        qmc_points,
+        qmc_weights,
     )
     arrived = shift_rows(carry, "seq", 1)
 
@@ -1274,13 +1332,13 @@
 
     up_group(0)
     for _ in range(hops - 1):
-        passed = line.step(pass_on, carry, arrived, lengths_here, first)
+        passed = line.step(pass_on, carry, arrived, lengths, first)
         arrived = shift_rows(passed, "seq", 1)
     reduction.step()
     up_group(1)
     attn_low, grad_q, grad_k, grad_v, carry_back = line.step(
         attention_middle,
-        lengths_here,
+        lengths,
         first,
         cot,
         dense_weight,
@@ -1310,13 +1368,13 @@
         down_bias,
     )
     for _ in range(hops - 1):
-        passed = line.step(pass_on, carry_back, arrived_back, lengths_here, first)
+        passed = line.step(pass_on, carry_back, arrived_back, lengths, first)
         arrived_back = shift_rows(passed, "seq", -1)
     shape = (D // owners, D)
     group("dense", shape, (0, 0), (low_own, low_in), (0,), (cot, cot_in), across)
     qkv_grad, qkv_send = line.step(
         attention_last,
-        lengths_here,
+        lengths,
         first,
         grad_q,
         grad_k,
@@ -1350,17 +1408,15 @@
 
     qkv_group(0)
     reduction.step()
-    vectors = Vectors(
-        line, (sums[0], sums[1], sums[2], sums[3], qkv_sums[0], sums[4], up_sums[0])
-    )
-    for part in range(1, 3):
-        qkv_group(part)
+    qkv_group(1)
+    vectors = Vectors(line, (sums, qkv_sums, up_sums))
+    reduction.step()
+    qkv_group(2)
+    vectors.take()
+    vectors.send()
+    while not reduction.finished():
+        reduction.step()
         vectors.take()
-        reduction.step()
-        vectors.send()
-    while not reduction.finished():
-        vectors.take()
-        reduction.step()
         vectors.send()
     totals = reduction.results()
     (
@@ -1368,8 +1424,8 @@
         attn_shift_total,
         mlp_gain_total,
         mlp_shift_total,
+        bias_total,
         qkv_bias_total,
-        bias_total,
         up_bias_total,
     ) = vectors.results()
 

time: 391 us -> 374 us (0.957)
  waiting for transfers between devices: 83.4 us -> 112 us
  other arithmetic: 14.3 us -> 1.25 us
  Pallas kernels: 185 us -> 172 us
  local copies, waits for them, and re-layouts: 17.8 us -> 6.38 us
  starting transfers between devices: 86.2 us -> 79.7 us
    ppermute x27, waiting for transfers between devices: 41.3 us -> 59.3 us  [swap(): lax.ppermute(value, 'batch', [(i, i ^ 1 << bit) for i in range(count)])]
    pallas_call x20, Pallas kernels: 88.9 us -> 74 us  [step(): out = function(*self.wait(*values))]
    ppermute x10, waiting for transfers between devices: 20.9 us -> 30.9 us  [step(): self.end = lax.ppermute(self.whole, 'seq', [(0, 1), (1, 0), (2, 3), (3, 2)])]
    ppermute x8, starting transfers between devices: 12.5 us -> 5.59 us  [step(): self.middle = lax.ppermute(self.inner[r - 2], 'seq', [(1, 2), (2, 1)])]
    add x5, other arithmetic: 5.87 us -> 0.04 us  [take(): self.held = self.line.step(lambda a, b: a + b, self.held, self.moving)]
  transfers between devices with their start and end apart: 52 -> 52, of which waited for: 21 -> 24; matrix products, arithmetic and copies ran while one was open for 8% -> 1% of each run, Pallas kernels for 32% -> 33%
where the time goes in v5:
time: 374 us; the launch traced here: 372 us
  Pallas kernels  172 us (46%)
  waiting for transfers between devices  112 us (30%)
  starting transfers between devices  79.7 us (21%)
  local copies, waits for them, and re-layouts  6.38 us (2%)
    pallas_call x20, Pallas kernels, step(): out = function(*self.wait(*values))  74 us
    ppermute x27, waiting for transfers between devices, swap(): lax.ppermute(value, 'batch', [(i, i ^ 1 << bit) for i in range(count)])  59.3 us
    ppermute x10, starting transfers between devices, step(): self.end = lax.ppermute(self.whole, 'seq', [(0, 1), (1, 0), (2, 3), (3, 2)])  33.1 us
    ppermute x10, waiting for transfers between devices, step(): self.end = lax.ppermute(self.whole, 'seq', [(0, 1), (1, 0), (2, 3), (3, 2)])  30.9 us
    ppermute x27, starting transfers between devices, swap(): lax.ppermute(value, 'batch', [(i, i ^ 1 << bit) for i in range(count)])  25.1 us
    pallas_call x1, Pallas kernels, attention_middle(): pl.pallas_call(partial(middle_kernel, seqs), grid=(pairs,), in_specs=[SME...  19.9 us
    ppermute x4, waiting for transfers between devices, shift_rows(): lax.ppermute(value, axis, [(i, i + by) for i in range(count) if 0 <= i +...  18.4 us
    pallas_call x1, Pallas kernels, mlp_back(): pl.pallas_call(back_kernel, grid=(FF // each,), in_specs=[total, pl.Block...  15.9 us
  transfers between devices with their start and end apart: 52, of which 24 were waited for; matrix products, arithmetic and copies ran while one was open for 1% of the time, Pallas kernels for 33%

profile of v5, /device:TPU:0, one launch (start us, length us, event | category | flops | bytes accessed | tf_op | source)
XLA Modules:
  0.0 371.9 jit_solution(1188564591018371164)
XLA Ops:
  0.7 3.9 %two_norms.1 = (bf16[256,1024]{1,0:T(8,128)(2,1)}, bf16[256,1024]{1,0:T(8,128)(2,1)}, f32[256,1024]{1,0:T(8,128)}, f32[256,128]{1,0:T(8,128)}) custom-call(bf16[256,1024]{1,0:T(8,128)(2,1)} %bitcast.36, bf16[1024]{0:T(1024)(128)(2,1)} %gain1.2, bf16[1024]{0:T(1024)(128)(2,1)} %bias1.1, bf16[1024]{0:T(1024)(128)(2,1)} %gain2.2, bf16[1024]{0:T(1024)(128)(2,1)} %bias2.1), custom_call_target="tpu_custom_call" | custom-call | flops 4600000000 | tf_op jit(solution)/shard_map/two_norms/pallas_call | solution.py:561
  4.6 11.1 %mlp_up.1 = (bf16[256,4096]{1,0:T(8,128)(2,1)}, f32[256,4096]{1,0:T(8,128)}, bf16[4,256,512]{2,1,0:T(8,128)(2,1)}, f32[4,256,512]{2,1,0:T(8,128)}) custom-call(s32[1]{0:T(128)} %bitcast.5.me_ref, bf16[256,1024]{1,0:T(8,128)(2,1)} %get-tuple-element.478.x_ref.refs_1_, bf16[1024,4096]{1,0:T(8,128)(2,1)} %up_ref, bf16[4096]{0:T(1024)(128)(2,1)} %bias_ref), custom_call_target="tpu_custom_call" | custom-call | flops 12650000384 | tf_op jit(solution)/shard_map/mlp_up/pallas_call | solution.py:609
  21.6 4.7 %piece_products.8 = (f32[512,512]{1,0:T(8,128)}, f32[512,512]{1,0:T(8,128)}, f32[512,512]{1,0:T(8,128)}, f32[512,512]{1,0:T(8,128)}) custom-call(bf16[4,256,512]{2,1,0:T(8,128)(2,1)} %get-tuple-element.519.refs_0_.refs_4_.refs_8_.refs_12_, f32[4,256,512]{2,1,0:T(8,128)S(1)} %collective-permute-done.refs_1_.refs_5_.refs_9_.refs_13_, ...), custom_call_target="tpu_custom_call" | custom-call | flops 5750000128 | tf_op jit(solution)/shard_map/piece_products/pallas_call | solution.py:94
  26.3 2.9 collective-permute-start.2
  30.7 15.9 %mlp_back.1 = (bf16[256,4096]{1,0:T(8,128)(2,1)}, f32[256,4096]{1,0:T(8,128)}, f32[1,4096]{1,0:T(1,128)}, f32[256,1024]{1,0:T(8,128)}, f32[256,1024]{1,0:T(8,128)}) custom-call(bf16[256,1024]{1,0:T(8,128)(2,1)} %bitcast.26, bf16[4096,1024]{1,0:T(8,128)(2,1)} %down_ref, bf16[1024,4096]{1,0:T(8,128)(2,1)} %up_ref, ...), custom_call_target="tpu_custom_call" | custom-call | flops 18400000000 | tf_op jit(solution)/shard_map/mlp_back/pallas_call | solution.py:673
  46.6 4.4 %piece_products.9 = (f32[768,512]{1,0:T(8,128)}, f32[768,512]{1,0:T(8,128)}, f32[512,512]{1,0:T(8,128)}, f32[512,512]{1,0:T(8,128)}) custom-call(bf16[4,256,512]{2,1,0:T(8,128)(2,1)} %get-tuple-element.519.refs_0_.refs_4_.refs_8_.refs_12_, f32[4,256,512]{2,1,0:T(8,128)S(1)} %collective-permute-done.refs_1_.refs_5_.refs_9_.refs_13_, ...), custom_call_target="tpu_custom_call" | custom-call | flops 5750000128 | tf_op jit(solution)/shard_map/piece_products/pallas_call | solution.py:94
  51.0 3.3 collective-permute-done.3.refs_2_
  54.4 2.9 reduce_round.12
  60.1 14.3 %attention_local.1 = (bf16[8,256,128]{2,1,0:T(8,128)(2,1)}, bf16[8,256,128]{2,1,0:T(8,128)(2,1)}, bf16[8,256,128]{2,1,0:T(8,128)(2,1)}, f32[8,256,128]{2,1,0:T(8...) custom-call(s32[2,3]{1,0:T(2,128)S(1)} %copy-done.10, ...), custom_call_target="tpu_custom_call" | custom-call | flops 16099999744 | tf_op jit(solution)/shard_map/attention_local/pallas_call | solution.py:1167
  74.4 3.5 collective-permute-start.4
  78.0 5.8 %piece_products.10 = (f32[768,512]{1,0:T(8,128)}, f32[768,512]{1,0:T(8,128)}, f32[512,512]{1,0:T(8,128)}, f32[512,512]{1,0:T(8,128)}) custom-call(bf16[2,256,512]{2,1,0:T(8,128)(2,1)} %get-tuple-element.808.refs_0_.refs_4_.refs_8_.refs_12_, f32[2,256,512]{2,1,0:T(8,128)S(1)} %collective-permute-done.5.refs_1_.refs_5_.refs_9_.refs_13_, ...), custom_call_target="tpu_custom_call" | custom-call | flops 5750000128 | tf_op jit(solution)/shard_map/piece_products/pallas_call | solution.py:94
  83.7 7.2 %collective-permute-done.4.arrived_ref = f32[2,8,72,128]{3,2,1,0:T(8,128)S(1)} collective-permute-done((f32[2,8,72,128]{3,2,1,0:T(8,128)}, f32[2,8,72,128]{3,2,1,0:T(8,128)S(1)}, u32[]{:S(2)}, u32[]{:S(2)}) %collective-permute-start.4) | collective-permute-done | bytes 589856 | tf_op jit(solution)/shard_map/ppermute | solution.py:47
  93.8 4.3 %collective-permute-start.7 = (f32[2,8,72,128]{3,2,1,0:T(8,128)}, f32[2,8,72,128]{3,2,1,0:T(8,128)S(1)}, u32[]{:S(2)}, u32[]{:S(2)}) collective-permute-start(f32[2,8,72,128]{3,2,1,0:T(8,128)} %pass_carry.2), channel_id=1, source_target_pairs={{0,8},{8,16},{16,24},{1,9},{9,17},{17,25},{2,10},{10,18},{18,26},{... | collective-permute-start | bytes 1769480 | tf_op jit(solution)/shard_map/ppermute | solution.py:47
  98.2 4.1 %reduce_round.13 = (f32[768,512]{1,0:T(8,128)}, f32[768,512]{1,0:T(8,128)}, f32[256,512]{1,0:T(8,128)}, f32[256,512]{1,0:T(8,128)}, f32[512,512]{1,0:T(8,128)}, /*index=5*/f32[512,512]{1,0:T(8,128)}) custom-call(s32[1]{0:T(128)} %bitcast.4.refs_0_, f32[768,512]{1,0:T(8,128)S(1)} %collective-permute-done.8.refs_1_, ...), custom_call_target="tpu_custom_call", output_to_operand_aliasing={{0}: (7, {}), {1}: (8, {})} | custom-call | flops 5750000128 | tf_op jit(solution)/shard_map/reduce_round/pallas_call | solution.py:94
  105.8 4.5 %piece_products.11 = (f32[768,512]{1,0:T(8,128)}, f32[768,512]{1,0:T(8,128)}, f32[512,512]{1,0:T(8,128)}, f32[512,512]{1,0:T(8,128)}) custom-call(bf16[2,256,512]{2,1,0:T(8,128)(2,1)} %get-tuple-element.808.refs_0_.refs_4_.refs_8_.refs_12_, f32[2,256,512]{2,1,0:T(8,128)S(1)} %collective-permute-done.5.refs_1_.refs_5_.refs_9_.refs_13_, ...), custom_call_target="tpu_custom_call" | custom-call | flops 5750000128 | tf_op jit(solution)/shard_map/piece_products/pallas_call | solution.py:94
  113.0 19.9 %attention_middle.1 = (bf16[256,1024]{1,0:T(8,128)(2,1)}, bf16[8,256,128]{2,1,0:T(8,128)(2,1)}, f32[8,256,128]{2,1,0:T(8,128)}, f32[8,256,128]{2,1,0:T(8,128)}, f32[2,8,72,128]{3,2,1,0:T(8,128)}) custom-call(s32[2,3]{1,0:T(2,128)S(1)} %copy-done.11, s32[2]{0:T(128)S(1)} %copy-done.16, bf16[256,1024]{1,0:T(8,128)(2,1)} %bitcast.31, ...), custom_call_target="tpu_custom_call" | custom-call | flops 23000000512 | tf_op jit(solution)/shard_map/attention_middle/pallas_call | solution.py:1200
  136.5 3.9 %collective-permute-done.11.refs_2_ = f32[768,512]{1,0:T(8,128)} collective-permute-done((f32[768,512]{1,0:T(8,128)}, f32[768,512]{1,0:T(8,128)}, u32[]{:S(2)}, u32[]{:S(2)}) %collective-permute-start.11) | collective-permute-done | bytes 1572896 | tf_op jit(solution)/shard_map/ppermute | solution.py:63
  140.4 4.7 %reduce_round.14 = (f32[768,512]{1,0:T(8,128)}, f32[768,512]{1,0:T(8,128)}, f32[256,512]{1,0:T(8,128)}, f32[256,512]{1,0:T(8,128)}, f32[512,512]{1,0:T(8,128)}, /*index=5*/f32[512,512]{1,0:T(8,128)}, f32[512,512]{1,0:T(8,128)}) custom-call(s32[1]{0:T(128)} %bitcast.4.refs_0_, ...), custom_call_target="tpu_custom_call", output_to_operand_aliasing={{0}: (9, {}), {1}: (10, {})} | custom-call | flops 5750000128 | tf_op jit(solution)/shard_map/reduce_round/pallas_call | solution.py:94
  145.1 3.4 layer_output.1
  156.6 3.1 piece_products.12
  159.6 9.3 %collective-permute-done.14.carry_ref = f32[2,8,72,128]{3,2,1,0:T(8,128)S(1)} collective-permute-done((f32[2,8,72,128]{3,2,1,0:T(8,128)}, f32[2,8,72,128]{3,2,1,0:T(8,128)S(1)}, u32[]{:S(2)}, u32[]{:S(2)}) %collective-permute-start.14) | collective-permute-done | bytes 589856 | tf_op jit(solution)/shard_map/ppermute | solution.py:47
  169.8 9.6 %attention_last.1 = (bf16[256,3072]{1,0:T(8,128)(2,1)}, f32[256,3072]{1,0:T(8,128)}) custom-call(s32[2,3]{1,0:T(2,128)S(1)} %copy-done.12, s32[2]{0:T(128)S(1)} %copy-done.17, bf16[8,256,128]{2,1,0:T(8,128)(2,1)} %get-tuple-element.680.gradq_ref, f32[8,256,128]{2,1,0:T(8,128)} %get-tuple-element.681.gradk_ref, f32[8,256,128]{2,1,0:T(8,128)} %get-tuple-element.682.gradv_ref, ...), custom_call_target="tpu_custom_call" | custom-call | flops 11500000256 | tf_op jit(solution)/shard_map/attention_last/pallas_call | solution.py:1225
  179.5 8.9 %collective-permute-done.18.refs_8_ = f32[512,512]{1,0:T(8,128)S(1)} collective-permute-done((f32[512,512]{1,0:T(8,128)}, f32[512,512]{1,0:T(8,128)S(1)}, u32[]{:S(2)}, u32[]{:S(2)}) %collective-permute-start.18) | collective-permute-done | bytes 1048608 | tf_op jit(solution)/shard_map/ppermute | solution.py:481
  190.5 4.6 %reduce_round.15 = (f32[512,512]{1,0:T(8,128)}, f32[512,512]{1,0:T(8,128)}, f32[256,512]{1,0:T(8,128)}, f32[256,512]{1,0:T(8,128)}, f32[512,512]{1,0:T(8,128)}, /*index=5*/f32[512,512]{1,0:T(8,128)}, f32[512,512]{1,0:T(8,128)}) custom-call(s32[1]{0:T(128)} %bitcast.4.refs_0_, ...), custom_call_target="tpu_custom_call", output_to_operand_aliasing={{0}: (11, {}), {1}: (12, {})} | custom-call | flops 5750000128 | tf_op jit(solution)/shard_map/reduce_round/pallas_call | solution.py:94
  196.3 4.7 %collective-permute-start.23 = (f32[512,512]{1,0:T(8,128)}, f32[512,512]{1,0:T(8,128)S(1)}, u32[]{:S(2)}, u32[]{:S(2)}) collective-permute-start(f32[512,512]{1,0:T(8,128)} %get-tuple-element.760.refs_11_), channel_id=1, source_target_pairs={{0,8},{8,0},{16,24},{24,16},{1,9},{9,1},{17,25},{25,17},{2,10},{10... | collective-permute-start | bytes 3145736 | tf_op jit(solution)/shard_map/ppermute | solution.py:481
  201.7 9.3 %norm_back.1 = (f32[256,1024]{1,0:T(8,128)}, f32[5,1024]{1,0:T(8,128)}, f32[1,3072]{1,0:T(1,128)}) custom-call(bf16[256,3072]{1,0:T(8,128)(2,1)} %get-tuple-element.810.qkv_ref.refs_2_.refs_6_, bf16[1024,3072]{1,0:T(8,128)(2,1)} %weight_ref.3, f32[256,1024]{1,0:T(8,128)} %get-tuple-element.719.mlp_ref, f32[256,1024]{1,0:T(8,128)} %get-tuple-element.720.unit_ref, ...), custom_call_target="tpu_custom_call" | custom-call | flops 10350000128 | tf_op jit(solution)/shard_map/norm_back/pallas_call | solution.py:781
  211.0 3.8 %piece_products.13 = (f32[384,512]{1,0:T(8,128)}, f32[384,512]{1,0:T(8,128)}, f32[256,512]{1,0:T(8,128)}, f32[256,512]{1,0:T(8,128)}) custom-call(bf16[2,256,512]{2,1,0:T(8,128)(2,1)} %get-tuple-element.808.refs_0_.refs_4_.refs_8_.refs_12_, f32[2,256,512]{2,1,0:T(8,128)S(1)} %collective-permute-done.5.refs_1_.refs_5_.refs_9_.refs_13_, ...), custom_call_target="tpu_custom_call" | custom-call | flops 5750000128 | tf_op jit(solution)/shard_map/piece_products/pallas_call | solution.py:94
  214.9 6.4 %collective-permute-done.22.refs_2_ = f32[512,512]{1,0:T(8,128)S(1)} collective-permute-done((f32[512,512]{1,0:T(8,128)}, f32[512,512]{1,0:T(8,128)S(1)}, u32[]{:S(2)}, u32[]{:S(2)}) %collective-permute-start.22) | collective-permute-done | bytes 1048608 | tf_op jit(solution)/shard_map/ppermute | solution.py:63
  221.3 3.2 collective-permute-done.23.refs_8_
  224.4 4.4 %reduce_round.16 = (f32[384,512]{1,0:T(8,128)}, f32[384,512]{1,0:T(8,128)}, f32[128,512]{1,0:T(8,128)}, f32[128,512]{1,0:T(8,128)}, f32[512,512]{1,0:T(8,128)}, ...) custom-call(s32[1]{0:T(128)} %bitcast.4.refs_0_, ...), custom_call_target="tpu_custom_call", output_to_operand_aliasing={{0}: (12, {}), {1}: (13, {})} | custom-call | flops 5750000128 | tf_op jit(solution)/shard_map/reduce_round/pallas_call | solution.py:94
  228.8 3.7 collective-permute-start.28
  236.3 3.1 piece_products.14
  240.8 11.0 %collective-permute-done.27.refs_2_ = f32[384,512]{1,0:T(8,128)} collective-permute-done((f32[384,512]{1,0:T(8,128)}, f32[384,512]{1,0:T(8,128)}, u32[]{:S(2)}, u32[]{:S(2)}) %collective-permute-start.27) | collective-permute-done | bytes 786464 | tf_op jit(solution)/shard_map/ppermute | solution.py:63
  255.1 4.6 %reduce_round.17 = (f32[384,512]{1,0:T(8,128)}, f32[384,512]{1,0:T(8,128)}, f32[128,512]{1,0:T(8,128)}, f32[128,512]{1,0:T(8,128)}, f32[256,512]{1,0:T(8,128)}, ...) custom-call(s32[1]{0:T(128)} %bitcast.4.refs_0_, ...), custom_call_target="tpu_custom_call", output_to_operand_aliasing={{0}: (12, {}), {1}: (13, {}), {7}: (14, {})} | custom-call | flops 5750000128 | tf_op jit(solution)/shard_map/reduce_round/pallas_call | solution.py:94
  259.7 3.7 collective-permute-start.33
  267.3 3.1 piece_products.15
  270.4 11.2 %collective-permute-done.32.refs_2_ = f32[384,512]{1,0:T(8,128)S(1)} collective-permute-done((f32[384,512]{1,0:T(8,128)}, f32[384,512]{1,0:T(8,128)S(1)}, u32[]{:S(2)}, u32[]{:S(2)}) %collective-permute-start.32) | collective-permute-done | bytes 786464 | tf_op jit(solution)/shard_map/ppermute | solution.py:63
  285.0 3.9 %reduce_round.18 = (f32[384,512]{1,0:T(8,128)}, f32[384,512]{1,0:T(8,128)}, f32[128,512]{1,0:T(8,128)}, f32[128,512]{1,0:T(8,128)}, f32[256,512]{1,0:T(8,128)}, ...) custom-call(s32[1]{0:T(128)} %bitcast.4.refs_0_, ...), custom_call_target="tpu_custom_call", output_to_operand_aliasing={{0}: (12, {}), {1}: (13, {})} | custom-call | flops 5750000128 | tf_op jit(solution)/shard_map/reduce_round/pallas_call | solution.py:94
  288.9 3.7 collective-permute-start.38
  296.9 13.7 %collective-permute-done.30 = f32[2,1536]{1,0:T(2,128)S(1)} collective-permute-done((f32[2,1536]{1,0:T(2,128)S(1)}, f32[2,1536]{1,0:T(2,128)S(1)}, u32[]{:S(2)}, u32[]{:S(2)}) %collective-permute-start.30) | collective-permute-done | bytes 12320 | tf_op jit(solution)/shard_map/ppermute | solution.py:63
  313.3 3.6 reduce_round.19
  323.0 3.1 collective-permute-done.35
  330.2 3.6 collective-permute-start.46
  334.5 3.4 collective-permute-start.40
  337.9 2.9 collective-permute-done.40
  344.5 5.2 %collective-permute-start.49 = (f32[256,512]{1,0:T(8,128)}, f32[256,512]{1,0:T(8,128)S(1)}, u32[]{:S(2)}, u32[]{:S(2)}) collective-permute-start(f32[256,512]{1,0:T(8,128)} %get-tuple-element.907.refs_4_), channel_id=1, source_target_pairs={{0,8},{8,0},{16,24},{24,16},{1,9},{9,1},{17,25},{25,17},{2,10},{10... | collective-permute-start | bytes 1572872 | tf_op jit(solution)/shard_map/ppermute | solution.py:481
  351.7 5.9 %collective-permute-done.49.refs_1_ = f32[256,512]{1,0:T(8,128)S(1)} collective-permute-done((f32[256,512]{1,0:T(8,128)}, f32[256,512]{1,0:T(8,128)S(1)}, u32[]{:S(2)}, u32[]{:S(2)}) %collective-permute-start.49) | collective-permute-done | bytes 524320 | tf_op jit(solution)/shard_map/ppermute | solution.py:481
  363.9 5.6 %collective-permute-done.51.refs_1_ = f32[256,512]{1,0:T(8,128)S(1)} collective-permute-done((f32[256,512]{1,0:T(8,128)}, f32[256,512]{1,0:T(8,128)S(1)}, u32[]{:S(2)}, u32[]{:S(2)}) %collective-permute-start.51) | collective-permute-done | bytes 524320 | tf_op jit(solution)/shard_map/ppermute | solution.py:481
  (162 shorter events, 83.7 us)
Async XLA Ops:
  15.7 6.0 %collective-permute-start = (f32[4,256,512]{2,1,0:T(8,128)}, f32[4,256,512]{2,1,0:T(8,128)S(1)}, u32[]{:S(2)}, u32[]{:S(2)}) collective-permute-start(f32[4,256,512]{2,1,0:T(8,128)} %get-tuple-element.474), channel_id=1, source_target_pairs={{0,1},{1,0},{2,3},{3,2},{4,5},{5,4},{6,7},{7,6},{8,9},{9,8},{10,11... | collective-permute-start | bytes 6291464 | tf_op jit(solution)/shard_map/ppermute | solution.py:63
  26.3 28.0 %collective-permute-start.2 = (f32[512,512]{1,0:T(8,128)}, f32[512,512]{1,0:T(8,128)S(1)}, u32[]{:S(2)}, u32[]{:S(2)}) collective-permute-start(f32[512,512]{1,0:T(8,128)} %get-tuple-element.496), channel_id=1, source_target_pairs={{0,2},{1,3},{2,0},{3,1},{4,6},{5,7},{6,4},{7,5},{8,10},{9,11},{10,... | collective-permute-start | bytes 3145736 | tf_op jit(solution)/shard_map/ppermute | solution.py:63
  29.2 25.1 %collective-permute-start.3 = (f32[512,512]{1,0:T(8,128)}, f32[512,512]{1,0:T(8,128)S(1)}, u32[]{:S(2)}, u32[]{:S(2)}) collective-permute-start(f32[512,512]{1,0:T(8,128)} %get-tuple-element.497), channel_id=1, source_target_pairs={{0,4},{1,5},{2,6},{3,7},{4,0},{5,1},{6,2},{7,3},{8,12},{9,13},{10,... | collective-permute-start | bytes 3145736 | tf_op jit(solution)/shard_map/ppermute | solution.py:63
  57.8 20.2 %collective-permute-start.6 = (f32[256,4096]{1,0:T(8,128)S(1)}, f32[256,4096]{1,0:T(8,128)S(1)}, u32[]{:S(2)}, u32[]{:S(2)}) collective-permute-start(f32[256,4096]{1,0:T(8,128)S(1)} %copy-done.22), channel_id=1, source_target_pairs={{0,1},{1,0},{2,3},{3,2},{4,5},{5,4},{6,7},{7,6},{8,9},{9,8},{10,11... | collective-permute-start | bytes 12582920 | tf_op jit(solution)/shard_map/ppermute | solution.py:63
  57.8 40.4 %collective-permute-start.8 = (f32[768,512]{1,0:T(8,128)}, f32[768,512]{1,0:T(8,128)S(1)}, u32[]{:S(2)}, u32[]{:S(2)}) collective-permute-start(f32[768,512]{1,0:T(8,128)} %get-tuple-element.535), channel_id=1, source_target_pairs={{0,2},{1,3},{2,0},{3,1},{4,6},{5,7},{6,4},{7,5},{8,10},{9,11},{10,... | collective-permute-start | bytes 4718600 | tf_op jit(solution)/shard_map/ppermute | solution.py:63
  58.2 19.8 %collective-permute-start.5 = (f32[2,256,512]{2,1,0:T(8,128)S(1)}, f32[2,256,512]{2,1,0:T(8,128)S(1)}, u32[]{:S(2)}, u32[]{:S(2)}) collective-permute-start(f32[2,256,512]{2,1,0:T(8,128)S(1)} %copy-done.24), channel_id=1, source_target_pairs={{0,1},{1,0},{2,3},{3,2},{4,5},{5,4},{6,7},{7,6},{8,9},{9,8},{10,11... | collective-permute-start | bytes 3145736 | tf_op jit(solution)/shard_map/ppermute | solution.py:63
  58.4 39.8 %collective-permute-start.9 = (f32[768,512]{1,0:T(8,128)}, f32[768,512]{1,0:T(8,128)}, u32[]{:S(2)}, u32[]{:S(2)}) collective-permute-start(f32[768,512]{1,0:T(8,128)} %get-tuple-element.579), channel_id=1, source_target_pairs={{0,4},{1,5},{2,6},{3,7},{4,0},{5,1},{6,2},{7,3},{8,12},{9,13},{10,... | collective-permute-start | bytes 4718600 | tf_op jit(solution)/shard_map/ppermute | solution.py:63
  74.4 16.5 %collective-permute-start.4 = (f32[2,8,72,128]{3,2,1,0:T(8,128)}, f32[2,8,72,128]{3,2,1,0:T(8,128)S(1)}, u32[]{:S(2)}, u32[]{:S(2)}) collective-permute-start(f32[2,8,72,128]{3,2,1,0:T(8,128)} %get-tuple-element.576.own_ref), channel_id=1, source_target_pairs={{0,8},{8,16},{16,24},{1,9},{9,17},{17,25},{2,10},{10,18},{18,26},{... | collective-permute-start | bytes 1769480 | tf_op jit(solution)/shard_map/ppermute | solution.py:47
  93.8 18.4 %collective-permute-start.7 = (f32[2,8,72,128]{3,2,1,0:T(8,128)}, f32[2,8,72,128]{3,2,1,0:T(8,128)S(1)}, u32[]{:S(2)}, u32[]{:S(2)}) collective-permute-start(f32[2,8,72,128]{3,2,1,0:T(8,128)} %pass_carry.2), channel_id=1, source_target_pairs={{0,8},{8,16},{16,24},{1,9},{9,17},{17,25},{2,10},{10,18},{18,26},{... | collective-permute-start | bytes 1769480 | tf_op jit(solution)/shard_map/ppermute | solution.py:47
  102.3 38.1 %collective-permute-start.10 = (f32[768,512]{1,0:T(8,128)}, f32[768,512]{1,0:T(8,128)S(1)}, u32[]{:S(2)}, u32[]{:S(2)}) collective-permute-start(f32[768,512]{1,0:T(8,128)} %get-tuple-element.594), channel_id=1, source_target_pairs={{0,2},{1,3},{2,0},{3,1},{4,6},{5,7},{6,4},{7,5},{8,10},{9,11},{10,... | collective-permute-start | bytes 4718600 | tf_op jit(solution)/shard_map/ppermute | solution.py:63
  103.8 32.7 %collective-permute-start.12 = (f32[512,512]{1,0:T(8,128)}, f32[512,512]{1,0:T(8,128)}, u32[]{:S(2)}, u32[]{:S(2)}) collective-permute-start(f32[512,512]{1,0:T(8,128)} %get-tuple-element.635), channel_id=1, source_target_pairs={{0,8},{8,0},{16,24},{24,16},{1,9},{9,1},{17,25},{25,17},{2,10},{10... | collective-permute-start | bytes 3145736 | tf_op jit(solution)/shard_map/ppermute | solution.py:481
  105.3 35.0 %collective-permute-start.11 = (f32[768,512]{1,0:T(8,128)}, f32[768,512]{1,0:T(8,128)}, u32[]{:S(2)}, u32[]{:S(2)}) collective-permute-start(f32[768,512]{1,0:T(8,128)} %get-tuple-element.629), channel_id=1, source_target_pairs={{0,4},{1,5},{2,6},{3,7},{4,0},{5,1},{6,2},{7,3},{8,12},{9,13},{10,... | collective-permute-start | bytes 4718600 | tf_op jit(solution)/shard_map/ppermute | solution.py:63
  132.9 15.6 %collective-permute-start.13 = (f32[2,8,72,128]{3,2,1,0:T(8,128)}, f32[2,8,72,128]{3,2,1,0:T(8,128)}, u32[]{:S(2)}, u32[]{:S(2)}) collective-permute-start(f32[2,8,72,128]{3,2,1,0:T(8,128)} %get-tuple-element.666.own_ref), channel_id=1, source_target_pairs={{8,0},{16,8},{24,16},{9,1},{17,9},{25,17},{10,2},{18,10},{26,18},{... | collective-permute-start | bytes 1769480 | tf_op jit(solution)/shard_map/ppermute | solution.py:47
  136.5 16.2 %collective-permute-start.15 = (f32[1,256,512]{2,1,0:T(8,128)}, f32[1,256,512]{2,1,0:T(8,128)S(1)}, u32[]{:S(2)}, u32[]{:S(2)}) collective-permute-start(f32[1,256,512]{2,1,0:T(8,128)} %get-tuple-element.668), channel_id=1, source_target_pairs={{0,1},{1,0},{2,3},{3,2},{4,5},{5,4},{6,7},{7,6},{8,9},{9,8},{10,11... | collective-permute-start | bytes 1572872 | tf_op jit(solution)/shard_map/ppermute | solution.py:63
  150.6 18.4 %collective-permute-start.14 = (f32[2,8,72,128]{3,2,1,0:T(8,128)}, f32[2,8,72,128]{3,2,1,0:T(8,128)S(1)}, u32[]{:S(2)}, u32[]{:S(2)}) collective-permute-start(f32[2,8,72,128]{3,2,1,0:T(8,128)} %pass_carry.3), channel_id=1, source_target_pairs={{8,0},{16,8},{24,16},{9,1},{17,9},{25,17},{10,2},{18,10},{26,18},{... | collective-permute-start | bytes 1769480 | tf_op jit(solution)/shard_map/ppermute | solution.py:47
  151.9 38.6 %collective-permute-start.16 = (f32[768,512]{1,0:T(8,128)}, f32[768,512]{1,0:T(8,128)S(1)}, u32[]{:S(2)}, u32[]{:S(2)}) collective-permute-start(f32[768,512]{1,0:T(8,128)} %get-tuple-element.651), channel_id=1, source_target_pairs={{0,2},{1,3},{2,0},{3,1},{4,6},{5,7},{6,4},{7,5},{8,10},{9,11},{10,... | collective-permute-start | bytes 4718600 | tf_op jit(solution)/shard_map/ppermute | solution.py:63
  152.6 35.7 %collective-permute-start.18 = (f32[512,512]{1,0:T(8,128)}, f32[512,512]{1,0:T(8,128)S(1)}, u32[]{:S(2)}, u32[]{:S(2)}) collective-permute-start(f32[512,512]{1,0:T(8,128)} %get-tuple-element.700), channel_id=1, source_target_pairs={{0,8},{8,0},{16,24},{24,16},{1,9},{9,1},{17,25},{25,17},{2,10},{10... | collective-permute-start | bytes 3145736 | tf_op jit(solution)/shard_map/ppermute | solution.py:481
  155.3 33.1 %collective-permute-start.19 = (f32[512,512]{1,0:T(8,128)}, f32[512,512]{1,0:T(8,128)S(1)}, u32[]{:S(2)}, u32[]{:S(2)}) collective-permute-start(f32[512,512]{1,0:T(8,128)} %get-tuple-element.712.refs_9_), channel_id=1, source_target_pairs={{8,16},{16,8},{9,17},{17,9},{10,18},{18,10},{11,19},{19,11},{12,20... | collective-permute-start | bytes 3145736 | tf_op jit(solution)/shard_map/ppermute | solution.py:484
  156.0 34.5 %collective-permute-start.17 = (f32[768,512]{1,0:T(8,128)}, f32[768,512]{1,0:T(8,128)S(1)}, u32[]{:S(2)}, u32[]{:S(2)}) collective-permute-start(f32[768,512]{1,0:T(8,128)} %get-tuple-element.694), channel_id=1, source_target_pairs={{0,4},{1,5},{2,6},{3,7},{4,0},{5,1},{6,2},{7,3},{8,12},{9,13},{10,... | collective-permute-start | bytes 4718600 | tf_op jit(solution)/shard_map/ppermute | solution.py:63
  195.1 15.9 %collective-permute-start.20 = (f32[256,3072]{1,0:T(8,128)S(1)}, f32[256,3072]{1,0:T(8,128)S(1)}, u32[]{:S(2)}, u32[]{:S(2)}) collective-permute-start(f32[256,3072]{1,0:T(8,128)S(1)} %copy-done.23), channel_id=1, source_target_pairs={{0,1},{1,0},{2,3},{3,2},{4,5},{5,4},{6,7},{7,6},{8,9},{9,8},{10,11... | collective-permute-start | bytes 9437192 | tf_op jit(solution)/shard_map/ppermute | solution.py:63
  195.2 29.2 %collective-permute-start.21 = (f32[512,512]{1,0:T(8,128)}, f32[512,512]{1,0:T(8,128)S(1)}, u32[]{:S(2)}, u32[]{:S(2)}) collective-permute-start(f32[512,512]{1,0:T(8,128)} %get-tuple-element.716), channel_id=1, source_target_pairs={{0,2},{1,3},{2,0},{3,1},{4,6},{5,7},{6,4},{7,5},{8,10},{9,11},{10,... | collective-permute-start | bytes 3145736 | tf_op jit(solution)/shard_map/ppermute | solution.py:63
  195.8 25.4 %collective-permute-start.22 = (f32[512,512]{1,0:T(8,128)}, f32[512,512]{1,0:T(8,128)S(1)}, u32[]{:S(2)}, u32[]{:S(2)}) collective-permute-start(f32[512,512]{1,0:T(8,128)} %get-tuple-element.731), channel_id=1, source_target_pairs={{0,4},{1,5},{2,6},{3,7},{4,0},{5,1},{6,2},{7,3},{8,12},{9,13},{10,... | collective-permute-start | bytes 3145736 | tf_op jit(solution)/shard_map/ppermute | solution.py:63
  196.3 28.1 %collective-permute-start.23 = (f32[512,512]{1,0:T(8,128)}, f32[512,512]{1,0:T(8,128)S(1)}, u32[]{:S(2)}, u32[]{:S(2)}) collective-permute-start(f32[512,512]{1,0:T(8,128)} %get-tuple-element.760.refs_11_), channel_id=1, source_target_pairs={{0,8},{8,0},{16,24},{24,16},{1,9},{9,1},{17,25},{25,17},{2,10},{10... | collective-permute-start | bytes 3145736 | tf_op jit(solution)/shard_map/ppermute | solution.py:481
  201.0 23.4 %collective-permute-start.24 = (f32[512,512]{1,0:T(8,128)}, f32[512,512]{1,0:T(8,128)S(1)}, u32[]{:S(2)}, u32[]{:S(2)}) collective-permute-start(f32[512,512]{1,0:T(8,128)} %get-tuple-element.758.refs_9_), channel_id=1, source_target_pairs={{8,16},{16,8},{9,17},{17,9},{10,18},{18,10},{11,19},{19,11},{12,20... | collective-permute-start | bytes 3145736 | tf_op jit(solution)/shard_map/ppermute | solution.py:484
  228.8 26.2 %collective-permute-start.28 = (f32[512,512]{1,0:T(8,128)}, f32[512,512]{1,0:T(8,128)S(1)}, u32[]{:S(2)}, u32[]{:S(2)}) collective-permute-start(f32[512,512]{1,0:T(8,128)} %get-tuple-element.799.refs_11_), channel_id=1, source_target_pairs={{0,8},{8,0},{16,24},{24,16},{1,9},{9,1},{17,25},{25,17},{2,10},{10... | collective-permute-start | bytes 3145736 | tf_op jit(solution)/shard_map/ppermute | solution.py:481
  232.5 22.6 %collective-permute-start.29 = (f32[512,512]{1,0:T(8,128)}, f32[512,512]{1,0:T(8,128)S(1)}, u32[]{:S(2)}, u32[]{:S(2)}) collective-permute-start(f32[512,512]{1,0:T(8,128)} %get-tuple-element.797.refs_9_), channel_id=1, source_target_pairs={{8,16},{16,8},{9,17},{17,9},{10,18},{18,10},{11,19},{19,11},{12,20... | collective-permute-start | bytes 3145736 | tf_op jit(solution)/shard_map/ppermute | solution.py:484
  233.2 18.6 %collective-permute-start.27 = (f32[384,512]{1,0:T(8,128)}, f32[384,512]{1,0:T(8,128)}, u32[]{:S(2)}, u32[]{:S(2)}) collective-permute-start(f32[384,512]{1,0:T(8,128)} %get-tuple-element.778), channel_id=1, source_target_pairs={{0,4},{1,5},{2,6},{3,7},{4,0},{5,1},{6,2},{7,3},{8,12},{9,13},{10,... | collective-permute-start | bytes 2359304 | tf_op jit(solution)/shard_map/ppermute | solution.py:63
  234.8 18.2 %collective-permute-start.26 = (f32[384,512]{1,0:T(8,128)}, f32[384,512]{1,0:T(8,128)}, u32[]{:S(2)}, u32[]{:S(2)}) collective-permute-start(f32[384,512]{1,0:T(8,128)} %get-tuple-element.763), channel_id=1, source_target_pairs={{0,2},{1,3},{2,0},{3,1},{4,6},{5,7},{6,4},{7,5},{8,10},{9,11},{10,... | collective-permute-start | bytes 2359304 | tf_op jit(solution)/shard_map/ppermute | solution.py:63
  259.7 25.3 %collective-permute-start.33 = (f32[512,512]{1,0:T(8,128)}, f32[512,512]{1,0:T(8,128)S(1)}, u32[]{:S(2)}, u32[]{:S(2)}) collective-permute-start(f32[512,512]{1,0:T(8,128)} %get-tuple-element.836.refs_11_), channel_id=1, source_target_pairs={{0,8},{8,0},{16,24},{24,16},{1,9},{9,1},{17,25},{25,17},{2,10},{10... | collective-permute-start | bytes 3145736 | tf_op jit(solution)/shard_map/ppermute | solution.py:481
  263.4 21.6 %collective-permute-start.34 = (f32[512,512]{1,0:T(8,128)}, f32[512,512]{1,0:T(8,128)S(1)}, u32[]{:S(2)}, u32[]{:S(2)}) collective-permute-start(f32[512,512]{1,0:T(8,128)} %get-tuple-element.834.refs_9_), channel_id=1, source_target_pairs={{8,16},{16,8},{9,17},{17,9},{10,18},{18,10},{11,19},{19,11},{12,20... | collective-permute-start | bytes 3145736 | tf_op jit(solution)/shard_map/ppermute | solution.py:484
  264.1 17.5 %collective-permute-start.32 = (f32[384,512]{1,0:T(8,128)}, f32[384,512]{1,0:T(8,128)S(1)}, u32[]{:S(2)}, u32[]{:S(2)}) collective-permute-start(f32[384,512]{1,0:T(8,128)} %get-tuple-element.816), channel_id=1, source_target_pairs={{0,4},{1,5},{2,6},{3,7},{4,0},{5,1},{6,2},{7,3},{8,12},{9,13},{10,... | collective-permute-start | bytes 2359304 | tf_op jit(solution)/shard_map/ppermute | solution.py:63
  265.7 17.2 %collective-permute-start.31 = (f32[384,512]{1,0:T(8,128)}, f32[384,512]{1,0:T(8,128)S(1)}, u32[]{:S(2)}, u32[]{:S(2)}) collective-permute-start(f32[384,512]{1,0:T(8,128)} %get-tuple-element.803), channel_id=1, source_target_pairs={{0,2},{1,3},{2,0},{3,1},{4,6},{5,7},{6,4},{7,5},{8,10},{9,11},{10,... | collective-permute-start | bytes 2359304 | tf_op jit(solution)/shard_map/ppermute | solution.py:63
  288.9 24.4 %collective-permute-start.38 = (f32[512,512]{1,0:T(8,128)}, f32[512,512]{1,0:T(8,128)S(1)}, u32[]{:S(2)}, u32[]{:S(2)}) collective-permute-start(f32[512,512]{1,0:T(8,128)} %get-tuple-element.863.refs_11_), channel_id=1, source_target_pairs={{0,8},{8,0},{16,24},{24,16},{1,9},{9,1},{17,25},{25,17},{2,10},{10... | collective-permute-start | bytes 3145736 | tf_op jit(solution)/shard_map/ppermute | solution.py:481
  292.6 18.1 %collective-permute-start.37 = (f32[384,512]{1,0:T(8,128)}, f32[384,512]{1,0:T(8,128)S(1)}, u32[]{:S(2)}, u32[]{:S(2)}) collective-permute-start(f32[384,512]{1,0:T(8,128)} %get-tuple-element.843), channel_id=1, source_target_pairs={{0,4},{1,5},{2,6},{3,7},{4,0},{5,1},{6,2},{7,3},{8,12},{9,13},{10,... | collective-permute-start | bytes 2359304 | tf_op jit(solution)/shard_map/ppermute | solution.py:63
  294.1 16.6 %collective-permute-start.36 = (f32[384,512]{1,0:T(8,128)}, f32[384,512]{1,0:T(8,128)S(1)}, u32[]{:S(2)}, u32[]{:S(2)}) collective-permute-start(f32[384,512]{1,0:T(8,128)} %get-tuple-element.839), channel_id=1, source_target_pairs={{0,2},{1,3},{2,0},{3,1},{4,6},{5,7},{6,4},{7,5},{8,10},{9,11},{10,... | collective-permute-start | bytes 2359304 | tf_op jit(solution)/shard_map/ppermute | solution.py:63
  295.6 15.1 %collective-permute-start.39 = (f32[256,512]{1,0:T(8,128)}, f32[256,512]{1,0:T(8,128)S(1)}, u32[]{:S(2)}, u32[]{:S(2)}) collective-permute-start(f32[256,512]{1,0:T(8,128)} %get-tuple-element.861.refs_9_), channel_id=1, source_target_pairs={{8,16},{16,8},{9,17},{17,9},{10,18},{18,10},{11,19},{19,11},{12,20... | collective-permute-start | bytes 1572872 | tf_op jit(solution)/shard_map/ppermute | solution.py:484
  296.3 14.3 %collective-permute-start.30 = (f32[2,1536]{1,0:T(2,128)S(1)}, f32[2,1536]{1,0:T(2,128)S(1)}, u32[]{:S(2)}, u32[]{:S(2)}) collective-permute-start(f32[2,1536]{1,0:T(2,128)S(1)} %get-tuple-element.815), channel_id=1, source_target_pairs={{0,2},{1,3},{2,0},{3,1},{4,6},{5,7},{6,4},{7,5},{8,10},{9,11},{10,... | collective-permute-start | bytes 36872 | tf_op jit(solution)/shard_map/ppermute | solution.py:63
  316.9 10.7 %collective-permute-start.43 = (f32[256,512]{1,0:T(8,128)}, f32[256,512]{1,0:T(8,128)S(1)}, u32[]{:S(2)}, u32[]{:S(2)}) collective-permute-start(f32[256,512]{1,0:T(8,128)} %get-tuple-element.884.refs_9_), channel_id=1, source_target_pairs={{0,8},{8,0},{16,24},{24,16},{1,9},{9,1},{17,25},{25,17},{2,10},{10... | collective-permute-start | bytes 1572872 | tf_op jit(solution)/shard_map/ppermute | solution.py:481
  318.7 8.9 %collective-permute-start.44 = (f32[256,512]{1,0:T(8,128)}, f32[256,512]{1,0:T(8,128)S(1)}, u32[]{:S(2)}, u32[]{:S(2)}) collective-permute-start(f32[256,512]{1,0:T(8,128)} %get-tuple-element.882.refs_7_), channel_id=1, source_target_pairs={{8,16},{16,8},{9,17},{17,9},{10,18},{18,10},{11,19},{19,11},{12,20... | collective-permute-start | bytes 1572872 | tf_op jit(solution)/shard_map/ppermute | solution.py:484
  319.4 6.8 %collective-permute-start.42 = (f32[128,512]{1,0:T(8,128)}, f32[128,512]{1,0:T(8,128)S(1)}, u32[]{:S(2)}, u32[]{:S(2)}) collective-permute-start(f32[128,512]{1,0:T(8,128)} %get-tuple-element.869), channel_id=1, source_target_pairs={{0,4},{1,5},{2,6},{3,7},{4,0},{5,1},{6,2},{7,3},{8,12},{9,13},{10,... | collective-permute-start | bytes 786440 | tf_op jit(solution)/shard_map/ppermute | solution.py:63
  320.9 6.6 %collective-permute-start.41 = (f32[128,512]{1,0:T(8,128)}, f32[128,512]{1,0:T(8,128)S(1)}, u32[]{:S(2)}, u32[]{:S(2)}) collective-permute-start(f32[128,512]{1,0:T(8,128)} %get-tuple-element.865), channel_id=1, source_target_pairs={{0,2},{1,3},{2,0},{3,1},{4,6},{5,7},{6,4},{7,5},{8,10},{9,11},{10,... | collective-permute-start | bytes 786440 | tf_op jit(solution)/shard_map/ppermute | solution.py:63
  330.2 11.2 %collective-permute-start.46 = (f32[256,512]{1,0:T(8,128)}, f32[256,512]{1,0:T(8,128)S(1)}, u32[]{:S(2)}, u32[]{:S(2)}) collective-permute-start(f32[256,512]{1,0:T(8,128)} %get-tuple-element.896.refs_5_), channel_id=1, source_target_pairs={{0,8},{8,0},{16,24},{24,16},{1,9},{9,1},{17,25},{25,17},{2,10},{10... | collective-permute-start | bytes 1572872 | tf_op jit(solution)/shard_map/ppermute | solution.py:481
  333.8 7.6 %collective-permute-start.47 = (f32[256,512]{1,0:T(8,128)}, f32[256,512]{1,0:T(8,128)S(1)}, u32[]{:S(2)}, u32[]{:S(2)}) collective-permute-start(f32[256,512]{1,0:T(8,128)} %get-tuple-element.894.refs_3_), channel_id=1, source_target_pairs={{8,16},{16,8},{9,17},{17,9},{10,18},{18,10},{11,19},{19,11},{12,20... | collective-permute-start | bytes 1572872 | tf_op jit(solution)/shard_map/ppermute | solution.py:484
  334.5 6.4 %collective-permute-start.40 = (f32[1,1536]{1,0:T(1,128)S(1)}, f32[1,1536]{1,0:T(1,128)S(1)}, u32[]{:S(2)}, u32[]{:S(2)}) collective-permute-start(f32[1,1536]{1,0:T(1,128)S(1)} %add.21), channel_id=1, source_target_pairs={{0,8},{24,16},{1,9},{25,17},{2,10},{26,18},{3,11},{27,19},{4,12},{... | collective-permute-start | bytes 18440 | tf_op jit(solution)/shard_map/ppermute | solution.py:155
  343.8 7.9 %collective-permute-start.50 = (f32[256,512]{1,0:T(8,128)}, f32[256,512]{1,0:T(8,128)S(1)}, u32[]{:S(2)}, u32[]{:S(2)}) collective-permute-start(f32[256,512]{1,0:T(8,128)} %get-tuple-element.905.refs_2_), channel_id=1, source_target_pairs={{8,16},{16,8},{9,17},{17,9},{10,18},{18,10},{11,19},{19,11},{12,20... | collective-permute-start | bytes 1572872 | tf_op jit(solution)/shard_map/ppermute | solution.py:484
  344.5 13.1 %collective-permute-start.49 = (f32[256,512]{1,0:T(8,128)}, f32[256,512]{1,0:T(8,128)S(1)}, u32[]{:S(2)}, u32[]{:S(2)}) collective-permute-start(f32[256,512]{1,0:T(8,128)} %get-tuple-element.907.refs_4_), channel_id=1, source_target_pairs={{0,8},{8,0},{16,24},{24,16},{1,9},{9,1},{17,25},{25,17},{2,10},{10... | collective-permute-start | bytes 1572872 | tf_op jit(solution)/shard_map/ppermute | solution.py:481
  350.4 11.8 %collective-permute-start.48 = (f32[1,1536]{1,0:T(1,128)S(1)}, f32[1,1536]{1,0:T(1,128)S(1)}, u32[]{:S(2)}, u32[]{:S(2)}) collective-permute-start(f32[1,1536]{1,0:T(1,128)S(1)} %add.23), channel_id=1, source_target_pairs={{8,0},{16,24},{9,1},{17,25},{10,2},{18,26},{11,3},{19,27},{12,4},{... | collective-permute-start | bytes 18440 | tf_op jit(solution)/shard_map/ppermute | solution.py:155
  359.7 9.9 %collective-permute-start.51 = (f32[256,512]{1,0:T(8,128)}, f32[256,512]{1,0:T(8,128)S(1)}, u32[]{:S(2)}, u32[]{:S(2)}) collective-permute-start(f32[256,512]{1,0:T(8,128)} %get-tuple-element.915.refs_2_), channel_id=1, source_target_pairs={{0,8},{8,0},{16,24},{24,16},{1,9},{9,1},{17,25},{25,17},{2,10},{10... | collective-permute-start | bytes 1572872 | tf_op jit(solution)/shard_map/ppermute | solution.py:481
  (32 other events, 310.6 us)

commit v6 on v5

--- a/solution.py
+++ b/solution.py
@@ -96,8 +96,8 @@
         return out
 
 
-def pack_kernel(order, sizes, me_ref, *refs):
-    ins, out_ref = refs[:-1], refs[-1]
+def pack_kernel(order, sizes, count, me_ref, *refs):
+    ins, out_ref = refs[:count], refs[-1]
     at, sizes = 0, list(sizes)
     for ref in ins:
         count = ref.shape[0]
@@ -110,19 +110,20 @@
         at += count * size
 
 
-def pack(order, sizes, me, *blocks):
+def pack(order, sizes, arriving, me, *blocks):
     return pl.pallas_call(
-        partial(pack_kernel, order, sizes),
+        partial(pack_kernel, order, sizes, len(blocks)),
         in_specs=[pl.BlockSpec(memory_space=pltpu.SMEM)]
-        + [pl.BlockSpec(memory_space=pltpu.VMEM)] * len(blocks),
+        + [pl.BlockSpec(memory_space=pltpu.VMEM)] * len(blocks)
+        + [pl.BlockSpec(memory_space=pl.ANY)] * len(arriving),
         out_specs=pl.BlockSpec(memory_space=pltpu.VMEM),
         out_shape=jax.ShapeDtypeStruct((len(order), sum(sizes)), WIDE),
         name="pack_vectors",
-    )(me, *blocks)
+    )(me, *blocks, *arriving)
 
 
 class Vectors:
-    def __init__(self, line, blocks):
+    def __init__(self, line, blocks, arriving):
         owners = lax.axis_size("batch")
         me = lax.axis_index("batch").astype(jnp.int32)
         self.line = line
@@ -135,13 +136,14 @@
             rows = [lax.dynamic_slice_in_dim(pieces, r ^ me, 1, 0) for r in order]
             self.held = jnp.concatenate(rows)
         else:
-            self.held = line.step(lambda *a: pack(order, self.sizes, *a), me[None], *blocks)
+            self.held = line.step(
+                lambda *a: pack(order, self.sizes, arriving, *a), me[None], *blocks
+            )
         count = lax.axis_size("seq")
         self.steps = [("swap", bit, 0) for bit in bits]
         self.steps += line_rounds(count) if count % 2 == 0 else []
         self.moving = None
         self.now = None
-        self.send()
 
     def send(self):
         if self.moving is not None or not self.steps:
@@ -219,15 +221,16 @@
         self.line, self.bits = line, bits
         self.pieces, self.outputs = [], {}
 
-    def prepare(self, target, pieces):
+    def prepare(self, target, pieces, *arrived):
         _, _, at, size = target
-        for left, left_in, block, right, right_in, (row, column) in pieces:
+        for left, left_in, block, right, right_in, (begin, each), (row, column) in pieces:
             wide = COLUMNS // Rounds.PARTS
             across = size[1] // wide
             starts = [((at[1] + i) * across + column) * wide for i in range(Rounds.PARTS)]
+            starts_in = [(begin + i * each) * wide for i in range(Rounds.PARTS)]
             right, right_in = (
-                jnp.concatenate([value[:, k : k + wide] for k in starts], axis=1)
-                for value in (right, right_in)
+                jnp.concatenate([value[:, k : k + wide] for k in places], axis=1)
+                for value, places in ((right, starts), (right_in, starts_in))
             )
             left = jnp.concatenate([left[block], rounded(left_in[block])], axis=0)
             right = jnp.concatenate([right, rounded(right_in)], axis=0)
@@ -236,6 +239,9 @@
 
     def step(self, *arrived):
         pass
+
+    def arriving(self):
+        return []
 
     def finished(self):
         return True
@@ -352,28 +358,31 @@
     def rows_spec(self, rows, at=0):
         return pl.BlockSpec((rows, self.wide), lambda i: (at, i))
 
-    def prepare(self, target, pieces):
+    def prepare(self, target, pieces, *arrived):
         r = self.made
         self.made += 1
-        self.targets.append((target, [piece[5] for piece in pieces]))
+        self.targets.append((target, [piece[-1] for piece in pieces]))
         count = len(pieces) // 2
         name, shape, at, size = target
         across = size[1] // self.wide
         args, specs = [], []
-        for left, left_in, block, right, right_in, (_, column) in pieces:
+        for left, left_in, block, right, right_in, (begin, each), (_, column) in pieces:
             for value in (left, left_in):
                 args += in_hbm(value) if value is left else [value]
                 specs.append(
                     pl.BlockSpec((1, *value.shape[1:]), lambda i, block=block: (block, 0, 0))
                 )
-            for value in (right, right_in):
+            mine = (at[1] * across + column, across)
+            for value, (begin, each) in ((right, mine), (right_in, (begin, each))):
                 args += in_hbm(value) if value is right else [value]
                 specs.append(
                     pl.BlockSpec(
                         (value.shape[0], self.wide),
-                        lambda i, c=column: (0, (at[1] + i) * across + c),
+                        lambda i, begin=begin, each=each: (0, begin + i * each),
                     )
                 )
+        args += arrived
+        specs += [pl.BlockSpec(memory_space=pl.ANY)] * len(arrived)
         rows = 2 * count * BLOCK
         total = rows + self.count(r - 1) * BLOCK
         call = pl.pallas_call(
@@ -383,7 +392,7 @@
             out_specs=[self.rows_spec(rows)] * 4,
             out_shape=[pltpu.HBM((total, COLUMNS), WIDE)] * 2
             + [pltpu.HBM((rows, COLUMNS), WIDE)] * 2,
-            cost_estimate=lasting(5.0),
+            cost_estimate=lasting(5),
         compiler_params=pltpu.CompilerParams(vmem_limit_bytes=25165824),
         name="piece_products",
         )
@@ -485,11 +494,29 @@
         if outward:
             self.outputs[name] = got.pop(0)
 
+    def arriving(self):
+        return [*self.moving[self.at], self.end, self.middle]
+
     def finished(self):
         return self.at == len(self.counts) + 4
 
     def results(self):
         return self.outputs
+
+
+def settle_kernel(*refs):
+    refs[-1][...] = jnp.zeros_like(refs[-1])
+
+
+def settle(arriving):
+    return pl.pallas_call(
+        settle_kernel,
+        in_specs=[pl.BlockSpec(memory_space=pl.ANY)] * len(arriving),
+        out_specs=pl.BlockSpec(memory_space=pltpu.VMEM),
+        out_shape=jax.ShapeDtypeStruct((8, 128), WIDE),
+        cost_estimate=lasting(12),
+        name="settle",
+    )(*arriving)
 
 
 def pick_kernel(me_ref, *refs):
@@ -796,7 +823,6 @@
             pltpu.HBM((5, D), WIDE),
             pltpu.HBM((1, 3 * D), WIDE),
         ],
-        cost_estimate=lasting(9.0),
         compiler_params=pltpu.CompilerParams(vmem_limit_bytes=25165824),
         name="norm_back",
     )(*in_hbm(qkv_grad, qkv_weight, mlp_norm_grad, unit, rate, cot, *gains))
@@ -1085,7 +1111,7 @@
     tables_ref,
     mix_ref,
     out_ref,
-    send_ref,
+    *send_refs,
 ):
     context = tables_ref.shape[1]
     first = first_ref[0]
@@ -1116,7 +1142,15 @@
         axis=1,
     ).astype(NARROW)
     out_ref[...] = grad
-    send_ref[...] = grad.astype(WIDE)
+    wide = grad.astype(WIDE)
+    for step in range(HEADS // 2):
+
+        @pl.when(pl.program_id(0) == step)
+        def _(step=step):
+            for k in range(3):
+                at = (3 * step + k) * PAIR
+                ref, at = (send_refs[0], at) if at < D else (send_refs[1], at - D)
+                ref[:, at : at + PAIR] = wide[:, k * PAIR : (k + 1) * PAIR]
 
 
 def pass_kernel(lengths_ref, first_ref, own_ref, arrived_ref, out_ref):
@@ -1226,12 +1260,13 @@
         partial(last_kernel, seqs),
         grid=(HEADS // 2,),
         in_specs=[SMEM_SPEC, SMEM_SPEC] + [pair_spec(tokens)] * 7 + [carry, *shared],
-        out_specs=[pl.BlockSpec((tokens, 3 * PAIR), lambda i: (0, i))] * 2,
+        out_specs=[pl.BlockSpec((tokens, 3 * PAIR), lambda i: (0, i))]
+        + [whole_spec((tokens, D)), whole_spec((tokens, 2 * D))],
         out_shape=[
             pltpu.HBM((tokens, 3 * D), NARROW),
-            pltpu.HBM((tokens, 3 * D), WIDE),
-        ],
-        cost_estimate=lasting(10.0),
+        ]
+        + [pltpu.HBM((tokens, D), WIDE), pltpu.HBM((tokens, 2 * D), WIDE)],
+        cost_estimate=lasting(10),
         compiler_params=pltpu.CompilerParams(vmem_limit_bytes=25165824),
         name="attention_last",
     )(*in_hbm(lengths, first, *rest))
@@ -1271,14 +1306,16 @@
     else:
         reduction = Singly(line, bits)
 
-    def group(name, shape, at, left, blocks, right, columns):
+    def group(name, shape, at, left, blocks, right, rights_in, columns, begin=0, arrived=()):
+        many = len(rights_in)
         pieces = [
-            (*left, block, *right, (row, column))
+            (*left, block, right, rights_in[column % many], place, (row, column))
             for column in range(columns)
             for row, block in enumerate(blocks)
+            for place in [(begin + column, columns) if many == 1 else (0, 1)]
         ]
         size = (len(blocks) * BLOCK_ROWS, columns * COLUMNS // Rounds.PARTS)
-        reduction.prepare((name, shape, at, size), pieces)
+        reduction.prepare((name, shape, at, size), pieces, *arrived)
 
     BLOCK_ROWS = min(BLOCK, D // owners)
     inputs_flat = inputs.reshape(tokens, D)
@@ -1299,7 +1336,7 @@
     def down_group(sub):
         shape = (FF // owners, D)
         at = (sub // 2, 0)
-        group("down", shape, at, (act_own, act_in), (sub, sub + 1), (cot, cot_in), across)
+        group("down", shape, at, (act_own, act_in), (sub, sub + 1), cot, [cot_in], across)
 
     down_group(0)
     up_grad, up_send, up_sums, mlp_out, mlp_norm_grad = line.step(
@@ -1328,7 +1365,7 @@
         shape = (D // owners, FF)
         at = (0, part * Rounds.PARTS)
         columns = FF // COLUMNS // 2
-        group("up", shape, at, (norm_own, norm_in), (1,), (up_grad, up_in), columns)
+        group("up", shape, at, (norm_own, norm_in), (1,), up_grad, [up_in], columns, part * Rounds.PARTS * columns)
 
     up_group(0)
     for _ in range(hops - 1):
@@ -1371,8 +1408,9 @@
         passed = line.step(pass_on, carry_back, arrived_back, lengths, first)
         arrived_back = shift_rows(passed, "seq", -1)
     shape = (D // owners, D)
-    group("dense", shape, (0, 0), (low_own, low_in), (0,), (cot, cot_in), across)
-    qkv_grad, qkv_send = line.step(
+    group("dense", shape, (0, 0), (low_own, low_in), (0,), cot, [cot_in], across)
+    reduction.step()
+    qkv_grad, *qkv_send = line.step(
         attention_last,
         lengths,
         first,
@@ -1387,8 +1425,19 @@
         tables,
         mix,
     )
+    qkv_in = [swap(qkv_send[0], 0)]
+    qkv_rest = swap(qkv_send[1], 0)
+    def qkv_group(part, *arrived):
+        shape = (D // owners, 3 * D)
+        at = (0, part * Rounds.PARTS)
+        left = (norm_own, norm_in)
+        group("qkv", shape, at, left, (0,), qkv_grad, qkv_in, 2, max(part - 1, 0) * 4, arrived)
+
+    arriving = reduction.arriving()
+    qkv_group(0, *([line.step(lambda *a: settle(a), *arriving)] if arriving else []))
     reduction.step()
-    qkv_in = line.send(qkv_send, lambda a: swap(a, 0))
+    qkv_in = [qkv_rest]
+    qkv_group(1)
     input_grad, sums, qkv_sums = line.step(
         norm_back,
         qkv_grad,
@@ -1401,15 +1450,8 @@
         ln2_gain,
     )
 
-    def qkv_group(part):
-        shape = (D // owners, 3 * D)
-        at = (0, part * Rounds.PARTS)
-        group("qkv", shape, at, (norm_own, norm_in), (0,), (qkv_grad, qkv_in), 2)
-
-    qkv_group(0)
-    reduction.step()
-    qkv_group(1)
-    vectors = Vectors(line, (sums, qkv_sums, up_sums))
+    vectors = Vectors(line, (sums, qkv_sums, up_sums), [])
+    vectors.send()
     reduction.step()
     qkv_group(2)
     vectors.take()

time: 374 us -> 368 us (0.984)
  waiting for transfers between devices: 112 us -> 97.4 us
    ppermute x4, waiting for transfers between devices: 18.4 us -> 9.98 us  [shift_rows(): lax.ppermute(value, axis, [(i, i + by) for i in range(count) if 0 <= i +...]
    ppermute x10, starting transfers between devices: 33.1 us -> 27.8 us  [step(): self.end = lax.ppermute(self.whole, 'seq', [(0, 1), (1, 0), (2, 3), (3, 2)])]
    ppermute x27 -> x28, starting transfers between devices: 25.1 us -> 29.3 us  [swap(): lax.ppermute(value, 'batch', [(i, i ^ 1 << bit) for i in range(count)])]
    ppermute x27 -> x28, waiting for transfers between devices: 59.3 us -> 57.2 us  [swap(): lax.ppermute(value, 'batch', [(i, i ^ 1 << bit) for i in range(count)])]
  transfers between devices with their start and end apart: 52 -> 53, of which waited for: 24 -> 23; matrix products, arithmetic and copies ran while one was open for 1% -> 1% of each run, Pallas kernels for 33% -> 36%
where the time goes in v6:
time: 368 us; the launch traced here: 367 us
  Pallas kernels  175 us (48%)
  waiting for transfers between devices  97.4 us (26%)
  starting transfers between devices  83 us (23%)
  local copies, waits for them, and re-layouts  8.45 us (2%)
    pallas_call x20, Pallas kernels, step(): out = function(*self.wait(*values))  76.2 us
    ppermute x28, waiting for transfers between devices, swap(): lax.ppermute(value, 'batch', [(i, i ^ 1 << bit) for i in range(count)])  57.2 us
    ppermute x28, starting transfers between devices, swap(): lax.ppermute(value, 'batch', [(i, i ^ 1 << bit) for i in range(count)])  29.3 us
    ppermute x10, waiting for transfers between devices, step(): self.end = lax.ppermute(self.whole, 'seq', [(0, 1), (1, 0), (2, 3), (3, 2)])  28.7 us
    ppermute x10, starting transfers between devices, step(): self.end = lax.ppermute(self.whole, 'seq', [(0, 1), (1, 0), (2, 3), (3, 2)])  27.8 us
    pallas_call x1, Pallas kernels, attention_middle(): pl.pallas_call(partial(middle_kernel, seqs), grid=(pairs,), in_specs=[SME...  19.9 us
    pallas_call x1, Pallas kernels, mlp_back(): pl.pallas_call(back_kernel, grid=(FF // each,), in_specs=[total, pl.Block...  16 us
    pallas_call x1, Pallas kernels, attention_local(): pl.pallas_call(partial(local_kernel, seqs), grid=(pairs,), in_specs=[SMEM...  14.3 us
  transfers between devices with their start and end apart: 53, of which 23 were waited for; matrix products, arithmetic and copies ran while one was open for 1% of the time, Pallas kernels for 36%

profile of v6, /device:TPU:0, one launch (start us, length us, event | category | flops | bytes accessed | tf_op | source)
XLA Modules:
  0.0 366.7 jit_solution(9255254834336652682)
XLA Ops:
  0.7 3.9 %two_norms.1 = (bf16[256,1024]{1,0:T(8,128)(2,1)}, bf16[256,1024]{1,0:T(8,128)(2,1)}, f32[256,1024]{1,0:T(8,128)}, f32[256,128]{1,0:T(8,128)}) custom-call(bf16[256,1024]{1,0:T(8,128)(2,1)} %bitcast.37, bf16[1024]{0:T(1024)(128)(2,1)} %gain1.2, bf16[1024]{0:T(1024)(128)(2,1)} %bias1.1, bf16[1024]{0:T(1024)(128)(2,1)} %gain2.2, bf16[1024]{0:T(1024)(128)(2,1)} %bias2.1), custom_call_target="tpu_custom_call" | custom-call | flops 4600000000 | tf_op jit(solution)/shard_map/two_norms/pallas_call | solution.py:588
  4.6 11.1 %mlp_up.1 = (bf16[256,4096]{1,0:T(8,128)(2,1)}, f32[256,4096]{1,0:T(8,128)}, bf16[4,256,512]{2,1,0:T(8,128)(2,1)}, f32[4,256,512]{2,1,0:T(8,128)}) custom-call(s32[1]{0:T(128)} %bitcast.5.me_ref, bf16[256,1024]{1,0:T(8,128)(2,1)} %get-tuple-element.483.x_ref.refs_1_, bf16[1024,4096]{1,0:T(8,128)(2,1)} %up_ref, bf16[4096]{0:T(1024)(128)(2,1)} %bias_ref), custom_call_target="tpu_custom_call" | custom-call | flops 12650000384 | tf_op jit(solution)/shard_map/mlp_up/pallas_call | solution.py:636
  18.3 2.8 pick_columns.2
  21.6 4.6 %piece_products.8 = (f32[512,512]{1,0:T(8,128)}, f32[512,512]{1,0:T(8,128)}, f32[512,512]{1,0:T(8,128)}, f32[512,512]{1,0:T(8,128)}) custom-call(bf16[4,256,512]{2,1,0:T(8,128)(2,1)} %get-tuple-element.524.refs_0_.refs_4_.refs_8_.refs_12_, f32[4,256,512]{2,1,0:T(8,128)S(1)} %collective-permute-done.refs_1_.refs_5_.refs_9_.refs_13_, ...), custom_call_target="tpu_custom_call" | custom-call | flops 5750000128 | tf_op jit(solution)/shard_map/piece_products/pallas_call | solution.py:94
  26.2 2.9 collective-permute-start.2
  30.6 16.0 %mlp_back.1 = (bf16[256,4096]{1,0:T(8,128)(2,1)}, f32[256,4096]{1,0:T(8,128)}, f32[1,4096]{1,0:T(1,128)}, f32[256,1024]{1,0:T(8,128)}, f32[256,1024]{1,0:T(8,128)}) custom-call(bf16[256,1024]{1,0:T(8,128)(2,1)} %bitcast.26, bf16[4096,1024]{1,0:T(8,128)(2,1)} %down_ref, bf16[1024,4096]{1,0:T(8,128)(2,1)} %up_ref, ...), custom_call_target="tpu_custom_call" | custom-call | flops 18400000000 | tf_op jit(solution)/shard_map/mlp_back/pallas_call | solution.py:700
  46.7 4.4 %piece_products.9 = (f32[768,512]{1,0:T(8,128)}, f32[768,512]{1,0:T(8,128)}, f32[512,512]{1,0:T(8,128)}, f32[512,512]{1,0:T(8,128)}) custom-call(bf16[4,256,512]{2,1,0:T(8,128)(2,1)} %get-tuple-element.524.refs_0_.refs_4_.refs_8_.refs_12_, f32[4,256,512]{2,1,0:T(8,128)S(1)} %collective-permute-done.refs_1_.refs_5_.refs_9_.refs_13_, ...), custom_call_target="tpu_custom_call" | custom-call | flops 5750000128 | tf_op jit(solution)/shard_map/piece_products/pallas_call | solution.py:94
  51.0 3.2 collective-permute-done.3.refs_2_
  54.3 2.9 reduce_round.12
  60.0 14.3 %attention_local.1 = (bf16[8,256,128]{2,1,0:T(8,128)(2,1)}, bf16[8,256,128]{2,1,0:T(8,128)(2,1)}, bf16[8,256,128]{2,1,0:T(8,128)(2,1)}, f32[8,256,128]{2,1,0:T(8...) custom-call(s32[2,3]{1,0:T(2,128)S(1)} %copy-done.10, ...), custom_call_target="tpu_custom_call" | custom-call | flops 16099999744 | tf_op jit(solution)/shard_map/attention_local/pallas_call | solution.py:1201
  74.3 3.5 collective-permute-start.4
  77.9 5.8 %piece_products.10 = (f32[768,512]{1,0:T(8,128)}, f32[768,512]{1,0:T(8,128)}, f32[512,512]{1,0:T(8,128)}, f32[512,512]{1,0:T(8,128)}) custom-call(bf16[2,256,512]{2,1,0:T(8,128)(2,1)} %get-tuple-element.818.refs_0_.refs_4_.refs_8_.refs_12_, f32[2,256,512]{2,1,0:T(8,128)S(1)} %collective-permute-done.5.refs_1_.refs_5_.refs_9_.refs_13_, ...), custom_call_target="tpu_custom_call" | custom-call | flops 5750000128 | tf_op jit(solution)/shard_map/piece_products/pallas_call | solution.py:94
  83.7 7.1 %collective-permute-done.4.arrived_ref = f32[2,8,72,128]{3,2,1,0:T(8,128)S(1)} collective-permute-done((f32[2,8,72,128]{3,2,1,0:T(8,128)}, f32[2,8,72,128]{3,2,1,0:T(8,128)S(1)}, u32[]{:S(2)}, u32[]{:S(2)}) %collective-permute-start.4) | collective-permute-done | bytes 589856 | tf_op jit(solution)/shard_map/ppermute | solution.py:47
  93.7 4.3 %collective-permute-start.7 = (f32[2,8,72,128]{3,2,1,0:T(8,128)}, f32[2,8,72,128]{3,2,1,0:T(8,128)S(1)}, u32[]{:S(2)}, u32[]{:S(2)}) collective-permute-start(f32[2,8,72,128]{3,2,1,0:T(8,128)} %pass_carry.2), channel_id=1, source_target_pairs={{0,8},{8,16},{16,24},{1,9},{9,17},{17,25},{2,10},{10,18},{18,26},{... | collective-permute-start | bytes 1769480 | tf_op jit(solution)/shard_map/ppermute | solution.py:47
  98.1 4.1 %reduce_round.13 = (f32[768,512]{1,0:T(8,128)}, f32[768,512]{1,0:T(8,128)}, f32[256,512]{1,0:T(8,128)}, f32[256,512]{1,0:T(8,128)}, f32[512,512]{1,0:T(8,128)}, /*index=5*/f32[512,512]{1,0:T(8,128)}) custom-call(s32[1]{0:T(128)} %bitcast.4.refs_0_, f32[768,512]{1,0:T(8,128)S(1)} %collective-permute-done.8.refs_1_, ...), custom_call_target="tpu_custom_call", output_to_operand_aliasing={{0}: (7, {}), {1}: (8, {})} | custom-call | flops 5750000128 | tf_op jit(solution)/shard_map/reduce_round/pallas_call | solution.py:94
  105.7 4.5 %piece_products.11 = (f32[768,512]{1,0:T(8,128)}, f32[768,512]{1,0:T(8,128)}, f32[512,512]{1,0:T(8,128)}, f32[512,512]{1,0:T(8,128)}) custom-call(bf16[2,256,512]{2,1,0:T(8,128)(2,1)} %get-tuple-element.818.refs_0_.refs_4_.refs_8_.refs_12_, f32[2,256,512]{2,1,0:T(8,128)S(1)} %collective-permute-done.5.refs_1_.refs_5_.refs_9_.refs_13_, ...), custom_call_target="tpu_custom_call" | custom-call | flops 5750000128 | tf_op jit(solution)/shard_map/piece_products/pallas_call | solution.py:94
  112.9 19.9 %attention_middle.1 = (bf16[256,1024]{1,0:T(8,128)(2,1)}, bf16[8,256,128]{2,1,0:T(8,128)(2,1)}, f32[8,256,128]{2,1,0:T(8,128)}, f32[8,256,128]{2,1,0:T(8,128)}, f32[2,8,72,128]{3,2,1,0:T(8,128)}) custom-call(s32[2,3]{1,0:T(2,128)S(1)} %copy-done.11, s32[2]{0:T(128)S(1)} %copy-done.16, bf16[256,1024]{1,0:T(8,128)(2,1)} %bitcast.31, ...), custom_call_target="tpu_custom_call" | custom-call | flops 23000000512 | tf_op jit(solution)/shard_map/attention_middle/pallas_call | solution.py:1234
  136.4 3.8 %collective-permute-done.11.refs_2_ = f32[768,512]{1,0:T(8,128)} collective-permute-done((f32[768,512]{1,0:T(8,128)}, f32[768,512]{1,0:T(8,128)}, u32[]{:S(2)}, u32[]{:S(2)}) %collective-permute-start.11) | collective-permute-done | bytes 1572896 | tf_op jit(solution)/shard_map/ppermute | solution.py:63
  140.3 4.7 %reduce_round.14 = (f32[768,512]{1,0:T(8,128)}, f32[768,512]{1,0:T(8,128)}, f32[256,512]{1,0:T(8,128)}, f32[256,512]{1,0:T(8,128)}, f32[512,512]{1,0:T(8,128)}, /*index=5*/f32[512,512]{1,0:T(8,128)}, f32[512,512]{1,0:T(8,128)}) custom-call(s32[1]{0:T(128)} %bitcast.4.refs_0_, ...), custom_call_target="tpu_custom_call", output_to_operand_aliasing={{0}: (9, {}), {1}: (10, {})} | custom-call | flops 5750000128 | tf_op jit(solution)/shard_map/reduce_round/pallas_call | solution.py:94
  149.3 3.4 layer_output.1
  157.3 3.0 piece_products.12
  160.3 12.1 %collective-permute-done.17.refs_8_ = f32[512,512]{1,0:T(8,128)} collective-permute-done((f32[512,512]{1,0:T(8,128)}, f32[512,512]{1,0:T(8,128)}, u32[]{:S(2)}, u32[]{:S(2)}) %collective-permute-start.17) | collective-permute-done | bytes 1048608 | tf_op jit(solution)/shard_map/ppermute | solution.py:490
  172.4 6.7 %collective-permute-done.16.refs_2_ = f32[768,512]{1,0:T(8,128)S(1)} collective-permute-done((f32[768,512]{1,0:T(8,128)}, f32[768,512]{1,0:T(8,128)S(1)}, u32[]{:S(2)}, u32[]{:S(2)}) %collective-permute-start.16) | collective-permute-done | bytes 1572896 | tf_op jit(solution)/shard_map/ppermute | solution.py:63
  179.4 5.4 %reduce_round.15 = (f32[512,512]{1,0:T(8,128)}, f32[512,512]{1,0:T(8,128)}, f32[256,512]{1,0:T(8,128)}, f32[256,512]{1,0:T(8,128)}, f32[512,512]{1,0:T(8,128)}, /*index=5*/f32[512,512]{1,0:T(8,128)}, f32[512,512]{1,0:T(8,128)}) custom-call(s32[1]{0:T(128)} %bitcast.4.refs_0_, ...), custom_call_target="tpu_custom_call", output_to_operand_aliasing={{0}: (11, {}), {1}: (12, {})} | custom-call | flops 5750000128 | tf_op jit(solution)/shard_map/reduce_round/pallas_call | solution.py:94
  187.0 2.7 collective-permute-start.23
  191.4 10.5 %attention_last.1 = (bf16[256,3072]{1,0:T(8,128)(2,1)}, f32[256,1024]{1,0:T(8,128)}, f32[256,2048]{1,0:T(8,128)}) custom-call(s32[2,3]{1,0:T(2,128)S(1)} %copy-done.12, s32[2]{0:T(128)S(1)} %copy-done.17, bf16[8,256,128]{2,1,0:T(8,128)(2,1)} %get-tuple-element.708.gradq_ref, f32[8,256,128]{2,1,0:T(8,128)} %get-tuple-element.709.gradk_ref, ...), custom_call_target="tpu_custom_call" | custom-call | flops 11500000256 | tf_op jit(solution)/shard_map/attention_last/pallas_call | solution.py:1259
  201.9 7.6 %collective-permute-done.22.refs_1_.refs_2_ = f32[512,512]{1,0:T(8,128)S(1)} collective-permute-done((f32[512,512]{1,0:T(8,128)}, f32[512,512]{1,0:T(8,128)S(1)}, u32[]{:S(2)}, u32[]{:S(2)}) %collective-permute-start.22) | collective-permute-done | bytes 1048608 | tf_op jit(solution)/shard_map/ppermute | solution.py:63
  213.6 3.4 piece_products.13
  217.0 5.3 %reduce_round.16 = (f32[384,512]{1,0:T(8,128)}, f32[384,512]{1,0:T(8,128)}, f32[128,512]{1,0:T(8,128)}, f32[128,512]{1,0:T(8,128)}, f32[512,512]{1,0:T(8,128)}, ...) custom-call(s32[1]{0:T(128)} %bitcast.4.refs_0_, ...), custom_call_target="tpu_custom_call", output_to_operand_aliasing={{0}: (12, {}), {1}: (13, {})} | custom-call | flops 5750000128 | tf_op jit(solution)/shard_map/reduce_round/pallas_call | solution.py:94
  222.3 3.7 %collective-permute-start.29 = (f32[512,512]{1,0:T(8,128)}, f32[512,512]{1,0:T(8,128)}, u32[]{:S(2)}, u32[]{:S(2)}) collective-permute-start(f32[512,512]{1,0:T(8,128)} %get-tuple-element.809.refs_11_), channel_id=1, source_target_pairs={{0,8},{8,0},{16,24},{24,16},{1,9},{9,1},{17,25},{25,17},{2,10},{10... | collective-permute-start | bytes 3145736 | tf_op jit(solution)/shard_map/ppermute | solution.py:490
  229.5 3.1 piece_products.14
  232.6 9.3 %norm_back.1 = (f32[256,1024]{1,0:T(8,128)}, f32[5,1024]{1,0:T(8,128)}, f32[1,3072]{1,0:T(1,128)}) custom-call(bf16[256,3072]{1,0:T(8,128)(2,1)} %get-tuple-element.820.refs_2_.refs_6_.qkv_ref, bf16[1024,3072]{1,0:T(8,128)(2,1)} %weight_ref.3, f32[256,1024]{1,0:T(8,128)} %get-tuple-element.773.mlp_ref, f32[256,1024]{1,0:T(8,128)} %get-tuple-element.774.unit_ref, ...), custom_call_target="tpu_custom_call" | custom-call | tf_op jit(solution)/shard_map/norm_back/pallas_call | solution.py:808
  247.7 5.2 %reduce_round.17 = (f32[384,512]{1,0:T(8,128)}, f32[384,512]{1,0:T(8,128)}, f32[128,512]{1,0:T(8,128)}, f32[128,512]{1,0:T(8,128)}, f32[256,512]{1,0:T(8,128)}, ...) custom-call(s32[1]{0:T(128)} %bitcast.4.refs_0_, ...), custom_call_target="tpu_custom_call", output_to_operand_aliasing={{0}: (12, {}), {1}: (13, {}), {7}: (14, {})} | custom-call | flops 5750000128 | tf_op jit(solution)/shard_map/reduce_round/pallas_call | solution.py:94
  252.9 3.7 %collective-permute-start.34 = (f32[512,512]{1,0:T(8,128)}, f32[512,512]{1,0:T(8,128)S(1)}, u32[]{:S(2)}, u32[]{:S(2)}) collective-permute-start(f32[512,512]{1,0:T(8,128)} %get-tuple-element.846.refs_11_), channel_id=1, source_target_pairs={{0,8},{8,0},{16,24},{24,16},{1,9},{9,1},{17,25},{25,17},{2,10},{10... | collective-permute-start | bytes 3145736 | tf_op jit(solution)/shard_map/ppermute | solution.py:490
  260.8 3.2 piece_products.15
  264.0 12.6 %collective-permute-done.33.refs_2_ = f32[384,512]{1,0:T(8,128)S(1)} collective-permute-done((f32[384,512]{1,0:T(8,128)}, f32[384,512]{1,0:T(8,128)S(1)}, u32[]{:S(2)}, u32[]{:S(2)}) %collective-permute-start.33) | collective-permute-done | bytes 786464 | tf_op jit(solution)/shard_map/ppermute | solution.py:63
  277.3 3.9 %reduce_round.18 = (f32[384,512]{1,0:T(8,128)}, f32[384,512]{1,0:T(8,128)}, f32[128,512]{1,0:T(8,128)}, f32[128,512]{1,0:T(8,128)}, f32[256,512]{1,0:T(8,128)}, ...) custom-call(s32[1]{0:T(128)} %bitcast.4.refs_0_, ...), custom_call_target="tpu_custom_call", output_to_operand_aliasing={{0}: (12, {}), {1}: (13, {})} | custom-call | flops 5750000128 | tf_op jit(solution)/shard_map/reduce_round/pallas_call | solution.py:94
  281.2 3.7 %collective-permute-start.39 = (f32[512,512]{1,0:T(8,128)}, f32[512,512]{1,0:T(8,128)S(1)}, u32[]{:S(2)}, u32[]{:S(2)}) collective-permute-start(f32[512,512]{1,0:T(8,128)} %get-tuple-element.873.refs_11_), channel_id=1, source_target_pairs={{0,8},{8,0},{16,24},{24,16},{1,9},{9,1},{17,25},{25,17},{2,10},{10... | collective-permute-start | bytes 3145736 | tf_op jit(solution)/shard_map/ppermute | solution.py:490
  284.9 3.2 collective-permute-start.38
  290.8 14.2 %collective-permute-done.31 = f32[2,1536]{1,0:T(2,128)S(1)} collective-permute-done((f32[2,1536]{1,0:T(2,128)S(1)}, f32[2,1536]{1,0:T(2,128)S(1)}, u32[]{:S(2)}, u32[]{:S(2)}) %collective-permute-start.31) | collective-permute-done | bytes 12320 | tf_op jit(solution)/shard_map/ppermute | solution.py:63
  305.1 3.6 reduce_round.19
  310.7 4.7 %collective-permute-start.43 = (f32[128,512]{1,0:T(8,128)}, f32[128,512]{1,0:T(8,128)S(1)}, u32[]{:S(2)}, u32[]{:S(2)}) collective-permute-start(f32[128,512]{1,0:T(8,128)} %get-tuple-element.879), channel_id=1, source_target_pairs={{0,4},{1,5},{2,6},{3,7},{4,0},{5,1},{6,2},{7,3},{8,12},{9,13},{10,... | collective-permute-start | bytes 786440 | tf_op jit(solution)/shard_map/ppermute | solution.py:63
  317.1 3.6 collective-permute-done.36
  322.0 2.7 reduce_round.20
  327.2 4.9 %collective-permute-start.41 = (f32[1,1536]{1,0:T(1,128)S(1)}, f32[1,1536]{1,0:T(1,128)S(1)}, u32[]{:S(2)}, u32[]{:S(2)}) collective-permute-start(f32[1,1536]{1,0:T(1,128)S(1)} %add.21), channel_id=1, source_target_pairs={{0,8},{24,16},{1,9},{25,17},{2,10},{26,18},{3,11},{27,19},{4,12},{... | collective-permute-start | bytes 18440 | tf_op jit(solution)/shard_map/ppermute | solution.py:157
  337.1 6.7 %collective-permute-start.50 = (f32[256,512]{1,0:T(8,128)}, f32[256,512]{1,0:T(8,128)S(1)}, u32[]{:S(2)}, u32[]{:S(2)}) collective-permute-start(f32[256,512]{1,0:T(8,128)} %get-tuple-element.917.refs_4_), channel_id=1, source_target_pairs={{0,8},{8,0},{16,24},{24,16},{1,9},{9,1},{17,25},{25,17},{2,10},{10... | collective-permute-start | bytes 1572872 | tf_op jit(solution)/shard_map/ppermute | solution.py:490
  345.8 7.0 %collective-permute-done.50.refs_1_ = f32[256,512]{1,0:T(8,128)S(1)} collective-permute-done((f32[256,512]{1,0:T(8,128)}, f32[256,512]{1,0:T(8,128)S(1)}, u32[]{:S(2)}, u32[]{:S(2)}) %collective-permute-start.50) | collective-permute-done | bytes 524320 | tf_op jit(solution)/shard_map/ppermute | solution.py:490
  358.7 5.6 %collective-permute-done.52.refs_1_ = f32[256,512]{1,0:T(8,128)S(1)} collective-permute-done((f32[256,512]{1,0:T(8,128)}, f32[256,512]{1,0:T(8,128)S(1)}, u32[]{:S(2)}, u32[]{:S(2)}) %collective-permute-start.52) | collective-permute-done | bytes 524320 | tf_op jit(solution)/shard_map/ppermute | solution.py:490
  (165 shorter events, 77.0 us)
Async XLA Ops:
  26.2 28.0 %collective-permute-start.2 = (f32[512,512]{1,0:T(8,128)}, f32[512,512]{1,0:T(8,128)S(1)}, u32[]{:S(2)}, u32[]{:S(2)}) collective-permute-start(f32[512,512]{1,0:T(8,128)} %get-tuple-element.501), channel_id=1, source_target_pairs={{0,2},{1,3},{2,0},{3,1},{4,6},{5,7},{6,4},{7,5},{8,10},{9,11},{10,... | collective-permute-start | bytes 3145736 | tf_op jit(solution)/shard_map/ppermute | solution.py:63
  29.1 25.1 %collective-permute-start.3 = (f32[512,512]{1,0:T(8,128)}, f32[512,512]{1,0:T(8,128)S(1)}, u32[]{:S(2)}, u32[]{:S(2)}) collective-permute-start(f32[512,512]{1,0:T(8,128)} %get-tuple-element.502), channel_id=1, source_target_pairs={{0,4},{1,5},{2,6},{3,7},{4,0},{5,1},{6,2},{7,3},{8,12},{9,13},{10,... | collective-permute-start | bytes 3145736 | tf_op jit(solution)/shard_map/ppermute | solution.py:63
  57.7 20.2 %collective-permute-start.6 = (f32[256,4096]{1,0:T(8,128)S(1)}, f32[256,4096]{1,0:T(8,128)S(1)}, u32[]{:S(2)}, u32[]{:S(2)}) collective-permute-start(f32[256,4096]{1,0:T(8,128)S(1)} %copy-done.23), channel_id=1, source_target_pairs={{0,1},{1,0},{2,3},{3,2},{4,5},{5,4},{6,7},{7,6},{8,9},{9,8},{10,11... | collective-permute-start | bytes 12582920 | tf_op jit(solution)/shard_map/ppermute | solution.py:63
  57.7 40.4 %collective-permute-start.8 = (f32[768,512]{1,0:T(8,128)}, f32[768,512]{1,0:T(8,128)S(1)}, u32[]{:S(2)}, u32[]{:S(2)}) collective-permute-start(f32[768,512]{1,0:T(8,128)} %get-tuple-element.540), channel_id=1, source_target_pairs={{0,2},{1,3},{2,0},{3,1},{4,6},{5,7},{6,4},{7,5},{8,10},{9,11},{10,... | collective-permute-start | bytes 4718600 | tf_op jit(solution)/shard_map/ppermute | solution.py:63
  58.1 19.8 %collective-permute-start.5 = (f32[2,256,512]{2,1,0:T(8,128)S(1)}, f32[2,256,512]{2,1,0:T(8,128)S(1)}, u32[]{:S(2)}, u32[]{:S(2)}) collective-permute-start(f32[2,256,512]{2,1,0:T(8,128)S(1)} %copy-done.24), channel_id=1, source_target_pairs={{0,1},{1,0},{2,3},{3,2},{4,5},{5,4},{6,7},{7,6},{8,9},{9,8},{10,11... | collective-permute-start | bytes 3145736 | tf_op jit(solution)/shard_map/ppermute | solution.py:63
  58.3 39.8 %collective-permute-start.9 = (f32[768,512]{1,0:T(8,128)}, f32[768,512]{1,0:T(8,128)}, u32[]{:S(2)}, u32[]{:S(2)}) collective-permute-start(f32[768,512]{1,0:T(8,128)} %get-tuple-element.584), channel_id=1, source_target_pairs={{0,4},{1,5},{2,6},{3,7},{4,0},{5,1},{6,2},{7,3},{8,12},{9,13},{10,... | collective-permute-start | bytes 4718600 | tf_op jit(solution)/shard_map/ppermute | solution.py:63
  74.3 16.5 %collective-permute-start.4 = (f32[2,8,72,128]{3,2,1,0:T(8,128)}, f32[2,8,72,128]{3,2,1,0:T(8,128)S(1)}, u32[]{:S(2)}, u32[]{:S(2)}) collective-permute-start(f32[2,8,72,128]{3,2,1,0:T(8,128)} %get-tuple-element.581.own_ref), channel_id=1, source_target_pairs={{0,8},{8,16},{16,24},{1,9},{9,17},{17,25},{2,10},{10,18},{18,26},{... | collective-permute-start | bytes 1769480 | tf_op jit(solution)/shard_map/ppermute | solution.py:47
  93.7 18.4 %collective-permute-start.7 = (f32[2,8,72,128]{3,2,1,0:T(8,128)}, f32[2,8,72,128]{3,2,1,0:T(8,128)S(1)}, u32[]{:S(2)}, u32[]{:S(2)}) collective-permute-start(f32[2,8,72,128]{3,2,1,0:T(8,128)} %pass_carry.2), channel_id=1, source_target_pairs={{0,8},{8,16},{16,24},{1,9},{9,17},{17,25},{2,10},{10,18},{18,26},{... | collective-permute-start | bytes 1769480 | tf_op jit(solution)/shard_map/ppermute | solution.py:47
  102.2 38.1 %collective-permute-start.10 = (f32[768,512]{1,0:T(8,128)}, f32[768,512]{1,0:T(8,128)S(1)}, u32[]{:S(2)}, u32[]{:S(2)}) collective-permute-start(f32[768,512]{1,0:T(8,128)} %get-tuple-element.599), channel_id=1, source_target_pairs={{0,2},{1,3},{2,0},{3,1},{4,6},{5,7},{6,4},{7,5},{8,10},{9,11},{10,... | collective-permute-start | bytes 4718600 | tf_op jit(solution)/shard_map/ppermute | solution.py:63
  103.7 32.7 %collective-permute-start.12 = (f32[512,512]{1,0:T(8,128)}, f32[512,512]{1,0:T(8,128)}, u32[]{:S(2)}, u32[]{:S(2)}) collective-permute-start(f32[512,512]{1,0:T(8,128)} %get-tuple-element.640), channel_id=1, source_target_pairs={{0,8},{8,0},{16,24},{24,16},{1,9},{9,1},{17,25},{25,17},{2,10},{10... | collective-permute-start | bytes 3145736 | tf_op jit(solution)/shard_map/ppermute | solution.py:490
  105.2 35.0 %collective-permute-start.11 = (f32[768,512]{1,0:T(8,128)}, f32[768,512]{1,0:T(8,128)}, u32[]{:S(2)}, u32[]{:S(2)}) collective-permute-start(f32[768,512]{1,0:T(8,128)} %get-tuple-element.634), channel_id=1, source_target_pairs={{0,4},{1,5},{2,6},{3,7},{4,0},{5,1},{6,2},{7,3},{8,12},{9,13},{10,... | collective-permute-start | bytes 4718600 | tf_op jit(solution)/shard_map/ppermute | solution.py:63
  132.8 14.7 %collective-permute-start.13 = (f32[2,8,72,128]{3,2,1,0:T(8,128)}, f32[2,8,72,128]{3,2,1,0:T(8,128)}, u32[]{:S(2)}, u32[]{:S(2)}) collective-permute-start(f32[2,8,72,128]{3,2,1,0:T(8,128)} %get-tuple-element.671.own_ref), channel_id=1, source_target_pairs={{8,0},{16,8},{24,16},{9,1},{17,9},{25,17},{10,2},{18,10},{26,18},{... | collective-permute-start | bytes 1769480 | tf_op jit(solution)/shard_map/ppermute | solution.py:47
  145.0 34.1 %collective-permute-start.16 = (f32[768,512]{1,0:T(8,128)}, f32[768,512]{1,0:T(8,128)S(1)}, u32[]{:S(2)}, u32[]{:S(2)}) collective-permute-start(f32[768,512]{1,0:T(8,128)} %get-tuple-element.673), channel_id=1, source_target_pairs={{0,4},{1,5},{2,6},{3,7},{4,0},{5,1},{6,2},{7,3},{8,12},{9,13},{10,... | collective-permute-start | bytes 4718600 | tf_op jit(solution)/shard_map/ppermute | solution.py:63
  145.6 33.8 %collective-permute-start.15 = (f32[768,512]{1,0:T(8,128)}, f32[768,512]{1,0:T(8,128)}, u32[]{:S(2)}, u32[]{:S(2)}) collective-permute-start(f32[768,512]{1,0:T(8,128)} %get-tuple-element.656), channel_id=1, source_target_pairs={{0,2},{1,3},{2,0},{3,1},{4,6},{5,7},{6,4},{7,5},{8,10},{9,11},{10,... | collective-permute-start | bytes 4718600 | tf_op jit(solution)/shard_map/ppermute | solution.py:63
  146.1 8.6 %collective-permute-start.19 = (f32[1,256,512]{2,1,0:T(8,128)}, f32[1,256,512]{2,1,0:T(8,128)S(1)}, u32[]{:S(2)}, u32[]{:S(2)}) collective-permute-start(f32[1,256,512]{2,1,0:T(8,128)} %get-tuple-element.681), channel_id=1, source_target_pairs={{0,1},{1,0},{2,3},{3,2},{4,5},{5,4},{6,7},{7,6},{8,9},{9,8},{10,11... | collective-permute-start | bytes 1572872 | tf_op jit(solution)/shard_map/ppermute | solution.py:63
  146.1 26.3 %collective-permute-start.17 = (f32[512,512]{1,0:T(8,128)}, f32[512,512]{1,0:T(8,128)}, u32[]{:S(2)}, u32[]{:S(2)}) collective-permute-start(f32[512,512]{1,0:T(8,128)} %get-tuple-element.679), channel_id=1, source_target_pairs={{0,8},{8,0},{16,24},{24,16},{1,9},{9,1},{17,25},{25,17},{2,10},{10... | collective-permute-start | bytes 3145736 | tf_op jit(solution)/shard_map/ppermute | solution.py:490
  147.6 24.8 %collective-permute-start.18 = (f32[512,512]{1,0:T(8,128)}, f32[512,512]{1,0:T(8,128)}, u32[]{:S(2)}, u32[]{:S(2)}) collective-permute-start(f32[512,512]{1,0:T(8,128)} %get-tuple-element.701.refs_9_), channel_id=1, source_target_pairs={{8,16},{16,8},{9,17},{17,9},{10,18},{18,10},{11,19},{19,11},{12,20... | collective-permute-start | bytes 3145736 | tf_op jit(solution)/shard_map/ppermute | solution.py:493
  154.7 30.7 %collective-permute-start.14 = (f32[2,8,72,128]{3,2,1,0:T(8,128)}, f32[2,8,72,128]{3,2,1,0:T(8,128)S(1)}, u32[]{:S(2)}, u32[]{:S(2)}) collective-permute-start(f32[2,8,72,128]{3,2,1,0:T(8,128)} %pass_carry.3), channel_id=1, source_target_pairs={{8,0},{16,8},{24,16},{9,1},{17,9},{25,17},{10,2},{18,10},{26,18},{... | collective-permute-start | bytes 1769480 | tf_op jit(solution)/shard_map/ppermute | solution.py:47
  184.9 25.7 %collective-permute-start.21 = (f32[512,512]{1,0:T(8,128)}, f32[512,512]{1,0:T(8,128)}, u32[]{:S(2)}, u32[]{:S(2)}) collective-permute-start(f32[512,512]{1,0:T(8,128)} %get-tuple-element.705), channel_id=1, source_target_pairs={{0,2},{1,3},{2,0},{3,1},{4,6},{5,7},{6,4},{7,5},{8,10},{9,11},{10,... | collective-permute-start | bytes 3145736 | tf_op jit(solution)/shard_map/ppermute | solution.py:63
  185.5 24.1 %collective-permute-start.22 = (f32[512,512]{1,0:T(8,128)}, f32[512,512]{1,0:T(8,128)S(1)}, u32[]{:S(2)}, u32[]{:S(2)}) collective-permute-start(f32[512,512]{1,0:T(8,128)} %get-tuple-element.723), channel_id=1, source_target_pairs={{0,4},{1,5},{2,6},{3,7},{4,0},{5,1},{6,2},{7,3},{8,12},{9,13},{10,... | collective-permute-start | bytes 3145736 | tf_op jit(solution)/shard_map/ppermute | solution.py:63
  187.0 25.3 %collective-permute-start.23 = (f32[512,512]{1,0:T(8,128)}, f32[512,512]{1,0:T(8,128)}, u32[]{:S(2)}, u32[]{:S(2)}) collective-permute-start(f32[512,512]{1,0:T(8,128)} %get-tuple-element.758.refs_11_), channel_id=1, source_target_pairs={{0,8},{8,0},{16,24},{24,16},{1,9},{9,1},{17,25},{25,17},{2,10},{10... | collective-permute-start | bytes 3145736 | tf_op jit(solution)/shard_map/ppermute | solution.py:490
  189.7 22.6 %collective-permute-start.24 = (f32[512,512]{1,0:T(8,128)}, f32[512,512]{1,0:T(8,128)}, u32[]{:S(2)}, u32[]{:S(2)}) collective-permute-start(f32[512,512]{1,0:T(8,128)} %get-tuple-element.756.refs_9_), channel_id=1, source_target_pairs={{8,16},{16,8},{9,17},{17,9},{10,18},{18,10},{11,19},{19,11},{12,20... | collective-permute-start | bytes 3145736 | tf_op jit(solution)/shard_map/ppermute | solution.py:493
  201.9 11.0 %collective-permute-start.25 = (f32[256,1024]{1,0:T(8,128)}, f32[256,1024]{1,0:T(8,128)}, u32[]{:S(2)}, u32[]{:S(2)}) collective-permute-start(f32[256,1024]{1,0:T(8,128)} %get-tuple-element.731), channel_id=1, source_target_pairs={{0,1},{1,0},{2,3},{3,2},{4,5},{5,4},{6,7},{7,6},{8,9},{9,8},{10,11... | collective-permute-start | bytes 3145736 | tf_op jit(solution)/shard_map/ppermute | solution.py:63
  210.5 19.0 %collective-permute-start.20 = (f32[256,2048]{1,0:T(8,128)}, f32[256,2048]{1,0:T(8,128)S(1)}, u32[]{:S(2)}, u32[]{:S(2)}) collective-permute-start(f32[256,2048]{1,0:T(8,128)} %get-tuple-element.722), channel_id=1, source_target_pairs={{0,1},{1,0},{2,3},{3,2},{4,5},{5,4},{6,7},{7,6},{8,9},{9,8},{10,11... | collective-permute-start | bytes 6291464 | tf_op jit(solution)/shard_map/ppermute | solution.py:63
  222.3 25.4 %collective-permute-start.29 = (f32[512,512]{1,0:T(8,128)}, f32[512,512]{1,0:T(8,128)}, u32[]{:S(2)}, u32[]{:S(2)}) collective-permute-start(f32[512,512]{1,0:T(8,128)} %get-tuple-element.809.refs_11_), channel_id=1, source_target_pairs={{0,8},{8,0},{16,24},{24,16},{1,9},{9,1},{17,25},{25,17},{2,10},{10... | collective-permute-start | bytes 3145736 | tf_op jit(solution)/shard_map/ppermute | solution.py:490
  226.0 21.7 %collective-permute-start.30 = (f32[512,512]{1,0:T(8,128)}, f32[512,512]{1,0:T(8,128)}, u32[]{:S(2)}, u32[]{:S(2)}) collective-permute-start(f32[512,512]{1,0:T(8,128)} %get-tuple-element.807.refs_9_), channel_id=1, source_target_pairs={{8,16},{16,8},{9,17},{17,9},{10,18},{18,10},{11,19},{19,11},{12,20... | collective-permute-start | bytes 3145736 | tf_op jit(solution)/shard_map/ppermute | solution.py:493
  227.7 17.5 %collective-permute-start.28 = (f32[384,512]{1,0:T(8,128)}, f32[384,512]{1,0:T(8,128)}, u32[]{:S(2)}, u32[]{:S(2)}) collective-permute-start(f32[384,512]{1,0:T(8,128)} %get-tuple-element.788), channel_id=1, source_target_pairs={{0,4},{1,5},{2,6},{3,7},{4,0},{5,1},{6,2},{7,3},{8,12},{9,13},{10,... | collective-permute-start | bytes 2359304 | tf_op jit(solution)/shard_map/ppermute | solution.py:63
  228.0 18.7 %collective-permute-start.27 = (f32[384,512]{1,0:T(8,128)}, f32[384,512]{1,0:T(8,128)}, u32[]{:S(2)}, u32[]{:S(2)}) collective-permute-start(f32[384,512]{1,0:T(8,128)} %get-tuple-element.761), channel_id=1, source_target_pairs={{0,2},{1,3},{2,0},{3,1},{4,6},{5,7},{6,4},{7,5},{8,10},{9,11},{10,... | collective-permute-start | bytes 2359304 | tf_op jit(solution)/shard_map/ppermute | solution.py:63
  252.9 24.4 %collective-permute-start.34 = (f32[512,512]{1,0:T(8,128)}, f32[512,512]{1,0:T(8,128)S(1)}, u32[]{:S(2)}, u32[]{:S(2)}) collective-permute-start(f32[512,512]{1,0:T(8,128)} %get-tuple-element.846.refs_11_), channel_id=1, source_target_pairs={{0,8},{8,0},{16,24},{24,16},{1,9},{9,1},{17,25},{25,17},{2,10},{10... | collective-permute-start | bytes 3145736 | tf_op jit(solution)/shard_map/ppermute | solution.py:490
  256.6 20.7 %collective-permute-start.35 = (f32[512,512]{1,0:T(8,128)}, f32[512,512]{1,0:T(8,128)S(1)}, u32[]{:S(2)}, u32[]{:S(2)}) collective-permute-start(f32[512,512]{1,0:T(8,128)} %get-tuple-element.844.refs_9_), channel_id=1, source_target_pairs={{8,16},{16,8},{9,17},{17,9},{10,18},{18,10},{11,19},{19,11},{12,20... | collective-permute-start | bytes 3145736 | tf_op jit(solution)/shard_map/ppermute | solution.py:493
  257.4 19.3 %collective-permute-start.32 = (f32[384,512]{1,0:T(8,128)}, f32[384,512]{1,0:T(8,128)S(1)}, u32[]{:S(2)}, u32[]{:S(2)}) collective-permute-start(f32[384,512]{1,0:T(8,128)} %get-tuple-element.813), channel_id=1, source_target_pairs={{0,2},{1,3},{2,0},{3,1},{4,6},{5,7},{6,4},{7,5},{8,10},{9,11},{10,... | collective-permute-start | bytes 2359304 | tf_op jit(solution)/shard_map/ppermute | solution.py:63
  259.0 17.7 %collective-permute-start.33 = (f32[384,512]{1,0:T(8,128)}, f32[384,512]{1,0:T(8,128)S(1)}, u32[]{:S(2)}, u32[]{:S(2)}) collective-permute-start(f32[384,512]{1,0:T(8,128)} %get-tuple-element.826), channel_id=1, source_target_pairs={{0,4},{1,5},{2,6},{3,7},{4,0},{5,1},{6,2},{7,3},{8,12},{9,13},{10,... | collective-permute-start | bytes 2359304 | tf_op jit(solution)/shard_map/ppermute | solution.py:63
  281.2 23.9 %collective-permute-start.39 = (f32[512,512]{1,0:T(8,128)}, f32[512,512]{1,0:T(8,128)S(1)}, u32[]{:S(2)}, u32[]{:S(2)}) collective-permute-start(f32[512,512]{1,0:T(8,128)} %get-tuple-element.873.refs_11_), channel_id=1, source_target_pairs={{0,8},{8,0},{16,24},{24,16},{1,9},{9,1},{17,25},{25,17},{2,10},{10... | collective-permute-start | bytes 3145736 | tf_op jit(solution)/shard_map/ppermute | solution.py:490
  284.9 20.2 %collective-permute-start.38 = (f32[384,512]{1,0:T(8,128)}, f32[384,512]{1,0:T(8,128)S(1)}, u32[]{:S(2)}, u32[]{:S(2)}) collective-permute-start(f32[384,512]{1,0:T(8,128)} %get-tuple-element.853), channel_id=1, source_target_pairs={{0,4},{1,5},{2,6},{3,7},{4,0},{5,1},{6,2},{7,3},{8,12},{9,13},{10,... | collective-permute-start | bytes 2359304 | tf_op jit(solution)/shard_map/ppermute | solution.py:63
  288.0 17.0 %collective-permute-start.37 = (f32[384,512]{1,0:T(8,128)}, f32[384,512]{1,0:T(8,128)S(1)}, u32[]{:S(2)}, u32[]{:S(2)}) collective-permute-start(f32[384,512]{1,0:T(8,128)} %get-tuple-element.849), channel_id=1, source_target_pairs={{0,2},{1,3},{2,0},{3,1},{4,6},{5,7},{6,4},{7,5},{8,10},{9,11},{10,... | collective-permute-start | bytes 2359304 | tf_op jit(solution)/shard_map/ppermute | solution.py:63
  289.6 15.5 %collective-permute-start.40 = (f32[256,512]{1,0:T(8,128)}, f32[256,512]{1,0:T(8,128)S(1)}, u32[]{:S(2)}, u32[]{:S(2)}) collective-permute-start(f32[256,512]{1,0:T(8,128)} %get-tuple-element.871.refs_9_), channel_id=1, source_target_pairs={{8,16},{16,8},{9,17},{17,9},{10,18},{18,10},{11,19},{19,11},{12,20... | collective-permute-start | bytes 1572872 | tf_op jit(solution)/shard_map/ppermute | solution.py:493
  290.3 14.8 %collective-permute-start.31 = (f32[2,1536]{1,0:T(2,128)S(1)}, f32[2,1536]{1,0:T(2,128)S(1)}, u32[]{:S(2)}, u32[]{:S(2)}) collective-permute-start(f32[2,1536]{1,0:T(2,128)S(1)} %get-tuple-element.825), channel_id=1, source_target_pairs={{0,2},{1,3},{2,0},{3,1},{4,6},{5,7},{6,4},{7,5},{8,10},{9,11},{10,... | collective-permute-start | bytes 36872 | tf_op jit(solution)/shard_map/ppermute | solution.py:63
  308.7 13.2 %collective-permute-start.44 = (f32[256,512]{1,0:T(8,128)}, f32[256,512]{1,0:T(8,128)S(1)}, u32[]{:S(2)}, u32[]{:S(2)}) collective-permute-start(f32[256,512]{1,0:T(8,128)} %get-tuple-element.894.refs_9_), channel_id=1, source_target_pairs={{0,8},{8,0},{16,24},{24,16},{1,9},{9,1},{17,25},{25,17},{2,10},{10... | collective-permute-start | bytes 1572872 | tf_op jit(solution)/shard_map/ppermute | solution.py:490
  310.0 12.0 %collective-permute-start.45 = (f32[256,512]{1,0:T(8,128)}, f32[256,512]{1,0:T(8,128)S(1)}, u32[]{:S(2)}, u32[]{:S(2)}) collective-permute-start(f32[256,512]{1,0:T(8,128)} %get-tuple-element.892.refs_7_), channel_id=1, source_target_pairs={{8,16},{16,8},{9,17},{17,9},{10,18},{18,10},{11,19},{19,11},{12,20... | collective-permute-start | bytes 1572872 | tf_op jit(solution)/shard_map/ppermute | solution.py:493
  310.7 10.0 %collective-permute-start.43 = (f32[128,512]{1,0:T(8,128)}, f32[128,512]{1,0:T(8,128)S(1)}, u32[]{:S(2)}, u32[]{:S(2)}) collective-permute-start(f32[128,512]{1,0:T(8,128)} %get-tuple-element.879), channel_id=1, source_target_pairs={{0,4},{1,5},{2,6},{3,7},{4,0},{5,1},{6,2},{7,3},{8,12},{9,13},{10,... | collective-permute-start | bytes 786440 | tf_op jit(solution)/shard_map/ppermute | solution.py:63
  315.4 6.6 %collective-permute-start.42 = (f32[128,512]{1,0:T(8,128)}, f32[128,512]{1,0:T(8,128)S(1)}, u32[]{:S(2)}, u32[]{:S(2)}) collective-permute-start(f32[128,512]{1,0:T(8,128)} %get-tuple-element.875), channel_id=1, source_target_pairs={{0,2},{1,3},{2,0},{3,1},{4,6},{5,7},{6,4},{7,5},{8,10},{9,11},{10,... | collective-permute-start | bytes 786440 | tf_op jit(solution)/shard_map/ppermute | solution.py:63
  324.7 9.4 %collective-permute-start.47 = (f32[256,512]{1,0:T(8,128)}, f32[256,512]{1,0:T(8,128)S(1)}, u32[]{:S(2)}, u32[]{:S(2)}) collective-permute-start(f32[256,512]{1,0:T(8,128)} %get-tuple-element.906.refs_5_), channel_id=1, source_target_pairs={{0,8},{8,0},{16,24},{24,16},{1,9},{9,1},{17,25},{25,17},{2,10},{10... | collective-permute-start | bytes 1572872 | tf_op jit(solution)/shard_map/ppermute | solution.py:490
  326.5 7.6 %collective-permute-start.48 = (f32[256,512]{1,0:T(8,128)}, f32[256,512]{1,0:T(8,128)S(1)}, u32[]{:S(2)}, u32[]{:S(2)}) collective-permute-start(f32[256,512]{1,0:T(8,128)} %get-tuple-element.904.refs_3_), channel_id=1, source_target_pairs={{8,16},{16,8},{9,17},{17,9},{10,18},{18,10},{11,19},{19,11},{12,20... | collective-permute-start | bytes 1572872 | tf_op jit(solution)/shard_map/ppermute | solution.py:493
  327.2 6.3 %collective-permute-start.41 = (f32[1,1536]{1,0:T(1,128)S(1)}, f32[1,1536]{1,0:T(1,128)S(1)}, u32[]{:S(2)}, u32[]{:S(2)}) collective-permute-start(f32[1,1536]{1,0:T(1,128)S(1)} %add.21), channel_id=1, source_target_pairs={{0,8},{24,16},{1,9},{25,17},{2,10},{26,18},{3,11},{27,19},{4,12},{... | collective-permute-start | bytes 18440 | tf_op jit(solution)/shard_map/ppermute | solution.py:157
  336.4 9.4 %collective-permute-start.51 = (f32[256,512]{1,0:T(8,128)}, f32[256,512]{1,0:T(8,128)S(1)}, u32[]{:S(2)}, u32[]{:S(2)}) collective-permute-start(f32[256,512]{1,0:T(8,128)} %get-tuple-element.915.refs_2_), channel_id=1, source_target_pairs={{8,16},{16,8},{9,17},{17,9},{10,18},{18,10},{11,19},{19,11},{12,20... | collective-permute-start | bytes 1572872 | tf_op jit(solution)/shard_map/ppermute | solution.py:493
  337.1 15.6 %collective-permute-start.50 = (f32[256,512]{1,0:T(8,128)}, f32[256,512]{1,0:T(8,128)S(1)}, u32[]{:S(2)}, u32[]{:S(2)}) collective-permute-start(f32[256,512]{1,0:T(8,128)} %get-tuple-element.917.refs_4_), channel_id=1, source_target_pairs={{0,8},{8,0},{16,24},{24,16},{1,9},{9,1},{17,25},{25,17},{2,10},{10... | collective-permute-start | bytes 1572872 | tf_op jit(solution)/shard_map/ppermute | solution.py:490
  344.5 12.5 %collective-permute-start.49 = (f32[1,1536]{1,0:T(1,128)S(1)}, f32[1,1536]{1,0:T(1,128)S(1)}, u32[]{:S(2)}, u32[]{:S(2)}) collective-permute-start(f32[1,1536]{1,0:T(1,128)S(1)} %add.23), channel_id=1, source_target_pairs={{8,0},{16,24},{9,1},{17,25},{10,2},{18,26},{11,3},{19,27},{12,4},{... | collective-permute-start | bytes 18440 | tf_op jit(solution)/shard_map/ppermute | solution.py:157
  354.8 9.5 %collective-permute-start.52 = (f32[256,512]{1,0:T(8,128)}, f32[256,512]{1,0:T(8,128)S(1)}, u32[]{:S(2)}, u32[]{:S(2)}) collective-permute-start(f32[256,512]{1,0:T(8,128)} %get-tuple-element.925.refs_2_), channel_id=1, source_target_pairs={{0,8},{8,0},{16,24},{24,16},{1,9},{9,1},{17,25},{25,17},{2,10},{10... | collective-permute-start | bytes 1572872 | tf_op jit(solution)/shard_map/ppermute | solution.py:490
  (33 other events, 262.7 us)

commit v7 on v6

--- a/solution.py
+++ b/solution.py
@@ -1452,6 +1452,8 @@
 
     vectors = Vectors(line, (sums, qkv_sums, up_sums), [])
     vectors.send()
+    vectors.take()
+    vectors.send()
     reduction.step()
     qkv_group(2)
     vectors.take()

time: 368 us -> 369 us (level)
    ppermute x3, waiting for transfers between devices: 1.48 us -> 9.29 us  [send(): lax.ppermute(a, 'seq', what)]
    ppermute x28, waiting for transfers between devices: 57.2 us -> 51.3 us  [swap(): lax.ppermute(value, 'batch', [(i, i ^ 1 << bit) for i in range(count)])]
where the time goes in v7:
time: 369 us; the launch traced here: 368 us
  Pallas kernels  175 us (47%)
  waiting for transfers between devices  98 us (27%)
  starting transfers between devices  82.6 us (22%)
  local copies, waits for them, and re-layouts  9.34 us (3%)
    pallas_call x20, Pallas kernels, step(): out = function(*self.wait(*values))  76 us
    ppermute x28, waiting for transfers between devices, swap(): lax.ppermute(value, 'batch', [(i, i ^ 1 << bit) for i in range(count)])  51.3 us
    ppermute x28, starting transfers between devices, swap(): lax.ppermute(value, 'batch', [(i, i ^ 1 << bit) for i in range(count)])  29.2 us
    ppermute x10, starting transfers between devices, step(): self.end = lax.ppermute(self.whole, 'seq', [(0, 1), (1, 0), (2, 3), (3, 2)])  28.8 us
    ppermute x10, waiting for transfers between devices, step(): self.end = lax.ppermute(self.whole, 'seq', [(0, 1), (1, 0), (2, 3), (3, 2)])  27.3 us
    pallas_call x1, Pallas kernels, attention_middle(): pl.pallas_call(partial(middle_kernel, seqs), grid=(pairs,), in_specs=[SME...  19.9 us
    pallas_call x1, Pallas kernels, mlp_back(): pl.pallas_call(back_kernel, grid=(FF // each,), in_specs=[total, pl.Block...  15.9 us
    pallas_call x1, Pallas kernels, attention_local(): pl.pallas_call(partial(local_kernel, seqs), grid=(pairs,), in_specs=[SMEM...  14.3 us
  transfers between devices with their start and end apart: 53, of which 23 were waited for; matrix products, arithmetic and copies ran while one was open for 1% of the time, Pallas kernels for 36%

profile of v7, /device:TPU:0, one launch (start us, length us, event | category | flops | bytes accessed | tf_op | source)
XLA Modules:
  0.0 367.6 jit_solution(11276650041357527023)
XLA Ops:
  0.7 3.9 %two_norms.1 = (bf16[256,1024]{1,0:T(8,128)(2,1)}, bf16[256,1024]{1,0:T(8,128)(2,1)}, f32[256,1024]{1,0:T(8,128)}, f32[256,128]{1,0:T(8,128)}) custom-call(bf16[256,1024]{1,0:T(8,128)(2,1)} %bitcast.37, bf16[1024]{0:T(1024)(128)(2,1)} %gain1.2, bf16[1024]{0:T(1024)(128)(2,1)} %bias1.1, bf16[1024]{0:T(1024)(128)(2,1)} %gain2.2, bf16[1024]{0:T(1024)(128)(2,1)} %bias2.1), custom_call_target="tpu_custom_call" | custom-call | flops 4600000000 | tf_op jit(solution)/shard_map/two_norms/pallas_call | solution.py:588
  4.6 11.1 %mlp_up.1 = (bf16[256,4096]{1,0:T(8,128)(2,1)}, f32[256,4096]{1,0:T(8,128)}, bf16[4,256,512]{2,1,0:T(8,128)(2,1)}, f32[4,256,512]{2,1,0:T(8,128)}) custom-call(s32[1]{0:T(128)} %bitcast.5.me_ref, bf16[256,1024]{1,0:T(8,128)(2,1)} %get-tuple-element.483.x_ref.refs_1_, bf16[1024,4096]{1,0:T(8,128)(2,1)} %up_ref, bf16[4096]{0:T(1024)(128)(2,1)} %bias_ref), custom_call_target="tpu_custom_call" | custom-call | flops 12650000384 | tf_op jit(solution)/shard_map/mlp_up/pallas_call | solution.py:636
  18.3 2.8 pick_columns.2
  21.6 4.6 %piece_products.8 = (f32[512,512]{1,0:T(8,128)}, f32[512,512]{1,0:T(8,128)}, f32[512,512]{1,0:T(8,128)}, f32[512,512]{1,0:T(8,128)}) custom-call(bf16[4,256,512]{2,1,0:T(8,128)(2,1)} %get-tuple-element.524.refs_0_.refs_4_.refs_8_.refs_12_, f32[4,256,512]{2,1,0:T(8,128)S(1)} %collective-permute-done.refs_1_.refs_5_.refs_9_.refs_13_, ...), custom_call_target="tpu_custom_call" | custom-call | flops 5750000128 | tf_op jit(solution)/shard_map/piece_products/pallas_call | solution.py:94
  26.2 2.9 collective-permute-start.2
  30.6 15.9 %mlp_back.1 = (bf16[256,4096]{1,0:T(8,128)(2,1)}, f32[256,4096]{1,0:T(8,128)}, f32[1,4096]{1,0:T(1,128)}, f32[256,1024]{1,0:T(8,128)}, f32[256,1024]{1,0:T(8,128)}) custom-call(bf16[256,1024]{1,0:T(8,128)(2,1)} %bitcast.26, bf16[4096,1024]{1,0:T(8,128)(2,1)} %down_ref, bf16[1024,4096]{1,0:T(8,128)(2,1)} %up_ref, ...), custom_call_target="tpu_custom_call" | custom-call | flops 18400000000 | tf_op jit(solution)/shard_map/mlp_back/pallas_call | solution.py:700
  46.5 4.4 %piece_products.9 = (f32[768,512]{1,0:T(8,128)}, f32[768,512]{1,0:T(8,128)}, f32[512,512]{1,0:T(8,128)}, f32[512,512]{1,0:T(8,128)}) custom-call(bf16[4,256,512]{2,1,0:T(8,128)(2,1)} %get-tuple-element.524.refs_0_.refs_4_.refs_8_.refs_12_, f32[4,256,512]{2,1,0:T(8,128)S(1)} %collective-permute-done.refs_1_.refs_5_.refs_9_.refs_13_, ...), custom_call_target="tpu_custom_call" | custom-call | flops 5750000128 | tf_op jit(solution)/shard_map/piece_products/pallas_call | solution.py:94
  50.9 3.3 collective-permute-done.3.refs_2_
  54.3 2.9 reduce_round.12
  60.0 14.3 %attention_local.1 = (bf16[8,256,128]{2,1,0:T(8,128)(2,1)}, bf16[8,256,128]{2,1,0:T(8,128)(2,1)}, bf16[8,256,128]{2,1,0:T(8,128)(2,1)}, f32[8,256,128]{2,1,0:T(8...) custom-call(s32[2,3]{1,0:T(2,128)S(1)} %copy-done.10, ...), custom_call_target="tpu_custom_call" | custom-call | flops 16099999744 | tf_op jit(solution)/shard_map/attention_local/pallas_call | solution.py:1201
  74.3 3.5 collective-permute-start.4
  77.9 5.8 %piece_products.10 = (f32[768,512]{1,0:T(8,128)}, f32[768,512]{1,0:T(8,128)}, f32[512,512]{1,0:T(8,128)}, f32[512,512]{1,0:T(8,128)}) custom-call(bf16[2,256,512]{2,1,0:T(8,128)(2,1)} %get-tuple-element.821.refs_0_.refs_4_.refs_8_.refs_12_, f32[2,256,512]{2,1,0:T(8,128)S(1)} %collective-permute-done.5.refs_1_.refs_5_.refs_9_.refs_13_, ...), custom_call_target="tpu_custom_call" | custom-call | flops 5750000128 | tf_op jit(solution)/shard_map/piece_products/pallas_call | solution.py:94
  83.7 7.1 %collective-permute-done.4.arrived_ref = f32[2,8,72,128]{3,2,1,0:T(8,128)S(1)} collective-permute-done((f32[2,8,72,128]{3,2,1,0:T(8,128)}, f32[2,8,72,128]{3,2,1,0:T(8,128)S(1)}, u32[]{:S(2)}, u32[]{:S(2)}) %collective-permute-start.4) | collective-permute-done | bytes 589856 | tf_op jit(solution)/shard_map/ppermute | solution.py:47
  93.7 4.3 %collective-permute-start.7 = (f32[2,8,72,128]{3,2,1,0:T(8,128)}, f32[2,8,72,128]{3,2,1,0:T(8,128)S(1)}, u32[]{:S(2)}, u32[]{:S(2)}) collective-permute-start(f32[2,8,72,128]{3,2,1,0:T(8,128)} %pass_carry.2), channel_id=1, source_target_pairs={{0,8},{8,16},{16,24},{1,9},{9,17},{17,25},{2,10},{10,18},{18,26},{... | collective-permute-start | bytes 1769480 | tf_op jit(solution)/shard_map/ppermute | solution.py:47
  98.1 4.1 %reduce_round.13 = (f32[768,512]{1,0:T(8,128)}, f32[768,512]{1,0:T(8,128)}, f32[256,512]{1,0:T(8,128)}, f32[256,512]{1,0:T(8,128)}, f32[512,512]{1,0:T(8,128)}, /*index=5*/f32[512,512]{1,0:T(8,128)}) custom-call(s32[1]{0:T(128)} %bitcast.4.refs_0_, f32[768,512]{1,0:T(8,128)S(1)} %collective-permute-done.8.refs_1_, ...), custom_call_target="tpu_custom_call", output_to_operand_aliasing={{0}: (7, {}), {1}: (8, {})} | custom-call | flops 5750000128 | tf_op jit(solution)/shard_map/reduce_round/pallas_call | solution.py:94
  105.7 4.4 %piece_products.11 = (f32[768,512]{1,0:T(8,128)}, f32[768,512]{1,0:T(8,128)}, f32[512,512]{1,0:T(8,128)}, f32[512,512]{1,0:T(8,128)}) custom-call(bf16[2,256,512]{2,1,0:T(8,128)(2,1)} %get-tuple-element.821.refs_0_.refs_4_.refs_8_.refs_12_, f32[2,256,512]{2,1,0:T(8,128)S(1)} %collective-permute-done.5.refs_1_.refs_5_.refs_9_.refs_13_, ...), custom_call_target="tpu_custom_call" | custom-call | flops 5750000128 | tf_op jit(solution)/shard_map/piece_products/pallas_call | solution.py:94
  112.9 19.9 %attention_middle.1 = (bf16[256,1024]{1,0:T(8,128)(2,1)}, bf16[8,256,128]{2,1,0:T(8,128)(2,1)}, f32[8,256,128]{2,1,0:T(8,128)}, f32[8,256,128]{2,1,0:T(8,128)}, f32[2,8,72,128]{3,2,1,0:T(8,128)}) custom-call(s32[2,3]{1,0:T(2,128)S(1)} %copy-done.11, s32[2]{0:T(128)S(1)} %copy-done.16, bf16[256,1024]{1,0:T(8,128)(2,1)} %bitcast.31, ...), custom_call_target="tpu_custom_call" | custom-call | flops 23000000512 | tf_op jit(solution)/shard_map/attention_middle/pallas_call | solution.py:1234
  136.4 3.8 %collective-permute-done.11.refs_2_ = f32[768,512]{1,0:T(8,128)} collective-permute-done((f32[768,512]{1,0:T(8,128)}, f32[768,512]{1,0:T(8,128)}, u32[]{:S(2)}, u32[]{:S(2)}) %collective-permute-start.11) | collective-permute-done | bytes 1572896 | tf_op jit(solution)/shard_map/ppermute | solution.py:63
  140.3 4.7 %reduce_round.14 = (f32[768,512]{1,0:T(8,128)}, f32[768,512]{1,0:T(8,128)}, f32[256,512]{1,0:T(8,128)}, f32[256,512]{1,0:T(8,128)}, f32[512,512]{1,0:T(8,128)}, /*index=5*/f32[512,512]{1,0:T(8,128)}, f32[512,512]{1,0:T(8,128)}) custom-call(s32[1]{0:T(128)} %bitcast.4.refs_0_, ...), custom_call_target="tpu_custom_call", output_to_operand_aliasing={{0}: (9, {}), {1}: (10, {})} | custom-call | flops 5750000128 | tf_op jit(solution)/shard_map/reduce_round/pallas_call | solution.py:94
  149.3 3.4 layer_output.1
  157.3 3.0 piece_products.12
  160.3 12.1 %collective-permute-done.17.refs_8_ = f32[512,512]{1,0:T(8,128)} collective-permute-done((f32[512,512]{1,0:T(8,128)}, f32[512,512]{1,0:T(8,128)}, u32[]{:S(2)}, u32[]{:S(2)}) %collective-permute-start.17) | collective-permute-done | bytes 1048608 | tf_op jit(solution)/shard_map/ppermute | solution.py:490
  172.4 6.7 %collective-permute-done.16.refs_2_ = f32[768,512]{1,0:T(8,128)S(1)} collective-permute-done((f32[768,512]{1,0:T(8,128)}, f32[768,512]{1,0:T(8,128)S(1)}, u32[]{:S(2)}, u32[]{:S(2)}) %collective-permute-start.16) | collective-permute-done | bytes 1572896 | tf_op jit(solution)/shard_map/ppermute | solution.py:63
  179.4 5.4 %reduce_round.15 = (f32[512,512]{1,0:T(8,128)}, f32[512,512]{1,0:T(8,128)}, f32[256,512]{1,0:T(8,128)}, f32[256,512]{1,0:T(8,128)}, f32[512,512]{1,0:T(8,128)}, /*index=5*/f32[512,512]{1,0:T(8,128)}, f32[512,512]{1,0:T(8,128)}) custom-call(s32[1]{0:T(128)} %bitcast.4.refs_0_, ...), custom_call_target="tpu_custom_call", output_to_operand_aliasing={{0}: (11, {}), {1}: (12, {})} | custom-call | flops 5750000128 | tf_op jit(solution)/shard_map/reduce_round/pallas_call | solution.py:94
  187.0 2.7 collective-permute-start.23
  191.3 10.5 %attention_last.1 = (bf16[256,3072]{1,0:T(8,128)(2,1)}, f32[256,1024]{1,0:T(8,128)}, f32[256,2048]{1,0:T(8,128)}) custom-call(s32[2,3]{1,0:T(2,128)S(1)} %copy-done.12, s32[2]{0:T(128)S(1)} %copy-done.17, bf16[8,256,128]{2,1,0:T(8,128)(2,1)} %get-tuple-element.708.gradq_ref, f32[8,256,128]{2,1,0:T(8,128)} %get-tuple-element.709.gradk_ref, ...), custom_call_target="tpu_custom_call" | custom-call | flops 11500000256 | tf_op jit(solution)/shard_map/attention_last/pallas_call | solution.py:1259
  202.0 7.6 %collective-permute-done.22.refs_1_.refs_2_ = f32[512,512]{1,0:T(8,128)S(1)} collective-permute-done((f32[512,512]{1,0:T(8,128)}, f32[512,512]{1,0:T(8,128)S(1)}, u32[]{:S(2)}, u32[]{:S(2)}) %collective-permute-start.22) | collective-permute-done | bytes 1048608 | tf_op jit(solution)/shard_map/ppermute | solution.py:63
  213.6 3.4 piece_products.13
  217.0 5.3 %reduce_round.16 = (f32[384,512]{1,0:T(8,128)}, f32[384,512]{1,0:T(8,128)}, f32[128,512]{1,0:T(8,128)}, f32[128,512]{1,0:T(8,128)}, f32[512,512]{1,0:T(8,128)}, ...) custom-call(s32[1]{0:T(128)} %bitcast.4.refs_0_, ...), custom_call_target="tpu_custom_call", output_to_operand_aliasing={{0}: (12, {}), {1}: (13, {})} | custom-call | flops 5750000128 | tf_op jit(solution)/shard_map/reduce_round/pallas_call | solution.py:94
  222.4 3.7 %collective-permute-start.30 = (f32[512,512]{1,0:T(8,128)}, f32[512,512]{1,0:T(8,128)}, u32[]{:S(2)}, u32[]{:S(2)}) collective-permute-start(f32[512,512]{1,0:T(8,128)} %get-tuple-element.812.refs_11_), channel_id=1, source_target_pairs={{0,8},{8,0},{16,24},{24,16},{1,9},{9,1},{17,25},{25,17},{2,10},{10... | collective-permute-start | bytes 3145736 | tf_op jit(solution)/shard_map/ppermute | solution.py:490
  229.5 3.1 piece_products.14
  232.6 9.2 %norm_back.1 = (f32[256,1024]{1,0:T(8,128)}, f32[5,1024]{1,0:T(8,128)}, f32[1,3072]{1,0:T(1,128)}) custom-call(bf16[256,3072]{1,0:T(8,128)(2,1)} %get-tuple-element.823.refs_2_.refs_6_.qkv_ref, bf16[1024,3072]{1,0:T(8,128)(2,1)} %weight_ref.3, f32[256,1024]{1,0:T(8,128)} %get-tuple-element.773.mlp_ref, f32[256,1024]{1,0:T(8,128)} %get-tuple-element.774.unit_ref, ...), custom_call_target="tpu_custom_call" | custom-call | tf_op jit(solution)/shard_map/norm_back/pallas_call | solution.py:808
  247.7 5.2 %reduce_round.17 = (f32[384,512]{1,0:T(8,128)}, f32[384,512]{1,0:T(8,128)}, f32[128,512]{1,0:T(8,128)}, f32[128,512]{1,0:T(8,128)}, f32[256,512]{1,0:T(8,128)}, ...) custom-call(s32[1]{0:T(128)} %bitcast.4.refs_0_, ...), custom_call_target="tpu_custom_call", output_to_operand_aliasing={{0}: (12, {}), {1}: (13, {}), {7}: (14, {})} | custom-call | flops 5750000128 | tf_op jit(solution)/shard_map/reduce_round/pallas_call | solution.py:94
  253.0 3.7 %collective-permute-start.35 = (f32[512,512]{1,0:T(8,128)}, f32[512,512]{1,0:T(8,128)S(1)}, u32[]{:S(2)}, u32[]{:S(2)}) collective-permute-start(f32[512,512]{1,0:T(8,128)} %get-tuple-element.849.refs_11_), channel_id=1, source_target_pairs={{0,8},{8,0},{16,24},{24,16},{1,9},{9,1},{17,25},{25,17},{2,10},{10... | collective-permute-start | bytes 3145736 | tf_op jit(solution)/shard_map/ppermute | solution.py:490
  261.3 3.1 piece_products.15
  264.4 9.8 %collective-permute-done.27 = f32[2,1536]{1,0:T(2,128)S(1)} collective-permute-done((f32[2,1536]{1,0:T(2,128)S(1)}, f32[2,1536]{1,0:T(2,128)S(1)}, u32[]{:S(2)}, u32[]{:S(2)}) %collective-permute-start.27) | collective-permute-done | bytes 12320 | tf_op jit(solution)/shard_map/ppermute | solution.py:63
  277.3 3.9 %reduce_round.18 = (f32[384,512]{1,0:T(8,128)}, f32[384,512]{1,0:T(8,128)}, f32[128,512]{1,0:T(8,128)}, f32[128,512]{1,0:T(8,128)}, f32[256,512]{1,0:T(8,128)}, ...) custom-call(s32[1]{0:T(128)} %bitcast.4.refs_0_, ...), custom_call_target="tpu_custom_call", output_to_operand_aliasing={{0}: (12, {}), {1}: (13, {})} | custom-call | flops 5750000128 | tf_op jit(solution)/shard_map/reduce_round/pallas_call | solution.py:94
  281.2 3.7 %collective-permute-start.40 = (f32[512,512]{1,0:T(8,128)}, f32[512,512]{1,0:T(8,128)S(1)}, u32[]{:S(2)}, u32[]{:S(2)}) collective-permute-start(f32[512,512]{1,0:T(8,128)} %get-tuple-element.876.refs_11_), channel_id=1, source_target_pairs={{0,8},{8,0},{16,24},{24,16},{1,9},{9,1},{17,25},{25,17},{2,10},{10... | collective-permute-start | bytes 3145736 | tf_op jit(solution)/shard_map/ppermute | solution.py:490
  284.9 3.2 collective-permute-start.39
  290.4 13.1 %collective-permute-done.32 = f32[1,1536]{1,0:T(1,128)S(1)} collective-permute-done((f32[1,1536]{1,0:T(1,128)S(1)}, f32[1,1536]{1,0:T(1,128)S(1)}, u32[]{:S(2)}, u32[]{:S(2)}) %collective-permute-start.32) | collective-permute-done | bytes 6176 | tf_op jit(solution)/shard_map/ppermute | solution.py:63
  304.8 3.6 reduce_round.19
  310.8 4.7 %collective-permute-start.44 = (f32[128,512]{1,0:T(8,128)}, f32[128,512]{1,0:T(8,128)S(1)}, u32[]{:S(2)}, u32[]{:S(2)}) collective-permute-start(f32[128,512]{1,0:T(8,128)} %get-tuple-element.882), channel_id=1, source_target_pairs={{0,4},{1,5},{2,6},{3,7},{4,0},{5,1},{6,2},{7,3},{8,12},{9,13},{10,... | collective-permute-start | bytes 786440 | tf_op jit(solution)/shard_map/ppermute | solution.py:63
  316.9 3.7 %collective-permute-start.37 = (f32[1,1536]{1,0:T(1,128)S(1)}, f32[1,1536]{1,0:T(1,128)S(1)}, u32[]{:S(2)}, u32[]{:S(2)}) collective-permute-start(f32[1,1536]{1,0:T(1,128)S(1)} %add.21), channel_id=1, source_target_pairs={{0,8},{24,16},{1,9},{25,17},{2,10},{26,18},{3,11},{27,19},{4,12},{... | collective-permute-start | bytes 18440 | tf_op jit(solution)/shard_map/ppermute | solution.py:157
  322.0 2.7 reduce_round.20
  328.4 6.1 %collective-permute-done.48.refs_2_ = f32[256,512]{1,0:T(8,128)S(1)} collective-permute-done((f32[256,512]{1,0:T(8,128)}, f32[256,512]{1,0:T(8,128)S(1)}, u32[]{:S(2)}, u32[]{:S(2)}) %collective-permute-start.48) | collective-permute-done | bytes 524320 | tf_op jit(solution)/shard_map/ppermute | solution.py:490
  337.5 7.0 %collective-permute-start.50 = (f32[256,512]{1,0:T(8,128)}, f32[256,512]{1,0:T(8,128)S(1)}, u32[]{:S(2)}, u32[]{:S(2)}) collective-permute-start(f32[256,512]{1,0:T(8,128)} %get-tuple-element.919.refs_4_), channel_id=1, source_target_pairs={{0,8},{8,0},{16,24},{24,16},{1,9},{9,1},{17,25},{25,17},{2,10},{10... | collective-permute-start | bytes 1572872 | tf_op jit(solution)/shard_map/ppermute | solution.py:490
  345.7 8.0 %collective-permute-done.47 = f32[1,1536]{1,0:T(1,128)S(1)} collective-permute-done((f32[1,1536]{1,0:T(1,128)S(1)}, f32[1,1536]{1,0:T(1,128)S(1)}, u32[]{:S(2)}, u32[]{:S(2)}) %collective-permute-start.47) | collective-permute-done | bytes 6176 | tf_op jit(solution)/shard_map/ppermute | solution.py:157
  359.6 5.7 %collective-permute-done.52.refs_1_ = f32[256,512]{1,0:T(8,128)S(1)} collective-permute-done((f32[256,512]{1,0:T(8,128)}, f32[256,512]{1,0:T(8,128)S(1)}, u32[]{:S(2)}, u32[]{:S(2)}) %collective-permute-start.52) | collective-permute-done | bytes 524320 | tf_op jit(solution)/shard_map/ppermute | solution.py:490
  (163 shorter events, 79.4 us)
Async XLA Ops:
  26.2 28.0 %collective-permute-start.2 = (f32[512,512]{1,0:T(8,128)}, f32[512,512]{1,0:T(8,128)S(1)}, u32[]{:S(2)}, u32[]{:S(2)}) collective-permute-start(f32[512,512]{1,0:T(8,128)} %get-tuple-element.501), channel_id=1, source_target_pairs={{0,2},{1,3},{2,0},{3,1},{4,6},{5,7},{6,4},{7,5},{8,10},{9,11},{10,... | collective-permute-start | bytes 3145736 | tf_op jit(solution)/shard_map/ppermute | solution.py:63
  29.1 25.1 %collective-permute-start.3 = (f32[512,512]{1,0:T(8,128)}, f32[512,512]{1,0:T(8,128)S(1)}, u32[]{:S(2)}, u32[]{:S(2)}) collective-permute-start(f32[512,512]{1,0:T(8,128)} %get-tuple-element.502), channel_id=1, source_target_pairs={{0,4},{1,5},{2,6},{3,7},{4,0},{5,1},{6,2},{7,3},{8,12},{9,13},{10,... | collective-permute-start | bytes 3145736 | tf_op jit(solution)/shard_map/ppermute | solution.py:63
  57.7 20.2 %collective-permute-start.6 = (f32[256,4096]{1,0:T(8,128)S(1)}, f32[256,4096]{1,0:T(8,128)S(1)}, u32[]{:S(2)}, u32[]{:S(2)}) collective-permute-start(f32[256,4096]{1,0:T(8,128)S(1)} %copy-done.22), channel_id=1, source_target_pairs={{0,1},{1,0},{2,3},{3,2},{4,5},{5,4},{6,7},{7,6},{8,9},{9,8},{10,11... | collective-permute-start | bytes 12582920 | tf_op jit(solution)/shard_map/ppermute | solution.py:63
  57.7 40.4 %collective-permute-start.8 = (f32[768,512]{1,0:T(8,128)}, f32[768,512]{1,0:T(8,128)S(1)}, u32[]{:S(2)}, u32[]{:S(2)}) collective-permute-start(f32[768,512]{1,0:T(8,128)} %get-tuple-element.540), channel_id=1, source_target_pairs={{0,2},{1,3},{2,0},{3,1},{4,6},{5,7},{6,4},{7,5},{8,10},{9,11},{10,... | collective-permute-start | bytes 4718600 | tf_op jit(solution)/shard_map/ppermute | solution.py:63
  58.1 19.8 %collective-permute-start.5 = (f32[2,256,512]{2,1,0:T(8,128)S(1)}, f32[2,256,512]{2,1,0:T(8,128)S(1)}, u32[]{:S(2)}, u32[]{:S(2)}) collective-permute-start(f32[2,256,512]{2,1,0:T(8,128)S(1)} %copy-done.23), channel_id=1, source_target_pairs={{0,1},{1,0},{2,3},{3,2},{4,5},{5,4},{6,7},{7,6},{8,9},{9,8},{10,11... | collective-permute-start | bytes 3145736 | tf_op jit(solution)/shard_map/ppermute | solution.py:63
  58.3 39.8 %collective-permute-start.9 = (f32[768,512]{1,0:T(8,128)}, f32[768,512]{1,0:T(8,128)}, u32[]{:S(2)}, u32[]{:S(2)}) collective-permute-start(f32[768,512]{1,0:T(8,128)} %get-tuple-element.584), channel_id=1, source_target_pairs={{0,4},{1,5},{2,6},{3,7},{4,0},{5,1},{6,2},{7,3},{8,12},{9,13},{10,... | collective-permute-start | bytes 4718600 | tf_op jit(solution)/shard_map/ppermute | solution.py:63
  74.3 16.5 %collective-permute-start.4 = (f32[2,8,72,128]{3,2,1,0:T(8,128)}, f32[2,8,72,128]{3,2,1,0:T(8,128)S(1)}, u32[]{:S(2)}, u32[]{:S(2)}) collective-permute-start(f32[2,8,72,128]{3,2,1,0:T(8,128)} %get-tuple-element.581.own_ref), channel_id=1, source_target_pairs={{0,8},{8,16},{16,24},{1,9},{9,17},{17,25},{2,10},{10,18},{18,26},{... | collective-permute-start | bytes 1769480 | tf_op jit(solution)/shard_map/ppermute | solution.py:47
  93.7 18.4 %collective-permute-start.7 = (f32[2,8,72,128]{3,2,1,0:T(8,128)}, f32[2,8,72,128]{3,2,1,0:T(8,128)S(1)}, u32[]{:S(2)}, u32[]{:S(2)}) collective-permute-start(f32[2,8,72,128]{3,2,1,0:T(8,128)} %pass_carry.2), channel_id=1, source_target_pairs={{0,8},{8,16},{16,24},{1,9},{9,17},{17,25},{2,10},{10,18},{18,26},{... | collective-permute-start | bytes 1769480 | tf_op jit(solution)/shard_map/ppermute | solution.py:47
  102.2 38.1 %collective-permute-start.10 = (f32[768,512]{1,0:T(8,128)}, f32[768,512]{1,0:T(8,128)S(1)}, u32[]{:S(2)}, u32[]{:S(2)}) collective-permute-start(f32[768,512]{1,0:T(8,128)} %get-tuple-element.599), channel_id=1, source_target_pairs={{0,2},{1,3},{2,0},{3,1},{4,6},{5,7},{6,4},{7,5},{8,10},{9,11},{10,... | collective-permute-start | bytes 4718600 | tf_op jit(solution)/shard_map/ppermute | solution.py:63
  103.7 32.7 %collective-permute-start.12 = (f32[512,512]{1,0:T(8,128)}, f32[512,512]{1,0:T(8,128)}, u32[]{:S(2)}, u32[]{:S(2)}) collective-permute-start(f32[512,512]{1,0:T(8,128)} %get-tuple-element.640), channel_id=1, source_target_pairs={{0,8},{8,0},{16,24},{24,16},{1,9},{9,1},{17,25},{25,17},{2,10},{10... | collective-permute-start | bytes 3145736 | tf_op jit(solution)/shard_map/ppermute | solution.py:490
  105.2 35.0 %collective-permute-start.11 = (f32[768,512]{1,0:T(8,128)}, f32[768,512]{1,0:T(8,128)}, u32[]{:S(2)}, u32[]{:S(2)}) collective-permute-start(f32[768,512]{1,0:T(8,128)} %get-tuple-element.634), channel_id=1, source_target_pairs={{0,4},{1,5},{2,6},{3,7},{4,0},{5,1},{6,2},{7,3},{8,12},{9,13},{10,... | collective-permute-start | bytes 4718600 | tf_op jit(solution)/shard_map/ppermute | solution.py:63
  132.8 14.8 %collective-permute-start.13 = (f32[2,8,72,128]{3,2,1,0:T(8,128)}, f32[2,8,72,128]{3,2,1,0:T(8,128)}, u32[]{:S(2)}, u32[]{:S(2)}) collective-permute-start(f32[2,8,72,128]{3,2,1,0:T(8,128)} %get-tuple-element.671.own_ref), channel_id=1, source_target_pairs={{8,0},{16,8},{24,16},{9,1},{17,9},{25,17},{10,2},{18,10},{26,18},{... | collective-permute-start | bytes 1769480 | tf_op jit(solution)/shard_map/ppermute | solution.py:47
  145.0 34.1 %collective-permute-start.16 = (f32[768,512]{1,0:T(8,128)}, f32[768,512]{1,0:T(8,128)S(1)}, u32[]{:S(2)}, u32[]{:S(2)}) collective-permute-start(f32[768,512]{1,0:T(8,128)} %get-tuple-element.673), channel_id=1, source_target_pairs={{0,4},{1,5},{2,6},{3,7},{4,0},{5,1},{6,2},{7,3},{8,12},{9,13},{10,... | collective-permute-start | bytes 4718600 | tf_op jit(solution)/shard_map/ppermute | solution.py:63
  145.6 33.8 %collective-permute-start.15 = (f32[768,512]{1,0:T(8,128)}, f32[768,512]{1,0:T(8,128)}, u32[]{:S(2)}, u32[]{:S(2)}) collective-permute-start(f32[768,512]{1,0:T(8,128)} %get-tuple-element.656), channel_id=1, source_target_pairs={{0,2},{1,3},{2,0},{3,1},{4,6},{5,7},{6,4},{7,5},{8,10},{9,11},{10,... | collective-permute-start | bytes 4718600 | tf_op jit(solution)/shard_map/ppermute | solution.py:63
  146.1 8.6 %collective-permute-start.19 = (f32[1,256,512]{2,1,0:T(8,128)}, f32[1,256,512]{2,1,0:T(8,128)S(1)}, u32[]{:S(2)}, u32[]{:S(2)}) collective-permute-start(f32[1,256,512]{2,1,0:T(8,128)} %get-tuple-element.681), channel_id=1, source_target_pairs={{0,1},{1,0},{2,3},{3,2},{4,5},{5,4},{6,7},{7,6},{8,9},{9,8},{10,11... | collective-permute-start | bytes 1572872 | tf_op jit(solution)/shard_map/ppermute | solution.py:63
  146.1 26.3 %collective-permute-start.17 = (f32[512,512]{1,0:T(8,128)}, f32[512,512]{1,0:T(8,128)}, u32[]{:S(2)}, u32[]{:S(2)}) collective-permute-start(f32[512,512]{1,0:T(8,128)} %get-tuple-element.679), channel_id=1, source_target_pairs={{0,8},{8,0},{16,24},{24,16},{1,9},{9,1},{17,25},{25,17},{2,10},{10... | collective-permute-start | bytes 3145736 | tf_op jit(solution)/shard_map/ppermute | solution.py:490
  147.6 24.8 %collective-permute-start.18 = (f32[512,512]{1,0:T(8,128)}, f32[512,512]{1,0:T(8,128)}, u32[]{:S(2)}, u32[]{:S(2)}) collective-permute-start(f32[512,512]{1,0:T(8,128)} %get-tuple-element.701.refs_9_), channel_id=1, source_target_pairs={{8,16},{16,8},{9,17},{17,9},{10,18},{18,10},{11,19},{19,11},{12,20... | collective-permute-start | bytes 3145736 | tf_op jit(solution)/shard_map/ppermute | solution.py:493
  154.7 30.7 %collective-permute-start.14 = (f32[2,8,72,128]{3,2,1,0:T(8,128)}, f32[2,8,72,128]{3,2,1,0:T(8,128)S(1)}, u32[]{:S(2)}, u32[]{:S(2)}) collective-permute-start(f32[2,8,72,128]{3,2,1,0:T(8,128)} %pass_carry.3), channel_id=1, source_target_pairs={{8,0},{16,8},{24,16},{9,1},{17,9},{25,17},{10,2},{18,10},{26,18},{... | collective-permute-start | bytes 1769480 | tf_op jit(solution)/shard_map/ppermute | solution.py:47
  184.8 25.7 %collective-permute-start.21 = (f32[512,512]{1,0:T(8,128)}, f32[512,512]{1,0:T(8,128)}, u32[]{:S(2)}, u32[]{:S(2)}) collective-permute-start(f32[512,512]{1,0:T(8,128)} %get-tuple-element.705), channel_id=1, source_target_pairs={{0,2},{1,3},{2,0},{3,1},{4,6},{5,7},{6,4},{7,5},{8,10},{9,11},{10,... | collective-permute-start | bytes 3145736 | tf_op jit(solution)/shard_map/ppermute | solution.py:63
  185.4 24.1 %collective-permute-start.22 = (f32[512,512]{1,0:T(8,128)}, f32[512,512]{1,0:T(8,128)S(1)}, u32[]{:S(2)}, u32[]{:S(2)}) collective-permute-start(f32[512,512]{1,0:T(8,128)} %get-tuple-element.723), channel_id=1, source_target_pairs={{0,4},{1,5},{2,6},{3,7},{4,0},{5,1},{6,2},{7,3},{8,12},{9,13},{10,... | collective-permute-start | bytes 3145736 | tf_op jit(solution)/shard_map/ppermute | solution.py:63
  187.0 25.3 %collective-permute-start.23 = (f32[512,512]{1,0:T(8,128)}, f32[512,512]{1,0:T(8,128)}, u32[]{:S(2)}, u32[]{:S(2)}) collective-permute-start(f32[512,512]{1,0:T(8,128)} %get-tuple-element.758.refs_11_), channel_id=1, source_target_pairs={{0,8},{8,0},{16,24},{24,16},{1,9},{9,1},{17,25},{25,17},{2,10},{10... | collective-permute-start | bytes 3145736 | tf_op jit(solution)/shard_map/ppermute | solution.py:490
  189.7 22.6 %collective-permute-start.24 = (f32[512,512]{1,0:T(8,128)}, f32[512,512]{1,0:T(8,128)}, u32[]{:S(2)}, u32[]{:S(2)}) collective-permute-start(f32[512,512]{1,0:T(8,128)} %get-tuple-element.756.refs_9_), channel_id=1, source_target_pairs={{8,16},{16,8},{9,17},{17,9},{10,18},{18,10},{11,19},{19,11},{12,20... | collective-permute-start | bytes 3145736 | tf_op jit(solution)/shard_map/ppermute | solution.py:493
  201.9 10.9 %collective-permute-start.25 = (f32[256,1024]{1,0:T(8,128)}, f32[256,1024]{1,0:T(8,128)}, u32[]{:S(2)}, u32[]{:S(2)}) collective-permute-start(f32[256,1024]{1,0:T(8,128)} %get-tuple-element.731), channel_id=1, source_target_pairs={{0,1},{1,0},{2,3},{3,2},{4,5},{5,4},{6,7},{7,6},{8,9},{9,8},{10,11... | collective-permute-start | bytes 3145736 | tf_op jit(solution)/shard_map/ppermute | solution.py:63
  210.5 19.0 %collective-permute-start.20 = (f32[256,2048]{1,0:T(8,128)}, f32[256,2048]{1,0:T(8,128)S(1)}, u32[]{:S(2)}, u32[]{:S(2)}) collective-permute-start(f32[256,2048]{1,0:T(8,128)} %get-tuple-element.722), channel_id=1, source_target_pairs={{0,1},{1,0},{2,3},{3,2},{4,5},{5,4},{6,7},{7,6},{8,9},{9,8},{10,11... | collective-permute-start | bytes 6291464 | tf_op jit(solution)/shard_map/ppermute | solution.py:63
  222.4 25.4 %collective-permute-start.30 = (f32[512,512]{1,0:T(8,128)}, f32[512,512]{1,0:T(8,128)}, u32[]{:S(2)}, u32[]{:S(2)}) collective-permute-start(f32[512,512]{1,0:T(8,128)} %get-tuple-element.812.refs_11_), channel_id=1, source_target_pairs={{0,8},{8,0},{16,24},{24,16},{1,9},{9,1},{17,25},{25,17},{2,10},{10... | collective-permute-start | bytes 3145736 | tf_op jit(solution)/shard_map/ppermute | solution.py:490
  226.1 21.7 %collective-permute-start.31 = (f32[512,512]{1,0:T(8,128)}, f32[512,512]{1,0:T(8,128)}, u32[]{:S(2)}, u32[]{:S(2)}) collective-permute-start(f32[512,512]{1,0:T(8,128)} %get-tuple-element.810.refs_9_), channel_id=1, source_target_pairs={{8,16},{16,8},{9,17},{17,9},{10,18},{18,10},{11,19},{19,11},{12,20... | collective-permute-start | bytes 3145736 | tf_op jit(solution)/shard_map/ppermute | solution.py:493
  227.7 17.8 %collective-permute-start.29 = (f32[384,512]{1,0:T(8,128)}, f32[384,512]{1,0:T(8,128)}, u32[]{:S(2)}, u32[]{:S(2)}) collective-permute-start(f32[384,512]{1,0:T(8,128)} %get-tuple-element.791), channel_id=1, source_target_pairs={{0,4},{1,5},{2,6},{3,7},{4,0},{5,1},{6,2},{7,3},{8,12},{9,13},{10,... | collective-permute-start | bytes 2359304 | tf_op jit(solution)/shard_map/ppermute | solution.py:63
  228.0 18.7 %collective-permute-start.28 = (f32[384,512]{1,0:T(8,128)}, f32[384,512]{1,0:T(8,128)}, u32[]{:S(2)}, u32[]{:S(2)}) collective-permute-start(f32[384,512]{1,0:T(8,128)} %get-tuple-element.761), channel_id=1, source_target_pairs={{0,2},{1,3},{2,0},{3,1},{4,6},{5,7},{6,4},{7,5},{8,10},{9,11},{10,... | collective-permute-start | bytes 2359304 | tf_op jit(solution)/shard_map/ppermute | solution.py:63
  253.0 24.4 %collective-permute-start.35 = (f32[512,512]{1,0:T(8,128)}, f32[512,512]{1,0:T(8,128)S(1)}, u32[]{:S(2)}, u32[]{:S(2)}) collective-permute-start(f32[512,512]{1,0:T(8,128)} %get-tuple-element.849.refs_11_), channel_id=1, source_target_pairs={{0,8},{8,0},{16,24},{24,16},{1,9},{9,1},{17,25},{25,17},{2,10},{10... | collective-permute-start | bytes 3145736 | tf_op jit(solution)/shard_map/ppermute | solution.py:490
  256.7 20.7 %collective-permute-start.36 = (f32[512,512]{1,0:T(8,128)}, f32[512,512]{1,0:T(8,128)S(1)}, u32[]{:S(2)}, u32[]{:S(2)}) collective-permute-start(f32[512,512]{1,0:T(8,128)} %get-tuple-element.847.refs_9_), channel_id=1, source_target_pairs={{8,16},{16,8},{9,17},{17,9},{10,18},{18,10},{11,19},{19,11},{12,20... | collective-permute-start | bytes 3145736 | tf_op jit(solution)/shard_map/ppermute | solution.py:493
  257.4 19.2 %collective-permute-start.33 = (f32[384,512]{1,0:T(8,128)}, f32[384,512]{1,0:T(8,128)S(1)}, u32[]{:S(2)}, u32[]{:S(2)}) collective-permute-start(f32[384,512]{1,0:T(8,128)} %get-tuple-element.816), channel_id=1, source_target_pairs={{0,2},{1,3},{2,0},{3,1},{4,6},{5,7},{6,4},{7,5},{8,10},{9,11},{10,... | collective-permute-start | bytes 2359304 | tf_op jit(solution)/shard_map/ppermute | solution.py:63
  259.0 17.7 %collective-permute-start.34 = (f32[384,512]{1,0:T(8,128)}, f32[384,512]{1,0:T(8,128)S(1)}, u32[]{:S(2)}, u32[]{:S(2)}) collective-permute-start(f32[384,512]{1,0:T(8,128)} %get-tuple-element.829), channel_id=1, source_target_pairs={{0,4},{1,5},{2,6},{3,7},{4,0},{5,1},{6,2},{7,3},{8,12},{9,13},{10,... | collective-permute-start | bytes 2359304 | tf_op jit(solution)/shard_map/ppermute | solution.py:63
  260.7 13.5 %collective-permute-start.27 = (f32[2,1536]{1,0:T(2,128)S(1)}, f32[2,1536]{1,0:T(2,128)S(1)}, u32[]{:S(2)}, u32[]{:S(2)}) collective-permute-start(f32[2,1536]{1,0:T(2,128)S(1)} %get-tuple-element.790), channel_id=1, source_target_pairs={{0,2},{1,3},{2,0},{3,1},{4,6},{5,7},{6,4},{7,5},{8,10},{9,11},{10,... | collective-permute-start | bytes 36872 | tf_op jit(solution)/shard_map/ppermute | solution.py:63
  281.2 23.6 %collective-permute-start.40 = (f32[512,512]{1,0:T(8,128)}, f32[512,512]{1,0:T(8,128)S(1)}, u32[]{:S(2)}, u32[]{:S(2)}) collective-permute-start(f32[512,512]{1,0:T(8,128)} %get-tuple-element.876.refs_11_), channel_id=1, source_target_pairs={{0,8},{8,0},{16,24},{24,16},{1,9},{9,1},{17,25},{25,17},{2,10},{10... | collective-permute-start | bytes 3145736 | tf_op jit(solution)/shard_map/ppermute | solution.py:490
  284.9 18.6 %collective-permute-start.39 = (f32[384,512]{1,0:T(8,128)}, f32[384,512]{1,0:T(8,128)S(1)}, u32[]{:S(2)}, u32[]{:S(2)}) collective-permute-start(f32[384,512]{1,0:T(8,128)} %get-tuple-element.856), channel_id=1, source_target_pairs={{0,4},{1,5},{2,6},{3,7},{4,0},{5,1},{6,2},{7,3},{8,12},{9,13},{10,... | collective-permute-start | bytes 2359304 | tf_op jit(solution)/shard_map/ppermute | solution.py:63
  288.1 16.7 %collective-permute-start.38 = (f32[384,512]{1,0:T(8,128)}, f32[384,512]{1,0:T(8,128)S(1)}, u32[]{:S(2)}, u32[]{:S(2)}) collective-permute-start(f32[384,512]{1,0:T(8,128)} %get-tuple-element.852), channel_id=1, source_target_pairs={{0,2},{1,3},{2,0},{3,1},{4,6},{5,7},{6,4},{7,5},{8,10},{9,11},{10,... | collective-permute-start | bytes 2359304 | tf_op jit(solution)/shard_map/ppermute | solution.py:63
  289.6 13.9 %collective-permute-start.41 = (f32[256,512]{1,0:T(8,128)}, f32[256,512]{1,0:T(8,128)S(1)}, u32[]{:S(2)}, u32[]{:S(2)}) collective-permute-start(f32[256,512]{1,0:T(8,128)} %get-tuple-element.874.refs_9_), channel_id=1, source_target_pairs={{8,16},{16,8},{9,17},{17,9},{10,18},{18,10},{11,19},{19,11},{12,20... | collective-permute-start | bytes 1572872 | tf_op jit(solution)/shard_map/ppermute | solution.py:493
  290.3 13.2 %collective-permute-start.32 = (f32[1,1536]{1,0:T(1,128)S(1)}, f32[1,1536]{1,0:T(1,128)S(1)}, u32[]{:S(2)}, u32[]{:S(2)}) collective-permute-start(f32[1,1536]{1,0:T(1,128)S(1)} %get-tuple-element.828), channel_id=1, source_target_pairs={{0,4},{1,5},{2,6},{3,7},{4,0},{5,1},{6,2},{7,3},{8,12},{9,13},{10,... | collective-permute-start | bytes 18440 | tf_op jit(solution)/shard_map/ppermute | solution.py:63
  308.5 13.6 %collective-permute-start.45 = (f32[256,512]{1,0:T(8,128)}, f32[256,512]{1,0:T(8,128)S(1)}, u32[]{:S(2)}, u32[]{:S(2)}) collective-permute-start(f32[256,512]{1,0:T(8,128)} %get-tuple-element.897.refs_9_), channel_id=1, source_target_pairs={{0,8},{8,0},{16,24},{24,16},{1,9},{9,1},{17,25},{25,17},{2,10},{10... | collective-permute-start | bytes 1572872 | tf_op jit(solution)/shard_map/ppermute | solution.py:490
  310.1 12.0 %collective-permute-start.46 = (f32[256,512]{1,0:T(8,128)}, f32[256,512]{1,0:T(8,128)S(1)}, u32[]{:S(2)}, u32[]{:S(2)}) collective-permute-start(f32[256,512]{1,0:T(8,128)} %get-tuple-element.895.refs_7_), channel_id=1, source_target_pairs={{8,16},{16,8},{9,17},{17,9},{10,18},{18,10},{11,19},{19,11},{12,20... | collective-permute-start | bytes 1572872 | tf_op jit(solution)/shard_map/ppermute | solution.py:493
  310.8 11.2 %collective-permute-start.44 = (f32[128,512]{1,0:T(8,128)}, f32[128,512]{1,0:T(8,128)S(1)}, u32[]{:S(2)}, u32[]{:S(2)}) collective-permute-start(f32[128,512]{1,0:T(8,128)} %get-tuple-element.882), channel_id=1, source_target_pairs={{0,4},{1,5},{2,6},{3,7},{4,0},{5,1},{6,2},{7,3},{8,12},{9,13},{10,... | collective-permute-start | bytes 786440 | tf_op jit(solution)/shard_map/ppermute | solution.py:63
  315.4 6.6 %collective-permute-start.43 = (f32[128,512]{1,0:T(8,128)}, f32[128,512]{1,0:T(8,128)S(1)}, u32[]{:S(2)}, u32[]{:S(2)}) collective-permute-start(f32[128,512]{1,0:T(8,128)} %get-tuple-element.878), channel_id=1, source_target_pairs={{0,2},{1,3},{2,0},{3,1},{4,6},{5,7},{6,4},{7,5},{8,10},{9,11},{10,... | collective-permute-start | bytes 786440 | tf_op jit(solution)/shard_map/ppermute | solution.py:63
  324.7 9.7 %collective-permute-start.48 = (f32[256,512]{1,0:T(8,128)}, f32[256,512]{1,0:T(8,128)S(1)}, u32[]{:S(2)}, u32[]{:S(2)}) collective-permute-start(f32[256,512]{1,0:T(8,128)} %get-tuple-element.909.refs_5_), channel_id=1, source_target_pairs={{0,8},{8,0},{16,24},{24,16},{1,9},{9,1},{17,25},{25,17},{2,10},{10... | collective-permute-start | bytes 1572872 | tf_op jit(solution)/shard_map/ppermute | solution.py:490
  327.0 7.5 %collective-permute-start.49 = (f32[256,512]{1,0:T(8,128)}, f32[256,512]{1,0:T(8,128)S(1)}, u32[]{:S(2)}, u32[]{:S(2)}) collective-permute-start(f32[256,512]{1,0:T(8,128)} %get-tuple-element.907.refs_3_), channel_id=1, source_target_pairs={{8,16},{16,8},{9,17},{17,9},{10,18},{18,10},{11,19},{19,11},{12,20... | collective-permute-start | bytes 1572872 | tf_op jit(solution)/shard_map/ppermute | solution.py:493
  336.8 16.9 %collective-permute-start.51 = (f32[256,512]{1,0:T(8,128)}, f32[256,512]{1,0:T(8,128)S(1)}, u32[]{:S(2)}, u32[]{:S(2)}) collective-permute-start(f32[256,512]{1,0:T(8,128)} %get-tuple-element.917.refs_2_), channel_id=1, source_target_pairs={{8,16},{16,8},{9,17},{17,9},{10,18},{18,10},{11,19},{19,11},{12,20... | collective-permute-start | bytes 1572872 | tf_op jit(solution)/shard_map/ppermute | solution.py:493
  337.5 16.2 %collective-permute-start.50 = (f32[256,512]{1,0:T(8,128)}, f32[256,512]{1,0:T(8,128)S(1)}, u32[]{:S(2)}, u32[]{:S(2)}) collective-permute-start(f32[256,512]{1,0:T(8,128)} %get-tuple-element.919.refs_4_), channel_id=1, source_target_pairs={{0,8},{8,0},{16,24},{24,16},{1,9},{9,1},{17,25},{25,17},{2,10},{10... | collective-permute-start | bytes 1572872 | tf_op jit(solution)/shard_map/ppermute | solution.py:490
  344.5 9.2 %collective-permute-start.47 = (f32[1,1536]{1,0:T(1,128)S(1)}, f32[1,1536]{1,0:T(1,128)S(1)}, u32[]{:S(2)}, u32[]{:S(2)}) collective-permute-start(f32[1,1536]{1,0:T(1,128)S(1)} %add.23), channel_id=1, source_target_pairs={{8,0},{16,24},{9,1},{17,25},{10,2},{18,26},{11,3},{19,27},{12,4},{... | collective-permute-start | bytes 18440 | tf_op jit(solution)/shard_map/ppermute | solution.py:157
  355.8 9.5 %collective-permute-start.52 = (f32[256,512]{1,0:T(8,128)}, f32[256,512]{1,0:T(8,128)S(1)}, u32[]{:S(2)}, u32[]{:S(2)}) collective-permute-start(f32[256,512]{1,0:T(8,128)} %get-tuple-element.925.refs_2_), channel_id=1, source_target_pairs={{0,8},{8,0},{16,24},{24,16},{1,9},{9,1},{17,25},{25,17},{2,10},{10... | collective-permute-start | bytes 1572872 | tf_op jit(solution)/shard_map/ppermute | solution.py:490
  (32 other events, 249.0 us)
